TPU v7x, 32 devices: a whole 2x2x4 slice. The times are simulated.
32 devices in a mesh: dp: 8 (over y, x, core), mp: 4 (over z).
Axes of the slice: x: 2, y: 2, z: 4, core: 2. Of those that a mesh axis runs over, the one named last changes fastest.
Arguments:
- tokens: bfloat16 [8, 2048, 512], P('dp', 'mp'), may hold values from -6 to 6
- cotangent: bfloat16 [8, 2048, 512], P('dp', 'mp'), may hold values from -6 to 6
- lengths: int32 [8], P('dp'), may hold values from 512 to 2048, as said below
- owners: int32 [96], replicated, may hold values from 0 to 7, as said below
- w_qkv: bfloat16 [512, 1536], P(None, 'mp'), may hold values from -0.25 to 0.25
- w_out: bfloat16 [512, 512], P('mp'), may hold values from -0.75 to 0.75
- w_in: bfloat16 [512, 2048], P(None, 'mp'), may hold values from -0.25 to 0.25
- w_down: bfloat16 [2048, 512], P('mp'), may hold values from -0.125 to 0.125
- master: float32 [192, 256, 128], P('dp', 'mp'), may hold values from -0.75 to 0.75
- first_moment: float32 [192, 256, 128], P('dp', 'mp'), may hold values from -28 to 28
- second_moment: float32 [192, 256, 128], P('dp', 'mp'), may hold values from 49.152 to 409.6
- norm_gains: float32 [2, 512], replicated, may hold values from 0.25 to 1.75
- norm_biases: float32 [2, 512], replicated, may hold values from -1.5 to 1.5
- norm_first: float32 [4, 512], replicated, may hold values from -64 to 64
- norm_second: float32 [4, 512], replicated, may hold values from 262.144 to 2064.384
Outputs:
- outputs: bfloat16 [8, 2048, 512], P('dp', 'mp')
- tokens_grad: float32 [8, 2048, 512], P('dp', 'mp')
- first_new: float32 [192, 256, 128], P('dp', 'mp')
- second_new: float32 [192, 256, 128], P('dp', 'mp')
- master_new: float32 [192, 256, 128], P('dp', 'mp')
- new_qkv: bfloat16 [512, 1536], P(None, 'mp')
- new_out: bfloat16 [512, 512], P('mp')
- new_in: bfloat16 [512, 2048], P(None, 'mp')
- new_down: bfloat16 [2048, 512], P('mp')
- norm_first_new: float32 [4, 512], replicated
- norm_second_new: float32 [4, 512], replicated
- norm_new: float32 [4, 512], replicated
Inputs may be any that keep to these rules, and one draw needn't show every extreme that they name: `lengths`: one sequence in every draw has all 2048 positions valid. `owners`: no owner holds more than 24 blocks and one owner holds exactly 24.
All inputs are finite; a program needn't handle non-finite values.
Results may differ from a plain program's by a relative error of at most 0.0097.
Values may be sent and summed in bfloat16 or wider, within the bound.
No kernel may reach another device: no remote copies, remote signals or barrier semaphores. Data moves between devices by JAX's collectives and lax.ppermute only.
A program may use at most 128 MiB of HBM per device.

v0:
```python
import jax
import jax.numpy as jnp
from jax import lax
from jax.sharding import PartitionSpec as P

HEAD = 64
BAND = 30
MARGIN = 32
QBLOCK = 512
STEP = 10


highest = lax.Precision.HIGHEST
learn_rate = 0.1
norm_rate = 0.3
decay_rate = 0.1
beta_one = 0.9
beta_two = 0.95
adam_epsilon = 1e-08
norm_epsilon = 1e-05


def layer_norm(values, scale_gain, shift_bias):
    row_mean = jnp.mean(values, axis=-1, keepdims=True)
    centered = values - row_mean
    variance = jnp.mean(centered * centered, axis=-1, keepdims=True)
    return centered * lax.rsqrt(variance + norm_epsilon) * scale_gain + shift_bias


def far_field(query, keys, values, key_mask, valid_count):
    masked = key_mask[:, None, None]
    feat_keys = (jax.nn.elu(keys) + 1.0) * masked
    tanh_keys = jnp.tanh(keys) * masked
    feat_query = jax.nn.elu(query) + 1.0
    tanh_query = jnp.tanh(query)
    state_one = jnp.einsum("lhe,lhf->hef", feat_keys, values, precision=highest)
    normaliser = jnp.sum(feat_keys, axis=0)
    denominator = jnp.einsum("lhe,he->lh", feat_query, normaliser, precision=highest)
    first_part = (
        jnp.einsum("lhe,hef->lhf", feat_query, state_one, precision=highest)
        / denominator[:, :, None]
    )
    state_two = jnp.einsum("lhe,lhf->hef", tanh_keys, values, precision=highest) / valid_count
    return first_part + jnp.einsum("lhe,hef->lhf", tanh_query, state_two, precision=highest)


def band_mask(anchor, length, seq_len, block):
    query_pos = anchor + jnp.arange(block, dtype=jnp.int32)
    key_pos = anchor - MARGIN + jnp.arange(block + 2 * MARGIN, dtype=jnp.int32)
    offsets = query_pos[:, None] - key_pos[None, :]
    inside = (key_pos >= 0) & (key_pos < seq_len)
    return (
        (jnp.abs(offsets) <= BAND)
        & inside[None, :]
        & ((key_pos < length)[None, :] | (offsets == 0))
    )


def cross(left, right):
    return lax.dot_general(
        left, right, (((0,), (0,)), ((), ())), preferred_element_type=jnp.float32
    )


def against(left, right):
    return lax.dot_general(
        left, right, (((1,), (1,)), ((), ())), preferred_element_type=jnp.float32
    )


def block_scores(query_blk, key_blk, anchor, length, seq_len, block):
    scores = (
        jnp.einsum("qhe,khe->hqk", query_blk, key_blk, preferred_element_type=jnp.float32) * 0.125
    )
    return jnp.where(band_mask(anchor, length, seq_len, block)[None], scores, -1e30)


def near_forward(query, key_pad, value_pad, length, seq_len, base, block):
    rows = query.shape[0]
    span = block + 2 * MARGIN

    def window(anchor):
        query_blk = lax.dynamic_slice_in_dim(query, anchor, block, 0)
        key_blk = lax.dynamic_slice_in_dim(key_pad, anchor, span, 0)
        value_blk = lax.dynamic_slice_in_dim(value_pad, anchor, span, 0)
        scores = block_scores(query_blk, key_blk, base + anchor, length, seq_len, block)
        row_max = jnp.max(scores, axis=-1, keepdims=True)
        exponent = jnp.exp(scores - row_max)
        summed = jnp.sum(exponent, axis=-1, keepdims=True)
        attn_probs = (exponent / summed).astype(jnp.bfloat16)
        result = jnp.einsum(
            "hqk,khe->qhe", attn_probs, value_blk, preferred_element_type=jnp.float32
        )
        return (result, (row_max + jnp.log(summed))[:, :, 0])

    anchors = jnp.arange(rows // block, dtype=jnp.int32) * block
    results, log_sums = lax.map(window, anchors)
    return (results.reshape(query.shape), log_sums)


def near_backward(query, key_pad, value_pad, grad_ctx, log_sums, length, seq_len, base, block):
    rows = query.shape[0]
    span = block + 2 * MARGIN
    padded_shape = key_pad.shape

    def visit(block_index, running):
        grad_query, grad_keys, grad_values = running
        anchor = block_index * block
        query_blk = lax.dynamic_slice_in_dim(query, anchor, block, 0)
        key_blk = lax.dynamic_slice_in_dim(key_pad, anchor, span, 0)
        value_blk = lax.dynamic_slice_in_dim(value_pad, anchor, span, 0)
        grad_blk = lax.dynamic_slice_in_dim(grad_ctx, anchor, block, 0)
        scores = block_scores(query_blk, key_blk, base + anchor, length, seq_len, block)
        attn_probs = jnp.exp(scores - log_sums[block_index][:, :, None])
        probs_low = attn_probs.astype(jnp.bfloat16)
        grad_probs = jnp.einsum(
            "qhe,khe->hqk", grad_blk, value_blk, preferred_element_type=jnp.float32
        )
        row_dot = jnp.sum(attn_probs * grad_probs, axis=-1, keepdims=True)
        grad_scores = (attn_probs * (grad_probs - row_dot)).astype(jnp.bfloat16)
        query_part = (
            jnp.einsum("hqk,khe->qhe", grad_scores, key_blk, preferred_element_type=jnp.float32)
            * 0.125
        )
        key_part = (
            jnp.einsum("hqk,qhe->khe", grad_scores, query_blk, preferred_element_type=jnp.float32)
            * 0.125
        )
        value_part = jnp.einsum(
            "hqk,qhe->khe", probs_low, grad_blk, preferred_element_type=jnp.float32
        )
        grad_query = lax.dynamic_update_slice_in_dim(grad_query, query_part, anchor, 0)
        grad_keys = lax.dynamic_update_slice_in_dim(
            grad_keys, lax.dynamic_slice_in_dim(grad_keys, anchor, span, 0) + key_part, anchor, 0
        )
        grad_values = lax.dynamic_update_slice_in_dim(
            grad_values,
            lax.dynamic_slice_in_dim(grad_values, anchor, span, 0) + value_part,
            anchor,
            0,
        )
        return (grad_query, grad_keys, grad_values)

    initial = (
        jnp.zeros(query.shape, jnp.float32),
        jnp.zeros(padded_shape, jnp.float32),
        jnp.zeros(padded_shape, jnp.float32),
    )
    return lax.fori_loop(0, rows // block, visit, initial)


def per_device(
    tokens,
    cotangent,
    lengths,
    owners,
    w_qkv,
    w_out,
    w_in,
    w_down,
    master,
    first_moment,
    second_moment,
    norm_gains,
    norm_biases,
    norm_first,
    norm_second,
):
    inputs = tokens[0].astype(jnp.float32)
    local_rows = inputs.shape[0]
    groups = lax.axis_size("mp")
    seq_len = local_rows * groups
    length = lengths[0]
    base = lax.axis_index("mp") * local_rows
    row_pos = base + jnp.arange(local_rows, dtype=jnp.int32)
    grad_output = cotangent[0].astype(jnp.float32) * (row_pos < length).astype(jnp.float32)[:, None]
    head_cols = w_out.shape[0]
    heads_dev = head_cols // HEAD
    valid_count = length.astype(jnp.float32)
    grad_mix = grad_output.astype(jnp.bfloat16)
    norm_one, norm_one_back = jax.vjp(layer_norm, inputs, norm_gains[0], norm_biases[0])
    first_local = norm_one.astype(jnp.bfloat16)
    first_all = lax.all_gather(first_local, "mp", axis=0, tiled=True)
    projected = jnp.dot(first_all, w_qkv, preferred_element_type=jnp.float32).astype(jnp.bfloat16)
    query = projected[:, :head_cols].reshape(seq_len, heads_dev, HEAD)
    keys = projected[:, head_cols : 2 * head_cols].reshape(seq_len, heads_dev, HEAD)
    values = projected[:, 2 * head_cols :].reshape(seq_len, heads_dev, HEAD)
    key_mask = (jnp.arange(seq_len, dtype=jnp.int32) < length).astype(jnp.float32)
    key_pad = jnp.pad(keys, ((MARGIN, MARGIN), (0, 0), (0, 0)))
    value_pad = jnp.pad(values, ((MARGIN, MARGIN), (0, 0), (0, 0)))
    near_part, log_sums = near_forward(query, key_pad, value_pad, length, seq_len, 0, QBLOCK)

    def far_local(query_f, keys_f, values_f):
        return far_field(query_f, keys_f, values_f, key_mask, valid_count)

    far_part, far_back = jax.vjp(
        far_local, query.astype(jnp.float32), keys.astype(jnp.float32), values.astype(jnp.float32)
    )
    context = (near_part + far_part).reshape(seq_len, head_cols).astype(jnp.bfloat16)
    second_in = inputs + lax.psum_scatter(
        jnp.dot(context, w_out, preferred_element_type=jnp.float32),
        "mp",
        scatter_dimension=0,
        tiled=True,
    )
    norm_two, norm_two_back = jax.vjp(layer_norm, second_in, norm_gains[1], norm_biases[1])
    second_local = norm_two.astype(jnp.bfloat16)
    second_all = lax.all_gather(second_local, "mp", axis=0, tiled=True)
    pre_act = jnp.dot(second_all, w_in, preferred_element_type=jnp.float32)
    activated, gelu_back = jax.vjp(jax.nn.gelu, pre_act)
    hidden = activated.astype(jnp.bfloat16)
    result = second_in + lax.psum_scatter(
        jnp.dot(hidden, w_down, preferred_element_type=jnp.float32),
        "mp",
        scatter_dimension=0,
        tiled=True,
    )
    portion = lax.all_gather(grad_mix, "mp", axis=0, tiled=True)
    grad_hidden = against(portion, w_down)
    grad_hidden, grad_down = (grad_hidden, cross(hidden, portion))
    grad_up = gelu_back(grad_hidden)[0].astype(jnp.bfloat16)
    grad_norm_two = lax.psum_scatter(against(grad_up, w_in), "mp", scatter_dimension=0, tiled=True)
    grad_inw = cross(second_all, grad_up)
    grad_second, grad_gain_two, grad_bias_two = norm_two_back(grad_norm_two)
    grad_second = grad_output + grad_second
    grad_attn = grad_second.astype(jnp.bfloat16)
    portion = lax.all_gather(grad_attn, "mp", axis=0, tiled=True)
    grad_context = against(portion, w_out)
    grad_context, grad_outw = (grad_context, cross(context, portion))
    grad_context = grad_context.astype(jnp.bfloat16).reshape(seq_len, heads_dev, HEAD)
    near_query, near_keys_pad, near_values_pad = near_backward(
        query, key_pad, value_pad, grad_context, log_sums, length, seq_len, 0, QBLOCK
    )
    near_keys = near_keys_pad[MARGIN : MARGIN + seq_len]
    near_values = near_values_pad[MARGIN : MARGIN + seq_len]
    far_query, far_keys, far_values = far_back(grad_context.astype(jnp.float32))
    grad_proj = jnp.concatenate(
        [
            (near_query + far_query).reshape(seq_len, head_cols),
            (near_keys + far_keys).reshape(seq_len, head_cols),
            (near_values + far_values).reshape(seq_len, head_cols),
        ],
        axis=1,
    ).astype(jnp.bfloat16)
    grad_norm_one = lax.psum_scatter(
        against(grad_proj, w_qkv), "mp", scatter_dimension=0, tiled=True
    )
    grad_qkvw = cross(first_all, grad_proj)
    block_rows = master.shape[1]
    grad_blocks = jnp.concatenate(
        [
            grad_qkvw.reshape(-1, 128),
            grad_outw.reshape(-1, 128),
            grad_inw.reshape(-1, 128),
            grad_down.reshape(-1, 128),
        ],
        axis=0,
    ).reshape(owners.shape[0], block_rows, 128)
    grad_first, grad_gain_one, grad_bias_one = norm_one_back(grad_norm_one)
    tokens_grad = grad_second + grad_first
    corr_one = 1.0 - beta_one**STEP
    corr_two = 1.0 - beta_two**STEP
    norm_grad = lax.psum(
        jnp.stack([grad_gain_one, grad_bias_one, grad_gain_two, grad_bias_two]), ("dp", "mp")
    )
    norm_params = jnp.stack([norm_gains[0], norm_biases[0], norm_gains[1], norm_biases[1]])
    norm_first_new = beta_one * norm_first + (1.0 - beta_one) * norm_grad
    norm_second_new = beta_two * norm_second + (1.0 - beta_two) * norm_grad * norm_grad
    norm_new = norm_params - norm_rate * (
        norm_first_new / corr_one / (jnp.sqrt(norm_second_new / corr_two) + adam_epsilon)
    )
    block_rows = master.shape[1]
    capacity = master.shape[0]
    blocks_all = owners.shape[0]
    dp_count = lax.axis_size("dp")
    onehot = (owners[:, None] == jnp.arange(dp_count, dtype=jnp.int32)[None, :]).astype(jnp.int32)
    slot_index = jnp.sum(jnp.cumsum(onehot, axis=0) * onehot, axis=1) - 1
    slot_rows = owners * capacity + slot_index
    my_rows = lax.axis_index("dp") * capacity + jnp.arange(capacity, dtype=jnp.int32)
    matches = slot_rows[None, :] == my_rows[:, None]
    filled = jnp.any(matches, axis=1)
    picked = jnp.sum(
        jnp.where(matches, jnp.arange(blocks_all, dtype=jnp.int32)[None, :], 0), axis=1
    )
    summed = lax.psum(grad_blocks, "dp")
    owned = summed[picked]
    first_upd = beta_one * first_moment + (1.0 - beta_one) * owned
    second_upd = beta_two * second_moment + (1.0 - beta_two) * owned * owned
    master_upd = master - learn_rate * (
        first_upd / corr_one / (jnp.sqrt(second_upd / corr_two) + adam_epsilon)
        + decay_rate * master
    )
    keep_mask = filled[:, None, None]
    first_new = jnp.where(keep_mask, first_upd, first_moment)
    second_new = jnp.where(keep_mask, second_upd, second_moment)
    master_new = jnp.where(keep_mask, master_upd, master)
    gathered = lax.all_gather(master_new.astype(jnp.bfloat16), "dp", axis=0, tiled=True)
    fresh = gathered[slot_rows].reshape(blocks_all * block_rows, 128)
    rows_q = w_qkv.size // 128
    rows_o = w_out.size // 128
    rows_i = w_in.size // 128
    new_qkv = fresh[:rows_q].reshape(w_qkv.shape)
    new_out = fresh[rows_q : rows_q + rows_o].reshape(w_out.shape)
    new_in = fresh[rows_q + rows_o : rows_q + rows_o + rows_i].reshape(w_in.shape)
    new_down = fresh[rows_q + rows_o + rows_i :].reshape(w_down.shape)
    return (
        result.astype(jnp.bfloat16)[None],
        tokens_grad[None],
        first_new,
        second_new,
        master_new,
        new_qkv,
        new_out,
        new_in,
        new_down,
        norm_first_new,
        norm_second_new,
        norm_new,
    )


def solution(mesh):
    return jax.shard_map(
        per_device,
        mesh=mesh,
        in_specs=(
            P("dp", "mp", None),
            P("dp", "mp", None),
            P("dp"),
            P(),
            P(None, "mp"),
            P("mp", None),
            P(None, "mp"),
            P("mp", None),
            P("dp", "mp", None),
            P("dp", "mp", None),
            P("dp", "mp", None),
            P(),
            P(),
            P(),
            P(),
        ),
        out_specs=(
            P("dp", "mp", None),
            P("dp", "mp", None),
            P("dp", "mp", None),
            P("dp", "mp", None),
            P("dp", "mp", None),
            P(None, "mp"),
            P("mp", None),
            P(None, "mp"),
            P("mp", None),
            P(),
            P(),
            P(),
        ),
        check_vma=False,
    )
```

profile of v0, /device:TPU:0, one launch (start us, length us, event | category | flops | bytes accessed | tf_op | source)
XLA Modules:
  0.0 863.9 jit_solution(8731403079336793505)
XLA Ops:
  13.6 48.1 %all-gather.6.cloned.1.call-done = bf16[2048,512]{1,0:T(8,128)(2,1)} async-done(((bf16[512,512]{1,0:T(8,128)(2,1)}), bf16[2048,512]{1,0:T(8,128)(2,1)}) %all-gather.6.cloned.1.call-update) | async-done | bytes 2097168 | tf_op jit(solution)/shard_map/all_gather | solution.py:183
  70.3 66.4 %while.33 = (s32[]{:T(128)}, f32[4,512,2,64]{1,0,3,2:T(4,128)}, f32[4,2,512]{2,1,0:T(2,128)}, s32[4]{0:T(128)S(1)}, bf16[2112,2,64]{0,2,1:T(8,128)(2,1)S(1)}, /*...) while((s32[]{:T(128)}, f32[4,512,2,64]{1,0,3,2:T(4,128)}, ...), condition=%wide.region_5.6_spmd, body=%wide.region_2.5_spmd.sunk | while | flops 160140160 | bytes 10071036 | solution.py:97
  80.8 6.1 dynamic_update_slice.52
  97.3 6.1 dynamic_update_slice.52
  113.9 6.1 dynamic_update_slice.52
  130.5 6.1 dynamic_update_slice.52
  136.6 3.9 convolution_bitcast_fusion.3
  140.5 3.0 reshape.404
  143.5 2.8 fusion.70
  151.1 73.6 %reduce-scatter.5.cloned.1.call-done = f32[512,512]{1,0:T(8,128)} async-done(((f32[2048,512]{1,0:T(8,128)}), f32[512,512]{1,0:T(8,128)}) %reduce-scatter.5.cloned.1.call-update) | async-done | bytes 1048592 | tf_op jit(solution)/shard_map/reduce_scatter | solution.py:200
  227.5 45.9 %all-gather.10.cloned.1.call-done = bf16[2048,512]{1,0:T(8,128)(2,1)} async-done(((bf16[512,512]{1,0:T(8,128)(2,1)}), bf16[2048,512]{1,0:T(8,128)(2,1)}) %all-gather.10.cloned.1.call-update) | async-done | bytes 2097168 | tf_op jit(solution)/shard_map/all_gather | solution.py:218
  273.4 4.8 fusion.198
  278.3 41.9 %all-gather.8.cloned.1.call-done = bf16[2048,512]{1,0:T(8,128)(2,1)} async-done(((bf16[512,512]{1,0:T(8,128)(2,1)}), bf16[2048,512]{1,0:T(8,128)(2,1)}) %all-gather.8.cloned.1.call-update) | async-done | bytes 2097168 | tf_op jit(solution)/shard_map/all_gather | solution.py:208
  320.2 6.9 fusion.53
  328.4 3.3 fusion.199
  331.8 5.9 fusion.187
  337.8 69.6 %reduce-scatter.9.cloned.1.call-done = f32[512,512]{1,0:T(8,128)} async-done(((f32[2048,512]{1,0:T(8,128)}), f32[512,512]{1,0:T(8,128)}) %reduce-scatter.9.cloned.1.call-update) | async-done | bytes 1048592 | tf_op jit(solution)/shard_map/reduce_scatter | solution.py:222
  409.6 77.2 %reduce-scatter.7.cloned.1.call-done = f32[512,512]{1,0:T(8,128)} async-done(((f32[2048,512]{1,0:T(8,128)}), f32[512,512]{1,0:T(8,128)}) %reduce-scatter.7.cloned.1.call-update) | async-done | bytes 1048592 | tf_op jit(solution)/shard_map/reduce_scatter | solution.py:212
  492.4 3.5 fusion.201
  497.0 4.8 fusion.186
  502.9 34.4 %all-gather.12.cloned.1.call-done = bf16[2048,512]{1,0:T(8,128)(2,1)} async-done(((bf16[512,512]{1,0:T(8,128)(2,1)}), bf16[2048,512]{1,0:T(8,128)(2,1)}) %all-gather.12.cloned.1.call-update) | async-done | bytes 2097168 | tf_op jit(solution)/shard_map/all_gather | solution.py:227
  540.1 3.8 fusion.111
  543.9 3.4 fusion.128
  549.5 50.2 %while.34 = (s32[]{:T(128)}, f32[2048,2,64]{0,2,1:T(8,128)}, f32[2112,2,64]{0,2,1:T(8,128)}, f32[2112,2,64]{0,2,1:T(8,128)S(1)}, bf16[2112,2,64]{0,2,1:T(8,128)(...) while((s32[]{:T(128)}, f32[2048,2,64]{0,2,1:T(8,128)}, ...), condition=%wide.region_16.17_spmd, body=%wide.region_14.16_spmd.sunk | while | flops 385149824 | bytes 24149072 | solution.py:149
  619.4 3.3 pad_maximum_fusion
  624.1 66.9 %all-reduce.4.cloned.1.call-done = f32[96,64,128]{2,1,0:T(8,128)} async-done(((f32[96,64,128]{2,1,0:T(8,128)}), f32[96,64,128]{2,1,0:T(8,128)}) %all-reduce.4.cloned.1.call-update) | async-done | bytes 3145744 | tf_op jit(solution)/shard_map/psum | solution.py:285
  693.5 4.2 fusion.189
  698.0 4.5 fusion.140
  702.5 27.7 %all-gather.14.cloned.1.call-done = bf16[192,64,128]{2,1,0:T(8,128)(2,1)} async-done(((bf16[24,64,128]{2,1,0:T(8,128)(2,1)}), bf16[192,64,128]{2,1,0:T(8,128)(2,1)}) %all-gather.14.cloned.1.call-update) | async-done | bytes 3145744 | tf_op jit(solution)/shard_map/all_gather | solution.py:297
  730.3 3.9 gather_fusion.1
  740.4 68.8 %reduce-scatter.11.cloned.1.call-done = f32[512,512]{1,0:T(8,128)} async-done(((f32[2048,512]{1,0:T(8,128)}), f32[512,512]{1,0:T(8,128)}) %reduce-scatter.11.cloned.1.call-update) | async-done | bytes 1048592 | tf_op jit(solution)/shard_map/reduce_scatter | solution.py:245
  812.8 40.8 %psum.15 = f32[4,512]{1,0:T(4,128)S(1)} all-reduce(f32[4,512]{1,0:T(4,128)S(1)} %pad_maximum_fusion.4), channel_id=1, replica_groups=mesh['dp'=8,'mp'=4] {'dp','mp'}, use_global_device_ids=true, to_apply=%region_30.31 | all-reduce | flops 2048 | bytes 16384 | tf_op jit(solution)/shard_map/psum | solution.py:263
  (311 shorter events, 150.3 us)
Async XLA Ops:
  7.2 313.0 %copy-start = (bf16[512,512]{1,0:T(8,128)(2,1)S(1)}, bf16[512,512]{1,0:T(8,128)(2,1)}, u32[]{:S(2)}) copy-start(bf16[512,512]{1,0:T(8,128)(2,1)} %param.25) | copy-start | bytes 1572868
  7.2 54.4 %copy-start.48 = (bf16[512,384]{1,0:T(8,128)(2,1)S(1)}, bf16[512,384]{1,0:T(8,128)(2,1)}, u32[]{:S(2)}) copy-start(bf16[512,384]{1,0:T(8,128)(2,1)} %param.23) | copy-start | bytes 1179652
  7.2 54.4 %all-gather.6.cloned.1.call-start = ((), (), s32[]{:S(2)}) async-start(), calls=%async_computation.4 | async-start | bytes 2621440 | tf_op jit(solution)/shard_map/all_gather | solution.py:183
  10.7 215.7 %copy-start.35 = (f32[1,512]{1,0:T(1,128)}, f32[1,512]{1,0:T(1,128)S(1)}, u32[]{:S(2)}) copy-start(f32[1,512]{1,0:T(1,128)S(1)} %get-tuple-element.443) | copy-start | bytes 6148
  10.7 476.1 %copy-start.25 = (f32[1,512]{1,0:T(1,128)}, f32[1,512]{1,0:T(1,128)S(1)}, u32[]{:S(2)}) copy-start(f32[1,512]{1,0:T(1,128)S(1)} %get-tuple-element.434) | copy-start | bytes 6148
  12.8 211.9 %reduce-scatter.5.cloned.1.call-start = ((), (), s32[]{:S(2)}) async-start(), calls=%async_computation.5 | async-start | bytes 5242880 | tf_op jit(solution)/shard_map/reduce_scatter | solution.py:200
  66.9 69.8 %copy-start.53 = (f32[2,64,64]{2,1,0:T(8,128)}, f32[2,64,64]{2,1,0:T(8,128)S(1)}, u32[]{:S(2)}) copy-start(f32[2,64,64]{2,1,0:T(8,128)S(1)} %fusion.126) | copy-start | bytes 98308
  69.5 74.0 %copy-start.39 = (f32[2,1,2048]{2,0,1:T(2,128)}, f32[2,1,2048]{2,0,1:T(2,128)S(1)}, u32[]{:S(2)}) copy-start(f32[2,1,2048]{2,0,1:T(2,128)S(1)} %copy.76) | copy-start | bytes 49156
  70.3 73.2 %copy-start.55 = (f32[2,64,64]{2,1,0:T(8,128)}, f32[2,64,64]{2,1,0:T(8,128)S(1)}, u32[]{:S(2)}) copy-start(f32[2,64,64]{2,1,0:T(8,128)S(1)} %fusion.90) | copy-start | bytes 98308
  149.1 75.7 %copy-start.2 = (bf16[1,512,512]{2,1,0:T(8,128)(2,1)S(1)}, bf16[1,512,512]{2,1,0:T(8,128)(2,1)}, u32[]{:S(2)}) copy-start(bf16[1,512,512]{2,1,0:T(8,128)(2,1)} %param.19) | copy-start | bytes 1572868
  149.1 124.4 %all-gather.10.cloned.1.call-start = ((), (), s32[]{:S(2)}) async-start(), calls=%async_computation.8 | async-start | bytes 2621440 | tf_op jit(solution)/shard_map/all_gather | solution.py:218
  150.1 339.5 %copy-start.29 = (f32[512]{0:T(512)}, f32[512]{0:T(512)S(1)}, u32[]{:S(2)}) copy-start(f32[512]{0:T(512)S(1)} %fusion.167) | copy-start | bytes 6148
  151.1 122.4 %copy-start.20 = (bf16[512,512]{1,0:T(8,128)(2,1)S(1)}, bf16[512,512]{1,0:T(8,128)(2,1)}, u32[]{:S(2)}) copy-start(bf16[512,512]{1,0:T(8,128)(2,1)} %param.26) | copy-start | bytes 1572868
  151.1 169.1 %all-gather.8.cloned.1.call-start = ((), (), s32[]{:S(2)}) async-start(), calls=%async_computation.6 | async-start | bytes 2621440 | tf_op jit(solution)/shard_map/all_gather | solution.py:208
  227.5 179.9 %reduce-scatter.9.cloned.1.call-start = ((), (), s32[]{:S(2)}) async-start(), calls=%async_computation.9 | async-start | bytes 5242880 | tf_op jit(solution)/shard_map/reduce_scatter | solution.py:222
  331.8 155.1 %reduce-scatter.7.cloned.1.call-start = ((), (), s32[]{:S(2)}) async-start(), calls=%async_computation.7 | async-start | bytes 5242880 | tf_op jit(solution)/shard_map/reduce_scatter | solution.py:212
  337.7 199.6 %all-gather.12.cloned.1.call-start = ((), (), s32[]{:S(2)}) async-start(), calls=%async_computation.10 | async-start | bytes 2621440 | tf_op jit(solution)/shard_map/all_gather | solution.py:227
  409.6 80.0 %copy-start.11 = (bf16[1,512,512]{2,1,0:T(8,128)(2,1)S(1)}, bf16[1,512,512]{2,1,0:T(8,128)(2,1)}, u32[]{:S(2)}) copy-start(bf16[1,512,512]{2,1,0:T(8,128)(2,1)} %param.20) | copy-start | bytes 1572868
  490.7 200.3 %all-reduce.4.cloned.1.call-start = ((), (), s32[]{:S(2)}) async-start(), calls=%async_computation.12 | async-start | bytes 6291456 | tf_op jit(solution)/shard_map/psum | solution.py:285
  622.7 107.6 %all-gather.14.cloned.1.call-start = ((), (), s32[]{:S(2)}) async-start(), calls=%async_computation.13 | async-start | bytes 3538944 | tf_op jit(solution)/shard_map/all_gather | solution.py:297
  697.7 111.5 %reduce-scatter.11.cloned.1.call-start = ((), (), s32[]{:S(2)}) async-start(), calls=%async_computation.11 | async-start | bytes 5242880 | tf_op jit(solution)/shard_map/reduce_scatter | solution.py:245
  737.1 73.7 %copy-start.32 = (f32[512]{0:T(512)S(1)}, f32[512]{0:T(512)}, u32[]{:S(2)}) copy-start(f32[512]{0:T(512)} %copy-done.31) | copy-start | bytes 6148
  737.2 73.7 %copy-start.28 = (f32[512]{0:T(512)S(1)}, f32[512]{0:T(512)}, u32[]{:S(2)}) copy-start(f32[512]{0:T(512)} %copy-done.27) | copy-start | bytes 6148
  738.3 74.5 %copy-start.44 = (f32[512]{0:T(512)S(1)}, f32[512]{0:T(512)}, u32[]{:S(2)}) copy-start(f32[512]{0:T(512)} %get-tuple-element.363) | copy-start | bytes 6148
  738.3 74.5 %copy-start.45 = (f32[512]{0:T(512)S(1)}, f32[512]{0:T(512)}, u32[]{:S(2)}) copy-start(f32[512]{0:T(512)} %get-tuple-element.368) | copy-start | bytes 6148
  738.3 115.3 %copy-start.26 = (f32[1,512]{1,0:T(1,128)S(1)}, f32[1,512]{1,0:T(1,128)}, u32[]{:S(2)}) copy-start(f32[1,512]{1,0:T(1,128)} %copy-done.25) | copy-start | bytes 6148
  738.3 115.3 %copy-start.34 = (f32[1,512]{1,0:T(1,128)S(1)}, f32[1,512]{1,0:T(1,128)}, u32[]{:S(2)}) copy-start(f32[1,512]{1,0:T(1,128)} %copy-done.33) | copy-start | bytes 6148
  738.3 115.3 %copy-start.36 = (f32[1,512]{1,0:T(1,128)S(1)}, f32[1,512]{1,0:T(1,128)}, u32[]{:S(2)}) copy-start(f32[1,512]{1,0:T(1,128)} %copy-done.35) | copy-start | bytes 6148
  738.3 115.3 %copy-start.42 = (f32[4,512]{1,0:T(4,128)S(1)}, f32[4,512]{1,0:T(4,128)}, u32[]{:S(2)}) copy-start(f32[4,512]{1,0:T(4,128)} %param.33) | copy-start | bytes 24580
  738.3 115.3 %copy-start.43 = (f32[4,512]{1,0:T(4,128)S(1)}, f32[4,512]{1,0:T(4,128)}, u32[]{:S(2)}) copy-start(f32[4,512]{1,0:T(4,128)} %param.32) | copy-start | bytes 24580
  739.3 115.0 %copy-start.30 = (f32[512]{0:T(512)S(1)}, f32[512]{0:T(512)}, u32[]{:S(2)}) copy-start(f32[512]{0:T(512)} %copy-done.29) | copy-start | bytes 6148
  739.3 115.0 %copy-start.38 = (f32[512]{0:T(512)S(1)}, f32[512]{0:T(512)}, u32[]{:S(2)}) copy-start(f32[512]{0:T(512)} %copy-done.37) | copy-start | bytes 6148
  (39 other events, 450.0 us)
Sparse Core Ops, SparseCore 0:
  13.0 48.6 all-gather.5
  149.2 75.4 reduce-scatter.4
  227.0 46.4 all-gather.9
  275.5 44.6 all-gather.7
  331.9 75.4 reduce-scatter.8
  409.5 77.2 reduce-scatter.6
  490.8 46.4 all-gather.11
  622.8 68.1 all-reduce.3
  697.9 32.3 all-gather.13
  732.4 76.7 reduce-scatter.10
where the time goes:
time: 876 us; the launch traced here: 864 us
  waiting for transfers between devices  554 us (63%)
  matrix products  115 us (13%)
  local copies, waits for them, and re-layouts  69.2 us (8%)
  other arithmetic  51.3 us (6%)
  blocking collectives  40.8 us (5%)
  loops' own time  16.3 us (2%)
  between operations  15.9 us (2%)
    reduce_scatter x1, waiting for transfers between devices, per_device(): lax.psum_scatter(jnp.dot(hidden, w_down, preferred_element_type=jnp.float...  77.2 us
    reduce_scatter x1, waiting for transfers between devices, per_device(): lax.psum_scatter(jnp.dot(context, w_out, preferred_element_type=jnp.float...  73.6 us
    reduce_scatter x1, waiting for transfers between devices, per_device(): lax.psum_scatter(against(grad_up, w_in), 'mp', scatter_dimension=0, tiled...  69.6 us
    reduce_scatter x1, waiting for transfers between devices, per_device(): lax.psum_scatter(against(grad_proj, w_qkv), 'mp', scatter_dimension=0, ti...  68.8 us
    psum x1, waiting for transfers between devices, per_device(): summed = lax.psum(grad_blocks, 'dp')  66.9 us
    all_gather x1, waiting for transfers between devices, per_device(): first_all = lax.all_gather(first_local, 'mp', axis=0, tiled=True)  48.1 us
    all_gather x1, waiting for transfers between devices, per_device(): portion = lax.all_gather(grad_mix, 'mp', axis=0, tiled=True)  45.9 us
    all_gather x1, waiting for transfers between devices, per_device(): second_all = lax.all_gather(second_local, 'mp', axis=0, tiled=True)  41.9 us
  transfers between devices with their start and end apart: 10, of which 10 were waited for; matrix products, arithmetic and copies ran while one was open for 5% of the time, Pallas kernels for 0%

commit v1 on v0

v1 whole, which is shorter than its diff:
```python
import functools

import jax
import jax.numpy as jnp
from jax import lax
from jax.experimental import pallas as pl
from jax.experimental.pallas import tpu as pltpu
from jax.sharding import PartitionSpec as P

HEAD = 64
BAND = 30
STEP = 10
HALO = 64
EDGE = 32
QB = 64
WIN = 128
PAIR = 128
STATE = 144

learn_rate = 0.1
norm_rate = 0.3
decay_rate = 0.1
beta_one = 0.9
beta_two = 0.95
adam_epsilon = 1e-08
norm_epsilon = 1e-05
GELU_C = 0.7978845608028654
GELU_A = 0.044715

f32 = jnp.float32
bf16 = jnp.bfloat16

VM = pl.BlockSpec(memory_space=pltpu.VMEM)
SM = pl.BlockSpec(memory_space=pltpu.SMEM)
ANY = pl.BlockSpec(memory_space=pl.ANY)


def call(body, outs, in_specs, scratch, flops, moved, vmem=48):
    return pl.pallas_call(
        body,
        out_shape=tuple(jax.ShapeDtypeStruct(s, d) for s, d in outs),
        in_specs=in_specs,
        out_specs=tuple(VM for _ in outs),
        scratch_shapes=scratch,
        compiler_params=pltpu.CompilerParams(vmem_limit_bytes=vmem << 20),
        cost_estimate=pl.CostEstimate(flops=flops, bytes_accessed=moved, transcendentals=0),
    )


def dot(a, b):
    return jnp.dot(a, b, preferred_element_type=f32)


def dot_nt(a, b):
    return lax.dot_general(a, b, (((1,), (1,)), ((), ())), preferred_element_type=f32)


def dot_tn(a, b):
    return lax.dot_general(a, b, (((0,), (0,)), ((), ())), preferred_element_type=f32)


def normalize(x):
    mean = jnp.mean(x, axis=-1, keepdims=True)
    cen = x - mean
    var = jnp.mean(cen * cen, axis=-1, keepdims=True)
    rstd = lax.rsqrt(var + norm_epsilon)
    return cen * rstd, rstd


def same_head(n=PAIR):
    r = lax.broadcasted_iota(jnp.int32, (n, n), 0)
    c = lax.broadcasted_iota(jnp.int32, (n, n), 1)
    return (r < HEAD) == (c < HEAD)


def pack_state(s1, s2, z):
    both = jnp.where(same_head(), s1, pltpu.roll(s2, HEAD, 1))
    hi = z.astype(bf16).astype(f32)
    row = lax.broadcasted_iota(jnp.int32, (16, PAIR), 0)
    tail = jnp.where(row == 0, hi, jnp.where(row == 1, z - hi, 0.0))
    return both.astype(bf16), tail.astype(bf16)


def unpack_state(refs, g):
    tot = refs[0][g].astype(f32)
    for r in refs[1:]:
        tot = tot + r[g].astype(f32)
    both = tot[:PAIR]
    diag = same_head()
    s1 = jnp.where(diag, both, 0.0)
    s2 = jnp.where(diag, pltpu.roll(both, HEAD, 1), 0.0)
    z = tot[PAIR : PAIR + 1] + tot[PAIR + 1 : PAIR + 2]
    return s1, s2, z


def split_dot(a, ones):
    hi, lo = two(a)
    return dot(hi, ones) + dot(lo, ones)


def two(a):
    hi = a.astype(bf16)
    return hi, (a - hi.astype(f32)).astype(bf16)


def phi(v):
    low = jnp.exp(jnp.minimum(v, 0.0))
    return jnp.where(v > 0, v + 1.0, low), jnp.where(v > 0, 1.0, low)


def band_parts():
    r = lax.broadcasted_iota(jnp.int32, (2 * QB, WIN), 0) % QB
    c = lax.broadcasted_iota(jnp.int32, (2 * QB, WIN), 1)
    off = r + EDGE - c
    return (jnp.abs(off) <= BAND), off == 0, c[:1]


def stacked(rows):
    lane = lax.broadcasted_iota(jnp.int32, (1, PAIR), 1)
    first = (lane < HEAD).astype(f32).astype(bf16)
    second = (lane >= HEAD).astype(f32).astype(bf16)
    return jnp.concatenate([rows * first, rows * second], axis=0)


def unstack(both):
    lane = lax.broadcasted_iota(jnp.int32, (QB, PAIR), 1)
    return jnp.where(lane < HEAD, both[:QB], both[QB:])


def softmax_block(qs, kw, mask):
    scores = jnp.where(mask, dot_nt(qs, kw) * 0.125, -1e30)
    top = jnp.max(scores, axis=-1, keepdims=True)
    ex = jnp.exp(scores - top)
    return ex / jnp.sum(ex, axis=-1, keepdims=True)


def fetch_pieces(meta, own, oth, lo, rows, place, sem):
    groups = own.shape[1]
    core = meta[2]
    copies = []
    for pq in range(4):
        for buf, row, half in ((own, meta[3 + pq], core), (oth, meta[7 + pq], 1 - core)):
            for g in range(groups):
                src = buf.at[row, g, pl.ds(lo, rows), :]
                copies.append(pltpu.make_async_copy(src, place(g, half * 4 + pq), sem))
    for c in copies:
        c.start()
    return copies


def qkv_body(meta, tok, left, right, gains, biases, own, oth, qkv_o, a1_o, st_o, w_o, a1e, sem):
    rows = tok.shape[0]
    groups = own.shape[1]
    pr = own.shape[2]
    copies = fetch_pieces(
        meta, own, oth, 0, pr,
        lambda g, p: w_o.at[g, pl.ds(pl.multiple_of(p * pr, pr), pr), :], sem,
    )
    gain, bias = gains[0:1, :], biases[0:1, :]

    def ln(x):
        return (normalize(x.astype(f32))[0] * gain + bias).astype(bf16)

    a1e[0:HALO, :] = ln(left[...])
    a1e[HALO + rows :, :] = ln(right[...])

    def chunk(i, _):
        at = pl.ds(pl.multiple_of(i * 64, 64), 64)
        val = ln(tok[at, :])
        a1_o[at, :] = val
        a1e[pl.ds(pl.multiple_of(i * 64 + HALO, 64), 64), :] = val
        return 0

    lax.fori_loop(0, rows // 64, chunk, 0)
    for c in copies:
        c.wait()
    length, base = meta[0], meta[1]
    pos = base + lax.broadcasted_iota(jnp.int32, (rows, 1), 0)
    valid = (pos < length).astype(f32)
    for g in range(groups):
        qkv_o[g] = dot(a1e[...], w_o[g]).astype(bf16)
        keys = qkv_o[g, HALO : HALO + rows, PAIR : 2 * PAIR].astype(f32)
        vals = qkv_o[g, HALO : HALO + rows, 2 * PAIR :]
        feat = phi(keys)[0] * valid
        z = jnp.sum(feat, axis=0, keepdims=True)
        fhi, flo = two(feat)
        thi, tlo = two(jnp.tanh(keys) * valid)
        s1 = dot_tn(fhi, vals) + dot_tn(flo, vals)
        s2 = dot_tn(thi, vals) + dot_tn(tlo, vals)
        st_o[g, :PAIR, :], st_o[g, PAIR:, :] = pack_state(s1, s2, z)


def near_body(meta, qkv, near_o):
    groups = qkv.shape[0]
    rows = near_o.shape[0]
    length, base = meta[0], meta[1]
    band, diag, lane = band_parts()

    def block(b, _):
        at = b * QB
        kpos = base + at - EDGE + lane
        mask = band & (((kpos >= 0) & (kpos < length)) | diag)
        q_at = pl.ds(pl.multiple_of(at + HALO, QB), QB)
        w_at = pl.ds(pl.multiple_of(at + HALO - EDGE, EDGE), WIN)
        for g in range(groups):
            qs = stacked(qkv[g, q_at, 0:PAIR])
            p = softmax_block(qs, qkv[g, w_at, PAIR : 2 * PAIR], mask)
            res = dot(p.astype(bf16), qkv[g, w_at, 2 * PAIR :])
            near_o[pl.ds(pl.multiple_of(at, QB), QB), g * PAIR : (g + 1) * PAIR] = unstack(res)
        return 0

    lax.fori_loop(0, rows // QB, block, 0)


def main_body(
    meta, near, qkv, s0, s1, s2, s3, tok, cot, gains, biases, own, oth,
    out_o, do_o, dx2_o, ctx_o, a2_o, dm_o, hid_o, du_o, dctx_o, dqf_o, dst_o, ng_o, wout_o,
    w_in, w_down, x2, u, dh, acc, da2, far1, inv, dnum, phq, thq, sem,
):
    groups = own.shape[1]
    rows, width = tok.shape
    pr, orow = 64 * own.shape[2] // 144, own.shape[2] // 9
    length, base = meta[0], meta[1]
    copies = fetch_pieces(
        meta, own, oth, 2 * pr, orow,
        lambda g, p: wout_o.at[pl.ds(pl.multiple_of(g * 8 * orow + p * orow, orow), orow), :], sem.at[0],
    )
    later = fetch_pieces(
        meta, own, oth, 0, pr,
        lambda g, p: w_in.at[g, pl.ds(pl.multiple_of(p * pr, pr), pr), :], sem.at[1],
    )
    later += fetch_pieces(
        meta, own, oth, pr, pr,
        lambda g, p: w_down.at[g, pl.ds(pl.multiple_of(p * pr, pr), pr), :], sem.at[2],
    )
    rlen = 1.0 / length.astype(f32)
    gain, bias = gains[1:2, :], biases[1:2, :]
    ones = same_head().astype(f32).astype(bf16)
    states = [unpack_state((s0, s1, s2, s3), g) for g in range(groups)]
    cr = 128

    def far_chunk(i, _):
        at = pl.ds(pl.multiple_of(i * cr, cr), cr)
        q_at = pl.ds(pl.multiple_of(i * cr + HALO, HALO), cr)
        for g in range(groups):
            cols = slice(g * PAIR, (g + 1) * PAIR)
            st1, st2, z = states[g]
            q = qkv[g, q_at, 0:PAIR].astype(f32)
            ph = phi(q)[0]
            phi_hi, phi_lo = two(ph)
            th_hi, th_lo = two(jnp.tanh(q))
            s1_hi, s1_lo = two(st1)
            s2_hi, s2_lo = two(st2)
            phq[at, cols] = phi_hi
            thq[at, cols] = th_hi
            rec = 1.0 / split_dot(ph * z, ones)
            part = (dot(phi_hi, s1_hi) + dot(phi_hi, s1_lo) + dot(phi_lo, s1_hi)) * rec
            part2 = dot(th_hi, s2_hi) + dot(th_hi, s2_lo) + dot(th_lo, s2_hi)
            inv[at, cols] = rec
            far1[at, cols] = part
            full = near[at, cols] + (part + part2 * rlen)
            ctx_o[at, cols] = full.astype(bf16)
        pos = base + i * cr + lax.broadcasted_iota(jnp.int32, (cr, 1), 0)
        dm_o[at, :] = (cot[at, :].astype(f32) * (pos < length).astype(f32)).astype(bf16)
        return 0

    lax.fori_loop(0, rows // cr, far_chunk, 0)
    for c in copies:
        c.wait()
    x2[...] = dot(ctx_o[...], wout_o[...])

    def norm_chunk(i, _):
        at = pl.ds(pl.multiple_of(i * 32, 32), 32)
        val = x2[at, :] + tok[at, :].astype(f32)
        x2[at, :] = val
        a2_o[at, :] = (normalize(val)[0] * gain + bias).astype(bf16)
        return 0

    lax.fori_loop(0, rows // 32, norm_chunk, 0)
    for c in later:
        c.wait()
    for g in range(groups):
        u[...] = dot(a2_o[...], w_in[g])
        dh[...] = dot_nt(dm_o[...], w_down[g])

        def act(i, _, g=g):
            at = pl.ds(pl.multiple_of(i * 16, 16), 16)
            v = u[at, :]
            sq = v * v
            t = jnp.tanh(GELU_C * v * (1.0 + GELU_A * sq))
            half = 0.5 * (1.0 + t)
            hid_o[g, at, :] = (v * half).astype(bf16)
            slope = half + 0.5 * v * (1.0 - t * t) * (GELU_C * (1.0 + 3.0 * GELU_A * sq))
            du_o[g, at, :] = (dh[at, :] * slope).astype(bf16)
            return 0

        lax.fori_loop(0, rows // 16, act, 0)
        if g == 0:
            acc[...] = dot(hid_o[g], w_down[g])
            da2[...] = dot_nt(du_o[g], w_in[g])
        else:
            acc[...] += dot(hid_o[g], w_down[g])
            da2[...] += dot_nt(du_o[g], w_in[g])

    def back_chunk(i, carry):
        dg, db = carry
        at = pl.ds(pl.multiple_of(i * 32, 32), 32)
        val = x2[at, :]
        out_o[at, :] = (val + acc[at, :]).astype(bf16)
        xh, rstd = normalize(val)
        d = da2[at, :]
        dg = dg + jnp.sum(d * xh, axis=0, keepdims=True)
        db = db + jnp.sum(d, axis=0, keepdims=True)
        e = d * gain
        m1 = jnp.mean(e, axis=-1, keepdims=True)
        m2 = jnp.mean(e * xh, axis=-1, keepdims=True)
        dx = dm_o[at, :].astype(f32) + rstd * (e - m1 - xh * m2)
        dx2_o[at, :] = dx
        do_o[at, :] = dx.astype(bf16)
        return dg, db

    zero = jnp.zeros((1, width), f32)
    dg, db = lax.fori_loop(0, rows // 32, back_chunk, (zero, zero))
    ng_o[0:1, :] = dg
    ng_o[1:2, :] = db
    dctx_o[...] = dot_nt(do_o[...], wout_o[...]).astype(bf16)

    def far_back(i, carry):
        at = pl.ds(pl.multiple_of(i * cr, cr), cr)
        q_at = pl.ds(pl.multiple_of(i * cr + HALO, HALO), cr)
        out = []
        for g in range(groups):
            cols = slice(g * PAIR, (g + 1) * PAIR)
            st1, st2, z = states[g]
            q = qkv[g, q_at, 0:PAIR].astype(f32)
            slope = phi(q)[1]
            th = thq[at, cols].astype(f32)
            dc = dctx_o[at, cols]
            dcf = dc.astype(f32)
            rec = inv[at, cols]
            dn = (dcf * rec).astype(bf16)
            dnum[at, cols] = dn
            dden = -split_dot(dcf * far1[at, cols], ones) * rec
            out.append(carry[g] + jnp.sum(phq[at, cols].astype(f32) * dden, axis=0, keepdims=True))
            dphi = dot_nt(dn, st1.astype(bf16)) + dden * z
            dth = dot_nt(dc, st2.astype(bf16)) * rlen
            dqf_o[at, cols] = dphi * slope + dth * (1.0 - th * th)
        return tuple(out)

    none = jnp.zeros((1, PAIR), f32)
    dz = lax.fori_loop(0, rows // cr, far_back, (none,) * groups)
    for g in range(groups):
        cols = slice(g * PAIR, (g + 1) * PAIR)
        d1 = dot_tn(phq[:, cols], dnum[:, cols])
        d2 = dot_tn(thq[:, cols], dctx_o[:, cols]) * rlen
        dst_o[g, :PAIR, :], dst_o[g, PAIR:, :] = pack_state(d1, d2, dz[g])


def put_halves(core, ref, g, lo, grad):
    n, width = grad.shape
    tiles = grad.reshape(n // 16, 2, 8, width)
    for h in range(2):
        half = tiles[:, h].reshape(n // 2, width).astype(ref.dtype)
        ref[h ^ core, g, lo : lo + n // 2, :] = half


def grads_body(meta, ctx, do, a2, dm, hid, du, g_o):
    core = meta[2]
    groups, rows, width = hid.shape
    n_out = ctx.shape[1] // groups
    for g in range(groups):
        put_halves(core, g_o, g, 0, dot_tn(ctx[:, g * n_out : (g + 1) * n_out], do[...]))
        put_halves(core, g_o, g, n_out // 2, dot_tn(a2[...], du[g]))
        put_halves(core, g_o, g, n_out // 2 + width // 2, dot_tn(hid[g], dm[...]))


def near_back_body(meta, qkv, dctx, do_l, do_r, wout, dqf, dq_o, dk_o, dv_o, dce, dqe, dke, dve):
    groups = qkv.shape[0]
    rows = dctx.shape[0]
    length, base = meta[0], meta[1]
    band, diag, lane = band_parts()
    dce[0:EDGE, :] = dot_nt(do_l[...], wout[...]).astype(bf16)
    dce[EDGE : EDGE + rows, :] = dctx[...]
    dce[EDGE + rows :, :] = dot_nt(do_r[...], wout[...]).astype(bf16)
    dke[...] = jnp.zeros(dke.shape, f32)
    dve[...] = jnp.zeros(dve.shape, f32)

    def block(b, _):
        at = b * QB
        kpos = base + at - HALO + lane
        mask = band & (((kpos >= 0) & (kpos < length)) | diag)
        c_at = pl.ds(pl.multiple_of(at, QB), QB)
        q_at = pl.ds(pl.multiple_of(at + EDGE, EDGE), QB)
        w_at = pl.ds(pl.multiple_of(at, QB), WIN)
        for g in range(groups):
            cols = slice(g * PAIR, (g + 1) * PAIR)
            qs = stacked(qkv[g, q_at, 0:PAIR])
            kw = qkv[g, w_at, PAIR : 2 * PAIR]
            p = softmax_block(qs, kw, mask)
            ds_ = stacked(dce[c_at, cols])
            dp = dot_nt(ds_, qkv[g, w_at, 2 * PAIR :])
            row = jnp.sum(p * dp, axis=-1, keepdims=True)
            dsc = (p * (dp - row)).astype(bf16)
            dqe[c_at, cols] = unstack(dot(dsc, kw))
            dke[w_at, cols] += dot_tn(dsc, qs)
            dve[w_at, cols] += dot_tn(p.astype(bf16), ds_)
        return 0

    lax.fori_loop(0, rows // QB + 1, block, 0)
    dq_o[...] = (dqe[EDGE : EDGE + rows, :] * 0.125 + dqf[...]).astype(bf16)
    dk_o[...] = dke[HALO : HALO + rows, :] * 0.125
    dv_o[...] = dve[HALO : HALO + rows, :]


def last_body(
    meta, qkv, dq, dkn, dvn, s0, s1, s2, s3, wqkv, a1, tok, dx2, gains, ng2,
    tg_o, gq_o, ng_o, dproj, da1, flat, pseudo, ngs,
):
    groups = qkv.shape[0]
    rows, width = tok.shape
    length, base, core = meta[0], meta[1], meta[2]
    gain = gains[0:1, :]
    cr = 128
    states = [unpack_state((s0, s1, s2, s3), g) for g in range(groups)]

    def far_chunk(i, _):
        at = pl.ds(pl.multiple_of(i * cr, cr), cr)
        e_at = pl.ds(pl.multiple_of(i * cr + HALO, HALO), cr)
        pos = base + i * cr + lax.broadcasted_iota(jnp.int32, (cr, 1), 0)
        valid = (pos < length).astype(f32)
        for g in range(groups):
            cols = slice(g * PAIR, (g + 1) * PAIR)
            d1, d2, dz = states[g]
            d1, d2 = d1.astype(bf16), d2.astype(bf16)
            k = qkv[g, e_at, PAIR : 2 * PAIR].astype(f32)
            v = qkv[g, e_at, 2 * PAIR :]
            ph, slope = phi(k)
            th = jnp.tanh(k)
            dk = (dot_nt(v, d1) + dz) * slope + dot_nt(v, d2) * (1.0 - th * th)
            dv = dot((ph * valid).astype(bf16), d1) + dot((th * valid).astype(bf16), d2)
            dproj[g, at, 0:PAIR] = dq[at, cols]
            dproj[g, at, PAIR : 2 * PAIR] = (dkn[at, cols] + dk * valid).astype(bf16)
            dproj[g, at, 2 * PAIR :] = (dvn[at, cols] + dv).astype(bf16)
        return 0

    lax.fori_loop(0, rows // cr, far_chunk, 0)
    n_flat = 3 * width
    for g in range(groups):
        grad = dot_tn(a1[...], dproj[g])
        for part in range(3):
            flat[pl.ds(part, width, stride=3), :] = grad[:, part * PAIR : (part + 1) * PAIR]
        for j in range(4):
            pseudo[:, j * 128 : (j + 1) * 128] = flat[pl.ds(j, n_flat // 4, stride=4), :]
        put_halves(core, gq_o, g, 0, pseudo[...])
        if g == 0:
            da1[...] = dot_nt(dproj[g], wqkv[g])
        else:
            da1[...] += dot_nt(dproj[g], wqkv[g])

    def back_chunk(i, carry):
        dg, db = carry
        at = pl.ds(pl.multiple_of(i * 32, 32), 32)
        xh, rstd = normalize(tok[at, :].astype(f32))
        d = da1[at, :]
        dg = dg + jnp.sum(d * xh, axis=0, keepdims=True)
        db = db + jnp.sum(d, axis=0, keepdims=True)
        e = d * gain
        m1 = jnp.mean(e, axis=-1, keepdims=True)
        m2 = jnp.mean(e * xh, axis=-1, keepdims=True)
        tg_o[at, :] = dx2[at, :] + rstd * (e - m1 - xh * m2)
        return dg, db

    zero = jnp.zeros((1, width), f32)
    dg, db = lax.fori_loop(0, rows // 32, back_chunk, (zero, zero))
    for k, val in enumerate((dg, db, ng2[0:1, :], ng2[1:2, :])):
        for j in range(width // 128):
            at = k * (width // 128) + j
            ngs[at : at + 1, :] = val[:, j * 128 : (j + 1) * 128]
    n = ngs.shape[0]
    hi = ngs[...].astype(bf16)
    ng_o[0:n, :] = hi
    ng_o[n:, :] = (ngs[...] - hi.astype(f32)).astype(bf16)


def route_body(blocks, zq, zm, send_o, piece, ngs):
    n_ng = 2 * ngs.shape[0]
    nq = zq.shape[1] - n_ng
    nm = zm.shape[1]
    dests, per, _ = send_o.shape
    caps = (per - n_ng) // 8
    src = range(zq.shape[0])
    piece[0:nq, :] = sum(zq[s, 0:nq, :].astype(f32) for s in src)
    piece[nq:, :] = sum(zm[s].astype(f32) for s in src)
    half = n_ng // 2
    ngs[...] = sum(zq[s, nq : nq + half, :].astype(f32) + zq[s, nq + half :, :].astype(f32) for s in src)
    hi = ngs[...].astype(bf16)
    lo = (ngs[...] - hi.astype(f32)).astype(bf16)

    def dest(d, _):
        for r in range(0, caps, 2):
            pair = [
                piece[pl.ds(pl.multiple_of(blocks[d * caps + r + k] * 8, 8), 8), :] for k in range(2)
            ]
            send_o[d, r * 8 : r * 8 + 16, :] = jnp.concatenate(pair, axis=0)
        send_o[d, caps * 8 : caps * 8 + half, :] = hi.astype(f32)
        send_o[d, caps * 8 + half :, :] = lo.astype(f32)
        return 0

    lax.fori_loop(0, dests, dest, 0)


def adam_body(filled, sources, recv, master, first, second, f_o, s_o, m_o, w_o, ng_o, two, grad):
    caps, br, _ = master.shape
    n_ng = recv.shape[1] - caps * 8
    corr_one = 1.0 - beta_one**STEP
    corr_two = 1.0 - beta_two**STEP
    for j in range(4):
        for c in range(2):
            two[:, c] = recv[sources[c * 4 + j], 0 : caps * 8, :].astype(f32).reshape(caps, 8, 128)
        grad[pl.ds(j, caps * 16, stride=4), :] = two[...].reshape(caps * 16, 128)
    half = n_ng // 2

    def add(s, tot):
        part = recv[s, caps * 8 :, :].astype(f32)
        return tot + (part[:half] + part[half:])

    ng_o[...] = lax.fori_loop(0, recv.shape[0], add, jnp.zeros(ng_o.shape, f32))

    def slot(r, _):
        g = grad[pl.ds(pl.multiple_of(r * br, br), br), :]
        m_old, f_old, s_old = master[r], first[r], second[r]
        fn = beta_one * f_old + (1.0 - beta_one) * g
        sn = beta_two * s_old + (1.0 - beta_two) * g * g
        step = fn / corr_one / (jnp.sqrt(sn / corr_two) + adam_epsilon)
        mn = m_old - learn_rate * (step + decay_rate * m_old)
        keep = jnp.full(g.shape, filled[r], jnp.int32) > 0
        f_o[r] = jnp.where(keep, fn, f_old)
        s_o[r] = jnp.where(keep, sn, s_old)
        m_o[r] = jnp.where(keep, mn, m_old)
        grad[pl.ds(pl.multiple_of(r * br, br), br), :] = mn
        return 0

    lax.fori_loop(0, caps, slot, 0)
    for j in range(4):
        val = grad[pl.ds(j, caps * 16, stride=4), :].astype(bf16)
        w_o[:, :, j * 128 : (j + 1) * 128] = val.reshape(caps, 16, 128)


def place_body(other, index, own, oth, q_o, out_o, in_o, down_o, pseudo, flat):
    def block(b):
        take = jnp.full((16, 512), other[b], jnp.int32) > 0
        return jnp.where(take, oth[index[b]].astype(f32), own[index[b]].astype(f32))

    first = 0
    for ref in (pseudo, out_o, in_o, down_o):
        n = ref.shape[0] // 16

        def move(b, _, ref=ref, first=first):
            ref[pl.ds(pl.multiple_of(b * 16, 16), 16), :] = block(first + b).astype(ref.dtype)
            return 0

        lax.fori_loop(0, n, move, 0)
        first += n
    rows = q_o.shape[0]
    for j in range(4):
        flat[pl.ds(j, 3 * rows // 4, stride=4), :] = pseudo[:, j * 128 : (j + 1) * 128]
    for part in range(3):
        q_o[:, part * 128 : (part + 1) * 128] = flat[pl.ds(part, rows, stride=3), :].astype(bf16)


def per_device(
    tokens, cotangent, lengths, owners, w_qkv, w_out, w_in, w_down,
    master, first_moment, second_moment, norm_gains, norm_biases, norm_first, norm_second,
):
    rows, width = tokens.shape[1], tokens.shape[2]
    groups = lax.axis_size("mp")
    ndp = lax.axis_size("dp")
    nbits = ndp.bit_length() - 1
    rest = list(range(1, nbits))
    order = (rest, rest[:2][::-1] + rest[2:][::-1])
    me, zi = lax.axis_index("dp"), lax.axis_index("mp")
    core = me & 1

    def bit_of(who, at, s):
        return (who >> jnp.where(at == 0, order[0][s], order[1][s])) & 1

    def swap(x, s):
        return lax.ppermute(x, "dp", [(i, i ^ (1 << order[i & 1][s])) for i in range(ndp)])

    def swap_core(x):
        return lax.ppermute(x, "dp", [(i, i ^ 1) for i in range(ndp)])

    def from_mp(x, step):
        return lax.ppermute(x, "mp", [(i, i + step) for i in range(groups) if 0 <= i + step < groups])

    def swap_mp(x, mask):
        return lax.ppermute(x, "mp", [(i, i ^ mask) for i in range(groups)])

    def exchange(x, axis):
        return lax.all_to_all(x, axis, 0, 0, tiled=True)

    def all_states(x):
        return [x] + [swap_mp(x, m) for m in range(1, groups)]

    q0, q1 = bit_of(me, core, 0), bit_of(me, core, 1)
    o0, o1 = bit_of(me, 1 - core, 0), bit_of(me, 1 - core, 1)
    length = lengths[0]
    base = zi * rows
    ids = [length, base, core]
    ids += [((t >> 1) ^ q0) + 2 * ((t & 1) ^ q1) for t in range(4)]
    ids += [((t >> 1) ^ o0) + 2 * ((t & 1) ^ o1) for t in range(4)]
    meta = jnp.stack(ids).astype(jnp.int32)

    def gather(piece):
        buf = exchange(jnp.broadcast_to(piece, (groups,) + piece.shape), "mp")[None]
        for s in range(2):
            buf = jnp.concatenate([buf, swap(buf, s)], axis=0)
        return buf, swap_core(buf)

    mine = core * 4 + q0 * 2 + q1

    def part_of(w):
        n = w.shape[0] // 8
        return lax.dynamic_slice_in_dim(w, mine * n, n, 0)

    tok, cot = tokens[0], cotangent[0]
    left, right = from_mp(tok[rows - HALO :], 1), from_mp(tok[:HALO], -1)
    qkv_own, qkv_oth = gather(part_of(w_qkv))
    ffn_own, ffn_oth = gather(jnp.concatenate([part_of(w_in), part_of(w_down), part_of(w_out)], axis=0))

    ext = rows + 2 * HALO
    mm = 2 * rows * width
    qkv, a1, state, wqkv = call(
        qkv_body,
        [
            ((groups, ext, 3 * PAIR), bf16), ((rows, width), bf16),
            ((groups, STATE, PAIR), bf16), ((groups, width, 3 * PAIR), bf16),
        ],
        [SM] + [VM] * 5 + [ANY] * 2,
        [pltpu.VMEM((ext, width), bf16), pltpu.SemaphoreType.DMA],
        2 * ext * width * 3 * width, 6 << 20,
    )(meta, tok, left, right, norm_gains, norm_biases, qkv_own, qkv_oth)
    states = all_states(state)
    [near] = call(
        near_body, [((rows, width), f32)], [SM, VM], [], mm * 1024, 12 << 20,
    )(meta, qkv)

    hid_w = w_in.shape[1]
    big = pltpu.VMEM((rows, width), f32)
    low = pltpu.VMEM((rows, width), bf16)
    (outputs, do, dx2, ctx, a2, dm, hid, du, dctx, dqf, dstate, ng2, wout) = call(
        main_body,
        [
            ((rows, width), bf16), ((rows, width), bf16), ((rows, width), f32), ((rows, width), bf16),
            ((rows, width), bf16), ((rows, width), bf16), ((groups, rows, hid_w), bf16),
            ((groups, rows, hid_w), bf16), ((rows, width), bf16), ((rows, width), f32),
            ((groups, STATE, PAIR), bf16), ((2, width), f32), ((width, width), bf16),
        ],
        [SM] + [VM] * 10 + [ANY] * 2,
        [
            pltpu.VMEM((groups, width, hid_w), bf16), pltpu.VMEM((groups, hid_w, width), bf16),
            big, pltpu.VMEM((rows, hid_w), f32), pltpu.VMEM((rows, hid_w), f32), big, big, big, big,
            low, low, low, pltpu.SemaphoreType.DMA((3,)),
        ],
        mm * hid_w * groups * 4, 24 << 20,
    )(meta, near, qkv, *states, tok, cot, norm_gains, norm_biases, ffn_own, ffn_oth)

    dstates = all_states(dstate)
    do_l, do_r = from_mp(do[rows - EDGE :], 1), from_mp(do[:EDGE], -1)
    n_m = (w_out.shape[0] + w_in.shape[0] + w_down.shape[0]) // 2
    [grad_m] = call(
        grads_body, [((2, groups, n_m, width), bf16)], [SM] + [VM] * 6, [],
        mm * (2 * hid_w * groups + width), 12 << 20,
    )(meta, ctx, do, a2, dm, hid, du)

    def reduce(both, extra=None):
        tot = both[0].astype(f32) + swap_core(both[1]).astype(f32)
        for s in range(nbits - 1):
            if s < 2:
                n = tot.shape[-1] // 2
                bit = bit_of(me, core, s)
                give = lax.dynamic_slice_in_dim(tot, (1 - bit) * n, n, 2).astype(bf16)
                tot = lax.dynamic_slice_in_dim(tot, bit * n, n, 2) + swap(give, s).astype(f32)
            else:
                tot = tot.astype(bf16).astype(f32) + swap(tot.astype(bf16), s).astype(f32)
        msg = tot.astype(bf16)
        if extra is not None:
            more = jnp.broadcast_to(extra, (groups,) + extra.shape)
            msg = jnp.concatenate([msg, more], axis=1)
        return exchange(msg, "mp")

    z_m = reduce(grad_m)
    dq, dkn, dvn = call(
        near_back_body,
        [((rows, width), bf16), ((rows, width), f32), ((rows, width), f32)],
        [SM] + [VM] * 6,
        [
            pltpu.VMEM((rows + 2 * EDGE, width), bf16), pltpu.VMEM((rows + 2 * EDGE, width), f32),
            pltpu.VMEM((ext, width), f32), pltpu.VMEM((ext, width), f32),
        ],
        mm * 2048, 24 << 20,
    )(meta, qkv, dctx, do_l, do_r, wout, dqf)
    n_q = w_qkv.size // width // 2
    n_ng = 4 * width // 128
    tokens_grad, grad_q, ng = call(
        last_body,
        [((rows, width), f32), ((2, groups, n_q, width), f32), ((2 * n_ng, 128), bf16)],
        [SM] + [VM] * 14,
        [
            pltpu.VMEM((groups, rows, 3 * PAIR), bf16), big, pltpu.VMEM((3 * width, 128), f32),
            pltpu.VMEM((2 * n_q, width), f32), pltpu.VMEM((n_ng, 128), f32),
        ],
        mm * 6 * width, 24 << 20,
    )(meta, qkv, dq, dkn, dvn, *dstates, wqkv, a1, tok, dx2, norm_gains, ng2)
    z_q = reduce(grad_q, ng)

    capacity, block_rows = master.shape[0], master.shape[1]
    blocks = owners.shape[0]
    earlier = jnp.arange(blocks)[None, :] < jnp.arange(blocks)[:, None]
    alike = owners[None, :] == owners[:, None]
    slot = jnp.sum((earlier & alike).astype(jnp.int32), axis=1)
    slot_rows = owners * capacity + slot
    hit = slot_rows[None, :] == jnp.arange(ndp * capacity, dtype=jnp.int32)[:, None]
    held = jnp.sum(jnp.where(hit, jnp.arange(blocks, dtype=jnp.int32)[None, :], 0), axis=1)
    filled = lax.dynamic_slice_in_dim(
        jnp.sum(hit.astype(jnp.int32), axis=1), me * capacity, capacity, 0
    )
    per = capacity * 8 + 2 * n_ng
    [send] = call(
        route_body, [((ndp, per, 128), f32)], [SM, VM, VM],
        [pltpu.VMEM((blocks * 8, 128), f32), pltpu.VMEM((n_ng, 128), f32)],
        1 << 20, 4 << 20,
    )(held, z_q, z_m)
    recv = exchange(send, "dp")
    high = me - (me & 7)
    sources = jnp.stack(
        [
            high + c + ((j >> 1) << order[c][0]) + ((j & 1) << order[c][1])
            for c in range(2)
            for j in range(4)
        ]
    ).astype(jnp.int32)
    state_shape = (capacity, block_rows, 128)
    first_new, second_new, master_new, fresh, norm_sum = call(
        adam_body,
        [(state_shape, f32)] * 3 + [((capacity, 16, 512), bf16), ((n_ng, 128), f32)],
        [SM, SM] + [VM] * 4,
        [pltpu.VMEM((capacity, 2, 8, 128), f32), pltpu.VMEM((capacity * block_rows, 128), f32)],
        1 << 20, 8 << 20,
    )(filled, sources, recv, master, first_moment, second_moment)

    buf = fresh[None]
    for s in range(nbits - 1):
        buf = jnp.concatenate([buf, swap(buf, s)], axis=0)
    oth = swap_core(buf)
    owner_core = owners & 1
    far_core = owner_core ^ core
    start = jnp.where(far_core == 1, me ^ 1, me)
    rel = start ^ owners
    at = sum(
        ((rel >> jnp.where(owner_core == 0, order[0][s], order[1][s])) & 1) << s for s in range(nbits - 1)
    )
    index = (at * capacity + slot).astype(jnp.int32)
    flat_shape = (buf.shape[0] * capacity, 16, 512)
    new_qkv, new_out, new_in, new_down = call(
        place_body,
        [(w_qkv.shape, bf16), (w_out.shape, bf16), (w_in.shape, bf16), (w_down.shape, bf16)],
        [SM, SM, VM, VM],
        [pltpu.VMEM((w_qkv.size // 512, 512), f32), pltpu.VMEM((w_qkv.size // 128, 128), f32)],
        1 << 20, 6 << 20,
    )(far_core, index, buf.reshape(flat_shape), oth.reshape(flat_shape))

    corr_one = 1.0 - beta_one**STEP
    corr_two = 1.0 - beta_two**STEP
    norm_grad = norm_sum.reshape(4, width)
    norm_params = jnp.stack([norm_gains[0], norm_biases[0], norm_gains[1], norm_biases[1]])
    norm_first_new = beta_one * norm_first + (1.0 - beta_one) * norm_grad
    norm_second_new = beta_two * norm_second + (1.0 - beta_two) * norm_grad * norm_grad
    norm_new = norm_params - norm_rate * (
        norm_first_new / corr_one / (jnp.sqrt(norm_second_new / corr_two) + adam_epsilon)
    )
    return (
        outputs[None], tokens_grad[None], first_new, second_new, master_new,
        new_qkv, new_out, new_in, new_down, norm_first_new, norm_second_new, norm_new,
    )


def solution(mesh):
    sharded = P("dp", "mp", None)
    return jax.shard_map(
        per_device,
        mesh=mesh,
        in_specs=(
            sharded, sharded, P("dp"), P(), P(None, "mp"), P("mp", None), P(None, "mp"), P("mp", None),
            sharded, sharded, sharded, P(), P(), P(), P(),
        ),
        out_specs=(
            sharded, sharded, sharded, sharded, sharded,
            P(None, "mp"), P("mp", None), P(None, "mp"), P("mp", None), P(), P(), P(),
        ),
        check_vma=False,
    )
```

time: 876 us -> 318 us (0.36); the launches traced: 864 us -> 317 us
  waiting for transfers between devices: 554 us -> 111 us
  matrix products: 115 us -> 0 us
  Pallas kernels: 0 us -> 92 us
  local copies, waits for them, and re-layouts: 69.2 us -> 19.4 us
  starting transfers between devices: 1.24 us -> 44.2 us
  other arithmetic: 51.3 us -> 15.6 us
  loops' own time: 16.3 us -> 0 us
  between operations: 15.9 us -> 1.79 us
    reduce_scatter x4 -> x0, waiting for transfers between devices: 289 us -> none  [the longest x1 77.2 us: per_device(): lax.psum_scatter(jnp.dot(hidden, w_down, preferred_element_type=jnp.float...]
    all_gather x5 -> x0, waiting for transfers between devices: 198 us -> none  [the longest x1 48.1 us: per_device(): first_all = lax.all_gather(first_local, 'mp', axis=0, tiled=True)]
    dot_general x54 -> x0, matrix products: 115 us -> none  [the longest x4 16.4 us: against(): lax.dot_general(left, right, (((1,), (1,)), ((), ())), preferred_element_...]
    pallas_call x0 -> x9, Pallas kernels: none -> 92 us  [the longest x1 25.3 us: per_device(): call(main_body, [((rows, width), bf16), ((rows, width), bf16), ((rows, wi...]
    ppermute x0 -> x25, waiting for transfers between devices: none -> 78.4 us  [the longest x10 69.3 us: swap(): lax.ppermute(x, 'dp', [(i, i ^ 1 << order[i & 1][s]) for i in range(ndp)])]
    psum x1 -> x0, waiting for transfers between devices: 66.9 us -> none  [per_device(): summed = lax.psum(grad_blocks, 'dp')]
    psum x1 -> x0, blocking collectives: 40.8 us -> none  [per_device(): lax.psum(jnp.stack([grad_gain_one, grad_bias_one, grad_gain_two, grad_bia...]
    dynamic_update_slice x16 -> x0, local copies, waits for them, and re-layouts: 35 us -> none  [the longest x8 25.6 us: near_forward(): results, log_sums = lax.map(window, anchors)]
  transfers between devices with their start and end apart: 10 -> 28, of which waited for: 10 -> 14; matrix products, arithmetic and copies ran while one was open for 5% -> 6% of each run, Pallas kernels for 0% -> 17%
where the time goes in v1:
time: 318 us; the launch traced here: 317 us
  waiting for transfers between devices  111 us (35%)
  Pallas kernels  92 us (29%)
  starting transfers between devices  44.2 us (14%)
  blocking collectives  32.8 us (10%)
  local copies, waits for them, and re-layouts  19.4 us (6%)
  other arithmetic  15.6 us (5%)
    ppermute x10, waiting for transfers between devices, swap(): lax.ppermute(x, 'dp', [(i, i ^ 1 << order[i & 1][s]) for i in range(ndp)])  69.3 us
    all_to_all x3, waiting for transfers between devices, exchange(): return lax.all_to_all(x, axis, 0, 0, tiled=True)  33 us
    all_to_all x2, blocking collectives, exchange(): return lax.all_to_all(x, axis, 0, 0, tiled=True)  32.8 us
    pallas_call x1, Pallas kernels, per_device(): call(main_body, [((rows, width), bf16), ((rows, width), bf16), ((rows, wi...  25.3 us
    pallas_call x1, Pallas kernels, per_device(): call(near_back_body, [((rows, width), bf16), ((rows, width), f32), ((rows...  19.8 us
    all_to_all x3, starting transfers between devices, exchange(): return lax.all_to_all(x, axis, 0, 0, tiled=True)  16.9 us
    pallas_call x1, Pallas kernels, per_device(): call(last_body, [((rows, width), f32), ((2, groups, n_q, width), f32), ((...  12.5 us
    pallas_call x1, Pallas kernels, per_device(): call(near_body, [((rows, width), f32)], [SM, VM], [], mm * 1024, 12 << 20)  11.8 us
  transfers between devices with their start and end apart: 28, of which 14 were waited for; matrix products, arithmetic and copies ran while one was open for 6% of the time, Pallas kernels for 17%

profile of v1, /device:TPU:0, one launch (start us, length us, event | category | flops | bytes accessed | tf_op | source)
XLA Modules:
  0.0 317.2 jit_solution(13737643742430000485)
XLA Ops:
  2.4 22.0 %all_to_all.25 = bf16[4,144,512]{2,1,0:T(8,128)(2,1)S(1)} all-to-all(bf16[4,144,512]{2,1,0:T(8,128)(2,1)S(1)} %broadcast_in_dim.61), channel_id=1, replica_groups=mesh['dp'=8,'mp'=4] {'mp'}, dimensions={0} | all-to-all | bytes 1179648 | tf_op jit(solution)/shard_map/all_to_all | solution.py:600
  25.9 8.4 %collective-permute-done.8 = bf16[1,4,144,512]{3,2,1,0:T(8,128)(2,1)S(1)} collective-permute-done((bf16[1,4,144,512]{3,2,1,0:T(8,128)(2,1)S(1)}, bf16[1,4,144,512]{3,2,1,0:T(8,128)(2,1)S(1)}, u32[]{:S(2)}, u32[]{:S(2)}) %collective-permute-start.8) | collective-permute-done | bytes 589856 | tf_op jit(solution)/shard_map/ppermute | solution.py:588
  36.0 14.7 %collective-permute-done.9 = bf16[2,4,144,512]{3,2,1,0:T(8,128)(2,1)S(1)} collective-permute-done((bf16[2,4,144,512]{3,2,1,0:T(8,128)(2,1)S(1)}, bf16[2,4,144,512]{3,2,1,0:T(8,128)(2,1)S(1)}, u32[]{:S(2)}, u32[]{:S(2)}) %collective-permute-start.9) | collective-permute-done | bytes 1179680 | tf_op jit(solution)/shard_map/ppermute | solution.py:588
  52.4 10.8 %all_to_all.26 = bf16[4,64,384]{2,1,0:T(8,128)(2,1)S(1)} all-to-all(bf16[4,64,384]{2,1,0:T(8,128)(2,1)S(1)} %broadcast_in_dim.59), channel_id=1, replica_groups=mesh['dp'=8,'mp'=4] {'mp'}, dimensions={0} | all-to-all | bytes 393216 | tf_op jit(solution)/shard_map/all_to_all | solution.py:600
  64.6 4.3 %collective-permute-done.2 = bf16[1,4,64,384]{3,2,1,0:T(8,128)(2,1)S(1)} collective-permute-done((bf16[1,4,64,384]{3,2,1,0:T(8,128)(2,1)S(1)}, bf16[1,4,64,384]{3,2,1,0:T(8,128)(2,1)S(1)}, u32[]{:S(2)}, u32[]{:S(2)}) %collective-permute-start.2) | collective-permute-done | bytes 196640 | tf_op jit(solution)/shard_map/ppermute | solution.py:588
  70.6 6.3 %collective-permute-done.3 = bf16[2,4,64,384]{3,2,1,0:T(8,128)(2,1)S(1)} collective-permute-done((bf16[2,4,64,384]{3,2,1,0:T(8,128)(2,1)S(1)}, bf16[2,4,64,384]{3,2,1,0:T(8,128)(2,1)S(1)}, u32[]{:S(2)}, u32[]{:S(2)}) %collective-permute-start.3) | collective-permute-done | bytes 393248 | tf_op jit(solution)/shard_map/ppermute | solution.py:588
  77.0 2.2 collective-permute-start
  81.3 4.1 %collective-permute-done.1.right = bf16[64,512]{1,0:T(8,128)(2,1)S(1)} collective-permute-done((bf16[64,512]{1,0:T(8,128)(2,1)S(1)}, bf16[64,512]{1,0:T(8,128)(2,1)S(1)}, u32[]{:S(2)}, u32[]{:S(2)}) %collective-permute-start.1) | collective-permute-done | bytes 65568 | tf_op jit(solution)/shard_map/ppermute | solution.py:594
  85.4 8.3 %shard_map.238 = (bf16[4,640,384]{2,1,0:T(8,128)(2,1)}, bf16[512,512]{1,0:T(8,128)(2,1)S(1)}, bf16[4,144,128]{2,1,0:T(8,128)(2,1)S(1)}, bf16[4,512,384]{2,1,0:T(8,128)(2,1)S(1)}) custom-call(s32[11]{0:T(128)S(1)} %stack.73.meta, bf16[512,512]{1,0:T(8,128)(2,1)S(1)} %bitcast.47, bf16[64,512]{1,0:T(8,128)(2,1)S(1)} %collective-permute-done.left, ...), custom_call_target="tpu_custom_call" | custom-call | flops 1006632960 | bytes 6291456 | tf_op jit(solution)/shard_map/pallas_call | solution.py:633
  96.5 2.8 collective-permute-start.7
  100.8 11.8 %shard_map.239.near = f32[512,512]{1,0:T(8,128)S(1)} custom-call(s32[11]{0:T(128)S(1)} %stack.73.meta, bf16[4,640,384]{2,1,0:T(8,128)(2,1)S(1)} %copy-done.2), custom_call_target="tpu_custom_call" | custom-call | flops 536870912 | bytes 12582912 | tf_op jit(solution)/shard_map/pallas_call | solution.py:644
  113.7 25.3 %shard_map.240 = (bf16[512,512]{1,0:T(8,128)(2,1)}, bf16[512,512]{1,0:T(8,128)(2,1)S(1)}, f32[512,512]{1,0:T(8,128)S(1)}, bf16[512,512]{1,0:T(8,128)(2,1)S(1)}, ...) custom-call(s32[11]{0:T(128)S(1)} %stack.73.meta, ...), custom_call_target="tpu_custom_call" | custom-call | flops 4294967296 | bytes 25165824 | tf_op jit(solution)/shard_map/pallas_call | solution.py:651
  140.5 6.7 %shard_map.243 = bf16[2,4,576,512]{3,2,1,0:T(8,128)(2,1)} custom-call(s32[11]{0:T(128)S(1)} %stack.73.meta, bf16[512,512]{1,0:T(8,128)(2,1)S(1)} %get-tuple-element.62.ctx, bf16[512,512]{1,0:T(8,128)(2,1)S(1)} %get-tuple-element.48.do, bf16[512,512]{1,0:T(8,128)(2,1)S(1)} %get-tuple-element.63.a2, bf16[512,512]{1,0:T(8,128)(2,1)S(1)} %get-tuple-element.64.dm, ...), custom_call_target="tpu_custom_call" | custom-call | flops 2415919104 | bytes 12582912 | tf_op jit(solution)/shard_map/pallas_call | solution.py:671
  153.1 2.3 collective-permute-start.15
  156.7 4.8 %collective-permute-done.12.do_r = bf16[32,512]{1,0:T(8,128)(2,1)S(1)} collective-permute-done((bf16[32,512]{1,0:T(8,128)(2,1)S(1)}, bf16[32,512]{1,0:T(8,128)(2,1)S(1)}, u32[]{:S(2)}, u32[]{:S(2)}) %collective-permute-start.12) | collective-permute-done | bytes 32800 | tf_op jit(solution)/shard_map/ppermute | solution.py:594
  161.5 19.8 %shard_map.241 = (bf16[512,512]{1,0:T(8,128)(2,1)S(1)}, f32[512,512]{1,0:T(8,128)S(1)}, f32[512,512]{1,0:T(8,128)S(1)}) custom-call(s32[11]{0:T(128)S(1)} %stack.73.meta, bf16[4,640,384]{2,1,0:T(8,128)(2,1)} %get-tuple-element.44.qkv, bf16[512,512]{1,0:T(8,128)(2,1)S(1)} %get-tuple-element.47.dctx, bf16[32,512]{1,0:T(8,128)(2,1)S(1)} %collective-permute-done.11.do_l, ...), custom_call_target="tpu_custom_call" | custom-call | flops 1073741824 | bytes 25165824 | tf_op jit(solution)/shard_map/pallas_call | solution.py:693
  181.3 12.5 %shard_map.242 = (f32[512,512]{1,0:T(8,128)}, f32[2,4,192,512]{3,2,1,0:T(8,128)}, bf16[32,128]{1,0:T(8,128)(2,1)S(1)}) custom-call(s32[11]{0:T(128)S(1)} %stack.73.meta, bf16[4,640,384]{2,1,0:T(8,128)(2,1)} %get-tuple-element.44.qkv, bf16[512,512]{1,0:T(8,128)(2,1)S(1)} %get-tuple-element.51.dq, f32[512,512]{1,0:T(8,128)S(1)} %get-tuple-element.52.dkn, ...), custom_call_target="tpu_custom_call" | custom-call | flops 1610612736 | bytes 25165824 | tf_op jit(solution)/shard_map/pallas_call | solution.py:705
  193.8 2.7 slice_bitcast_fusion.2
  196.5 3.3 %convert_add_fusion = f32[4,576,512]{2,1,0:T(8,128)S(1)} fusion(bf16[4,576,512]{2,1,0:T(8,128)(2,1)} %collective-permute-done.19, bf16[2,4,576,512]{3,2,1,0:T(8,128)(2,1)} %shard_map.243), kind=kLoop, calls=%fused_computation | loop fusion | flops 3538944 | bytes 9437184 | tf_op jit(solution)/shard_map/add | solution.py:677
  199.8 2.2 copy-done.16
  207.1 16.7 %collective-permute-done.17 = bf16[4,192,256]{2,1,0:T(8,128)(2,1)S(1)} collective-permute-done((bf16[4,192,256]{2,1,0:T(8,128)(2,1)S(1)}, bf16[4,192,256]{2,1,0:T(8,128)(2,1)S(1)}, u32[]{:S(2)}, u32[]{:S(2)}) %collective-permute-start.17) | collective-permute-done | bytes 393248 | tf_op jit(solution)/shard_map/ppermute | solution.py:588
  225.6 2.4 convert_add_fusion.1
  231.5 9.9 %all-to-all-start.2 = ((bf16[4,224,128]{2,1,0:T(8,128)(2,1)}), bf16[4,224,128]{2,1,0:T(8,128)(2,1)S(1)}, u32[]{:S(2)}, u32[]{:S(2)}) async-start(bf16[4,224,128]{2,1,0:T(8,128)(2,1)} %pad_maximum_fusion.6), calls=%async_computation.2 | async-start | bytes 458752 | tf_op jit(solution)/shard_map/all_to_all | solution.py:600
  243.4 5.7 %all-to-all-done.2.zq = bf16[4,224,128]{2,1,0:T(8,128)(2,1)S(1)} async-done(((bf16[4,224,128]{2,1,0:T(8,128)(2,1)}), bf16[4,224,128]{2,1,0:T(8,128)(2,1)S(1)}, u32[]{:S(2)}, u32[]{:S(2)}) %all-to-all-start.2) | async-done | bytes 229408 | tf_op jit(solution)/shard_map/all_to_all | solution.py:600
  249.2 3.5 %all-to-all-start.3 = ((bf16[4,576,128]{2,1,0:T(8,128)(2,1)}), bf16[4,576,128]{2,1,0:T(8,128)(2,1)S(1)}, u32[]{:S(2)}, u32[]{:S(2)}) async-start(bf16[4,576,128]{2,1,0:T(8,128)(2,1)} %add_convert_fusion), calls=%async_computation.3 | async-start | bytes 1179648 | tf_op jit(solution)/shard_map/all_to_all | solution.py:600
  253.7 13.5 %all-to-all-done.3.zm = bf16[4,576,128]{2,1,0:T(8,128)(2,1)S(1)} async-done(((bf16[4,576,128]{2,1,0:T(8,128)(2,1)}), bf16[4,576,128]{2,1,0:T(8,128)(2,1)S(1)}, u32[]{:S(2)}, u32[]{:S(2)}) %all-to-all-start.3) | async-done | bytes 589856 | tf_op jit(solution)/shard_map/all_to_all | solution.py:600
  269.0 3.6 %all-to-all-start.4 = ((f32[8,224,128]{2,1,0:T(8,128)}), f32[8,224,128]{2,1,0:T(8,128)S(1)}, u32[]{:S(2)}, u32[]{:S(2)}) async-start(f32[8,224,128]{2,1,0:T(8,128)} %shard_map.244), calls=%async_computation.4 | async-start | bytes 1835008 | tf_op jit(solution)/shard_map/all_to_all | solution.py:600
  272.8 13.8 %all-to-all-done.4.recv = f32[8,224,128]{2,1,0:T(8,128)S(1)} async-done(((f32[8,224,128]{2,1,0:T(8,128)}), f32[8,224,128]{2,1,0:T(8,128)S(1)}, u32[]{:S(2)}, u32[]{:S(2)}) %all-to-all-start.4) | async-done | bytes 917536 | tf_op jit(solution)/shard_map/all_to_all | solution.py:600
  286.5 3.0 shard_map.245
  290.0 7.3 %collective-permute-done.22 = bf16[1,24,16,512]{3,2,1,0:T(8,128)(2,1)S(1)} collective-permute-done((bf16[1,24,16,512]{3,2,1,0:T(8,128)(2,1)S(1)}, bf16[1,24,16,512]{3,2,1,0:T(8,128)(2,1)S(1)}, u32[]{:S(2)}, u32[]{:S(2)}) %collective-permute-start.22) | collective-permute-done | bytes 393248 | tf_op jit(solution)/shard_map/ppermute | solution.py:588
  298.0 11.5 %collective-permute-done.23 = bf16[2,24,16,512]{3,2,1,0:T(8,128)(2,1)S(1)} collective-permute-done((bf16[2,24,16,512]{3,2,1,0:T(8,128)(2,1)S(1)}, bf16[2,24,16,512]{3,2,1,0:T(8,128)(2,1)S(1)}, u32[]{:S(2)}, u32[]{:S(2)}) %collective-permute-start.23) | collective-permute-done | bytes 786464 | tf_op jit(solution)/shard_map/ppermute | solution.py:588
  314.4 2.8 shard_map.246
  (115 shorter events, 46.7 us)
Async XLA Ops:
  0.6 51.7 %copy-start = (bf16[512,384]{1,0:T(8,128)(2,1)S(1)}, bf16[512,384]{1,0:T(8,128)(2,1)}, u32[]{:S(2)}) copy-start(bf16[512,384]{1,0:T(8,128)(2,1)} %param.19) | copy-start | bytes 1179652
  24.4 9.9 %collective-permute-start.8 = (bf16[1,4,144,512]{3,2,1,0:T(8,128)(2,1)S(1)}, bf16[1,4,144,512]{3,2,1,0:T(8,128)(2,1)S(1)}, u32[]{:S(2)}, u32[]{:S(2)}) collective-permute-start(bf16[1,4,144,512]{3,2,1,0:T(8,128)(2,1)S(1)} %bitcast.51), channel_id=1, source_target_pairs={{0,8},{4,20},{8,0},{12,28},{16,24},{20,4},{24,16},{28,12},{1,9},{5... | collective-permute-start | bytes 1769480 | tf_op jit(solution)/shard_map/ppermute | solution.py:588
  34.4 16.3 %collective-permute-start.9 = (bf16[2,4,144,512]{3,2,1,0:T(8,128)(2,1)S(1)}, bf16[2,4,144,512]{3,2,1,0:T(8,128)(2,1)S(1)}, u32[]{:S(2)}, u32[]{:S(2)}) collective-permute-start(bf16[2,4,144,512]{3,2,1,0:T(8,128)(2,1)S(1)} %pad_maximum_fusion.2), channel_id=1, source_target_pairs={{0,16},{4,12},{8,24},{12,4},{16,0},{20,28},{24,8},{28,20},{1,17},{... | collective-permute-start | bytes 3538952 | tf_op jit(solution)/shard_map/ppermute | solution.py:588
  52.3 61.3 %collective-permute-start.10 = (bf16[4,4,144,512]{3,2,1,0:T(8,128)(2,1)}, bf16[4,4,144,512]{3,2,1,0:T(8,128)(2,1)}, u32[]{:S(2)}, u32[]{:S(2)}) collective-permute-start(bf16[4,4,144,512]{3,2,1,0:T(8,128)(2,1)} %pad_maximum_fusion.own), channel_id=1, source_target_pairs={{0,4},{4,0},{8,12},{12,8},{16,20},{20,16},{24,28},{28,24},{1,5},{5... | collective-permute-start | bytes 7077896 | tf_op jit(solution)/shard_map/ppermute | solution.py:591
  63.1 5.8 %collective-permute-start.2 = (bf16[1,4,64,384]{3,2,1,0:T(8,128)(2,1)S(1)}, bf16[1,4,64,384]{3,2,1,0:T(8,128)(2,1)S(1)}, u32[]{:S(2)}, u32[]{:S(2)}) collective-permute-start(bf16[1,4,64,384]{3,2,1,0:T(8,128)(2,1)S(1)} %bitcast.54), channel_id=1, source_target_pairs={{0,8},{4,20},{8,0},{12,28},{16,24},{20,4},{24,16},{28,12},{1,9},{5... | collective-permute-start | bytes 589832 | tf_op jit(solution)/shard_map/ppermute | solution.py:588
  69.0 7.8 %collective-permute-start.3 = (bf16[2,4,64,384]{3,2,1,0:T(8,128)(2,1)S(1)}, bf16[2,4,64,384]{3,2,1,0:T(8,128)(2,1)S(1)}, u32[]{:S(2)}, u32[]{:S(2)}) collective-permute-start(bf16[2,4,64,384]{3,2,1,0:T(8,128)(2,1)S(1)} %pad_maximum_fusion.5), channel_id=1, source_target_pairs={{0,16},{4,12},{8,24},{12,4},{16,0},{20,28},{24,8},{28,20},{1,17},{... | collective-permute-start | bytes 1179656 | tf_op jit(solution)/shard_map/ppermute | solution.py:588
  76.9 8.5 %collective-permute-start.4 = (bf16[4,4,64,384]{3,2,1,0:T(8,128)(2,1)S(1)}, bf16[4,4,64,384]{3,2,1,0:T(8,128)(2,1)S(1)}, u32[]{:S(2)}, u32[]{:S(2)}) collective-permute-start(bf16[4,4,64,384]{3,2,1,0:T(8,128)(2,1)S(1)} %pad_maximum_fusion.3.own), channel_id=1, source_target_pairs={{0,4},{4,0},{8,12},{12,8},{16,20},{20,16},{24,28},{28,24},{1,5},{5... | collective-permute-start | bytes 2359304 | tf_op jit(solution)/shard_map/ppermute | solution.py:591
  77.0 4.3 %collective-permute-start = (bf16[64,512]{1,0:T(8,128)(2,1)S(1)}, bf16[64,512]{1,0:T(8,128)(2,1)S(1)}, u32[]{:S(2)}, u32[]{:S(2)}) collective-permute-start(bf16[64,512]{1,0:T(8,128)(2,1)S(1)} %get-tuple-element.84), channel_id=1, source_target_pairs={{0,1},{1,2},{2,3},{4,5},{5,6},{6,7},{8,9},{9,10},{10,11},{12,13},{... | collective-permute-start | bytes 196616 | tf_op jit(solution)/shard_map/ppermute | solution.py:594
  79.2 6.2 %collective-permute-start.1 = (bf16[64,512]{1,0:T(8,128)(2,1)S(1)}, bf16[64,512]{1,0:T(8,128)(2,1)S(1)}, u32[]{:S(2)}, u32[]{:S(2)}) collective-permute-start(bf16[64,512]{1,0:T(8,128)(2,1)S(1)} %get-tuple-element.83), channel_id=1, source_target_pairs={{1,0},{2,1},{3,2},{5,4},{6,5},{7,6},{9,8},{10,9},{11,10},{13,12},{... | collective-permute-start | bytes 196616 | tf_op jit(solution)/shard_map/ppermute | solution.py:594
  94.9 18.7 %collective-permute-start.5 = (bf16[4,144,128]{2,1,0:T(8,128)(2,1)S(1)}, bf16[4,144,128]{2,1,0:T(8,128)(2,1)S(1)}, u32[]{:S(2)}, u32[]{:S(2)}) collective-permute-start(bf16[4,144,128]{2,1,0:T(8,128)(2,1)S(1)} %get-tuple-element.45.s0), channel_id=1, source_target_pairs={{0,1},{1,0},{2,3},{3,2},{4,5},{5,4},{6,7},{7,6},{8,9},{9,8},{10,11... | collective-permute-start | bytes 442376 | tf_op jit(solution)/shard_map/ppermute | solution.py:597
  95.4 18.2 %collective-permute-start.6 = (bf16[4,144,128]{2,1,0:T(8,128)(2,1)S(1)}, bf16[4,144,128]{2,1,0:T(8,128)(2,1)S(1)}, u32[]{:S(2)}, u32[]{:S(2)}) collective-permute-start(bf16[4,144,128]{2,1,0:T(8,128)(2,1)S(1)} %get-tuple-element.45.s0), channel_id=1, source_target_pairs={{0,2},{1,3},{2,0},{3,1},{4,6},{5,7},{6,4},{7,5},{8,10},{9,11},{10,... | collective-permute-start | bytes 442376 | tf_op jit(solution)/shard_map/ppermute | solution.py:597
  96.5 17.1 %collective-permute-start.7 = (bf16[4,144,128]{2,1,0:T(8,128)(2,1)S(1)}, bf16[4,144,128]{2,1,0:T(8,128)(2,1)S(1)}, u32[]{:S(2)}, u32[]{:S(2)}) collective-permute-start(bf16[4,144,128]{2,1,0:T(8,128)(2,1)S(1)} %get-tuple-element.45.s0), channel_id=1, source_target_pairs={{0,3},{1,2},{2,1},{3,0},{4,7},{5,6},{6,5},{7,4},{8,11},{9,10},{10,... | collective-permute-start | bytes 442376 | tf_op jit(solution)/shard_map/ppermute | solution.py:597
  149.1 47.4 %collective-permute-start.19 = (bf16[4,576,512]{2,1,0:T(8,128)(2,1)S(1)}, bf16[4,576,512]{2,1,0:T(8,128)(2,1)}, u32[]{:S(2)}, u32[]{:S(2)}) collective-permute-start(bf16[4,576,512]{2,1,0:T(8,128)(2,1)S(1)} %slice_bitcast_fusion), channel_id=1, source_target_pairs={{0,4},{4,0},{8,12},{12,8},{16,20},{20,16},{24,28},{28,24},{1,5},{5... | collective-permute-start | bytes 7077896 | tf_op jit(solution)/shard_map/ppermute | solution.py:591
  149.2 6.2 %collective-permute-start.11 = (bf16[32,512]{1,0:T(8,128)(2,1)S(1)}, bf16[32,512]{1,0:T(8,128)(2,1)S(1)}, u32[]{:S(2)}, u32[]{:S(2)}) collective-permute-start(bf16[32,512]{1,0:T(8,128)(2,1)S(1)} %get-tuple-element.82), channel_id=1, source_target_pairs={{0,1},{1,2},{2,3},{4,5},{5,6},{6,7},{8,9},{9,10},{10,11},{12,13},{... | collective-permute-start | bytes 98312 | tf_op jit(solution)/shard_map/ppermute | solution.py:594
  150.9 30.4 %collective-permute-start.13 = (bf16[4,144,128]{2,1,0:T(8,128)(2,1)S(1)}, bf16[4,144,128]{2,1,0:T(8,128)(2,1)S(1)}, u32[]{:S(2)}, u32[]{:S(2)}) collective-permute-start(bf16[4,144,128]{2,1,0:T(8,128)(2,1)S(1)} %get-tuple-element.54.s0), channel_id=1, source_target_pairs={{0,1},{1,0},{2,3},{3,2},{4,5},{5,4},{6,7},{7,6},{8,9},{9,8},{10,11... | collective-permute-start | bytes 442376 | tf_op jit(solution)/shard_map/ppermute | solution.py:597
  152.6 28.7 %collective-permute-start.14 = (bf16[4,144,128]{2,1,0:T(8,128)(2,1)S(1)}, bf16[4,144,128]{2,1,0:T(8,128)(2,1)S(1)}, u32[]{:S(2)}, u32[]{:S(2)}) collective-permute-start(bf16[4,144,128]{2,1,0:T(8,128)(2,1)S(1)} %get-tuple-element.54.s0), channel_id=1, source_target_pairs={{0,2},{1,3},{2,0},{3,1},{4,6},{5,7},{6,4},{7,5},{8,10},{9,11},{10,... | collective-permute-start | bytes 442376 | tf_op jit(solution)/shard_map/ppermute | solution.py:597
  153.1 28.3 %collective-permute-start.15 = (bf16[4,144,128]{2,1,0:T(8,128)(2,1)S(1)}, bf16[4,144,128]{2,1,0:T(8,128)(2,1)S(1)}, u32[]{:S(2)}, u32[]{:S(2)}) collective-permute-start(bf16[4,144,128]{2,1,0:T(8,128)(2,1)S(1)} %get-tuple-element.54.s0), channel_id=1, source_target_pairs={{0,3},{1,2},{2,1},{3,0},{4,7},{5,6},{6,5},{7,4},{8,11},{9,10},{10,... | collective-permute-start | bytes 442376 | tf_op jit(solution)/shard_map/ppermute | solution.py:597
  155.4 6.1 %collective-permute-start.12 = (bf16[32,512]{1,0:T(8,128)(2,1)S(1)}, bf16[32,512]{1,0:T(8,128)(2,1)S(1)}, u32[]{:S(2)}, u32[]{:S(2)}) collective-permute-start(bf16[32,512]{1,0:T(8,128)(2,1)S(1)} %get-tuple-element.81), channel_id=1, source_target_pairs={{1,0},{2,1},{3,2},{5,4},{6,5},{7,6},{9,8},{10,9},{11,10},{13,12},{... | collective-permute-start | bytes 98312 | tf_op jit(solution)/shard_map/ppermute | solution.py:594
  196.5 8.1 %collective-permute-start.16 = (f32[4,192,512]{2,1,0:T(8,128)}, f32[4,192,512]{2,1,0:T(8,128)}, u32[]{:S(2)}, u32[]{:S(2)}) collective-permute-start(f32[4,192,512]{2,1,0:T(8,128)} %slice_bitcast_fusion.2), channel_id=1, source_target_pairs={{0,4},{4,0},{8,12},{12,8},{16,20},{20,16},{24,28},{28,24},{1,5},{5... | collective-permute-start | bytes 4718600 | tf_op jit(solution)/shard_map/ppermute | solution.py:591
  203.2 22.4 %collective-permute-start.20 = (bf16[4,576,256]{2,1,0:T(8,128)(2,1)}, bf16[4,576,256]{2,1,0:T(8,128)(2,1)}, u32[]{:S(2)}, u32[]{:S(2)}) collective-permute-start(bf16[4,576,256]{2,1,0:T(8,128)(2,1)} %dynamic-slice_convert_fusion), channel_id=1, source_target_pairs={{0,8},{4,20},{8,0},{12,28},{16,24},{20,4},{24,16},{28,12},{1,9},{5... | collective-permute-start | bytes 3538952 | tf_op jit(solution)/shard_map/ppermute | solution.py:588
  206.5 17.3 %collective-permute-start.17 = (bf16[4,192,256]{2,1,0:T(8,128)(2,1)S(1)}, bf16[4,192,256]{2,1,0:T(8,128)(2,1)S(1)}, u32[]{:S(2)}, u32[]{:S(2)}) collective-permute-start(bf16[4,192,256]{2,1,0:T(8,128)(2,1)S(1)} %dynamic-slice_convert_fusion.2), channel_id=1, source_target_pairs={{0,8},{4,20},{8,0},{12,28},{16,24},{20,4},{24,16},{28,12},{1,9},{5... | collective-permute-start | bytes 1179656 | tf_op jit(solution)/shard_map/ppermute | solution.py:588
  224.0 5.8 %collective-permute-start.18 = (bf16[4,192,128]{2,1,0:T(8,128)(2,1)S(1)}, bf16[4,192,128]{2,1,0:T(8,128)(2,1)}, u32[]{:S(2)}, u32[]{:S(2)}) collective-permute-start(bf16[4,192,128]{2,1,0:T(8,128)(2,1)S(1)} %dynamic-slice_convert_fusion.3), channel_id=1, source_target_pairs={{0,16},{4,12},{8,24},{12,4},{16,0},{20,28},{24,8},{28,20},{1,17},{... | collective-permute-start | bytes 589832 | tf_op jit(solution)/shard_map/ppermute | solution.py:588
  228.9 12.6 %collective-permute-start.21 = (bf16[4,576,128]{2,1,0:T(8,128)(2,1)}, bf16[4,576,128]{2,1,0:T(8,128)(2,1)}, u32[]{:S(2)}, u32[]{:S(2)}) collective-permute-start(bf16[4,576,128]{2,1,0:T(8,128)(2,1)} %dynamic-slice_convert_fusion.1), channel_id=1, source_target_pairs={{0,16},{4,12},{8,24},{12,4},{16,0},{20,28},{24,8},{28,20},{1,17},{... | collective-permute-start | bytes 1769480 | tf_op jit(solution)/shard_map/ppermute | solution.py:588
  231.5 17.7 %all-to-all-start.2 = ((bf16[4,224,128]{2,1,0:T(8,128)(2,1)}), bf16[4,224,128]{2,1,0:T(8,128)(2,1)S(1)}, u32[]{:S(2)}, u32[]{:S(2)}) async-start(bf16[4,224,128]{2,1,0:T(8,128)(2,1)} %pad_maximum_fusion.6), calls=%async_computation.2 | async-start | bytes 458752 | tf_op jit(solution)/shard_map/all_to_all | solution.py:600
  249.2 18.0 %all-to-all-start.3 = ((bf16[4,576,128]{2,1,0:T(8,128)(2,1)}), bf16[4,576,128]{2,1,0:T(8,128)(2,1)S(1)}, u32[]{:S(2)}, u32[]{:S(2)}) async-start(bf16[4,576,128]{2,1,0:T(8,128)(2,1)} %add_convert_fusion), calls=%async_computation.3 | async-start | bytes 1179648 | tf_op jit(solution)/shard_map/all_to_all | solution.py:600
  252.7 33.9 %copy-start.8 = (f32[24,64,128]{2,1,0:T(8,128)S(1)}, f32[24,64,128]{2,1,0:T(8,128)}, u32[]{:S(2)}) copy-start(f32[24,64,128]{2,1,0:T(8,128)} %master.1) | copy-start | bytes 2359300
  252.7 33.8 %copy-start.9 = (f32[24,64,128]{2,1,0:T(8,128)S(1)}, f32[24,64,128]{2,1,0:T(8,128)}, u32[]{:S(2)}) copy-start(f32[24,64,128]{2,1,0:T(8,128)} %first.1) | copy-start | bytes 2359300
  252.7 33.8 %copy-start.10 = (f32[24,64,128]{2,1,0:T(8,128)S(1)}, f32[24,64,128]{2,1,0:T(8,128)}, u32[]{:S(2)}) copy-start(f32[24,64,128]{2,1,0:T(8,128)} %second.1) | copy-start | bytes 2359300
  269.0 17.5 %all-to-all-start.4 = ((f32[8,224,128]{2,1,0:T(8,128)}), f32[8,224,128]{2,1,0:T(8,128)S(1)}, u32[]{:S(2)}, u32[]{:S(2)}) async-start(f32[8,224,128]{2,1,0:T(8,128)} %shard_map.244), calls=%async_computation.4 | async-start | bytes 1835008 | tf_op jit(solution)/shard_map/all_to_all | solution.py:600
  289.5 7.8 %collective-permute-start.22 = (bf16[1,24,16,512]{3,2,1,0:T(8,128)(2,1)S(1)}, bf16[1,24,16,512]{3,2,1,0:T(8,128)(2,1)S(1)}, u32[]{:S(2)}, u32[]{:S(2)}) collective-permute-start(bf16[1,24,16,512]{3,2,1,0:T(8,128)(2,1)S(1)} %bitcast.44), channel_id=1, source_target_pairs={{0,8},{4,20},{8,0},{12,28},{16,24},{20,4},{24,16},{28,12},{1,9},{5... | collective-permute-start | bytes 1179656 | tf_op jit(solution)/shard_map/ppermute | solution.py:588
  297.4 12.1 %collective-permute-start.23 = (bf16[2,24,16,512]{3,2,1,0:T(8,128)(2,1)S(1)}, bf16[2,24,16,512]{3,2,1,0:T(8,128)(2,1)S(1)}, u32[]{:S(2)}, u32[]{:S(2)}) collective-permute-start(bf16[2,24,16,512]{3,2,1,0:T(8,128)(2,1)S(1)} %pad_maximum_fusion.4), channel_id=1, source_target_pairs={{0,16},{4,12},{8,24},{12,4},{16,0},{20,28},{24,8},{28,20},{1,17},{... | collective-permute-start | bytes 2359304 | tf_op jit(solution)/shard_map/ppermute | solution.py:588
  309.6 3.5 %collective-permute-start.24 = (bf16[4,24,16,512]{3,2,1,0:T(8,128)(2,1)S(1)}, bf16[4,24,16,512]{3,2,1,0:T(8,128)(2,1)S(1)}, u32[]{:S(2)}, u32[]{:S(2)}) collective-permute-start(bf16[4,24,16,512]{3,2,1,0:T(8,128)(2,1)S(1)} %pad_maximum_fusion.1), channel_id=1, source_target_pairs={{0,4},{4,0},{8,12},{12,8},{16,20},{20,16},{24,28},{28,24},{1,5},{5... | collective-permute-start | bytes 4718600 | tf_op jit(solution)/shard_map/ppermute | solution.py:591
  (17 other events, 185.2 us)

commit v2 on v1

v2 whole, which is shorter than its diff:
```python
import functools

import jax
import jax.numpy as jnp
from jax import lax
from jax.experimental import pallas as pl
from jax.experimental.pallas import tpu as pltpu
from jax.sharding import PartitionSpec as P

HEAD = 64
BAND = 30
STEP = 10
HALO = 64
EDGE = 32
QB = 64
WIN = 128
PAIR = 128
COST = 1
STATE = 144

learn_rate = 0.1
norm_rate = 0.3
decay_rate = 0.1
beta_one = 0.9
beta_two = 0.95
adam_epsilon = 1e-08
norm_epsilon = 1e-05
GELU_C = 0.7978845608028654
GELU_A = 0.044715

f32 = jnp.float32
bf16 = jnp.bfloat16

VM = pl.BlockSpec(memory_space=pltpu.VMEM)
HB = pl.BlockSpec(memory_space=pltpu.HBM)
SM = pl.BlockSpec(memory_space=pltpu.SMEM)


def call(body, outs, in_specs, scratch, flops, moved, vmem=48, out_specs=None):
    specs = out_specs or tuple(VM for _ in outs)
    run = pl.pallas_call(
        body,
        out_shape=tuple(
            pltpu.HBM(s, d) if spec is HB else jax.ShapeDtypeStruct(s, d) for (s, d), spec in zip(outs, specs)
        ),
        in_specs=in_specs,
        out_specs=specs,
        scratch_shapes=scratch,
        compiler_params=pltpu.CompilerParams(vmem_limit_bytes=vmem << 20),
        cost_estimate=pl.CostEstimate(flops=flops // COST, bytes_accessed=moved // COST, transcendentals=0),
    )

    def fixed(*args):
        return run(
            *[
                pltpu.with_memory_space_constraint(x, pltpu.HBM) if spec is HB else x
                for x, spec in zip(args, in_specs)
            ]
        )

    return fixed


def dot(a, b):
    return jnp.dot(a, b, preferred_element_type=f32)


def turned(a):
    return a.astype(f32).T.astype(bf16)


def dot_nt(a, b):
    return dot(a, turned(b))


def dot_tn(a, b):
    return lax.dot_general(a, b, (((0,), (0,)), ((), ())), preferred_element_type=f32)


def normalize(x):
    mean = jnp.mean(x, axis=-1, keepdims=True)
    cen = x - mean
    var = jnp.mean(cen * cen, axis=-1, keepdims=True)
    rstd = lax.rsqrt(var + norm_epsilon)
    return cen * rstd, rstd


def same_head(n=PAIR):
    r = lax.broadcasted_iota(jnp.int32, (n, n), 0)
    c = lax.broadcasted_iota(jnp.int32, (n, n), 1)
    return (r < HEAD) == (c < HEAD)


def pack_state(s1, s2, z):
    both = jnp.where(same_head(), s1, pltpu.roll(s2, HEAD, 1))
    hi = z.astype(bf16).astype(f32)
    row = lax.broadcasted_iota(jnp.int32, (16, PAIR), 0)
    tail = jnp.where(row == 0, hi, jnp.where(row == 1, z - hi, 0.0))
    return both.astype(bf16), tail.astype(bf16)


def unpack_state(refs, g):
    tot = refs[0][g].astype(f32)
    for r in refs[1:]:
        tot = tot + r[g].astype(f32)
    both = tot[:PAIR]
    diag = same_head()
    s1 = jnp.where(diag, both, 0.0)
    s2 = jnp.where(diag, pltpu.roll(both, HEAD, 1), 0.0)
    z = tot[PAIR : PAIR + 1] + tot[PAIR + 1 : PAIR + 2]
    return s1, s2, z


def split_dot(a, ones):
    hi, lo = two(a)
    return dot(hi, ones) + dot(lo, ones)


def two(a):
    hi = a.astype(bf16)
    return hi, (a - hi.astype(f32)).astype(bf16)


def phi(v):
    low = jnp.exp(jnp.minimum(v, 0.0))
    return jnp.where(v > 0, v + 1.0, low), jnp.where(v > 0, 1.0, low)


def band_parts():
    c = lax.broadcasted_iota(jnp.int32, (WIN, 2 * QB), 0)
    r = lax.broadcasted_iota(jnp.int32, (WIN, 2 * QB), 1) % QB
    off = r + EDGE - c
    return (jnp.abs(off) <= BAND), off == 0, c


def stacked(rows):
    lane = lax.broadcasted_iota(jnp.int32, (1, PAIR), 1)
    first = (lane < HEAD).astype(f32).astype(bf16)
    second = (lane >= HEAD).astype(f32).astype(bf16)
    return jnp.concatenate([rows * first, rows * second], axis=0)


def unstack(both):
    lane = lax.broadcasted_iota(jnp.int32, (QB, PAIR), 1)
    return jnp.where(lane < HEAD, both[:QB], both[QB:])


def softmax_of(raw, mask):
    scores = jnp.where(mask, raw * 0.125, -1e30)
    ex = jnp.exp(scores - jnp.max(scores, axis=0, keepdims=True))
    return ex * (1.0 / jnp.sum(ex, axis=0, keepdims=True))


def fetch_pieces(meta, first, own, oth, lo, rows, weight, sem):
    n = own.shape[0]
    core = meta[2]
    copies = []
    for pq in range(n):
        for buf, row, half in ((own, meta[first + pq], core), (oth, meta[first + n + pq], 1 - core)):
            at = pl.ds(pl.multiple_of((half * n + pq) * rows, rows), rows)
            for m in range(buf.shape[1]):
                src = buf.at[row, m, pl.ds(lo, rows), :]
                copies.append(pltpu.make_async_copy(src, weight.at[meta[15] ^ m, at, :], sem))
    for c in copies:
        c.start()
    return copies


def norm_body(tok, left, right, gains, biases, a1e_o):
    rows = tok.shape[0]
    gain, bias = gains[0:1, :], biases[0:1, :]

    def ln(x):
        return (normalize(x.astype(f32))[0] * gain + bias).astype(bf16)

    a1e_o[0:HALO, :] = ln(left[...])
    a1e_o[HALO + rows :, :] = ln(right[...])

    def chunk(i, _):
        at = pl.ds(pl.multiple_of(i * 128, 128), 128)
        a1e_o[pl.ds(pl.multiple_of(i * 128 + HALO, 64), 128), :] = ln(tok[at, :])
        return 0

    lax.fori_loop(0, rows // 128, chunk, 0)


def qkv_body(meta, a1e, own, oth, qkv_o, st_o, w, sem):
    ext = a1e.shape[0]
    rows = ext - 2 * HALO
    groups = own.shape[1]
    for c in fetch_pieces(meta, 11, own, oth, 0, own.shape[2], w, sem):
        c.wait()
    length, base = meta[0], meta[1]
    pos = base + lax.broadcasted_iota(jnp.int32, (rows, 1), 0)
    valid = (pos < length).astype(f32)
    gs = range(groups)
    for g in gs:
        qkv_o[g] = dot(a1e[...], w[g]).astype(bf16)
    own_rows = slice(HALO, HALO + rows)
    parts = []
    for g in gs:
        keys = qkv_o[g, own_rows, PAIR : 2 * PAIR].astype(f32)
        feat = phi(keys)[0] * valid
        parts.append((jnp.sum(feat, axis=0, keepdims=True), two(feat), two(jnp.tanh(keys) * valid)))
    for g in gs:
        z, (fhi, flo), (thi, tlo) = parts[g]
        vals = qkv_o[g, own_rows, 2 * PAIR :]
        s1 = dot_tn(fhi, vals) + dot_tn(flo, vals)
        s2 = dot_tn(thi, vals) + dot_tn(tlo, vals)
        st_o[g, :PAIR, :], st_o[g, PAIR:, :] = pack_state(s1, s2, z)


def near_body(meta, qkv, near_o):
    groups = qkv.shape[0]
    rows = near_o.shape[0]
    length, base = meta[0], meta[1]
    band, diag, lane = band_parts()

    def block(b, _):
        at = b * QB
        kpos = base + at - EDGE + lane
        mask = band & (((kpos >= 0) & (kpos < length)) | diag)
        q_at = pl.ds(pl.multiple_of(at + HALO, QB), QB)
        w_at = pl.ds(pl.multiple_of(at + HALO - EDGE, EDGE), WIN)
        gs = range(groups)
        sc = [dot_nt(qkv[g, w_at, PAIR : 2 * PAIR], stacked(qkv[g, q_at, 0:PAIR])) for g in gs]
        p = [softmax_of(sc[g], mask).astype(bf16) for g in gs]
        res = [dot_tn(p[g], qkv[g, w_at, 2 * PAIR :]) for g in gs]
        for g in gs:
            near_o[pl.ds(pl.multiple_of(at, QB), QB), g * PAIR : (g + 1) * PAIR] = unstack(res[g])
        return 0

    lax.fori_loop(0, rows // QB, block, 0, unroll=4)


def put_halves(core, keep, give, g, lo, grad):
    n, width = grad.shape
    tiles = grad.reshape(n // 16, 2, 8, width)
    even, odd = tiles[:, 0].reshape(n // 2, width), tiles[:, 1].reshape(n // 2, width)
    first = jnp.full(even.shape, core, jnp.int32) == 0
    at = slice(lo, lo + n // 2)
    keep[g, at, :] = jnp.where(first, even, odd).astype(keep.dtype)
    give[g, at, :] = jnp.where(first, odd, even).astype(give.dtype)


def main_body(
    meta, near, qkv, s0, s1, s2, s3, tok, cot, gains, biases, io_own, io_oth, dn_own, dn_oth,
    out_h, do_o, dx2_h, dctx_o, dqf_h, dst_o, ng_o, wout_o, keep_h, give_h,
    w_in, w_down, x2, xhat, rs, u, dh, acc, da2, far1, inv, dnum, phq, thq,
    ctx_o, a2_o, dm_o, hid_o, du_o, out_o, give, sem, out_sem,
):
    rows, width = tok.shape
    groups = dn_own.shape[1]
    pr = dn_own.shape[2]
    orow = io_own.shape[2] - pr
    core = meta[2]
    sent = []

    def send(src, dst):
        sent.append(pltpu.make_async_copy(src, dst, out_sem))
        sent[-1].start()

    length, base = meta[0], meta[1]
    copies = fetch_pieces(meta, 3, io_own, io_oth, pr, orow, wout_o, sem.at[0])
    later = fetch_pieces(meta, 3, io_own, io_oth, 0, pr, w_in, sem.at[1])
    last = fetch_pieces(meta, 3, dn_own, dn_oth, 0, pr, w_down, sem.at[2])
    rlen = 1.0 / length.astype(f32)
    gain, bias = gains[1:2, :], biases[1:2, :]
    ones = same_head().astype(f32).astype(bf16)
    gs = range(groups)
    cols = [slice(g * PAIR, (g + 1) * PAIR) for g in gs]
    states = [unpack_state((s0, s1, s2, s3), g) for g in gs]
    s1b, s2b = [two(st[0]) for st in states], [two(st[1]) for st in states]
    cr = 128

    def far_chunk(i, _):
        at = pl.ds(pl.multiple_of(i * cr, cr), cr)
        q_at = pl.ds(pl.multiple_of(i * cr + HALO, HALO), cr)
        q = [qkv[g, q_at, 0:PAIR].astype(f32) for g in gs]
        ph = [phi(q[g])[0] for g in gs]
        ph2 = [two(ph[g]) for g in gs]
        th2 = [two(jnp.tanh(q[g])) for g in gs]
        den = [split_dot(ph[g] * states[g][2], ones) for g in gs]
        num = [dot(ph2[g][0], s1b[g][0]) + dot(ph2[g][0], s1b[g][1]) + dot(ph2[g][1], s1b[g][0]) for g in gs]
        sec = [dot(th2[g][0], s2b[g][0]) + dot(th2[g][0], s2b[g][1]) + dot(th2[g][1], s2b[g][0]) for g in gs]
        for g in gs:
            phq[at, cols[g]] = ph2[g][0]
            thq[at, cols[g]] = th2[g][0]
        rec = [1.0 / den[g] for g in gs]
        for g in gs:
            part = num[g] * rec[g]
            inv[at, cols[g]] = rec[g]
            far1[at, cols[g]] = part
            ctx_o[at, cols[g]] = (near[at, cols[g]] + (part + sec[g] * rlen)).astype(bf16)
        pos = base + i * cr + lax.broadcasted_iota(jnp.int32, (cr, 1), 0)
        dm_o[at, :] = (cot[at, :].astype(f32) * (pos < length).astype(f32)).astype(bf16)
        return 0

    lax.fori_loop(0, rows // cr, far_chunk, 0)
    for c in copies:
        c.wait()
    wout = wout_o[...].reshape(width, width)
    x2[...] = dot(ctx_o[...], wout)

    def norm_chunk(i, _):
        at = pl.ds(pl.multiple_of(i * 64, 64), 64)
        val = x2[at, :] + tok[at, :].astype(f32)
        x2[at, :] = val
        xh, rstd = normalize(val)
        xhat[at, :] = xh
        rs[at, :] = jnp.broadcast_to(rstd, (64, 128))
        a2_o[at, :] = (xh * gain + bias).astype(bf16)
        return 0

    lax.fori_loop(0, rows // 64, norm_chunk, 0)
    for c in later + last:
        c.wait()
    for g in gs:
        u[g, 0:rows, :] = dot(a2_o[...], w_in[g])
        dh[g, 0:rows, :] = dot_nt(dm_o[...], w_down[g])

    def act(i, _):
        at = pl.ds(pl.multiple_of(i * 16, 16), 16)
        for g in gs:
            v = u[g, at, :]
            sq = v * v
            half = 0.5 + 0.5 * jnp.tanh(v * (GELU_C + GELU_C * GELU_A * sq))
            hid = v * half
            hid_o[g, at, :] = hid.astype(bf16)
            slope = half + (hid * (1.0 - half)) * (2.0 * GELU_C + 6.0 * GELU_C * GELU_A * sq)
            du_o[g, at, :] = (dh[g, at, :] * slope).astype(bf16)
        return 0

    lax.fori_loop(0, rows // 16, act, 0)
    acc[...] = sum(dot(hid_o[g], w_down[g]) for g in gs)
    da2[...] = sum(dot_nt(du_o[g], w_in[g]) for g in gs)

    def back_chunk(i, carry):
        dg, db = carry
        at = pl.ds(pl.multiple_of(i * 64, 64), 64)
        out_o[at, :] = (x2[at, :] + acc[at, :]).astype(bf16)
        xh = xhat[at, :]
        rstd = rs[at, 0:1]
        d = da2[at, :]
        dg = dg + jnp.sum(d * xh, axis=0, keepdims=True)
        db = db + jnp.sum(d, axis=0, keepdims=True)
        e = d * gain
        m1 = jnp.mean(e, axis=-1, keepdims=True)
        m2 = jnp.mean(e * xh, axis=-1, keepdims=True)
        dx = dm_o[at, :].astype(f32) + rstd * (e - m1 - xh * m2)
        acc[at, :] = dx
        do_o[at, :] = dx.astype(bf16)
        return dg, db

    zero = jnp.zeros((1, width), f32)
    dg, db = lax.fori_loop(0, rows // 64, back_chunk, (zero, zero))
    send(out_o, out_h)
    send(acc, dx2_h)
    ng_o[0:1, :] = dg
    ng_o[1:2, :] = db
    dctx_o[...] = dot_nt(do_o[...], wout).astype(bf16)

    def far_back(i, carry):
        at = pl.ds(pl.multiple_of(i * cr, cr), cr)
        q_at = pl.ds(pl.multiple_of(i * cr + HALO, HALO), cr)
        dc = [dctx_o[at, cols[g]] for g in gs]
        dcf = [dc[g].astype(f32) for g in gs]
        rec = [inv[at, cols[g]] for g in gs]
        dn = [(dcf[g] * rec[g]).astype(bf16) for g in gs]
        dots = [split_dot(dcf[g] * far1[at, cols[g]], ones) for g in gs]
        dph = [dot_nt(dn[g], s1b[g][0]) for g in gs]
        dth = [dot_nt(dc[g], s2b[g][0]) for g in gs]
        out = []
        for g in gs:
            dnum[at, cols[g]] = dn[g]
            dden = -dots[g] * rec[g]
            out.append(carry[g] + jnp.sum(phq[at, cols[g]].astype(f32) * dden, axis=0, keepdims=True))
            slope = phi(qkv[g, q_at, 0:PAIR].astype(f32))[1]
            th = thq[at, cols[g]].astype(f32)
            da2[at, cols[g]] = (dph[g] + dden * states[g][2]) * slope + dth[g] * rlen * (1.0 - th * th)
        return tuple(out)

    none = jnp.zeros((1, PAIR), f32)
    dz = lax.fori_loop(0, rows // cr, far_back, (none,) * groups)
    for g in gs:
        d1 = dot_tn(phq[:, cols[g]], dnum[:, cols[g]])
        d2 = dot_tn(thq[:, cols[g]], dctx_o[:, cols[g]]) * rlen
        dst_o[g, :PAIR, :], dst_o[g, PAIR:, :] = pack_state(d1, d2, dz[g])
    send(da2, dqf_h)
    n_out = ctx_o.shape[1] // groups
    hw = hid_o.shape[2]
    keep = u

    def finish(g, lo, n, grad):
        put_halves(core, keep, give, g, lo, grad)
        part = pl.ds(lo, n)
        send(keep.at[g, part, :], keep_h.at[g, part, :])
        send(give.at[g, part, :], give_h.at[g, part, :])

    for g in gs:
        finish(g, n_out // 2, width // 2, dot_tn(a2_o[...], du_o[g]))
    for g in gs:
        finish(g, 0, n_out // 2, dot_tn(ctx_o[:, g * n_out : (g + 1) * n_out], do_o[...]))
    for g in gs:
        finish(g, n_out // 2 + width // 2, hw // 2, dot_tn(hid_o[g], dm_o[...]))
    for c in sent:
        c.wait()


def near_back_body(
    meta, qkv, dctx, do_l, do_r, wout_h, dqf_h, dq_o, dk_o, dv_o, dce, dqe, dke, dve, wout, dqf, sem,
):
    groups = qkv.shape[0]
    rows = dctx.shape[0]
    length, base = meta[0], meta[1]
    band, diag, lane = band_parts()
    first = pltpu.make_async_copy(wout_h, wout, sem.at[0])
    first.start()
    second = pltpu.make_async_copy(dqf_h, dqf, sem.at[1])
    second.start()
    first.wait()
    w = wout[...].reshape(dctx.shape[1], -1)
    dce[0:EDGE, :] = dot_nt(do_l[...], w).astype(bf16)
    dce[EDGE : EDGE + rows, :] = dctx[...]
    dce[EDGE + rows :, :] = dot_nt(do_r[...], w).astype(bf16)
    dke[...] = jnp.zeros(dke.shape, f32)
    dve[...] = jnp.zeros(dve.shape, f32)

    def block(b, _):
        at = b * QB
        kpos = base + at - HALO + lane
        mask = band & (((kpos >= 0) & (kpos < length)) | diag)
        c_at = pl.ds(pl.multiple_of(at, QB), QB)
        q_at = pl.ds(pl.multiple_of(at + EDGE, EDGE), QB)
        w_at = pl.ds(pl.multiple_of(at, QB), WIN)
        gs = range(groups)
        cols = [slice(g * PAIR, (g + 1) * PAIR) for g in gs]
        qs = [stacked(qkv[g, q_at, 0:PAIR]) for g in gs]
        cs = [stacked(dce[c_at, cols[g]]) for g in gs]
        kw = [qkv[g, w_at, PAIR : 2 * PAIR] for g in gs]
        sc = [dot_nt(kw[g], qs[g]) for g in gs]
        dp = [dot_nt(qkv[g, w_at, 2 * PAIR :], cs[g]) for g in gs]
        p = [softmax_of(sc[g], mask) for g in gs]
        row = [jnp.sum(p[g] * dp[g], axis=0, keepdims=True) for g in gs]
        ds = [(p[g] * (dp[g] - row[g])).astype(bf16) for g in gs]
        pb = [p[g].astype(bf16) for g in gs]
        for g in gs:
            dke[w_at, cols[g]] += dot(ds[g], qs[g])
            dve[w_at, cols[g]] += dot(pb[g], cs[g])
        dq = [dot_tn(ds[g], kw[g]) for g in gs]
        for g in gs:
            dqe[c_at, cols[g]] = unstack(dq[g])
        return 0

    lax.fori_loop(0, rows // QB + 1, block, 0, unroll=3)
    second.wait()
    dq_o[...] = (dqe[EDGE : EDGE + rows, :] * 0.125 + dqf[...]).astype(bf16)
    dk_o[...] = dke[HALO : HALO + rows, :] * 0.125
    dv_o[...] = dve[HALO : HALO + rows, :]


def proj_body(meta, qkv, dq, dkn, dvn, s0, s1, s2, s3, a1e, dproj_h, keep_o, give_o, dproj, flat, pseudo, sem):
    groups = qkv.shape[0]
    rows, width = dq.shape
    length, base, core = meta[0], meta[1], meta[2]
    cr = 128
    gs = range(groups)
    cols = [slice(g * PAIR, (g + 1) * PAIR) for g in gs]
    states = [unpack_state((s0, s1, s2, s3), g) for g in gs]
    s1b, s2b = [st[0].astype(bf16) for st in states], [st[1].astype(bf16) for st in states]

    def far_chunk(i, _):
        at = pl.ds(pl.multiple_of(i * cr, cr), cr)
        e_at = pl.ds(pl.multiple_of(i * cr + HALO, HALO), cr)
        pos = base + i * cr + lax.broadcasted_iota(jnp.int32, (cr, 1), 0)
        valid = (pos < length).astype(f32)
        k = [qkv[g, e_at, PAIR : 2 * PAIR].astype(f32) for g in gs]
        v = [qkv[g, e_at, 2 * PAIR :] for g in gs]
        feat = [phi(k[g]) for g in gs]
        th = [jnp.tanh(k[g]) for g in gs]
        vd1 = [dot_nt(v[g], s1b[g]) for g in gs]
        vd2 = [dot_nt(v[g], s2b[g]) for g in gs]
        dv = [
            dot((feat[g][0] * valid).astype(bf16), s1b[g]) + dot((th[g] * valid).astype(bf16), s2b[g]) for g in gs
        ]
        for g in gs:
            dk = (vd1[g] + states[g][2]) * feat[g][1] + vd2[g] * (1.0 - th[g] * th[g])
            dproj[g, at, 0:PAIR] = dq[at, cols[g]]
            dproj[g, at, PAIR : 2 * PAIR] = (dkn[at, cols[g]] + dk * valid).astype(bf16)
            dproj[g, at, 2 * PAIR :] = (dvn[at, cols[g]] + dv[g]).astype(bf16)
        return 0

    lax.fori_loop(0, rows // cr, far_chunk, 0)
    out = pltpu.make_async_copy(dproj, dproj_h, sem)
    out.start()
    n_flat = 3 * width
    for g in gs:
        grad = dot_tn(a1e[HALO : HALO + rows, :], dproj[g])
        for part in range(3):
            flat[pl.ds(part, width, stride=3), :] = grad[:, part * PAIR : (part + 1) * PAIR]
        for j in range(4):
            pseudo[:, j * 128 : (j + 1) * 128] = flat[pl.ds(j, n_flat // 4, stride=4), :]
        put_halves(core, keep_o, give_o, g, 0, pseudo[...])
    out.wait()


def last_body(
    meta, dproj_h, own, oth, tok, dx2_h, gains, ng2, tg_o, ng_o, da1, ngs, wqkv, dproj, dx2, sem, sems,
):
    groups = dproj.shape[0]
    rows, width = tok.shape
    gain = gains[0:1, :]
    copies = fetch_pieces(meta, 11, own, oth, 0, own.shape[2], wqkv, sem)
    copies.append(pltpu.make_async_copy(dproj_h, dproj, sems.at[0]))
    copies[-1].start()
    late = pltpu.make_async_copy(dx2_h, dx2, sems.at[1])
    late.start()
    for c in copies:
        c.wait()
    da1[...] = sum(dot_nt(dproj[g], wqkv[g]) for g in range(groups))

    late.wait()

    def back_chunk(i, carry):
        dg, db = carry
        at = pl.ds(pl.multiple_of(i * 64, 64), 64)
        xh, rstd = normalize(tok[at, :].astype(f32))
        d = da1[at, :]
        dg = dg + jnp.sum(d * xh, axis=0, keepdims=True)
        db = db + jnp.sum(d, axis=0, keepdims=True)
        e = d * gain
        m1 = jnp.mean(e, axis=-1, keepdims=True)
        m2 = jnp.mean(e * xh, axis=-1, keepdims=True)
        tg_o[at, :] = dx2[at, :] + rstd * (e - m1 - xh * m2)
        return dg, db

    zero = jnp.zeros((1, width), f32)
    dg, db = lax.fori_loop(0, rows // 64, back_chunk, (zero, zero))
    for k, val in enumerate((dg, db, ng2[0:1, :], ng2[1:2, :])):
        for j in range(width // 128):
            at = k * (width // 128) + j
            ngs[at : at + 1, :] = val[:, j * 128 : (j + 1) * 128]
    n = ngs.shape[0]
    hi = ngs[...].astype(bf16)
    ng_o[0:n, :] = hi
    ng_o[n:, :] = (ngs[...] - hi.astype(f32)).astype(bf16)


def slices_body(where, master, first, second, out_h, held, parts, sem, out_sem):
    caps = held.shape[1] // 64
    copies = [pltpu.make_async_copy(ref, held.at[t], sem.at[t]) for t, ref in enumerate((master, first, second))]
    for c in copies:
        c.start()
    sent = []
    for t in range(3):
        copies[t].wait()
        for j in range(4):
            val = held[t, pl.ds(j, caps * 16, stride=4), :].reshape(caps, 2, 8, 128)
            for c in range(2):
                parts[t, c, j] = val[:, c].reshape(caps * 8, 128)
                for d in where[c][j]:
                    sent.append(pltpu.make_async_copy(parts.at[t, c, j], out_h.at[d, t], out_sem))
                    sent[-1].start()
    for c in sent:
        c.wait()


def adam(g, m_old, f_old, s_old):
    corr_one = 1.0 - beta_one**STEP
    corr_two = 1.0 - beta_two**STEP
    fn = beta_one * f_old + (1.0 - beta_one) * g
    sn = beta_two * s_old + (1.0 - beta_two) * g * g
    step = fn / corr_one / (jnp.sqrt(sn / corr_two) + adam_epsilon)
    return fn, sn, m_old - learn_rate * (step + decay_rate * m_old)


def pieces_body(first, count, owners, slots, *refs):
    parts, st, piece_o, w_o, norms = refs[:count], refs[count], refs[count + 1], refs[count + 2], refs[count + 3 :]
    n = piece_o.shape[0]
    src = [(r, s) for r in parts for s in range(r.shape[0])]
    piece_o[...] = sum(r[s, 0:n, :].astype(f32) for r, s in src)
    if norms:
        k = (parts[0].shape[1] - n) // 2
        norms[0][...] = sum(r[s, n : n + k, :].astype(f32) + r[s, n + k :, :].astype(f32) for r, s in src)

    def pair(i, _):
        new = []
        for k in range(2):
            b = i * 2 + k
            at = pl.ds(pl.multiple_of(slots[first + b] * 8, 8), 8)
            own = owners[first + b]
            g = piece_o[pl.ds(pl.multiple_of(b * 8, 8), 8), :]
            new.append(adam(g, st[own, 0, at, :], st[own, 1, at, :], st[own, 2, at, :])[2])
        w_o[pl.ds(pl.multiple_of(i * 16, 16), 16), :] = jnp.concatenate(new, axis=0).astype(bf16)
        return 0

    lax.fori_loop(0, n // 16, pair, 0, unroll=4)


def route_body(blocks, pq, pm, ng, send_o):
    nq = pq.shape[0] // 8
    dests, per, _ = send_o.shape
    caps = (per - ng.shape[0]) // 8

    def dest(d, _):
        for r in range(caps):
            b = blocks[d * caps + r]
            one = pq[pl.ds(pl.multiple_of(jnp.minimum(b, nq - 1) * 8, 8), 8), :]
            two_ = pm[pl.ds(pl.multiple_of(jnp.maximum(b - nq, 0) * 8, 8), 8), :]
            send_o[d, r * 8 : r * 8 + 8, :] = jnp.where(jnp.full((8, 128), b, jnp.int32) < nq, one, two_)
        send_o[d, caps * 8 :, :] = ng[...]
        return 0

    lax.fori_loop(0, dests, dest, 0)


def adam_body(filled, sources, recv, master, first, second, f_o, s_o, m_o, ng_o, two, grad):
    caps, br, _ = master.shape
    for j in range(4):
        for c in range(2):
            two[:, c] = recv[sources[c * 4 + j], 0 : caps * 8, :].reshape(caps, 8, 128)
        grad[pl.ds(j, caps * 16, stride=4), :] = two[...].reshape(caps * 16, 128)

    def add(s, tot):
        return tot + recv[s, caps * 8 :, :]

    ng_o[...] = lax.fori_loop(0, recv.shape[0], add, jnp.zeros(ng_o.shape, f32))

    def slot(r, _):
        g = grad[pl.ds(pl.multiple_of(r * br, br), br), :]
        m_old, f_old, s_old = master[r], first[r], second[r]
        fn, sn, mn = adam(g, m_old, f_old, s_old)
        keep = jnp.full(g.shape, filled[r], jnp.int32) > 0
        f_o[r] = jnp.where(keep, fn, f_old)
        s_o[r] = jnp.where(keep, sn, s_old)
        m_o[r] = jnp.where(keep, mn, m_old)
        return 0

    lax.fori_loop(0, caps, slot, 0, unroll=2)


def columns(meta, own, oth, j, lo, n):
    core = meta[2]
    a = own[meta[3 + j], lo : lo + n, :].astype(f32)
    b = oth[meta[7 + j], lo : lo + n, :].astype(f32)
    first = jnp.full(a.shape, core, jnp.int32) == 0
    even, odd = jnp.where(first, a, b), jnp.where(first, b, a)
    both = jnp.concatenate([even.reshape(n // 8, 1, 8, 128), odd.reshape(n // 8, 1, 8, 128)], axis=1)
    return both.reshape(2 * n, 128)


def place_body(meta, own, oth, out_o, in_o, down_o):
    lo = 0
    for ref in (out_o, in_o, down_o):
        n = ref.shape[0] // 2
        for j in range(4):
            ref[:, j * 128 : (j + 1) * 128] = columns(meta, own, oth, j, lo, n).astype(bf16)
        lo += n


def place_qkv_body(meta, own, oth, q_o, flat):
    n = own.shape[1]
    rows = q_o.shape[0]
    for j in range(4):
        flat[pl.ds(j, 2 * n, stride=4), :] = columns(meta, own, oth, j, 0, n)
    for part in range(3):
        q_o[:, part * 128 : (part + 1) * 128] = flat[pl.ds(part, rows, stride=3), :].astype(bf16)


def per_device(
    tokens, cotangent, lengths, owners, w_qkv, w_out, w_in, w_down,
    master, first_moment, second_moment, norm_gains, norm_biases, norm_first, norm_second,
):
    rows, width = tokens.shape[1], tokens.shape[2]
    groups = lax.axis_size("mp")
    ndp = lax.axis_size("dp")
    nbits = ndp.bit_length() - 1
    rest = list(range(1, nbits))
    order = (rest, rest[:2][::-1] + rest[2:][::-1])
    me, zi = lax.axis_index("dp"), lax.axis_index("mp")
    core = me & 1

    def bit_of(who, at, s):
        return (who >> jnp.where(at == 0, order[0][s], order[1][s])) & 1

    def swap(x, s):
        return lax.ppermute(x, "dp", [(i, i ^ (1 << order[i & 1][s])) for i in range(ndp)])

    def swap_core(x):
        return lax.ppermute(x, "dp", [(i, i ^ 1) for i in range(ndp)])

    def from_mp(x, step):
        return lax.ppermute(x, "mp", [(i, i + step) for i in range(groups) if 0 <= i + step < groups])

    def swap_mp(x, mask):
        return lax.ppermute(x, "mp", [(i, i ^ mask) for i in range(groups)])

    def exchange(x, axis):
        return lax.all_to_all(x, axis, 0, 0, tiled=True)

    def all_states(x):
        return [x] + [swap_mp(x, m) for m in range(1, groups)]

    q0, q1 = bit_of(me, core, 0), bit_of(me, core, 1)
    o0, o1 = bit_of(me, 1 - core, 0), bit_of(me, 1 - core, 1)
    length = lengths[0]
    base = zi * rows
    ids = [length, base, core]
    ids += [((t >> 1) ^ q0) + 2 * ((t & 1) ^ q1) for t in range(4)]
    ids += [((t >> 1) ^ o0) + 2 * ((t & 1) ^ o1) for t in range(4)]
    ids += [q0, 1 - q0, o0, 1 - o0, zi]
    meta = jnp.stack(ids).astype(jnp.int32)

    def after(x, *deps):
        return lax.optimization_barrier((x,) + deps)[0]

    def over_mp(piece):
        return jnp.stack([piece] + [swap_mp(piece, m) for m in range(1, groups)])[None]

    def grow(buf, s):
        return jnp.concatenate([buf, swap(buf, s)], axis=0)

    def part_of(w, n, at):
        return lax.dynamic_slice_in_dim(w, at * (w.shape[0] // n), w.shape[0] // n, 0)

    mine = core * 4 + q0 * 2 + q1
    tok, cot = tokens[0], cotangent[0]
    ext = rows + 2 * HALO
    mm = 2 * rows * width
    qkv_z = over_mp(part_of(w_qkv, 4, core * 2 + q0))
    left, right = from_mp(tok[rows - HALO :], 1), from_mp(tok[:HALO], -1)
    io_piece = jnp.concatenate([part_of(w_in, 8, mine), part_of(w_out, 8, mine)], axis=0)
    io_z = over_mp(io_piece)
    dn_z = over_mp(part_of(w_down, 8, mine))
    [a1e] = call(norm_body, [((ext, width), bf16)], [VM] * 5, [], 4 * mm, 1 << 20, 16)(
        tok, left, right, norm_gains, norm_biases
    )
    qkv_own = grow(after(qkv_z, a1e), 0)
    io_z = after(io_z, qkv_own)
    qkv_oth = swap_core(after(qkv_own, io_z))
    io_one = grow(io_z, 0)
    proj_w = pltpu.VMEM((groups, width, 3 * PAIR), bf16)
    qkv, state = call(
        qkv_body,
        [((groups, ext, 3 * PAIR), bf16), ((groups, STATE, PAIR), bf16)],
        [SM, VM, HB, HB],
        [proj_w, pltpu.SemaphoreType.DMA],
        2 * ext * width * 3 * width, 6 << 20, 20,
    )(meta, after(a1e, dn_z), qkv_own, qkv_oth)
    states = all_states(state)
    io_one = after(io_one, qkv)
    dn_one = grow(after(dn_z, io_one), 0)
    io_own = grow(io_one, 1)
    capacity, block_rows = master.shape[0], master.shape[1]
    where = [[[] for _ in range(4)] for _ in range(2)]
    for d in range(ndp):
        b = order[d & 1]
        where[d & 1][2 * ((d >> b[0]) & 1) + ((d >> b[1]) & 1)].append(d)
    flat_state = [x.reshape(capacity * block_rows, 128) for x in (master, first_moment, second_moment)]
    [parts] = call(
        functools.partial(slices_body, where), [((ndp, 3, capacity * 8, 128), f32)], [HB] * 3,
        [
            pltpu.VMEM((3, capacity * block_rows, 128), f32), pltpu.VMEM((3, 2, 4, capacity * 8, 128), f32),
            pltpu.SemaphoreType.DMA((3,)), pltpu.SemaphoreType.DMA,
        ],
        1 << 20, 4 << 20, 12, (HB,),
    )(*flat_state)
    [near] = call(
        near_body, [((rows, width), f32)], [SM, VM], [], mm * 1024, 12 << 20, 16,
    )(meta, after(qkv, dn_one, parts, *states))
    io_oth = swap_core(after(io_own, near))
    dn_own = grow(after(dn_one, *states), 1)
    dn_oth = swap_core(after(dn_own, near))

    held_state = exchange(after(parts, dn_own), "dp")

    hid_w = w_in.shape[1]
    big = pltpu.VMEM((rows, width), f32)
    low = pltpu.VMEM((rows, width), bf16)
    n_m = (w_out.shape[0] + w_in.shape[0] + w_down.shape[0]) // 2
    wide = pltpu.VMEM((groups, max(rows, n_m), hid_w), f32)
    four = pltpu.VMEM((groups, rows, hid_w), bf16)
    (outputs, do, dx2, dctx, dqf, dstate, ng2, wout, grad_m, give_m) = call(
        main_body,
        [
            ((rows, width), bf16), ((rows, width), bf16), ((rows, width), f32), ((rows, width), bf16),
            ((rows, width), f32), ((groups, STATE, PAIR), bf16), ((2, width), f32),
            ((groups,) + w_out.shape, bf16), ((groups, n_m, width), f32), ((groups, n_m, width), bf16),
        ],
        [SM] + [VM] * 10 + [HB] * 4,
        [
            pltpu.VMEM((groups, width, hid_w), bf16), pltpu.VMEM((groups, hid_w, width), bf16),
            big, big, pltpu.VMEM((rows, 128), f32), wide, wide, big, big, big, big,
            low, low, low, low, low, low, four, four, low, pltpu.VMEM((groups, n_m, width), bf16),
            pltpu.SemaphoreType.DMA((3,)), pltpu.SemaphoreType.DMA,
        ],
        mm * hid_w * groups * 6, 24 << 20, 44,
        (HB, VM, HB, VM, HB, VM, VM, VM, HB, HB),
    )(meta, near, qkv, *states, tok, cot, norm_gains, norm_biases, io_own, io_oth, dn_own, dn_oth)

    do, dstate, give_m, grad_m, _ = lax.optimization_barrier((do, dstate, give_m, grad_m, held_state))
    dstates = all_states(dstate)
    do_l, do_r = from_mp(do[rows - EDGE :], 1), from_mp(do[:EDGE], -1)

    def halve(own, got, s):
        n = own.shape[-1] // 2
        bit = bit_of(me, core, s)

        def half(at, own, got):
            a = lax.dynamic_slice_in_dim(own, at * n, n, own.ndim - 1).astype(f32)
            return a + lax.dynamic_slice_in_dim(got, at * n, n, own.ndim - 1).astype(f32)

        give = half(1 - bit, own, got).astype(bf16)
        own, got = after(own, give), after(got, give)
        return give, half(bit, own, got)

    def finish(keep, got, extra=None):
        tot = keep + got.astype(f32)
        for s in range(2, nbits - 1):
            tot = tot.astype(bf16).astype(f32) + swap(tot.astype(bf16), s).astype(f32)
        msg = tot.astype(bf16)
        if extra is None:
            return [exchange(msg, "mp")]
        more = jnp.broadcast_to(extra, (groups,) + extra.shape)
        msg = jnp.concatenate([msg, more], axis=1)
        part = [lax.dynamic_slice_in_dim(msg, zi ^ m, 1, 0) for m in range(groups)]
        return part[:1] + [swap_mp(part[m], m) for m in range(1, groups)]

    give_m, keep_m = halve(grad_m, swap_core(give_m), 0)
    got_m = swap(give_m, 0)
    dq, dkn, dvn = call(
        near_back_body,
        [((rows, width), bf16), ((rows, width), f32), ((rows, width), f32)],
        [SM] + [VM] * 4 + [HB] * 2,
        [
            pltpu.VMEM((rows + 2 * EDGE, width), bf16), pltpu.VMEM((rows + 2 * EDGE, width), f32),
            pltpu.VMEM((ext, width), f32), pltpu.VMEM((ext, width), f32),
            pltpu.VMEM(wout.shape, bf16), big, pltpu.SemaphoreType.DMA((2,)),
        ],
        mm * 2048, 24 << 20, 20,
    )(meta, qkv, after(dctx, give_m, *dstates), do_l, do_r, wout, dqf)
    give_m, keep_m = halve(keep_m, after(got_m, dq), 1)
    got_m = swap(give_m, 1)
    n_q = w_qkv.size // width // 2
    n_ng = 4 * width // 128
    dproj, grad_q, give_q = call(
        proj_body,
        [((groups, rows, 3 * PAIR), bf16), ((groups, n_q, width), f32), ((groups, n_q, width), f32)],
        [SM] + [VM] * 9,
        [
            pltpu.VMEM((groups, rows, 3 * PAIR), bf16), pltpu.VMEM((3 * width, 128), f32),
            pltpu.VMEM((2 * n_q, width), f32), pltpu.SemaphoreType.DMA,
        ],
        mm * 3 * width, 24 << 20, 20, (HB, VM, VM),
    )(meta, qkv, after(dq, give_m), dkn, dvn, *dstates, a1e)
    got_q = swap_core(after(give_q, got_m))
    tokens_grad, ng = call(
        last_body,
        [((rows, width), f32), ((2 * n_ng, 128), bf16)],
        [SM, HB, HB, HB, VM, HB, VM, VM],
        [
            big, pltpu.VMEM((n_ng, 128), f32), proj_w, pltpu.VMEM((groups, rows, 3 * PAIR), bf16), big,
            pltpu.SemaphoreType.DMA, pltpu.SemaphoreType.DMA((2,)),
        ],
        mm * 3 * width, 8 << 20, 16,
    )(meta, dproj, qkv_own, qkv_oth, tok, dx2, norm_gains, ng2)
    give_q, keep_q = halve(grad_q, got_q, 0)
    got_q = swap(give_q, 0)
    z_m = finish(keep_m, got_m)
    give_q, keep_q = halve(keep_q, got_q, 1)
    got_q = swap(give_q, 1)
    z_q = finish(keep_q, got_q, ng)

    blocks = owners.shape[0]
    earlier = jnp.arange(blocks)[None, :] < jnp.arange(blocks)[:, None]
    alike = owners[None, :] == owners[:, None]
    slot = jnp.sum((earlier & alike).astype(jnp.int32), axis=1)
    slot_rows = owners * capacity + slot
    hit = slot_rows[None, :] == jnp.arange(ndp * capacity, dtype=jnp.int32)[:, None]
    held = jnp.sum(jnp.where(hit, jnp.arange(blocks, dtype=jnp.int32)[None, :], 0), axis=1)
    filled = lax.dynamic_slice_in_dim(
        jnp.sum(hit.astype(jnp.int32), axis=1), me * capacity, capacity, 0
    )
    nb_q = n_q * 2 // 16

    def updated(z, n, first, extra=()):
        return call(
            functools.partial(pieces_body, first, len(z)),
            [((n, 128), f32), ((n, 128), bf16)] + list(extra),
            [SM, SM] + [VM] * (len(z) + 1), [], 1 << 20, 4 << 20, 20,
        )(owners, slot, *z, held_state)

    def everywhere(piece):
        buf = piece[None]
        for s in range(2):
            buf = grow(buf, s)
        return buf, swap_core(buf)

    piece_m, fresh_m = updated(z_m, n_m, nb_q)
    m_own, m_oth = everywhere(fresh_m)
    piece_q, fresh_q, ng_z = updated(z_q, n_q, 0, [((n_ng, 128), f32)])
    q_own, q_oth = everywhere(fresh_q)
    [send] = call(
        route_body, [((ndp, capacity * 8 + n_ng, 128), f32)], [SM, VM, VM, VM], [], 1 << 20, 4 << 20, 16,
    )(held, piece_q, piece_m, ng_z)
    recv = exchange(send, "dp")
    high = me - (me & 7)
    sources = jnp.stack(
        [
            high + c + ((j >> 1) << order[c][0]) + ((j & 1) << order[c][1])
            for c in range(2)
            for j in range(4)
        ]
    ).astype(jnp.int32)
    state_shape = (capacity, block_rows, 128)
    first_new, second_new, master_new, norm_sum = call(
        adam_body,
        [(state_shape, f32)] * 3 + [((n_ng, 128), f32)],
        [SM, SM] + [VM] * 4,
        [pltpu.VMEM((capacity, 2, 8, 128), f32), pltpu.VMEM((capacity * block_rows, 128), f32)],
        1 << 20, 8 << 20, 20,
    )(filled, sources, recv, master, first_moment, second_moment)
    new_out, new_in, new_down = call(
        place_body, [(w_out.shape, bf16), (w_in.shape, bf16), (w_down.shape, bf16)],
        [SM, VM, VM], [], 1 << 20, 4 << 20, 16,
    )(meta, m_own, m_oth)
    [new_qkv] = call(
        place_qkv_body, [(w_qkv.shape, bf16)], [SM, VM, VM],
        [pltpu.VMEM((w_qkv.size // 128, 128), f32)], 1 << 20, 2 << 20, 16,
    )(meta, q_own, q_oth)

    corr_one = 1.0 - beta_one**STEP
    corr_two = 1.0 - beta_two**STEP
    norm_grad = norm_sum.reshape(4, width)
    norm_params = jnp.stack([norm_gains[0], norm_biases[0], norm_gains[1], norm_biases[1]])
    norm_first_new = beta_one * norm_first + (1.0 - beta_one) * norm_grad
    norm_second_new = beta_two * norm_second + (1.0 - beta_two) * norm_grad * norm_grad
    norm_new = norm_params - norm_rate * (
        norm_first_new / corr_one / (jnp.sqrt(norm_second_new / corr_two) + adam_epsilon)
    )
    return (
        outputs[None], tokens_grad[None], first_new, second_new, master_new,
        new_qkv, new_out, new_in, new_down, norm_first_new, norm_second_new, norm_new,
    )


def solution(mesh):
    sharded = P("dp", "mp", None)
    return jax.shard_map(
        per_device,
        mesh=mesh,
        in_specs=(
            sharded, sharded, P("dp"), P(), P(None, "mp"), P("mp", None), P(None, "mp"), P("mp", None),
            sharded, sharded, sharded, P(), P(), P(), P(),
        ),
        out_specs=(
            sharded, sharded, sharded, sharded, sharded,
            P(None, "mp"), P("mp", None), P(None, "mp"), P("mp", None), P(), P(), P(),
        ),
        check_vma=False,
    )
```

time: 318 us -> 254 us (0.80)
  waiting for transfers between devices: 111 us -> 69.2 us
  blocking collectives: 32.8 us -> 0 us
  Pallas kernels: 92 us -> 62.3 us
  starting transfers between devices: 44.2 us -> 68 us
  local copies, waits for them, and re-layouts: 19.4 us -> 28.1 us
  other arithmetic: 15.6 us -> 22.3 us
    ppermute x10 -> x13, waiting for transfers between devices: 69.3 us -> 17.9 us  [swap(): lax.ppermute(x, 'dp', [(i, i ^ 1 << order[i & 1][s]) for i in range(ndp)])]
    all_to_all x2 -> x0, blocking collectives: 32.8 us -> none  [exchange(): return lax.all_to_all(x, axis, 0, 0, tiled=True)]
    pallas_call x9 -> x14, Pallas kernels: 92 us -> 62.3 us  [fixed(): run(*[pltpu.with_memory_space_constraint(x, pltpu.HBM) if spec is HB else...]
    ppermute x6 -> x18, waiting for transfers between devices: 0.02 us -> 27.3 us  [swap_mp(): return lax.ppermute(x, 'mp', [(i, i ^ mask) for i in range(groups)])]
    all_to_all x3, waiting for transfers between devices: 33 us -> 12.7 us  [exchange(): return lax.all_to_all(x, axis, 0, 0, tiled=True)]
    ppermute x6 -> x18, starting transfers between devices: 8.84 us -> 28.5 us  [swap_mp(): return lax.ppermute(x, 'mp', [(i, i ^ mask) for i in range(groups)])]
    unnamed x42 -> x116, local copies, waits for them, and re-layouts: 8.82 us -> 18.9 us
    convert_element_type x2 -> x6, other arithmetic: 2.97 us -> 12.2 us  [the longest x4 8.54 us: halve(): give = half(1 - bit, own, got).astype(bf16)]
  transfers between devices with their start and end apart: 28 -> 45, of which waited for: 14 -> 18; matrix products, arithmetic and copies ran while one was open for 6% -> 11% of each run, Pallas kernels for 17% -> 22%
where the time goes in v2:
time: 254 us; the launch traced here: 252 us
  waiting for transfers between devices  69.2 us (27%)
  starting transfers between devices  68 us (27%)
  Pallas kernels  62.3 us (25%)
  local copies, waits for them, and re-layouts  28.1 us (11%)
  other arithmetic  22.3 us (9%)
    pallas_call x14, Pallas kernels, fixed(): run(*[pltpu.with_memory_space_constraint(x, pltpu.HBM) if spec is HB else...  62.3 us
    ppermute x18, starting transfers between devices, swap_mp(): return lax.ppermute(x, 'mp', [(i, i ^ mask) for i in range(groups)])  28.5 us
    ppermute x18, waiting for transfers between devices, swap_mp(): return lax.ppermute(x, 'mp', [(i, i ^ mask) for i in range(groups)])  27.3 us
    unnamed x116, local copies, waits for them, and re-layouts  18.9 us
    ppermute x13, waiting for transfers between devices, swap(): lax.ppermute(x, 'dp', [(i, i ^ 1 << order[i & 1][s]) for i in range(ndp)])  17.9 us
    ppermute x13, starting transfers between devices, swap(): lax.ppermute(x, 'dp', [(i, i ^ 1 << order[i & 1][s]) for i in range(ndp)])  16.6 us
    all_to_all x3, starting transfers between devices, exchange(): return lax.all_to_all(x, axis, 0, 0, tiled=True)  12.7 us
    all_to_all x3, waiting for transfers between devices, exchange(): return lax.all_to_all(x, axis, 0, 0, tiled=True)  12.7 us
  transfers between devices with their start and end apart: 45, of which 18 were waited for; matrix products, arithmetic and copies ran while one was open for 11% of the time, Pallas kernels for 22%

profile of v2, /device:TPU:0, one launch (start us, length us, event | category | flops | bytes accessed | tf_op | source)
XLA Modules:
  0.0 252.0 jit_solution(16988282029279005673)
XLA Ops:
  1.6 3.1 %collective-permute-start.5 = (bf16[128,384]{1,0:T(8,128)(2,1)S(1)}, bf16[128,384]{1,0:T(8,128)(2,1)S(1)}, u32[]{:S(2)}, u32[]{:S(2)}) collective-permute-start(bf16[128,384]{1,0:T(8,128)(2,1)S(1)} %constant_dynamic-slice_fusion.2), channel_id=1, source_target_pairs={{0,1},{1,0},{2,3},{3,2},{4,5},{5,4},{6,7},{7,6},{8,9},{9,8},{10,11... | collective-permute-start | bytes 294920 | tf_op jit(solution)/shard_map/ppermute | solution.py:696
  4.7 2.6 %collective-permute-start.6 = (bf16[128,384]{1,0:T(8,128)(2,1)S(1)}, bf16[128,384]{1,0:T(8,128)(2,1)S(1)}, u32[]{:S(2)}, u32[]{:S(2)}) collective-permute-start(bf16[128,384]{1,0:T(8,128)(2,1)S(1)} %constant_dynamic-slice_fusion.2), channel_id=1, source_target_pairs={{0,2},{1,3},{2,0},{3,1},{4,6},{5,7},{6,4},{7,5},{8,10},{9,11},{10,... | collective-permute-start | bytes 294920 | tf_op jit(solution)/shard_map/ppermute | solution.py:696
  8.2 2.8 %collective-permute-start = (bf16[64,512]{1,0:T(8,128)(2,1)S(1)}, bf16[64,512]{1,0:T(8,128)(2,1)S(1)}, u32[]{:S(2)}, u32[]{:S(2)}) collective-permute-start(bf16[64,512]{1,0:T(8,128)(2,1)S(1)} %get-tuple-element.138), channel_id=1, source_target_pairs={{0,1},{1,2},{2,3},{4,5},{5,6},{6,7},{8,9},{9,10},{10,11},{12,13},{... | collective-permute-start | bytes 196616 | tf_op jit(solution)/shard_map/ppermute | solution.py:693
  14.8 2.4 collective-permute-done.1.right
  27.4 2.6 %collective-permute-done.10 = bf16[80,512]{1,0:T(8,128)(2,1)S(1)} collective-permute-done((bf16[80,512]{1,0:T(8,128)(2,1)S(1)}, bf16[80,512]{1,0:T(8,128)(2,1)S(1)}, u32[]{:S(2)}, u32[]{:S(2)}) %collective-permute-start.10) | collective-permute-done | bytes 81952 | tf_op jit(solution)/shard_map/ppermute | solution.py:696
  30.0 2.6 %collective-permute-done.11 = bf16[80,512]{1,0:T(8,128)(2,1)S(1)} collective-permute-done((bf16[80,512]{1,0:T(8,128)(2,1)S(1)}, bf16[80,512]{1,0:T(8,128)(2,1)S(1)}, u32[]{:S(2)}, u32[]{:S(2)}) %collective-permute-start.11) | collective-permute-done | bytes 81952 | tf_op jit(solution)/shard_map/ppermute | solution.py:696
  38.7 4.7 %collective-permute-done.3 = bf16[64,512]{1,0:T(8,128)(2,1)S(1)} collective-permute-done((bf16[64,512]{1,0:T(8,128)(2,1)S(1)}, bf16[64,512]{1,0:T(8,128)(2,1)S(1)}, u32[]{:S(2)}, u32[]{:S(2)}) %collective-permute-start.3) | collective-permute-done | bytes 65568 | tf_op jit(solution)/shard_map/ppermute | solution.py:696
  47.8 4.4 %shard_map.239 = (bf16[4,640,384]{2,1,0:T(8,128)(2,1)S(1)}, bf16[4,144,128]{2,1,0:T(8,128)(2,1)S(1)}) custom-call(s32[16]{0:T(128)S(1)} %stack.138.meta, bf16[640,512]{1,0:T(8,128)(2,1)S(1)} %shard_map.238.a1e, bf16[2,4,128,384]{3,2,1,0:T(8,128)(2,1)} %copy-done.40, bf16[2,4,128,384]{3,2,1,0:T(8,128)(2,1)} %copy-done.41), custom_call_target="tpu_custom_call" | custom-call | flops 1006632960 | bytes 6291456 | tf_op jit(solution)/shard_map/pallas_call | solution.py:54
  59.8 8.0 %collective-permute-done.16.s2 = bf16[4,144,128]{2,1,0:T(8,128)(2,1)S(1)} collective-permute-done((bf16[4,144,128]{2,1,0:T(8,128)(2,1)S(1)}, bf16[4,144,128]{2,1,0:T(8,128)(2,1)S(1)}, u32[]{:S(2)}, u32[]{:S(2)}) %collective-permute-start.16) | collective-permute-done | bytes 147488 | tf_op jit(solution)/shard_map/ppermute | solution.py:696
  69.9 2.6 %shard_map.240 = f32[8,3,192,128]{3,2,1,0:T(8,128)} custom-call(f32[1536,128]{1,0:T(8,128)} %bitcast.57, f32[1536,128]{1,0:T(8,128)} %bitcast.58, f32[1536,128]{1,0:T(8,128)} %bitcast.59), custom_call_target="tpu_custom_call" | custom-call | flops 1048576 | bytes 4194304 | tf_op jit(solution)/shard_map/pallas_call | solution.py:54
  74.6 2.5 collective-permute-done.20
  78.1 3.8 %all-to-all-start = ((f32[8,3,192,128]{3,2,1,0:T(8,128)}), f32[8,3,192,128]{3,2,1,0:T(8,128)S(1)}, u32[]{:S(2)}, u32[]{:S(2)}) async-start(f32[8,3,192,128]{3,2,1,0:T(8,128)} %shard_map.240), calls=%async_computation | async-start | bytes 4718592 | tf_op jit(solution)/shard_map/all_to_all | solution.py:699
  83.5 3.8 %shard_map.241.near = f32[512,512]{1,0:T(8,128)S(1)} custom-call(s32[16]{0:T(128)S(1)} %stack.138.meta, bf16[4,640,384]{2,1,0:T(8,128)(2,1)S(1)} %copy-done.3), custom_call_target="tpu_custom_call" | custom-call | flops 536870912 | bytes 12582912 | tf_op jit(solution)/shard_map/pallas_call | solution.py:54
  89.8 4.2 %collective-permute-done.21.dn_oth = bf16[4,4,64,512]{3,2,1,0:T(8,128)(2,1)S(1)} collective-permute-done((bf16[4,4,64,512]{3,2,1,0:T(8,128)(2,1)}, bf16[4,4,64,512]{3,2,1,0:T(8,128)(2,1)S(1)}, u32[]{:S(2)}, u32[]{:S(2)}) %collective-permute-start.21) | collective-permute-done | bytes 1048608 | tf_op jit(solution)/shard_map/ppermute | solution.py:690
  95.5 19.9 %shard_map.242 = (bf16[512,512]{1,0:T(8,128)(2,1)}, bf16[512,512]{1,0:T(8,128)(2,1)S(1)}, f32[512,512]{1,0:T(8,128)}, bf16[512,512]{1,0:T(8,128)(2,1)S(1)}, f32[...) custom-call(s32[16]{0:T(128)S(1)} %stack.138.meta, ...), custom_call_target="tpu_custom_call" | custom-call | flops 6442450944 | bytes 25165824 | tf_op jit(solution)/shard_map/pallas_call | solution.py:54
  118.1 4.7 %collective-permute-done.22 = bf16[4,576,512]{2,1,0:T(8,128)(2,1)} collective-permute-done((bf16[4,576,512]{2,1,0:T(8,128)(2,1)}, bf16[4,576,512]{2,1,0:T(8,128)(2,1)}, u32[]{:S(2)}, u32[]{:S(2)}) %collective-permute-start.22) | collective-permute-done | bytes 2359328 | tf_op jit(solution)/shard_map/ppermute | solution.py:690
  122.7 3.3 %add_convert_fusion = bf16[4,576,256]{2,1,0:T(8,128)(2,1)} fusion(f32[4,576,512]{2,1,0:T(8,128)} %get-tuple-element.98, s32[]{:T(128)S(6)} %select_n.77, bf16[4,576,512]{2,1,0:T(8,128)(2,1)} %collective-permute-done.22), kind=kLoop, calls=%fused_computation.1 | loop fusion | flops 1769472 | bytes 4718596 | tf_op jit(solution)/shard_map/convert_element_type | solution.py:813
  133.7 3.5 %collective-permute-start.26 = (bf16[32,512]{1,0:T(8,128)(2,1)}, bf16[32,512]{1,0:T(8,128)(2,1)}, u32[]{:S(2)}, u32[]{:S(2)}) collective-permute-start(bf16[32,512]{1,0:T(8,128)(2,1)} %get-tuple-element.136), channel_id=1, source_target_pairs={{0,1},{1,2},{2,3},{4,5},{5,6},{6,7},{8,9},{9,10},{10,11},{12,13},{... | collective-permute-start | bytes 98312 | tf_op jit(solution)/shard_map/ppermute | solution.py:693
  139.4 4.7 %collective-permute-done.24.s2 = bf16[4,144,128]{2,1,0:T(8,128)(2,1)} collective-permute-done((bf16[4,144,128]{2,1,0:T(8,128)(2,1)}, bf16[4,144,128]{2,1,0:T(8,128)(2,1)}, u32[]{:S(2)}, u32[]{:S(2)}) %collective-permute-start.24) | collective-permute-done | bytes 147488 | tf_op jit(solution)/shard_map/ppermute | solution.py:696
  146.9 6.9 %shard_map.243 = (bf16[512,512]{1,0:T(8,128)(2,1)S(1)}, f32[512,512]{1,0:T(8,128)S(1)}, f32[512,512]{1,0:T(8,128)S(1)}) custom-call(s32[16]{0:T(128)S(1)} %stack.138.meta, bf16[4,640,384]{2,1,0:T(8,128)(2,1)S(1)} %copy-done.5, bf16[512,512]{1,0:T(8,128)(2,1)S(1)} %copy-done.15, bf16[32,512]{1,0:T(8,128)(2,1)} %collective-permute-done.26.do_l, ...), custom_call_target="tpu_custom_call" | custom-call | flops 1073741824 | bytes 25165824 | tf_op jit(solution)/shard_map/pallas_call | solution.py:54
  153.8 2.2 convert_add_fusion
  159.2 5.6 %shard_map.244 = (bf16[4,512,384]{2,1,0:T(8,128)(2,1)}, f32[4,192,512]{2,1,0:T(8,128)S(1)}, f32[4,192,512]{2,1,0:T(8,128)}) custom-call(s32[16]{0:T(128)S(1)} %stack.138.meta, bf16[4,640,384]{2,1,0:T(8,128)(2,1)S(1)} %copy-done.6, bf16[512,512]{1,0:T(8,128)(2,1)S(1)} %get-tuple-element.101.dq, f32[512,512]{1,0:T(8,128)S(1)} %get-tuple-element.102.dkn, ...), custom_call_target="tpu_custom_call" | custom-call | flops 805306368 | bytes 25165824 | tf_op jit(solution)/shard_map/pallas_call | solution.py:54
  168.7 2.6 %add_convert_fusion.1 = bf16[4,576,128]{2,1,0:T(8,128)(2,1)} fusion(bf16[4,576,128]{2,1,0:T(8,128)(2,1)} %copy-done.44, f32[4,576,256]{2,1,0:T(8,128)} %copy-done.37, s32[]{:T(128)S(6)} %select_n.82, bf16[4,576,256]{2,1,0:T(8,128)(2,1)} %collective-permute-done.28), kind=kLoop, calls=%fused_computation.2 | loop fusion | flops 1474560 | bytes 2949124 | tf_op jit(solution)/shard_map/convert_element_type | solution.py:821
  171.3 5.4 %all-to-all-start.1 = ((bf16[4,576,128]{2,1,0:T(8,128)(2,1)}), bf16[4,576,128]{2,1,0:T(8,128)(2,1)S(1)}, u32[]{:S(2)}, u32[]{:S(2)}) async-start(bf16[4,576,128]{2,1,0:T(8,128)(2,1)} %add_convert_fusion.1), calls=%async_computation.1 | async-start | bytes 1179648 | tf_op jit(solution)/shard_map/all_to_all | solution.py:699
  180.6 12.7 %all-to-all-done.1.refs_0_ = bf16[4,576,128]{2,1,0:T(8,128)(2,1)S(1)} async-done(((bf16[4,576,128]{2,1,0:T(8,128)(2,1)}), bf16[4,576,128]{2,1,0:T(8,128)(2,1)S(1)}, u32[]{:S(2)}, u32[]{:S(2)}) %all-to-all-start.1) | async-done | bytes 589856 | tf_op jit(solution)/shard_map/all_to_all | solution.py:699
  199.5 6.9 %shard_map.245 = (f32[512,512]{1,0:T(8,128)}, bf16[32,128]{1,0:T(8,128)(2,1)S(1)}) custom-call(s32[16]{0:T(128)S(1)} %stack.138.meta, bf16[4,512,384]{2,1,0:T(8,128)(2,1)} %get-tuple-element.104.dproj_h, bf16[2,4,128,384]{3,2,1,0:T(8,128)(2,1)} %copy-done.40, bf16[2,4,128,384]{3,2,1,0:T(8,128)(2,1)} %copy-done.41, bf16[512,512]{1,0:T(8,128)(2,1)S(1)} %bitcast.62, ...), custom_call_target="tpu_custom_call" | custom-call | flops 805306368 | bytes 8388608 | tf_op jit(solution)/shard_map/pallas_call | solution.py:54
  212.9 2.4 collective-permute-start.35
  216.2 2.7 %collective-permute-done.35.refs_3_ = bf16[1,224,128]{2,1,0:T(8,128)(2,1)S(1)} collective-permute-done((bf16[1,224,128]{2,1,0:T(8,128)(2,1)S(1)}, bf16[1,224,128]{2,1,0:T(8,128)(2,1)S(1)}, u32[]{:S(2)}, u32[]{:S(2)}) %collective-permute-start.35) | collective-permute-done | bytes 57376 | tf_op jit(solution)/shard_map/ppermute | solution.py:696
  221.8 3.5 %all-to-all-start.2 = ((f32[8,208,128]{2,1,0:T(8,128)}), f32[8,208,128]{2,1,0:T(8,128)S(1)}, u32[]{:S(2)}, u32[]{:S(2)}) async-start(f32[8,208,128]{2,1,0:T(8,128)} %shard_map.248), calls=%async_computation.2 | async-start | bytes 1703936 | tf_op jit(solution)/shard_map/all_to_all | solution.py:699
  228.4 9.7 %collective-permute-done.36 = bf16[1,192,128]{2,1,0:T(8,128)(2,1)S(1)} collective-permute-done((bf16[1,192,128]{2,1,0:T(8,128)(2,1)S(1)}, bf16[1,192,128]{2,1,0:T(8,128)(2,1)S(1)}, u32[]{:S(2)}, u32[]{:S(2)}) %collective-permute-start.36) | collective-permute-done | bytes 49184 | tf_op jit(solution)/shard_map/ppermute | solution.py:687
  240.4 2.5 collective-permute-done.37
  248.4 2.8 %shard_map.249 = (f32[24,64,128]{2,1,0:T(8,128)}, f32[24,64,128]{2,1,0:T(8,128)}, f32[24,64,128]{2,1,0:T(8,128)}, f32[16,128]{1,0:T(8,128)S(1)}) custom-call(s32[24]{0:T(128)S(1)} %copy-done.27, s32[8]{0:T(128)S(1)} %stack.162.sources, f32[8,208,128]{2,1,0:T(8,128)S(1)} %all-to-all-done.2.recv, f32[24,64,128]{2,1,0:T(8,128)S(1)} %copy-done.7, ...), custom_call_target="tpu_custom_call" | custom-call | flops 1048576 | bytes 8388608 | tf_op jit(solution)/shard_map/pallas_call | solution.py:54
  (228 shorter events, 97.7 us)
Async XLA Ops:
  1.6 19.0 %collective-permute-start.5 = (bf16[128,384]{1,0:T(8,128)(2,1)S(1)}, bf16[128,384]{1,0:T(8,128)(2,1)S(1)}, u32[]{:S(2)}, u32[]{:S(2)}) collective-permute-start(bf16[128,384]{1,0:T(8,128)(2,1)S(1)} %constant_dynamic-slice_fusion.2), channel_id=1, source_target_pairs={{0,1},{1,0},{2,3},{3,2},{4,5},{5,4},{6,7},{7,6},{8,9},{9,8},{10,11... | collective-permute-start | bytes 294920 | tf_op jit(solution)/shard_map/ppermute | solution.py:696
  4.7 15.9 %collective-permute-start.6 = (bf16[128,384]{1,0:T(8,128)(2,1)S(1)}, bf16[128,384]{1,0:T(8,128)(2,1)S(1)}, u32[]{:S(2)}, u32[]{:S(2)}) collective-permute-start(bf16[128,384]{1,0:T(8,128)(2,1)S(1)} %constant_dynamic-slice_fusion.2), channel_id=1, source_target_pairs={{0,2},{1,3},{2,0},{3,1},{4,6},{5,7},{6,4},{7,5},{8,10},{9,11},{10,... | collective-permute-start | bytes 294920 | tf_op jit(solution)/shard_map/ppermute | solution.py:696
  7.3 13.4 %collective-permute-start.7 = (bf16[128,384]{1,0:T(8,128)(2,1)S(1)}, bf16[128,384]{1,0:T(8,128)(2,1)S(1)}, u32[]{:S(2)}, u32[]{:S(2)}) collective-permute-start(bf16[128,384]{1,0:T(8,128)(2,1)S(1)} %constant_dynamic-slice_fusion.2), channel_id=1, source_target_pairs={{0,3},{1,2},{2,1},{3,0},{4,7},{5,6},{6,5},{7,4},{8,11},{9,10},{10,... | collective-permute-start | bytes 294920 | tf_op jit(solution)/shard_map/ppermute | solution.py:696
  8.2 6.6 %collective-permute-start = (bf16[64,512]{1,0:T(8,128)(2,1)S(1)}, bf16[64,512]{1,0:T(8,128)(2,1)S(1)}, u32[]{:S(2)}, u32[]{:S(2)}) collective-permute-start(bf16[64,512]{1,0:T(8,128)(2,1)S(1)} %get-tuple-element.138), channel_id=1, source_target_pairs={{0,1},{1,2},{2,3},{4,5},{5,6},{6,7},{8,9},{9,10},{10,11},{12,13},{... | collective-permute-start | bytes 196616 | tf_op jit(solution)/shard_map/ppermute | solution.py:693
  20.8 11.9 %collective-permute-start.8 = (bf16[1,4,128,384]{3,2,1,0:T(8,128)(2,1)S(1)}, bf16[1,4,128,384]{3,2,1,0:T(8,128)(2,1)S(1)}, u32[]{:S(2)}, u32[]{:S(2)}) collective-permute-start(bf16[1,4,128,384]{3,2,1,0:T(8,128)(2,1)S(1)} %maximum_bitcast_fusion), channel_id=1, source_target_pairs={{0,8},{4,20},{8,0},{12,28},{16,24},{20,4},{24,16},{28,12},{1,9},{5... | collective-permute-start | bytes 1179656 | tf_op jit(solution)/shard_map/ppermute | solution.py:687
  32.7 14.2 %collective-permute-start.12 = (bf16[2,4,128,384]{3,2,1,0:T(8,128)(2,1)S(1)}, bf16[2,4,128,384]{3,2,1,0:T(8,128)(2,1)S(1)}, u32[]{:S(2)}, u32[]{:S(2)}) collective-permute-start(bf16[2,4,128,384]{3,2,1,0:T(8,128)(2,1)S(1)} %constant_dynamic-update-slice_fusion.own), channel_id=1, source_target_pairs={{0,4},{4,0},{8,12},{12,8},{16,20},{20,16},{24,28},{28,24},{1,5},{5... | collective-permute-start | bytes 2359304 | tf_op jit(solution)/shard_map/ppermute | solution.py:690
  32.8 12.2 %collective-permute-start.13 = (bf16[1,4,80,512]{3,2,1,0:T(8,128)(2,1)S(1)}, bf16[1,4,80,512]{3,2,1,0:T(8,128)(2,1)}, u32[]{:S(2)}, u32[]{:S(2)}) collective-permute-start(bf16[1,4,80,512]{3,2,1,0:T(8,128)(2,1)S(1)} %maximum_bitcast_fusion.1), channel_id=1, source_target_pairs={{0,8},{4,20},{8,0},{12,28},{16,24},{20,4},{24,16},{28,12},{1,9},{5... | collective-permute-start | bytes 983048 | tf_op jit(solution)/shard_map/ppermute | solution.py:687
  35.0 8.4 %collective-permute-start.3 = (bf16[64,512]{1,0:T(8,128)(2,1)S(1)}, bf16[64,512]{1,0:T(8,128)(2,1)S(1)}, u32[]{:S(2)}, u32[]{:S(2)}) collective-permute-start(bf16[64,512]{1,0:T(8,128)(2,1)S(1)} %constant_dynamic-slice_fusion.3), channel_id=1, source_target_pairs={{0,2},{1,3},{2,0},{3,1},{4,6},{5,7},{6,4},{7,5},{8,10},{9,11},{10,... | collective-permute-start | bytes 196616 | tf_op jit(solution)/shard_map/ppermute | solution.py:696
  36.8 6.7 %collective-permute-start.4 = (bf16[64,512]{1,0:T(8,128)(2,1)S(1)}, bf16[64,512]{1,0:T(8,128)(2,1)S(1)}, u32[]{:S(2)}, u32[]{:S(2)}) collective-permute-start(bf16[64,512]{1,0:T(8,128)(2,1)S(1)} %constant_dynamic-slice_fusion.3), channel_id=1, source_target_pairs={{0,3},{1,2},{2,1},{3,0},{4,7},{5,6},{6,5},{7,4},{8,11},{9,10},{10,... | collective-permute-start | bytes 196616 | tf_op jit(solution)/shard_map/ppermute | solution.py:696
  52.2 6.4 %collective-permute-start.14 = (bf16[1,4,64,512]{3,2,1,0:T(8,128)(2,1)S(1)}, bf16[1,4,64,512]{3,2,1,0:T(8,128)(2,1)S(1)}, u32[]{:S(2)}, u32[]{:S(2)}) collective-permute-start(bf16[1,4,64,512]{3,2,1,0:T(8,128)(2,1)S(1)} %maximum_bitcast_fusion.2), channel_id=1, source_target_pairs={{0,8},{4,20},{8,0},{12,28},{16,24},{20,4},{24,16},{28,12},{1,9},{5... | collective-permute-start | bytes 786440 | tf_op jit(solution)/shard_map/ppermute | solution.py:687
  52.8 7.0 %collective-permute-start.15 = (bf16[4,144,128]{2,1,0:T(8,128)(2,1)S(1)}, bf16[4,144,128]{2,1,0:T(8,128)(2,1)S(1)}, u32[]{:S(2)}, u32[]{:S(2)}) collective-permute-start(bf16[4,144,128]{2,1,0:T(8,128)(2,1)S(1)} %get-tuple-element.78.s0), channel_id=1, source_target_pairs={{0,1},{1,0},{2,3},{3,2},{4,5},{5,4},{6,7},{7,6},{8,9},{9,8},{10,11... | collective-permute-start | bytes 442376 | tf_op jit(solution)/shard_map/ppermute | solution.py:696
  54.2 13.6 %collective-permute-start.16 = (bf16[4,144,128]{2,1,0:T(8,128)(2,1)S(1)}, bf16[4,144,128]{2,1,0:T(8,128)(2,1)S(1)}, u32[]{:S(2)}, u32[]{:S(2)}) collective-permute-start(bf16[4,144,128]{2,1,0:T(8,128)(2,1)S(1)} %get-tuple-element.78.s0), channel_id=1, source_target_pairs={{0,2},{1,3},{2,0},{3,1},{4,6},{5,7},{6,4},{7,5},{8,10},{9,11},{10,... | collective-permute-start | bytes 442376 | tf_op jit(solution)/shard_map/ppermute | solution.py:696
  55.6 12.2 %collective-permute-start.17 = (bf16[4,144,128]{2,1,0:T(8,128)(2,1)S(1)}, bf16[4,144,128]{2,1,0:T(8,128)(2,1)S(1)}, u32[]{:S(2)}, u32[]{:S(2)}) collective-permute-start(bf16[4,144,128]{2,1,0:T(8,128)(2,1)S(1)} %get-tuple-element.78.s0), channel_id=1, source_target_pairs={{0,3},{1,2},{2,1},{3,0},{4,7},{5,6},{6,5},{7,4},{8,11},{9,10},{10,... | collective-permute-start | bytes 442376 | tf_op jit(solution)/shard_map/ppermute | solution.py:696
  67.8 9.2 %collective-permute-start.20 = (bf16[2,4,64,512]{3,2,1,0:T(8,128)(2,1)S(1)}, bf16[2,4,64,512]{3,2,1,0:T(8,128)(2,1)S(1)}, u32[]{:S(2)}, u32[]{:S(2)}) collective-permute-start(bf16[2,4,64,512]{3,2,1,0:T(8,128)(2,1)S(1)} %constant_dynamic-update-slice_fusion.2), channel_id=1, source_target_pairs={{0,16},{4,12},{8,24},{12,4},{16,0},{20,28},{24,8},{28,20},{1,17},{... | collective-permute-start | bytes 1572872 | tf_op jit(solution)/shard_map/ppermute | solution.py:687
  69.2 18.1 %collective-permute-start.18 = (bf16[2,4,80,512]{3,2,1,0:T(8,128)(2,1)}, bf16[2,4,80,512]{3,2,1,0:T(8,128)(2,1)}, u32[]{:S(2)}, u32[]{:S(2)}) collective-permute-start(bf16[2,4,80,512]{3,2,1,0:T(8,128)(2,1)} %pad_maximum_fusion), channel_id=1, source_target_pairs={{0,16},{4,12},{8,24},{12,4},{16,0},{20,28},{24,8},{28,20},{1,17},{... | collective-permute-start | bytes 1966088 | tf_op jit(solution)/shard_map/ppermute | solution.py:687
  78.1 39.8 %all-to-all-start = ((f32[8,3,192,128]{3,2,1,0:T(8,128)}), f32[8,3,192,128]{3,2,1,0:T(8,128)S(1)}, u32[]{:S(2)}, u32[]{:S(2)}) async-start(f32[8,3,192,128]{3,2,1,0:T(8,128)} %shard_map.240), calls=%async_computation | async-start | bytes 4718592 | tf_op jit(solution)/shard_map/all_to_all | solution.py:699
  126.0 30.0 %collective-permute-start.28 = (bf16[4,576,256]{2,1,0:T(8,128)(2,1)}, bf16[4,576,256]{2,1,0:T(8,128)(2,1)}, u32[]{:S(2)}, u32[]{:S(2)}) collective-permute-start(bf16[4,576,256]{2,1,0:T(8,128)(2,1)} %add_convert_fusion), channel_id=1, source_target_pairs={{0,8},{4,20},{8,0},{12,28},{16,24},{20,4},{24,16},{28,12},{1,9},{5... | collective-permute-start | bytes 3538952 | tf_op jit(solution)/shard_map/ppermute | solution.py:687
  127.8 9.5 %collective-permute-start.23 = (bf16[4,144,128]{2,1,0:T(8,128)(2,1)}, bf16[4,144,128]{2,1,0:T(8,128)(2,1)S(1)}, u32[]{:S(2)}, u32[]{:S(2)}) collective-permute-start(bf16[4,144,128]{2,1,0:T(8,128)(2,1)} %get-tuple-element.92.s0), channel_id=1, source_target_pairs={{0,1},{1,0},{2,3},{3,2},{4,5},{5,4},{6,7},{7,6},{8,9},{9,8},{10,11... | collective-permute-start | bytes 442376 | tf_op jit(solution)/shard_map/ppermute | solution.py:696
  129.9 14.3 %collective-permute-start.24 = (bf16[4,144,128]{2,1,0:T(8,128)(2,1)}, bf16[4,144,128]{2,1,0:T(8,128)(2,1)}, u32[]{:S(2)}, u32[]{:S(2)}) collective-permute-start(bf16[4,144,128]{2,1,0:T(8,128)(2,1)} %get-tuple-element.92.s0), channel_id=1, source_target_pairs={{0,2},{1,3},{2,0},{3,1},{4,6},{5,7},{6,4},{7,5},{8,10},{9,11},{10,... | collective-permute-start | bytes 442376 | tf_op jit(solution)/shard_map/ppermute | solution.py:696
  130.9 13.3 %collective-permute-start.25 = (bf16[4,144,128]{2,1,0:T(8,128)(2,1)}, bf16[4,144,128]{2,1,0:T(8,128)(2,1)}, u32[]{:S(2)}, u32[]{:S(2)}) collective-permute-start(bf16[4,144,128]{2,1,0:T(8,128)(2,1)} %get-tuple-element.92.s0), channel_id=1, source_target_pairs={{0,3},{1,2},{2,1},{3,0},{4,7},{5,6},{6,5},{7,4},{8,11},{9,10},{10,... | collective-permute-start | bytes 442376 | tf_op jit(solution)/shard_map/ppermute | solution.py:696
  133.7 10.4 %collective-permute-start.26 = (bf16[32,512]{1,0:T(8,128)(2,1)}, bf16[32,512]{1,0:T(8,128)(2,1)}, u32[]{:S(2)}, u32[]{:S(2)}) collective-permute-start(bf16[32,512]{1,0:T(8,128)(2,1)} %get-tuple-element.136), channel_id=1, source_target_pairs={{0,1},{1,2},{2,3},{4,5},{5,6},{6,7},{8,9},{9,10},{10,11},{12,13},{... | collective-permute-start | bytes 98312 | tf_op jit(solution)/shard_map/ppermute | solution.py:693
  137.9 6.4 %collective-permute-start.27 = (bf16[32,512]{1,0:T(8,128)(2,1)}, bf16[32,512]{1,0:T(8,128)(2,1)}, u32[]{:S(2)}, u32[]{:S(2)}) collective-permute-start(bf16[32,512]{1,0:T(8,128)(2,1)} %get-tuple-element.135), channel_id=1, source_target_pairs={{1,0},{2,1},{3,2},{5,4},{6,5},{7,6},{9,8},{10,9},{11,10},{13,12},{... | collective-permute-start | bytes 98312 | tf_op jit(solution)/shard_map/ppermute | solution.py:693
  157.9 9.9 %collective-permute-start.29 = (bf16[4,576,128]{2,1,0:T(8,128)(2,1)S(1)}, bf16[4,576,128]{2,1,0:T(8,128)(2,1)S(1)}, u32[]{:S(2)}, u32[]{:S(2)}) collective-permute-start(bf16[4,576,128]{2,1,0:T(8,128)(2,1)S(1)} %add_convert_fusion.2), channel_id=1, source_target_pairs={{0,16},{4,12},{8,24},{12,4},{16,0},{20,28},{24,8},{28,20},{1,17},{... | collective-permute-start | bytes 1769480 | tf_op jit(solution)/shard_map/ppermute | solution.py:687
  168.7 8.0 %collective-permute-start.30 = (f32[4,192,512]{2,1,0:T(8,128)}, f32[4,192,512]{2,1,0:T(8,128)}, u32[]{:S(2)}, u32[]{:S(2)}) collective-permute-start(f32[4,192,512]{2,1,0:T(8,128)} %get-tuple-element.110), channel_id=1, source_target_pairs={{0,4},{4,0},{8,12},{12,8},{16,20},{20,16},{24,28},{28,24},{1,5},{5... | collective-permute-start | bytes 4718600 | tf_op jit(solution)/shard_map/ppermute | solution.py:690
  171.3 21.9 %all-to-all-start.1 = ((bf16[4,576,128]{2,1,0:T(8,128)(2,1)}), bf16[4,576,128]{2,1,0:T(8,128)(2,1)S(1)}, u32[]{:S(2)}, u32[]{:S(2)}) async-start(bf16[4,576,128]{2,1,0:T(8,128)(2,1)} %add_convert_fusion.1), calls=%async_computation.1 | async-start | bytes 1179648 | tf_op jit(solution)/shard_map/all_to_all | solution.py:699
  178.9 18.9 %collective-permute-start.31 = (bf16[4,192,256]{2,1,0:T(8,128)(2,1)}, bf16[4,192,256]{2,1,0:T(8,128)(2,1)}, u32[]{:S(2)}, u32[]{:S(2)}) collective-permute-start(bf16[4,192,256]{2,1,0:T(8,128)(2,1)} %add_convert_fusion.3), channel_id=1, source_target_pairs={{0,8},{4,20},{8,0},{12,28},{16,24},{20,4},{24,16},{28,12},{1,9},{5... | collective-permute-start | bytes 1179656 | tf_op jit(solution)/shard_map/ppermute | solution.py:687
  194.9 11.5 %collective-permute-start.39 = (bf16[1,576,128]{2,1,0:T(8,128)(2,1)}, bf16[1,576,128]{2,1,0:T(8,128)(2,1)S(1)}, u32[]{:S(2)}, u32[]{:S(2)}) collective-permute-start(bf16[1,576,128]{2,1,0:T(8,128)(2,1)} %bitcast.48), channel_id=1, source_target_pairs={{0,8},{4,20},{8,0},{12,28},{16,24},{20,4},{24,16},{28,12},{1,9},{5... | collective-permute-start | bytes 442376 | tf_op jit(solution)/shard_map/ppermute | solution.py:687
  199.0 10.8 %collective-permute-start.32 = (bf16[4,192,128]{2,1,0:T(8,128)(2,1)S(1)}, bf16[4,192,128]{2,1,0:T(8,128)(2,1)S(1)}, u32[]{:S(2)}, u32[]{:S(2)}) collective-permute-start(bf16[4,192,128]{2,1,0:T(8,128)(2,1)S(1)} %add_convert_fusion.5), channel_id=1, source_target_pairs={{0,16},{4,12},{8,24},{12,4},{16,0},{20,28},{24,8},{28,20},{1,17},{... | collective-permute-start | bytes 589832 | tf_op jit(solution)/shard_map/ppermute | solution.py:687
  208.2 19.1 %collective-permute-start.40 = (bf16[2,576,128]{2,1,0:T(8,128)(2,1)}, bf16[2,576,128]{2,1,0:T(8,128)(2,1)}, u32[]{:S(2)}, u32[]{:S(2)}) collective-permute-start(bf16[2,576,128]{2,1,0:T(8,128)(2,1)} %pad_maximum_fusion.2), channel_id=1, source_target_pairs={{0,16},{4,12},{8,24},{12,4},{16,0},{20,28},{24,8},{28,20},{1,17},{... | collective-permute-start | bytes 884744 | tf_op jit(solution)/shard_map/ppermute | solution.py:687
  221.8 25.5 %all-to-all-start.2 = ((f32[8,208,128]{2,1,0:T(8,128)}), f32[8,208,128]{2,1,0:T(8,128)S(1)}, u32[]{:S(2)}, u32[]{:S(2)}) async-start(f32[8,208,128]{2,1,0:T(8,128)} %shard_map.248), calls=%async_computation.2 | async-start | bytes 1703936 | tf_op jit(solution)/shard_map/all_to_all | solution.py:699
  225.3 12.8 %collective-permute-start.36 = (bf16[1,192,128]{2,1,0:T(8,128)(2,1)S(1)}, bf16[1,192,128]{2,1,0:T(8,128)(2,1)S(1)}, u32[]{:S(2)}, u32[]{:S(2)}) collective-permute-start(bf16[1,192,128]{2,1,0:T(8,128)(2,1)S(1)} %bitcast.63), channel_id=1, source_target_pairs={{0,8},{4,20},{8,0},{12,28},{16,24},{20,4},{24,16},{28,12},{1,9},{5... | collective-permute-start | bytes 147464 | tf_op jit(solution)/shard_map/ppermute | solution.py:687
  228.3 15.2 %collective-permute-start.41 = (bf16[4,576,128]{2,1,0:T(8,128)(2,1)S(1)}, bf16[4,576,128]{2,1,0:T(8,128)(2,1)}, u32[]{:S(2)}, u32[]{:S(2)}) collective-permute-start(bf16[4,576,128]{2,1,0:T(8,128)(2,1)S(1)} %pad_maximum_fusion.1.own), channel_id=1, source_target_pairs={{0,4},{4,0},{8,12},{12,8},{16,20},{20,16},{24,28},{28,24},{1,5},{5... | collective-permute-start | bytes 1769480 | tf_op jit(solution)/shard_map/ppermute | solution.py:690
  (69 other events, 436.0 us)

commit v3 on v2

--- a/solution.py
+++ b/solution.py
@@ -151,16 +151,23 @@
     return ex * (1.0 / jnp.sum(ex, axis=0, keepdims=True))
 
 
-def fetch_pieces(meta, first, own, oth, lo, rows, weight, sem):
-    n = own.shape[0]
-    core = meta[2]
+def piece_at(meta, r, bits, other):
+    b0, b1 = (meta[6], meta[7]) if other else (meta[4], meta[5])
+    core = 1 - meta[2] if other else meta[2]
+    if bits == 1:
+        return core * 2 + (b0 ^ r)
+    return core * 4 + (b0 ^ (r & 1)) * 2 + (b1 ^ (r >> 1))
+
+
+def fetch_pieces(meta, bufs, lo, rows, weight, sem):
+    n = len(bufs) // 2
     copies = []
-    for pq in range(n):
-        for buf, row, half in ((own, meta[first + pq], core), (oth, meta[first + n + pq], 1 - core)):
-            at = pl.ds(pl.multiple_of((half * n + pq) * rows, rows), rows)
-            for m in range(buf.shape[1]):
-                src = buf.at[row, m, pl.ds(lo, rows), :]
-                copies.append(pltpu.make_async_copy(src, weight.at[meta[15] ^ m, at, :], sem))
+    for k, buf in enumerate(bufs):
+        p = piece_at(meta, k % n, n // 2, k >= n)
+        at = pl.ds(pl.multiple_of(p * rows, rows), rows)
+        for m in range(buf.shape[0]):
+            src = buf.at[m, pl.ds(lo, rows), :]
+            copies.append(pltpu.make_async_copy(src, weight.at[meta[3] ^ m, at, :], sem))
     for c in copies:
         c.start()
     return copies
@@ -184,11 +191,12 @@
     lax.fori_loop(0, rows // 128, chunk, 0)
 
 
-def qkv_body(meta, a1e, own, oth, qkv_o, st_o, w, sem):
+def qkv_body(meta, a1e, *refs):
+    bufs, (qkv_o, st_o, w, sem) = refs[:4], refs[4:]
     ext = a1e.shape[0]
     rows = ext - 2 * HALO
-    groups = own.shape[1]
-    for c in fetch_pieces(meta, 11, own, oth, 0, own.shape[2], w, sem):
+    groups = bufs[0].shape[0]
+    for c in fetch_pieces(meta, bufs, 0, bufs[0].shape[1], w, sem):
         c.wait()
     length, base = meta[0], meta[1]
     pos = base + lax.broadcasted_iota(jnp.int32, (rows, 1), 0)
@@ -243,16 +251,15 @@
     give[g, at, :] = jnp.where(first, odd, even).astype(give.dtype)
 
 
-def main_body(
-    meta, near, qkv, s0, s1, s2, s3, tok, cot, gains, biases, io_own, io_oth, dn_own, dn_oth,
-    out_h, do_o, dx2_h, dctx_o, dqf_h, dst_o, ng_o, wout_o, keep_h, give_h,
-    w_in, w_down, x2, xhat, rs, u, dh, acc, da2, far1, inv, dnum, phq, thq,
-    ctx_o, a2_o, dm_o, hid_o, du_o, out_o, give, sem, out_sem,
-):
+def main_body(meta, near, qkv, s0, s1, s2, s3, tok, cot, gains, biases, *refs):
+    bufs, refs = refs[:8], refs[8:]
+    out_h, do_o, head_o, tail_o, dx2_h, dctx_o, dqf_h, dst_o, ng_o, wout_o, keep_h, give_h = refs[:12]
+    w_in, w_down, x2, xhat, rs, u, dh, acc, da2, far1, inv, dnum, phq, thq = refs[12:26]
+    ctx_o, a2_o, dm_o, hid_o, du_o, out_o, keep, give, sem, out_sem = refs[26:]
     rows, width = tok.shape
-    groups = dn_own.shape[1]
-    pr = dn_own.shape[2]
-    orow = io_own.shape[2] - pr
+    groups, hw = hid_o.shape[0], hid_o.shape[2]
+    pr = hw // 8
+    orow = bufs[0].shape[1] - 2 * pr
     core = meta[2]
     sent = []
 
@@ -261,9 +268,9 @@
         sent[-1].start()
 
     length, base = meta[0], meta[1]
-    copies = fetch_pieces(meta, 3, io_own, io_oth, pr, orow, wout_o, sem.at[0])
-    later = fetch_pieces(meta, 3, io_own, io_oth, 0, pr, w_in, sem.at[1])
-    last = fetch_pieces(meta, 3, dn_own, dn_oth, 0, pr, w_down, sem.at[2])
+    copies = fetch_pieces(meta, bufs, 2 * pr, orow, wout_o, sem.at[0])
+    later = fetch_pieces(meta, bufs, 0, pr, w_in, sem.at[1])
+    last = fetch_pieces(meta, bufs, pr, pr, w_down, sem.at[2])
     rlen = 1.0 / length.astype(f32)
     gain, bias = gains[1:2, :], biases[1:2, :]
     ones = same_head().astype(f32).astype(bf16)
@@ -316,8 +323,8 @@
     for c in later + last:
         c.wait()
     for g in gs:
-        u[g, 0:rows, :] = dot(a2_o[...], w_in[g])
-        dh[g, 0:rows, :] = dot_nt(dm_o[...], w_down[g])
+        u[g] = dot(a2_o[...], w_in[g])
+        dh[g] = dot_nt(dm_o[...], w_down[g])
 
     def act(i, _):
         at = pl.ds(pl.multiple_of(i * 16, 16), 16)
@@ -354,6 +361,8 @@
 
     zero = jnp.zeros((1, width), f32)
     dg, db = lax.fori_loop(0, rows // 64, back_chunk, (zero, zero))
+    head_o[...] = do_o[0:EDGE, :]
+    tail_o[...] = do_o[rows - EDGE :, :]
     send(out_o, out_h)
     send(acc, dx2_h)
     ng_o[0:1, :] = dg
@@ -388,8 +397,6 @@
         dst_o[g, :PAIR, :], dst_o[g, PAIR:, :] = pack_state(d1, d2, dz[g])
     send(da2, dqf_h)
     n_out = ctx_o.shape[1] // groups
-    hw = hid_o.shape[2]
-    keep = u
 
     def finish(g, lo, n, grad):
         put_halves(core, keep, give, g, lo, grad)
@@ -452,7 +459,7 @@
             dqe[c_at, cols[g]] = unstack(dq[g])
         return 0
 
-    lax.fori_loop(0, rows // QB + 1, block, 0, unroll=3)
+    lax.fori_loop(0, rows // QB + 1, block, 0, unroll=9)
     second.wait()
     dq_o[...] = (dqe[EDGE : EDGE + rows, :] * 0.125 + dqf[...]).astype(bf16)
     dk_o[...] = dke[HALO : HALO + rows, :] * 0.125
@@ -504,13 +511,12 @@
     out.wait()
 
 
-def last_body(
-    meta, dproj_h, own, oth, tok, dx2_h, gains, ng2, tg_o, ng_o, da1, ngs, wqkv, dproj, dx2, sem, sems,
-):
+def last_body(meta, dproj_h, tok, dx2_h, gains, ng2, *refs):
+    bufs, (tg_o, ng_o, da1, ngs, wqkv, dproj, dx2, sem, sems) = refs[:4], refs[4:]
     groups = dproj.shape[0]
     rows, width = tok.shape
     gain = gains[0:1, :]
-    copies = fetch_pieces(meta, 11, own, oth, 0, own.shape[2], wqkv, sem)
+    copies = fetch_pieces(meta, bufs, 0, bufs[0].shape[1], wqkv, sem)
     copies.append(pltpu.make_async_copy(dproj_h, dproj, sems.at[0]))
     copies[-1].start()
     late = pltpu.make_async_copy(dx2_h, dx2, sems.at[1])
@@ -540,10 +546,7 @@
         for j in range(width // 128):
             at = k * (width // 128) + j
             ngs[at : at + 1, :] = val[:, j * 128 : (j + 1) * 128]
-    n = ngs.shape[0]
-    hi = ngs[...].astype(bf16)
-    ng_o[0:n, :] = hi
-    ng_o[n:, :] = (ngs[...] - hi.astype(f32)).astype(bf16)
+    ng_o[...] = ngs[...]
 
 
 def slices_body(where, master, first, second, out_h, held, parts, sem, out_sem):
@@ -580,8 +583,7 @@
     src = [(r, s) for r in parts for s in range(r.shape[0])]
     piece_o[...] = sum(r[s, 0:n, :].astype(f32) for r, s in src)
     if norms:
-        k = (parts[0].shape[1] - n) // 2
-        norms[0][...] = sum(r[s, n : n + k, :].astype(f32) + r[s, n + k :, :].astype(f32) for r, s in src)
+        norms[0][...] = sum(r[s, n:, :] for r, s in src)
 
     def pair(i, _):
         new = []
@@ -600,15 +602,20 @@
 def route_body(blocks, pq, pm, ng, send_o):
     nq = pq.shape[0] // 8
     dests, per, _ = send_o.shape
-    caps = (per - ng.shape[0]) // 8
+    k_ng = ng.shape[0]
+    caps = (per - 2 * k_ng) // 8
+    hi, lo = two(ng[...])
 
     def dest(d, _):
-        for r in range(caps):
-            b = blocks[d * caps + r]
-            one = pq[pl.ds(pl.multiple_of(jnp.minimum(b, nq - 1) * 8, 8), 8), :]
-            two_ = pm[pl.ds(pl.multiple_of(jnp.maximum(b - nq, 0) * 8, 8), 8), :]
-            send_o[d, r * 8 : r * 8 + 8, :] = jnp.where(jnp.full((8, 128), b, jnp.int32) < nq, one, two_)
-        send_o[d, caps * 8 :, :] = ng[...]
+        for r in range(0, caps, 2):
+            both = []
+            for k in range(2):
+                b = blocks[d * caps + r + k]
+                x = pq[pl.ds(pl.multiple_of(jnp.minimum(b, nq - 1) * 8, 8), 8), :]
+                y = pm[pl.ds(pl.multiple_of(jnp.maximum(b - nq, 0) * 8, 8), 8), :]
+                both.append(jnp.where(jnp.full((8, 128), b, jnp.int32) < nq, x, y))
+            send_o[d, r * 8 : r * 8 + 16, :] = jnp.concatenate(both, axis=0).astype(bf16)
+        send_o[d, caps * 8 : caps * 8 + k_ng, :], send_o[d, caps * 8 + k_ng :, :] = hi, lo
         return 0
 
     lax.fori_loop(0, dests, dest, 0)
@@ -618,11 +625,12 @@
     caps, br, _ = master.shape
     for j in range(4):
         for c in range(2):
-            two[:, c] = recv[sources[c * 4 + j], 0 : caps * 8, :].reshape(caps, 8, 128)
+            two[:, c] = recv[sources[c * 4 + j], 0 : caps * 8, :].astype(f32).reshape(caps, 8, 128)
         grad[pl.ds(j, caps * 16, stride=4), :] = two[...].reshape(caps * 16, 128)
 
     def add(s, tot):
-        return tot + recv[s, caps * 8 :, :]
+        part = recv[s, caps * 8 :, :].astype(f32)
+        return tot + (part[: part.shape[0] // 2] + part[part.shape[0] // 2 :])
 
     ng_o[...] = lax.fori_loop(0, recv.shape[0], add, jnp.zeros(ng_o.shape, f32))
 
@@ -639,30 +647,38 @@
     lax.fori_loop(0, caps, slot, 0, unroll=2)
 
 
-def columns(meta, own, oth, j, lo, n):
-    core = meta[2]
-    a = own[meta[3 + j], lo : lo + n, :].astype(f32)
-    b = oth[meta[7 + j], lo : lo + n, :].astype(f32)
-    first = jnp.full(a.shape, core, jnp.int32) == 0
-    even, odd = jnp.where(first, a, b), jnp.where(first, b, a)
-    both = jnp.concatenate([even.reshape(n // 8, 1, 8, 128), odd.reshape(n // 8, 1, 8, 128)], axis=1)
-    return both.reshape(2 * n, 128)
-
-
-def place_body(meta, own, oth, out_o, in_o, down_o):
+def collect(meta, bufs, held, sem):
+    copies = []
+    for k, buf in enumerate(bufs):
+        copies.append(pltpu.make_async_copy(buf, held.at[piece_at(meta, k % 4, 2, k >= 4)], sem))
+        copies[-1].start()
+    for c in copies:
+        c.wait()
+
+
+def columns(held, j, lo, n):
+    even, odd = [held[c * 4 + j, lo : lo + n, :].astype(f32).reshape(n // 8, 1, 8, 128) for c in range(2)]
+    return jnp.concatenate([even, odd], axis=1).reshape(2 * n, 128)
+
+
+def place_body(meta, *refs):
+    bufs, outs, (held, sem) = refs[:8], refs[8:11], refs[11:]
+    collect(meta, bufs, held, sem)
     lo = 0
-    for ref in (out_o, in_o, down_o):
+    for ref in outs:
         n = ref.shape[0] // 2
         for j in range(4):
-            ref[:, j * 128 : (j + 1) * 128] = columns(meta, own, oth, j, lo, n).astype(bf16)
+            ref[:, j * 128 : (j + 1) * 128] = columns(held, j, lo, n).astype(bf16)
         lo += n
 
 
-def place_qkv_body(meta, own, oth, q_o, flat):
-    n = own.shape[1]
+def place_qkv_body(meta, *refs):
+    bufs, (q_o, held, flat, sem) = refs[:8], refs[8:]
+    collect(meta, bufs, held, sem)
+    n = held.shape[1]
     rows = q_o.shape[0]
     for j in range(4):
-        flat[pl.ds(j, 2 * n, stride=4), :] = columns(meta, own, oth, j, 0, n)
+        flat[pl.ds(j, 2 * n, stride=4), :] = columns(held, j, 0, n)
     for part in range(3):
         q_o[:, part * 128 : (part + 1) * 128] = flat[pl.ds(part, rows, stride=3), :].astype(bf16)
 
@@ -705,20 +721,17 @@
     o0, o1 = bit_of(me, 1 - core, 0), bit_of(me, 1 - core, 1)
     length = lengths[0]
     base = zi * rows
-    ids = [length, base, core]
-    ids += [((t >> 1) ^ q0) + 2 * ((t & 1) ^ q1) for t in range(4)]
-    ids += [((t >> 1) ^ o0) + 2 * ((t & 1) ^ o1) for t in range(4)]
-    ids += [q0, 1 - q0, o0, 1 - o0, zi]
+    ids = [length, base, core, zi, q0, q1, o0, o1]
     meta = jnp.stack(ids).astype(jnp.int32)
 
     def after(x, *deps):
         return lax.optimization_barrier((x,) + deps)[0]
 
     def over_mp(piece):
-        return jnp.stack([piece] + [swap_mp(piece, m) for m in range(1, groups)])[None]
-
-    def grow(buf, s):
-        return jnp.concatenate([buf, swap(buf, s)], axis=0)
+        return jnp.stack([piece] + [swap_mp(piece, m) for m in range(1, groups)])
+
+    def both_cores(bufs):
+        return bufs + [swap_core(b) for b in bufs]
 
     def part_of(w, n, at):
         return lax.dynamic_slice_in_dim(w, at * (w.shape[0] // n), w.shape[0] // n, 0)
@@ -729,28 +742,25 @@
     mm = 2 * rows * width
     qkv_z = over_mp(part_of(w_qkv, 4, core * 2 + q0))
     left, right = from_mp(tok[rows - HALO :], 1), from_mp(tok[:HALO], -1)
-    io_piece = jnp.concatenate([part_of(w_in, 8, mine), part_of(w_out, 8, mine)], axis=0)
-    io_z = over_mp(io_piece)
-    dn_z = over_mp(part_of(w_down, 8, mine))
+    qkv_bufs = [qkv_z, swap(qkv_z, 0)]
+    ffn_piece = jnp.concatenate([part_of(w, 8, mine) for w in (w_in, w_down, w_out)], axis=0)
+    ffn_z = over_mp(after(ffn_piece, qkv_z))
     [a1e] = call(norm_body, [((ext, width), bf16)], [VM] * 5, [], 4 * mm, 1 << 20, 16)(
         tok, left, right, norm_gains, norm_biases
     )
-    qkv_own = grow(after(qkv_z, a1e), 0)
-    io_z = after(io_z, qkv_own)
-    qkv_oth = swap_core(after(qkv_own, io_z))
-    io_one = grow(io_z, 0)
+    qkv_bufs = both_cores([qkv_bufs[0], after(qkv_bufs[1], a1e)])
     proj_w = pltpu.VMEM((groups, width, 3 * PAIR), bf16)
     qkv, state = call(
         qkv_body,
         [((groups, ext, 3 * PAIR), bf16), ((groups, STATE, PAIR), bf16)],
-        [SM, VM, HB, HB],
+        [SM, VM] + [HB] * 4,
         [proj_w, pltpu.SemaphoreType.DMA],
         2 * ext * width * 3 * width, 6 << 20, 20,
-    )(meta, after(a1e, dn_z), qkv_own, qkv_oth)
+    )(meta, after(a1e, ffn_z), *qkv_bufs)
     states = all_states(state)
-    io_one = after(io_one, qkv)
-    dn_one = grow(after(dn_z, io_one), 0)
-    io_own = grow(io_one, 1)
+    ffn_z = after(ffn_z, a1e, qkv_bufs[1])
+    ffn_x, ffn_y = swap(ffn_z, 0), swap(ffn_z, 1)
+    ffn_bufs = [ffn_z, ffn_x, ffn_y, swap(after(ffn_x, ffn_y, *states), 1)]
     capacity, block_rows = master.shape[0], master.shape[1]
     where = [[[] for _ in range(4)] for _ in range(2)]
     for d in range(ndp):
@@ -767,40 +777,38 @@
     )(*flat_state)
     [near] = call(
         near_body, [((rows, width), f32)], [SM, VM], [], mm * 1024, 12 << 20, 16,
-    )(meta, after(qkv, dn_one, parts, *states))
-    io_oth = swap_core(after(io_own, near))
-    dn_own = grow(after(dn_one, *states), 1)
-    dn_oth = swap_core(after(dn_own, near))
-
-    held_state = exchange(after(parts, dn_own), "dp")
+    )(meta, after(qkv, parts, ffn_bufs[1], ffn_bufs[2], *states))
+    ffn_bufs = both_cores(ffn_bufs)
+    held_state = exchange(after(parts, ffn_bufs[3]), "dp")
 
     hid_w = w_in.shape[1]
     big = pltpu.VMEM((rows, width), f32)
     low = pltpu.VMEM((rows, width), bf16)
     n_m = (w_out.shape[0] + w_in.shape[0] + w_down.shape[0]) // 2
-    wide = pltpu.VMEM((groups, max(rows, n_m), hid_w), f32)
+    wide = pltpu.VMEM((groups, rows, hid_w), f32)
+    half = pltpu.VMEM((groups, n_m, width), bf16)
     four = pltpu.VMEM((groups, rows, hid_w), bf16)
-    (outputs, do, dx2, dctx, dqf, dstate, ng2, wout, grad_m, give_m) = call(
+    (outputs, do, head, tail, dx2, dctx, dqf, dstate, ng2, wout, grad_m, give_m) = call(
         main_body,
         [
-            ((rows, width), bf16), ((rows, width), bf16), ((rows, width), f32), ((rows, width), bf16),
-            ((rows, width), f32), ((groups, STATE, PAIR), bf16), ((2, width), f32),
-            ((groups,) + w_out.shape, bf16), ((groups, n_m, width), f32), ((groups, n_m, width), bf16),
+            ((rows, width), bf16), ((rows, width), bf16), ((EDGE, width), bf16), ((EDGE, width), bf16),
+            ((rows, width), f32), ((rows, width), bf16), ((rows, width), f32), ((groups, STATE, PAIR), bf16), ((2, width), f32),
+            ((groups,) + w_out.shape, bf16), ((groups, n_m, width), bf16), ((groups, n_m, width), bf16),
         ],
-        [SM] + [VM] * 10 + [HB] * 4,
+        [SM] + [VM] * 10 + [HB] * 8,
         [
             pltpu.VMEM((groups, width, hid_w), bf16), pltpu.VMEM((groups, hid_w, width), bf16),
             big, big, pltpu.VMEM((rows, 128), f32), wide, wide, big, big, big, big,
-            low, low, low, low, low, low, four, four, low, pltpu.VMEM((groups, n_m, width), bf16),
+            low, low, low, low, low, low, four, four, low, half, half,
             pltpu.SemaphoreType.DMA((3,)), pltpu.SemaphoreType.DMA,
         ],
         mm * hid_w * groups * 6, 24 << 20, 44,
-        (HB, VM, HB, VM, HB, VM, VM, VM, HB, HB),
-    )(meta, near, qkv, *states, tok, cot, norm_gains, norm_biases, io_own, io_oth, dn_own, dn_oth)
-
-    do, dstate, give_m, grad_m, _ = lax.optimization_barrier((do, dstate, give_m, grad_m, held_state))
+        (HB, VM, VM, VM, HB, VM, HB, VM, VM, VM, HB, HB),
+    )(meta, near, qkv, *states, tok, cot, norm_gains, norm_biases, *ffn_bufs)
+
+    head, tail, dstate, give_m, _ = lax.optimization_barrier((head, tail, dstate, give_m, held_state))
     dstates = all_states(dstate)
-    do_l, do_r = from_mp(do[rows - EDGE :], 1), from_mp(do[:EDGE], -1)
+    do_l, do_r = from_mp(tail, 1), from_mp(head, -1)
 
     def halve(own, got, s):
         n = own.shape[-1] // 2
@@ -818,15 +826,13 @@
         tot = keep + got.astype(f32)
         for s in range(2, nbits - 1):
             tot = tot.astype(bf16).astype(f32) + swap(tot.astype(bf16), s).astype(f32)
-        msg = tot.astype(bf16)
         if extra is None:
-            return [exchange(msg, "mp")]
-        more = jnp.broadcast_to(extra, (groups,) + extra.shape)
-        msg = jnp.concatenate([msg, more], axis=1)
+            return [exchange(tot.astype(bf16), "mp")]
+        msg = jnp.concatenate([tot, jnp.broadcast_to(extra, (groups,) + extra.shape)], axis=1)
         part = [lax.dynamic_slice_in_dim(msg, zi ^ m, 1, 0) for m in range(groups)]
         return part[:1] + [swap_mp(part[m], m) for m in range(1, groups)]
 
-    give_m, keep_m = halve(grad_m, swap_core(give_m), 0)
+    give_m, keep_m = halve(grad_m, after(swap_core(give_m), do_l, do_r, dstates[1]), 0)
     got_m = swap(give_m, 0)
     dq, dkn, dvn = call(
         near_back_body,
@@ -838,9 +844,7 @@
             pltpu.VMEM(wout.shape, bf16), big, pltpu.SemaphoreType.DMA((2,)),
         ],
         mm * 2048, 24 << 20, 20,
-    )(meta, qkv, after(dctx, give_m, *dstates), do_l, do_r, wout, dqf)
-    give_m, keep_m = halve(keep_m, after(got_m, dq), 1)
-    got_m = swap(give_m, 1)
+    )(meta, qkv, after(dctx, give_m), do_l, do_r, wout, dqf)
     n_q = w_qkv.size // width // 2
     n_ng = 4 * width // 128
     dproj, grad_q, give_q = call(
@@ -852,24 +856,27 @@
             pltpu.VMEM((2 * n_q, width), f32), pltpu.SemaphoreType.DMA,
         ],
         mm * 3 * width, 24 << 20, 20, (HB, VM, VM),
-    )(meta, qkv, after(dq, give_m), dkn, dvn, *dstates, a1e)
-    got_q = swap_core(after(give_q, got_m))
+    )(meta, qkv, dq, dkn, dvn, *dstates, a1e)
+    got_q = swap_core(give_q)
+    give_m, keep_m = halve(keep_m, after(got_m, give_q), 1)
+    got_m = swap(give_m, 1)
+    give_q, keep_q = halve(grad_q, got_q, 0)
+    got_q = swap(give_q, 0)
     tokens_grad, ng = call(
         last_body,
-        [((rows, width), f32), ((2 * n_ng, 128), bf16)],
-        [SM, HB, HB, HB, VM, HB, VM, VM],
+        [((rows, width), f32), ((n_ng, 128), f32)],
+        [SM, HB, VM, HB, VM, VM] + [HB] * 4,
         [
             big, pltpu.VMEM((n_ng, 128), f32), proj_w, pltpu.VMEM((groups, rows, 3 * PAIR), bf16), big,
             pltpu.SemaphoreType.DMA, pltpu.SemaphoreType.DMA((2,)),
         ],
         mm * 3 * width, 8 << 20, 16,
-    )(meta, dproj, qkv_own, qkv_oth, tok, dx2, norm_gains, ng2)
-    give_q, keep_q = halve(grad_q, got_q, 0)
-    got_q = swap(give_q, 0)
-    z_m = finish(keep_m, got_m)
-    give_q, keep_q = halve(keep_q, got_q, 1)
+    )(meta, after(dproj, give_q), tok, dx2, norm_gains, ng2, *qkv_bufs)
+    z_m = finish(keep_m, after(got_m, give_q))
+    give_q, keep_q = halve(keep_q, after(got_q, ng), 1)
     got_q = swap(give_q, 1)
-    z_q = finish(keep_q, got_q, ng)
+    z_m = [after(z_m[0], give_q)]
+
 
     blocks = owners.shape[0]
     earlier = jnp.arange(blocks)[None, :] < jnp.arange(blocks)[:, None]
@@ -891,17 +898,17 @@
         )(owners, slot, *z, held_state)
 
     def everywhere(piece):
-        buf = piece[None]
-        for s in range(2):
-            buf = grow(buf, s)
-        return buf, swap_core(buf)
+        x, y = swap(piece, 0), swap(piece, 1)
+        return both_cores([piece, x, y, swap(x, 1)])
 
     piece_m, fresh_m = updated(z_m, n_m, nb_q)
-    m_own, m_oth = everywhere(fresh_m)
+    m_bufs = everywhere(fresh_m)
+    z_q = finish(keep_q, after(got_q, fresh_m), ng)
+    z_q[0] = after(z_q[0], m_bufs[1], m_bufs[2])
     piece_q, fresh_q, ng_z = updated(z_q, n_q, 0, [((n_ng, 128), f32)])
-    q_own, q_oth = everywhere(fresh_q)
+    q_bufs = everywhere(fresh_q)
     [send] = call(
-        route_body, [((ndp, capacity * 8 + n_ng, 128), f32)], [SM, VM, VM, VM], [], 1 << 20, 4 << 20, 16,
+        route_body, [((ndp, capacity * 8 + 2 * n_ng, 128), bf16)], [SM, VM, VM, VM], [], 1 << 20, 4 << 20, 16,
     )(held, piece_q, piece_m, ng_z)
     recv = exchange(send, "dp")
     high = me - (me & 7)
@@ -922,12 +929,17 @@
     )(filled, sources, recv, master, first_moment, second_moment)
     new_out, new_in, new_down = call(
         place_body, [(w_out.shape, bf16), (w_in.shape, bf16), (w_down.shape, bf16)],
-        [SM, VM, VM], [], 1 << 20, 4 << 20, 16,
-    )(meta, m_own, m_oth)
+        [SM] + [HB] * 8, [pltpu.VMEM((8, n_m, 128), bf16), pltpu.SemaphoreType.DMA],
+        1 << 20, 4 << 20, 16,
+    )(meta, *m_bufs)
     [new_qkv] = call(
-        place_qkv_body, [(w_qkv.shape, bf16)], [SM, VM, VM],
-        [pltpu.VMEM((w_qkv.size // 128, 128), f32)], 1 << 20, 2 << 20, 16,
-    )(meta, q_own, q_oth)
+        place_qkv_body, [(w_qkv.shape, bf16)], [SM] + [HB] * 8,
+        [
+            pltpu.VMEM((8, n_q, 128), bf16), pltpu.VMEM((w_qkv.size // 128, 128), f32),
+            pltpu.SemaphoreType.DMA,
+        ],
+        1 << 20, 2 << 20, 16,
+    )(meta, *q_bufs)
 
     corr_one = 1.0 - beta_one**STEP
     corr_two = 1.0 - beta_two**STEP

time: 254 us -> 226 us (0.89)
  local copies, waits for them, and re-layouts: 28.1 us -> 12.6 us
  waiting for transfers between devices: 69.2 us -> 59.4 us
  other arithmetic: 22.3 us -> 18.1 us
  starting transfers between devices: 68 us -> 70.9 us
    ppermute x4, waiting for transfers between devices: 2.46 us -> 12.7 us  [from_mp(): lax.ppermute(x, 'mp', [(i, i + step) for i in range(groups) if 0 <= i + s...]
    all_to_all x3, waiting for transfers between devices: 12.7 us -> 2.47 us  [exchange(): return lax.all_to_all(x, axis, 0, 0, tiled=True)]
    unnamed x116 -> x100, local copies, waits for them, and re-layouts: 18.9 us -> 10.7 us
    ppermute x7 -> x16, waiting for transfers between devices: 8.9 us -> 0.82 us  [swap_core(): return lax.ppermute(x, 'dp', [(i, i ^ 1) for i in range(ndp)])]
    concatenate x6 -> x2, other arithmetic: 4.7 us -> 0.05 us  [the longest x1 0.04 us: finish(): jnp.concatenate([tot, jnp.broadcast_to(extra, (groups,) + extra.shape)],...]
    ppermute x18 -> x15, waiting for transfers between devices: 27.3 us -> 23.2 us  [swap_mp(): return lax.ppermute(x, 'mp', [(i, i ^ mask) for i in range(groups)])]
    ppermute x13 -> x14, starting transfers between devices: 16.6 us -> 20.3 us  [swap(): lax.ppermute(x, 'dp', [(i, i ^ 1 << order[i & 1][s]) for i in range(ndp)])]
    ppermute x13 -> x14, waiting for transfers between devices: 17.9 us -> 20.1 us  [swap(): lax.ppermute(x, 'dp', [(i, i ^ 1 << order[i & 1][s]) for i in range(ndp)])]
  transfers between devices with their start and end apart: 45 -> 52, of which waited for: 18 -> 13; matrix products, arithmetic and copies ran while one was open for 11% -> 7% of each run, Pallas kernels for 22% -> 25%
where the time goes in v3:
time: 226 us; the launch traced here: 225 us
  starting transfers between devices  70.9 us (31%)
  Pallas kernels  62.1 us (27%)
  waiting for transfers between devices  59.4 us (26%)
  other arithmetic  18.1 us (8%)
  local copies, waits for them, and re-layouts  12.6 us (6%)
    pallas_call x14, Pallas kernels, fixed(): run(*[pltpu.with_memory_space_constraint(x, pltpu.HBM) if spec is HB else...  62.1 us
    ppermute x15, starting transfers between devices, swap_mp(): return lax.ppermute(x, 'mp', [(i, i ^ mask) for i in range(groups)])  27.7 us
    ppermute x15, waiting for transfers between devices, swap_mp(): return lax.ppermute(x, 'mp', [(i, i ^ mask) for i in range(groups)])  23.2 us
    ppermute x14, starting transfers between devices, swap(): lax.ppermute(x, 'dp', [(i, i ^ 1 << order[i & 1][s]) for i in range(ndp)])  20.3 us
    ppermute x14, waiting for transfers between devices, swap(): lax.ppermute(x, 'dp', [(i, i ^ 1 << order[i & 1][s]) for i in range(ndp)])  20.1 us
    ppermute x4, waiting for transfers between devices, from_mp(): lax.ppermute(x, 'mp', [(i, i + step) for i in range(groups) if 0 <= i + s...  12.7 us
    all_to_all x3, starting transfers between devices, exchange(): return lax.all_to_all(x, axis, 0, 0, tiled=True)  12.4 us
    unnamed x100, local copies, waits for them, and re-layouts  10.7 us
  transfers between devices with their start and end apart: 52, of which 13 were waited for; matrix products, arithmetic and copies ran while one was open for 7% of the time, Pallas kernels for 25%

profile of v3, /device:TPU:0, one launch (start us, length us, event | category | flops | bytes accessed | tf_op | source)
XLA Modules:
  0.0 225.2 jit_solution(12907974792053280685)
XLA Ops:
  1.7 3.1 %collective-permute-start.2 = (bf16[128,384]{1,0:T(8,128)(2,1)S(1)}, bf16[128,384]{1,0:T(8,128)(2,1)S(1)}, u32[]{:S(2)}, u32[]{:S(2)}) collective-permute-start(bf16[128,384]{1,0:T(8,128)(2,1)S(1)} %constant_dynamic-slice_fusion), channel_id=1, source_target_pairs={{0,1},{1,0},{2,3},{3,2},{4,5},{5,4},{6,7},{7,6},{8,9},{9,8},{10,11... | collective-permute-start | bytes 294920 | tf_op jit(solution)/shard_map/ppermute | solution.py:712
  4.8 2.6 %collective-permute-start.3 = (bf16[128,384]{1,0:T(8,128)(2,1)S(1)}, bf16[128,384]{1,0:T(8,128)(2,1)S(1)}, u32[]{:S(2)}, u32[]{:S(2)}) collective-permute-start(bf16[128,384]{1,0:T(8,128)(2,1)S(1)} %constant_dynamic-slice_fusion), channel_id=1, source_target_pairs={{0,2},{1,3},{2,0},{3,1},{4,6},{5,7},{6,4},{7,5},{8,10},{9,11},{10,... | collective-permute-start | bytes 294920 | tf_op jit(solution)/shard_map/ppermute | solution.py:712
  9.0 6.2 %collective-permute-done.3 = bf16[128,384]{1,0:T(8,128)(2,1)S(1)} collective-permute-done((bf16[128,384]{1,0:T(8,128)(2,1)S(1)}, bf16[128,384]{1,0:T(8,128)(2,1)S(1)}, u32[]{:S(2)}, u32[]{:S(2)}) %collective-permute-start.3) | collective-permute-done | bytes 98336 | tf_op jit(solution)/shard_map/ppermute | solution.py:712
  21.3 2.6 %collective-permute-start = (bf16[64,512]{1,0:T(8,128)(2,1)S(1)}, bf16[64,512]{1,0:T(8,128)(2,1)S(1)}, u32[]{:S(2)}, u32[]{:S(2)}) collective-permute-start(bf16[64,512]{1,0:T(8,128)(2,1)S(1)} %get-tuple-element.140), channel_id=1, source_target_pairs={{0,1},{1,2},{2,3},{4,5},{5,6},{6,7},{8,9},{9,10},{10,11},{12,13},{... | collective-permute-start | bytes 196616 | tf_op jit(solution)/shard_map/ppermute | solution.py:709
  23.9 4.0 %collective-permute-done.left = bf16[64,512]{1,0:T(8,128)(2,1)S(1)} collective-permute-done((bf16[64,512]{1,0:T(8,128)(2,1)S(1)}, bf16[64,512]{1,0:T(8,128)(2,1)S(1)}, u32[]{:S(2)}, u32[]{:S(2)}) %collective-permute-start) | collective-permute-done | bytes 65568 | tf_op jit(solution)/shard_map/ppermute | solution.py:709
  29.2 8.7 %collective-permute-done.1.right = bf16[64,512]{1,0:T(8,128)(2,1)S(1)} collective-permute-done((bf16[64,512]{1,0:T(8,128)(2,1)S(1)}, bf16[64,512]{1,0:T(8,128)(2,1)S(1)}, u32[]{:S(2)}, u32[]{:S(2)}) %collective-permute-start.1) | collective-permute-done | bytes 65568 | tf_op jit(solution)/shard_map/ppermute | solution.py:709
  42.6 4.4 %shard_map.239 = (bf16[4,640,384]{2,1,0:T(8,128)(2,1)S(1)}, bf16[4,144,128]{2,1,0:T(8,128)(2,1)S(1)}) custom-call(s32[8]{0:T(128)S(1)} %stack.91.meta, bf16[640,512]{1,0:T(8,128)(2,1)S(1)} %shard_map.238.a1e, bf16[4,128,384]{2,1,0:T(8,128)(2,1)} %copy-done.33, bf16[4,128,384]{2,1,0:T(8,128)(2,1)} %copy-done.35, ...), custom_call_target="tpu_custom_call" | custom-call | flops 1006632960 | bytes 6291456 | tf_op jit(solution)/shard_map/pallas_call | solution.py:54
  47.0 2.5 %collective-permute-start.13 = (bf16[4,144,128]{2,1,0:T(8,128)(2,1)S(1)}, bf16[4,144,128]{2,1,0:T(8,128)(2,1)S(1)}, u32[]{:S(2)}, u32[]{:S(2)}) collective-permute-start(bf16[4,144,128]{2,1,0:T(8,128)(2,1)S(1)} %get-tuple-element.78.s0), channel_id=1, source_target_pairs={{0,1},{1,0},{2,3},{3,2},{4,5},{5,4},{6,7},{7,6},{8,9},{9,8},{10,11... | collective-permute-start | bytes 442376 | tf_op jit(solution)/shard_map/ppermute | solution.py:712
  52.4 2.5 %collective-permute-done.13.s1 = bf16[4,144,128]{2,1,0:T(8,128)(2,1)S(1)} collective-permute-done((bf16[4,144,128]{2,1,0:T(8,128)(2,1)S(1)}, bf16[4,144,128]{2,1,0:T(8,128)(2,1)S(1)}, u32[]{:S(2)}, u32[]{:S(2)}) %collective-permute-start.13) | collective-permute-done | bytes 147488 | tf_op jit(solution)/shard_map/ppermute | solution.py:712
  55.0 8.5 %collective-permute-done.14.s2 = bf16[4,144,128]{2,1,0:T(8,128)(2,1)S(1)} collective-permute-done((bf16[4,144,128]{2,1,0:T(8,128)(2,1)S(1)}, bf16[4,144,128]{2,1,0:T(8,128)(2,1)S(1)}, u32[]{:S(2)}, u32[]{:S(2)}) %collective-permute-start.14) | collective-permute-done | bytes 147488 | tf_op jit(solution)/shard_map/ppermute | solution.py:712
  65.1 2.6 %shard_map.240 = f32[8,3,192,128]{3,2,1,0:T(8,128)} custom-call(f32[1536,128]{1,0:T(8,128)} %bitcast.35, f32[1536,128]{1,0:T(8,128)} %bitcast.36, f32[1536,128]{1,0:T(8,128)} %bitcast.37), custom_call_target="tpu_custom_call" | custom-call | flops 1048576 | bytes 4194304 | tf_op jit(solution)/shard_map/pallas_call | solution.py:54
  67.7 5.9 %collective-permute-done.16.refs_3_ = bf16[4,144,512]{2,1,0:T(8,128)(2,1)S(1)} collective-permute-done((bf16[4,144,512]{2,1,0:T(8,128)(2,1)}, bf16[4,144,512]{2,1,0:T(8,128)(2,1)S(1)}, u32[]{:S(2)}, u32[]{:S(2)}) %collective-permute-start.16) | collective-permute-done | bytes 589856 | tf_op jit(solution)/shard_map/ppermute | solution.py:703
  74.4 3.8 %all-to-all-start = ((f32[8,3,192,128]{3,2,1,0:T(8,128)}), f32[8,3,192,128]{3,2,1,0:T(8,128)S(1)}, u32[]{:S(2)}, u32[]{:S(2)}) async-start(f32[8,3,192,128]{3,2,1,0:T(8,128)} %shard_map.240), calls=%async_computation | async-start | bytes 4718592 | tf_op jit(solution)/shard_map/all_to_all | solution.py:715
  80.9 3.8 %shard_map.241.near = f32[512,512]{1,0:T(8,128)S(1)} custom-call(s32[8]{0:T(128)S(1)} %stack.91.meta, bf16[4,640,384]{2,1,0:T(8,128)(2,1)S(1)} %copy-done.2), custom_call_target="tpu_custom_call" | custom-call | flops 536870912 | bytes 12582912 | tf_op jit(solution)/shard_map/pallas_call | solution.py:54
  87.1 19.9 %shard_map.242 = (bf16[512,512]{1,0:T(8,128)(2,1)}, bf16[512,512]{1,0:T(8,128)(2,1)}, bf16[32,512]{1,0:T(8,128)(2,1)S(1)}, bf16[32,512]{1,0:T(8,128)(2,1)}, f32[...) custom-call(s32[8]{0:T(128)S(1)} %stack.91.meta, ...), custom_call_target="tpu_custom_call" | custom-call | flops 6442450944 | bytes 25165824 | tf_op jit(solution)/shard_map/pallas_call | solution.py:54
  114.3 4.0 %collective-permute-start.25 = (bf16[4,144,128]{2,1,0:T(8,128)(2,1)S(1)}, bf16[4,144,128]{2,1,0:T(8,128)(2,1)S(1)}, u32[]{:S(2)}, u32[]{:S(2)}) collective-permute-start(bf16[4,144,128]{2,1,0:T(8,128)(2,1)S(1)} %get-tuple-element.92.s0), channel_id=1, source_target_pairs={{0,2},{1,3},{2,0},{3,1},{4,6},{5,7},{6,4},{7,5},{8,10},{9,11},{10,... | collective-permute-start | bytes 442376 | tf_op jit(solution)/shard_map/ppermute | solution.py:712
  119.9 3.1 %add_convert_fusion = bf16[4,576,256]{2,1,0:T(8,128)(2,1)} fusion(bf16[4,576,512]{2,1,0:T(8,128)(2,1)} %collective-permute-done.21, s32[]{:T(128)S(6)} %select_n.77, bf16[4,576,512]{2,1,0:T(8,128)(2,1)} %get-tuple-element.113), kind=kLoop, calls=%fused_computation.1 | loop fusion | flops 2359296 | bytes 3538948 | tf_op jit(solution)/shard_map/convert_element_type | solution.py:821
  124.7 5.9 %shard_map.243 = (bf16[512,512]{1,0:T(8,128)(2,1)S(1)}, f32[512,512]{1,0:T(8,128)S(1)}, f32[512,512]{1,0:T(8,128)S(1)}) custom-call(s32[8]{0:T(128)S(1)} %stack.91.meta, bf16[4,640,384]{2,1,0:T(8,128)(2,1)S(1)} %copy-done.4, bf16[512,512]{1,0:T(8,128)(2,1)S(1)} %copy-done.15, bf16[32,512]{1,0:T(8,128)(2,1)S(1)} %collective-permute-done.22.do_l, ...), custom_call_target="tpu_custom_call" | custom-call | flops 1073741824 | bytes 25165824 | tf_op jit(solution)/shard_map/pallas_call | solution.py:54
  130.6 5.5 %shard_map.244 = (bf16[4,512,384]{2,1,0:T(8,128)(2,1)}, f32[4,192,512]{2,1,0:T(8,128)S(1)}, f32[4,192,512]{2,1,0:T(8,128)}) custom-call(s32[8]{0:T(128)S(1)} %stack.91.meta, bf16[4,640,384]{2,1,0:T(8,128)(2,1)S(1)} %copy-done.4, bf16[512,512]{1,0:T(8,128)(2,1)S(1)} %get-tuple-element.97.dq, f32[512,512]{1,0:T(8,128)S(1)} %get-tuple-element.98.dkn, ...), custom_call_target="tpu_custom_call" | custom-call | flops 805306368 | bytes 25165824 | tf_op jit(solution)/shard_map/pallas_call | solution.py:54
  137.3 3.4 %convert_add_fusion = f32[4,576,256]{2,1,0:T(8,128)} fusion(bf16[4,576,512]{2,1,0:T(8,128)(2,1)} %collective-permute-done.21, s32[]{:T(128)S(6)} %select_n.80, bf16[4,576,512]{2,1,0:T(8,128)(2,1)} %get-tuple-element.113), kind=kLoop, calls=%fused_computation | loop fusion | flops 1769472 | bytes 4718596 | tf_op jit(solution)/shard_map/add | solution.py:819
  146.8 6.5 %collective-permute-done.31 = bf16[4,576,128]{2,1,0:T(8,128)(2,1)} collective-permute-done((bf16[4,576,128]{2,1,0:T(8,128)(2,1)}, bf16[4,576,128]{2,1,0:T(8,128)(2,1)}, u32[]{:S(2)}, u32[]{:S(2)}) %collective-permute-start.31) | collective-permute-done | bytes 589856 | tf_op jit(solution)/shard_map/ppermute | solution.py:703
  153.3 2.6 %add_convert_fusion.1 = bf16[4,576,128]{2,1,0:T(8,128)(2,1)} fusion(bf16[4,576,128]{2,1,0:T(8,128)(2,1)} %collective-permute-done.31, f32[4,576,256]{2,1,0:T(8,128)} %convert_add_fusion, s32[]{:T(128)S(6)} %select_n.82, bf16[4,576,256]{2,1,0:T(8,128)(2,1)} %collective-permute-done.30), kind=kLoop, calls=%fused_computation.2 | loop fusion | flops 1474560 | bytes 2949124 | tf_op jit(solution)/shard_map/convert_element_type | solution.py:830
  155.9 5.0 %all-to-all-start.1 = ((bf16[4,576,128]{2,1,0:T(8,128)(2,1)}), bf16[4,576,128]{2,1,0:T(8,128)(2,1)}, u32[]{:S(2)}, u32[]{:S(2)}) async-start(bf16[4,576,128]{2,1,0:T(8,128)(2,1)} %add_convert_fusion.1), calls=%async_computation.1 | async-start | bytes 1179648 | tf_op jit(solution)/shard_map/all_to_all | solution.py:715
  162.7 7.1 %shard_map.245 = (f32[512,512]{1,0:T(8,128)}, f32[16,128]{1,0:T(8,128)S(1)}) custom-call(s32[8]{0:T(128)S(1)} %stack.91.meta, bf16[4,512,384]{2,1,0:T(8,128)(2,1)} %get-tuple-element.103.dproj_h, bf16[512,512]{1,0:T(8,128)(2,1)S(1)} %bitcast.40, f32[512,512]{1,0:T(8,128)} %get-tuple-element.104.dx2_h, f32[2,512]{1,0:T(2,128)S(1)} %copy-done.19, ...), custom_call_target="tpu_custom_call" | custom-call | flops 805306368 | bytes 8388608 | tf_op jit(solution)/shard_map/pallas_call | solution.py:54
  174.6 2.5 %all-to-all-done.1.refs_0_ = bf16[4,576,128]{2,1,0:T(8,128)(2,1)} async-done(((bf16[4,576,128]{2,1,0:T(8,128)(2,1)}), bf16[4,576,128]{2,1,0:T(8,128)(2,1)}, u32[]{:S(2)}, u32[]{:S(2)}) %all-to-all-start.1) | async-done | bytes 589856 | tf_op jit(solution)/shard_map/all_to_all | solution.py:715
  183.6 2.4 %collective-permute-start.35 = (f32[1,208,128]{2,1,0:T(8,128)S(1)}, f32[1,208,128]{2,1,0:T(8,128)S(1)}, u32[]{:S(2)}, u32[]{:S(2)}) collective-permute-start(f32[1,208,128]{2,1,0:T(8,128)S(1)} %get-tuple-element.144), channel_id=1, source_target_pairs={{0,2},{1,3},{2,0},{3,1},{4,6},{5,7},{6,4},{7,5},{8,10},{9,11},{10,... | collective-permute-start | bytes 319496 | tf_op jit(solution)/shard_map/ppermute | solution.py:712
  188.2 5.6 %collective-permute-done.35.refs_2_ = f32[1,208,128]{2,1,0:T(8,128)S(1)} collective-permute-done((f32[1,208,128]{2,1,0:T(8,128)S(1)}, f32[1,208,128]{2,1,0:T(8,128)S(1)}, u32[]{:S(2)}, u32[]{:S(2)}) %collective-permute-start.35) | collective-permute-done | bytes 106528 | tf_op jit(solution)/shard_map/ppermute | solution.py:712
  196.5 3.6 %all-to-all-start.2 = ((bf16[8,224,128]{2,1,0:T(8,128)(2,1)}), bf16[8,224,128]{2,1,0:T(8,128)(2,1)S(1)}, u32[]{:S(2)}, u32[]{:S(2)}) async-start(bf16[8,224,128]{2,1,0:T(8,128)(2,1)} %copy-done.11), calls=%async_computation.2 | async-start | bytes 917504 | tf_op jit(solution)/shard_map/all_to_all | solution.py:715
  204.0 5.6 %collective-permute-done.37.refs_1_ = bf16[192,128]{1,0:T(8,128)(2,1)S(1)} collective-permute-done((bf16[192,128]{1,0:T(8,128)(2,1)S(1)}, bf16[192,128]{1,0:T(8,128)(2,1)S(1)}, u32[]{:S(2)}, u32[]{:S(2)}) %collective-permute-start.37) | collective-permute-done | bytes 49184 | tf_op jit(solution)/shard_map/ppermute | solution.py:703
  216.0 2.4 %shard_map.250 = bf16[512,384]{1,0:T(8,128)(2,1)} custom-call(s32[8]{0:T(128)S(1)} %stack.91.meta, bf16[192,128]{1,0:T(8,128)(2,1)} %copy-done.18, bf16[192,128]{1,0:T(8,128)(2,1)} %copy-done.38, bf16[192,128]{1,0:T(8,128)(2,1)} %copy-done.39, bf16[192,128]{1,0:T(8,128)(2,1)} %collective-permute-done.39.refs_3_, bf16[192,128]{1,0:T(8,128)(2,1)} %copy-done.40, ...), custom_call_target="tpu_custom_call" | custom-call | flops 1048576 | bytes 2097152 | tf_op jit(solution)/shard_map/pallas_call | solution.py:54
  218.5 3.1 %shard_map.251 = (bf16[128,512]{1,0:T(8,128)(2,1)}, bf16[512,512]{1,0:T(8,128)(2,1)}, bf16[512,512]{1,0:T(8,128)(2,1)}) custom-call(s32[8]{0:T(128)S(1)} %stack.91.meta, bf16[576,128]{1,0:T(8,128)(2,1)} %copy-done.17, bf16[576,128]{1,0:T(8,128)(2,1)} %copy-done.36, bf16[576,128]{1,0:T(8,128)(2,1)} %copy-done.37, ...), custom_call_target="tpu_custom_call" | custom-call | flops 1048576 | bytes 4194304 | tf_op jit(solution)/shard_map/pallas_call | solution.py:54
  221.7 2.8 %shard_map.249 = (f32[24,64,128]{2,1,0:T(8,128)}, f32[24,64,128]{2,1,0:T(8,128)}, f32[24,64,128]{2,1,0:T(8,128)}, f32[16,128]{1,0:T(8,128)S(1)}) custom-call(s32[24]{0:T(128)S(1)} %dynamic_slice.83.filled, s32[8]{0:T(128)S(1)} %stack.110.sources, bf16[8,224,128]{2,1,0:T(8,128)(2,1)S(1)} %all-to-all-done.2.recv, f32[24,64,128]{2,1,0:T(8,128)S(1)} %copy-done.5, ...), custom_call_target="tpu_custom_call" | custom-call | flops 1048576 | bytes 8388608 | tf_op jit(solution)/shard_map/pallas_call | solution.py:54
  (213 shorter events, 70.9 us)
Async XLA Ops:
  4.8 10.4 %collective-permute-start.3 = (bf16[128,384]{1,0:T(8,128)(2,1)S(1)}, bf16[128,384]{1,0:T(8,128)(2,1)S(1)}, u32[]{:S(2)}, u32[]{:S(2)}) collective-permute-start(bf16[128,384]{1,0:T(8,128)(2,1)S(1)} %constant_dynamic-slice_fusion), channel_id=1, source_target_pairs={{0,2},{1,3},{2,0},{3,1},{4,6},{5,7},{6,4},{7,5},{8,10},{9,11},{10,... | collective-permute-start | bytes 294920 | tf_op jit(solution)/shard_map/ppermute | solution.py:712
  7.3 7.8 %collective-permute-start.4 = (bf16[128,384]{1,0:T(8,128)(2,1)S(1)}, bf16[128,384]{1,0:T(8,128)(2,1)S(1)}, u32[]{:S(2)}, u32[]{:S(2)}) collective-permute-start(bf16[128,384]{1,0:T(8,128)(2,1)S(1)} %constant_dynamic-slice_fusion), channel_id=1, source_target_pairs={{0,3},{1,2},{2,1},{3,0},{4,7},{5,6},{6,5},{7,4},{8,11},{9,10},{10,... | collective-permute-start | bytes 294920 | tf_op jit(solution)/shard_map/ppermute | solution.py:712
  15.3 23.9 %collective-permute-start.8 = (bf16[4,128,384]{2,1,0:T(8,128)(2,1)S(1)}, bf16[4,128,384]{2,1,0:T(8,128)(2,1)S(1)}, u32[]{:S(2)}, u32[]{:S(2)}) collective-permute-start(bf16[4,128,384]{2,1,0:T(8,128)(2,1)S(1)} %pad_maximum_fusion.1.refs_0_), channel_id=1, source_target_pairs={{0,8},{4,20},{8,0},{12,28},{16,24},{20,4},{24,16},{28,12},{1,9},{5... | collective-permute-start | bytes 1179656 | tf_op jit(solution)/shard_map/ppermute | solution.py:703
  16.8 22.8 %collective-permute-start.5 = (bf16[144,512]{1,0:T(8,128)(2,1)S(1)}, bf16[144,512]{1,0:T(8,128)(2,1)S(1)}, u32[]{:S(2)}, u32[]{:S(2)}) collective-permute-start(bf16[144,512]{1,0:T(8,128)(2,1)S(1)} %pad_maximum_fusion.2), channel_id=1, source_target_pairs={{0,1},{1,0},{2,3},{3,2},{4,5},{5,4},{6,7},{7,6},{8,9},{9,8},{10,11... | collective-permute-start | bytes 442376 | tf_op jit(solution)/shard_map/ppermute | solution.py:712
  18.5 21.1 %collective-permute-start.6 = (bf16[144,512]{1,0:T(8,128)(2,1)S(1)}, bf16[144,512]{1,0:T(8,128)(2,1)S(1)}, u32[]{:S(2)}, u32[]{:S(2)}) collective-permute-start(bf16[144,512]{1,0:T(8,128)(2,1)S(1)} %pad_maximum_fusion.2), channel_id=1, source_target_pairs={{0,2},{1,3},{2,0},{3,1},{4,6},{5,7},{6,4},{7,5},{8,10},{9,11},{10,... | collective-permute-start | bytes 442376 | tf_op jit(solution)/shard_map/ppermute | solution.py:712
  19.9 19.7 %collective-permute-start.7 = (bf16[144,512]{1,0:T(8,128)(2,1)S(1)}, bf16[144,512]{1,0:T(8,128)(2,1)S(1)}, u32[]{:S(2)}, u32[]{:S(2)}) collective-permute-start(bf16[144,512]{1,0:T(8,128)(2,1)S(1)} %pad_maximum_fusion.2), channel_id=1, source_target_pairs={{0,3},{1,2},{2,1},{3,0},{4,7},{5,6},{6,5},{7,4},{8,11},{9,10},{10,... | collective-permute-start | bytes 442376 | tf_op jit(solution)/shard_map/ppermute | solution.py:712
  28.0 10.0 %collective-permute-start.1 = (bf16[64,512]{1,0:T(8,128)(2,1)S(1)}, bf16[64,512]{1,0:T(8,128)(2,1)S(1)}, u32[]{:S(2)}, u32[]{:S(2)}) collective-permute-start(bf16[64,512]{1,0:T(8,128)(2,1)S(1)} %get-tuple-element.139), channel_id=1, source_target_pairs={{1,0},{2,1},{3,2},{5,4},{6,5},{7,6},{9,8},{10,9},{11,10},{13,12},{... | collective-permute-start | bytes 196616 | tf_op jit(solution)/shard_map/ppermute | solution.py:709
  39.7 23.7 %collective-permute-start.11 = (bf16[4,144,512]{2,1,0:T(8,128)(2,1)S(1)}, bf16[4,144,512]{2,1,0:T(8,128)(2,1)}, u32[]{:S(2)}, u32[]{:S(2)}) collective-permute-start(bf16[4,144,512]{2,1,0:T(8,128)(2,1)S(1)} %pad_maximum_fusion.refs_0_), channel_id=1, source_target_pairs={{0,8},{4,20},{8,0},{12,28},{16,24},{20,4},{24,16},{28,12},{1,9},{5... | collective-permute-start | bytes 1769480 | tf_op jit(solution)/shard_map/ppermute | solution.py:703
  41.3 22.2 %collective-permute-start.12 = (bf16[4,144,512]{2,1,0:T(8,128)(2,1)S(1)}, bf16[4,144,512]{2,1,0:T(8,128)(2,1)}, u32[]{:S(2)}, u32[]{:S(2)}) collective-permute-start(bf16[4,144,512]{2,1,0:T(8,128)(2,1)S(1)} %pad_maximum_fusion.refs_0_), channel_id=1, source_target_pairs={{0,16},{4,12},{8,24},{12,4},{16,0},{20,28},{24,8},{28,20},{1,17},{... | collective-permute-start | bytes 1769480 | tf_op jit(solution)/shard_map/ppermute | solution.py:703
  47.0 8.0 %collective-permute-start.13 = (bf16[4,144,128]{2,1,0:T(8,128)(2,1)S(1)}, bf16[4,144,128]{2,1,0:T(8,128)(2,1)S(1)}, u32[]{:S(2)}, u32[]{:S(2)}) collective-permute-start(bf16[4,144,128]{2,1,0:T(8,128)(2,1)S(1)} %get-tuple-element.78.s0), channel_id=1, source_target_pairs={{0,1},{1,0},{2,3},{3,2},{4,5},{5,4},{6,7},{7,6},{8,9},{9,8},{10,11... | collective-permute-start | bytes 442376 | tf_op jit(solution)/shard_map/ppermute | solution.py:712
  49.5 13.9 %collective-permute-start.14 = (bf16[4,144,128]{2,1,0:T(8,128)(2,1)S(1)}, bf16[4,144,128]{2,1,0:T(8,128)(2,1)S(1)}, u32[]{:S(2)}, u32[]{:S(2)}) collective-permute-start(bf16[4,144,128]{2,1,0:T(8,128)(2,1)S(1)} %get-tuple-element.78.s0), channel_id=1, source_target_pairs={{0,2},{1,3},{2,0},{3,1},{4,6},{5,7},{6,4},{7,5},{8,10},{9,11},{10,... | collective-permute-start | bytes 442376 | tf_op jit(solution)/shard_map/ppermute | solution.py:712
  51.1 12.4 %collective-permute-start.15 = (bf16[4,144,128]{2,1,0:T(8,128)(2,1)S(1)}, bf16[4,144,128]{2,1,0:T(8,128)(2,1)S(1)}, u32[]{:S(2)}, u32[]{:S(2)}) collective-permute-start(bf16[4,144,128]{2,1,0:T(8,128)(2,1)S(1)} %get-tuple-element.78.s0), channel_id=1, source_target_pairs={{0,3},{1,2},{2,1},{3,0},{4,7},{5,6},{6,5},{7,4},{8,11},{9,10},{10,... | collective-permute-start | bytes 442376 | tf_op jit(solution)/shard_map/ppermute | solution.py:712
  63.5 10.2 %collective-permute-start.16 = (bf16[4,144,512]{2,1,0:T(8,128)(2,1)}, bf16[4,144,512]{2,1,0:T(8,128)(2,1)S(1)}, u32[]{:S(2)}, u32[]{:S(2)}) collective-permute-start(bf16[4,144,512]{2,1,0:T(8,128)(2,1)} %collective-permute-done.11.refs_1_), channel_id=1, source_target_pairs={{0,16},{4,12},{8,24},{12,4},{16,0},{20,28},{24,8},{28,20},{1,17},{... | collective-permute-start | bytes 1769480 | tf_op jit(solution)/shard_map/ppermute | solution.py:703
  74.4 34.1 %all-to-all-start = ((f32[8,3,192,128]{3,2,1,0:T(8,128)}), f32[8,3,192,128]{3,2,1,0:T(8,128)S(1)}, u32[]{:S(2)}, u32[]{:S(2)}) async-start(f32[8,3,192,128]{3,2,1,0:T(8,128)} %shard_map.240), calls=%async_computation | async-start | bytes 4718592 | tf_op jit(solution)/shard_map/all_to_all | solution.py:715
  108.6 11.3 %collective-permute-start.21 = (bf16[4,576,512]{2,1,0:T(8,128)(2,1)}, bf16[4,576,512]{2,1,0:T(8,128)(2,1)}, u32[]{:S(2)}, u32[]{:S(2)}) collective-permute-start(bf16[4,576,512]{2,1,0:T(8,128)(2,1)} %get-tuple-element.89), channel_id=1, source_target_pairs={{0,4},{4,0},{8,12},{12,8},{16,20},{20,16},{24,28},{28,24},{1,5},{5... | collective-permute-start | bytes 7077896 | tf_op jit(solution)/shard_map/ppermute | solution.py:706
  108.8 11.1 %collective-permute-start.24 = (bf16[4,144,128]{2,1,0:T(8,128)(2,1)S(1)}, bf16[4,144,128]{2,1,0:T(8,128)(2,1)}, u32[]{:S(2)}, u32[]{:S(2)}) collective-permute-start(bf16[4,144,128]{2,1,0:T(8,128)(2,1)S(1)} %get-tuple-element.92.s0), channel_id=1, source_target_pairs={{0,1},{1,0},{2,3},{3,2},{4,5},{5,4},{6,7},{7,6},{8,9},{9,8},{10,11... | collective-permute-start | bytes 442376 | tf_op jit(solution)/shard_map/ppermute | solution.py:712
  110.9 7.4 %collective-permute-start.22 = (bf16[32,512]{1,0:T(8,128)(2,1)}, bf16[32,512]{1,0:T(8,128)(2,1)S(1)}, u32[]{:S(2)}, u32[]{:S(2)}) collective-permute-start(bf16[32,512]{1,0:T(8,128)(2,1)} %get-tuple-element.90), channel_id=1, source_target_pairs={{0,1},{1,2},{2,3},{4,5},{5,6},{6,7},{8,9},{9,10},{10,11},{12,13},{... | collective-permute-start | bytes 98312 | tf_op jit(solution)/shard_map/ppermute | solution.py:709
  114.3 16.3 %collective-permute-start.25 = (bf16[4,144,128]{2,1,0:T(8,128)(2,1)S(1)}, bf16[4,144,128]{2,1,0:T(8,128)(2,1)S(1)}, u32[]{:S(2)}, u32[]{:S(2)}) collective-permute-start(bf16[4,144,128]{2,1,0:T(8,128)(2,1)S(1)} %get-tuple-element.92.s0), channel_id=1, source_target_pairs={{0,2},{1,3},{2,0},{3,1},{4,6},{5,7},{6,4},{7,5},{8,10},{9,11},{10,... | collective-permute-start | bytes 442376 | tf_op jit(solution)/shard_map/ppermute | solution.py:712
  118.3 12.3 %collective-permute-start.26 = (bf16[4,144,128]{2,1,0:T(8,128)(2,1)S(1)}, bf16[4,144,128]{2,1,0:T(8,128)(2,1)S(1)}, u32[]{:S(2)}, u32[]{:S(2)}) collective-permute-start(bf16[4,144,128]{2,1,0:T(8,128)(2,1)S(1)} %get-tuple-element.92.s0), channel_id=1, source_target_pairs={{0,3},{1,2},{2,1},{3,0},{4,7},{5,6},{6,5},{7,4},{8,11},{9,10},{10,... | collective-permute-start | bytes 442376 | tf_op jit(solution)/shard_map/ppermute | solution.py:712
  123.0 17.7 %collective-permute-start.30 = (bf16[4,576,256]{2,1,0:T(8,128)(2,1)}, bf16[4,576,256]{2,1,0:T(8,128)(2,1)}, u32[]{:S(2)}, u32[]{:S(2)}) collective-permute-start(bf16[4,576,256]{2,1,0:T(8,128)(2,1)} %add_convert_fusion), channel_id=1, source_target_pairs={{0,8},{4,20},{8,0},{12,28},{16,24},{20,4},{24,16},{28,12},{1,9},{5... | collective-permute-start | bytes 3538952 | tf_op jit(solution)/shard_map/ppermute | solution.py:703
  143.1 10.2 %collective-permute-start.31 = (bf16[4,576,128]{2,1,0:T(8,128)(2,1)}, bf16[4,576,128]{2,1,0:T(8,128)(2,1)}, u32[]{:S(2)}, u32[]{:S(2)}) collective-permute-start(bf16[4,576,128]{2,1,0:T(8,128)(2,1)} %add_convert_fusion.2), channel_id=1, source_target_pairs={{0,16},{4,12},{8,24},{12,4},{16,0},{20,28},{24,8},{28,20},{1,17},{... | collective-permute-start | bytes 1769480 | tf_op jit(solution)/shard_map/ppermute | solution.py:703
  155.9 21.2 %all-to-all-start.1 = ((bf16[4,576,128]{2,1,0:T(8,128)(2,1)}), bf16[4,576,128]{2,1,0:T(8,128)(2,1)}, u32[]{:S(2)}, u32[]{:S(2)}) async-start(bf16[4,576,128]{2,1,0:T(8,128)(2,1)} %add_convert_fusion.1), calls=%async_computation.1 | async-start | bytes 1179648 | tf_op jit(solution)/shard_map/all_to_all | solution.py:715
  160.9 10.3 %collective-permute-start.28 = (bf16[4,192,256]{2,1,0:T(8,128)(2,1)}, bf16[4,192,256]{2,1,0:T(8,128)(2,1)}, u32[]{:S(2)}, u32[]{:S(2)}) collective-permute-start(bf16[4,192,256]{2,1,0:T(8,128)(2,1)} %add_convert_fusion.3), channel_id=1, source_target_pairs={{0,8},{4,20},{8,0},{12,28},{16,24},{20,4},{24,16},{28,12},{1,9},{5... | collective-permute-start | bytes 1179656 | tf_op jit(solution)/shard_map/ppermute | solution.py:703
  173.0 8.9 %collective-permute-start.29 = (bf16[4,192,128]{2,1,0:T(8,128)(2,1)S(1)}, bf16[4,192,128]{2,1,0:T(8,128)(2,1)}, u32[]{:S(2)}, u32[]{:S(2)}) collective-permute-start(bf16[4,192,128]{2,1,0:T(8,128)(2,1)S(1)} %add_convert_fusion.4), channel_id=1, source_target_pairs={{0,16},{4,12},{8,24},{12,4},{16,0},{20,28},{24,8},{28,20},{1,17},{... | collective-permute-start | bytes 589832 | tf_op jit(solution)/shard_map/ppermute | solution.py:703
  178.7 9.0 %collective-permute-start.32 = (bf16[576,128]{1,0:T(8,128)(2,1)S(1)}, bf16[576,128]{1,0:T(8,128)(2,1)S(1)}, u32[]{:S(2)}, u32[]{:S(2)}) collective-permute-start(bf16[576,128]{1,0:T(8,128)(2,1)S(1)} %get-tuple-element.120.refs_0_), channel_id=1, source_target_pairs={{0,8},{4,20},{8,0},{12,28},{16,24},{20,4},{24,16},{28,12},{1,9},{5... | collective-permute-start | bytes 442376 | tf_op jit(solution)/shard_map/ppermute | solution.py:703
  183.6 10.1 %collective-permute-start.35 = (f32[1,208,128]{2,1,0:T(8,128)S(1)}, f32[1,208,128]{2,1,0:T(8,128)S(1)}, u32[]{:S(2)}, u32[]{:S(2)}) collective-permute-start(f32[1,208,128]{2,1,0:T(8,128)S(1)} %get-tuple-element.144), channel_id=1, source_target_pairs={{0,2},{1,3},{2,0},{3,1},{4,6},{5,7},{6,4},{7,5},{8,10},{9,11},{10,... | collective-permute-start | bytes 319496 | tf_op jit(solution)/shard_map/ppermute | solution.py:712
  186.0 7.8 %collective-permute-start.36 = (f32[1,208,128]{2,1,0:T(8,128)S(1)}, f32[1,208,128]{2,1,0:T(8,128)S(1)}, u32[]{:S(2)}, u32[]{:S(2)}) collective-permute-start(f32[1,208,128]{2,1,0:T(8,128)S(1)} %get-tuple-element.141), channel_id=1, source_target_pairs={{0,3},{1,2},{2,1},{3,0},{4,7},{5,6},{6,5},{7,4},{8,11},{9,10},{10,... | collective-permute-start | bytes 319496 | tf_op jit(solution)/shard_map/ppermute | solution.py:712
  196.5 25.2 %all-to-all-start.2 = ((bf16[8,224,128]{2,1,0:T(8,128)(2,1)}), bf16[8,224,128]{2,1,0:T(8,128)(2,1)S(1)}, u32[]{:S(2)}, u32[]{:S(2)}) async-start(bf16[8,224,128]{2,1,0:T(8,128)(2,1)} %copy-done.11), calls=%async_computation.2 | async-start | bytes 917504 | tf_op jit(solution)/shard_map/all_to_all | solution.py:715
  200.1 14.4 %collective-permute-start.44 = (bf16[576,128]{1,0:T(8,128)(2,1)}, bf16[576,128]{1,0:T(8,128)(2,1)}, u32[]{:S(2)}, u32[]{:S(2)}) collective-permute-start(bf16[576,128]{1,0:T(8,128)(2,1)} %copy-done.36), channel_id=1, source_target_pairs={{0,16},{4,12},{8,24},{12,4},{16,0},{20,28},{24,8},{28,20},{1,17},{... | collective-permute-start | bytes 442376 | tf_op jit(solution)/shard_map/ppermute | solution.py:703
  202.0 7.6 %collective-permute-start.37 = (bf16[192,128]{1,0:T(8,128)(2,1)S(1)}, bf16[192,128]{1,0:T(8,128)(2,1)S(1)}, u32[]{:S(2)}, u32[]{:S(2)}) collective-permute-start(bf16[192,128]{1,0:T(8,128)(2,1)S(1)} %get-tuple-element.129.refs_0_), channel_id=1, source_target_pairs={{0,8},{4,20},{8,0},{12,28},{16,24},{20,4},{24,16},{28,12},{1,9},{5... | collective-permute-start | bytes 147464 | tf_op jit(solution)/shard_map/ppermute | solution.py:703
  203.5 7.7 %collective-permute-start.38 = (bf16[192,128]{1,0:T(8,128)(2,1)S(1)}, bf16[192,128]{1,0:T(8,128)(2,1)S(1)}, u32[]{:S(2)}, u32[]{:S(2)}) collective-permute-start(bf16[192,128]{1,0:T(8,128)(2,1)S(1)} %get-tuple-element.129.refs_0_), channel_id=1, source_target_pairs={{0,16},{4,12},{8,24},{12,4},{16,0},{20,28},{24,8},{28,20},{1,17},{... | collective-permute-start | bytes 147464 | tf_op jit(solution)/shard_map/ppermute | solution.py:703
  204.0 7.6 %collective-permute-start.40 = (bf16[192,128]{1,0:T(8,128)(2,1)S(1)}, bf16[192,128]{1,0:T(8,128)(2,1)S(1)}, u32[]{:S(2)}, u32[]{:S(2)}) collective-permute-start(bf16[192,128]{1,0:T(8,128)(2,1)S(1)} %get-tuple-element.129.refs_0_), channel_id=1, source_target_pairs={{0,4},{4,0},{8,12},{12,8},{16,20},{20,16},{24,28},{28,24},{1,5},{5... | collective-permute-start | bytes 147464 | tf_op jit(solution)/shard_map/ppermute | solution.py:706
  (70 other events, 553.9 us)

commit v4 on v3

--- a/solution.py
+++ b/solution.py
@@ -61,6 +61,13 @@
     return fixed
 
 
+def load(pairs, sem):
+    copies = [pltpu.make_async_copy(a, b, sem) for a, b in pairs]
+    for c in copies:
+        c.start()
+    return copies
+
+
 def dot(a, b):
     return jnp.dot(a, b, preferred_element_type=f32)
 
@@ -173,7 +180,7 @@
     return copies
 
 
-def norm_body(tok, left, right, gains, biases, a1e_o):
+def norm_body(tok, left, right, gains, biases, a1e_h, a1e_o, sem):
     rows = tok.shape[0]
     gain, bias = gains[0:1, :], biases[0:1, :]
 
@@ -189,15 +196,21 @@
         return 0
 
     lax.fori_loop(0, rows // 128, chunk, 0)
-
-
-def qkv_body(meta, a1e, *refs):
-    bufs, (qkv_o, st_o, w, sem) = refs[:4], refs[4:]
+    out = pltpu.make_async_copy(a1e_o, a1e_h, sem)
+    out.start()
+    out.wait()
+
+
+def qkv_body(meta, a1e_h, *refs):
+    bufs, (qkv_h, st_o, w, qkv_o, a1e, sem, out_sem) = refs[:4], refs[4:]
+    pull = pltpu.make_async_copy(a1e_h, a1e, out_sem)
+    pull.start()
     ext = a1e.shape[0]
     rows = ext - 2 * HALO
     groups = bufs[0].shape[0]
     for c in fetch_pieces(meta, bufs, 0, bufs[0].shape[1], w, sem):
         c.wait()
+    pull.wait()
     length, base = meta[0], meta[1]
     pos = base + lax.broadcasted_iota(jnp.int32, (rows, 1), 0)
     valid = (pos < length).astype(f32)
@@ -205,6 +218,8 @@
     for g in gs:
         qkv_o[g] = dot(a1e[...], w[g]).astype(bf16)
     own_rows = slice(HALO, HALO + rows)
+    out = pltpu.make_async_copy(qkv_o, qkv_h, out_sem)
+    out.start()
     parts = []
     for g in gs:
         keys = qkv_o[g, own_rows, PAIR : 2 * PAIR].astype(f32)
@@ -216,13 +231,17 @@
         s1 = dot_tn(fhi, vals) + dot_tn(flo, vals)
         s2 = dot_tn(thi, vals) + dot_tn(tlo, vals)
         st_o[g, :PAIR, :], st_o[g, PAIR:, :] = pack_state(s1, s2, z)
-
-
-def near_body(meta, qkv, near_o):
+    out.wait()
+
+
+def near_body(meta, qkv_h, near_h, qkv, near_o, sem):
+    pull = pltpu.make_async_copy(qkv_h, qkv, sem)
+    pull.start()
     groups = qkv.shape[0]
     rows = near_o.shape[0]
     length, base = meta[0], meta[1]
     band, diag, lane = band_parts()
+    pull.wait()
 
     def block(b, _):
         at = b * QB
@@ -239,6 +258,9 @@
         return 0
 
     lax.fori_loop(0, rows // QB, block, 0, unroll=4)
+    out = pltpu.make_async_copy(near_o, near_h, sem)
+    out.start()
+    out.wait()
 
 
 def put_halves(core, keep, give, g, lo, grad):
@@ -251,13 +273,18 @@
     give[g, at, :] = jnp.where(first, odd, even).astype(give.dtype)
 
 
-def main_body(meta, near, qkv, s0, s1, s2, s3, tok, cot, gains, biases, *refs):
+def main_body(meta, near_h, qkv_h, h0, h1, h2, h3, tok_h, cot_h, gains, biases, *refs):
     bufs, refs = refs[:8], refs[8:]
-    out_h, do_o, head_o, tail_o, dx2_h, dctx_o, dqf_h, dst_o, ng_o, wout_o, keep_h, give_h = refs[:12]
+    out_h, head_o, tail_o, dx2_h, dctx_h, dqf_h, dst_o, ng_o, wout_h, keep_h, give_h = refs[:11]
+    refs = refs[11:]
+    do_o, dctx_o, wout_o, near, tok, cot, st = refs[:7]
+    refs = (None,) * 5 + refs
     w_in, w_down, x2, xhat, rs, u, dh, acc, da2, far1, inv, dnum, phq, thq = refs[12:26]
-    ctx_o, a2_o, dm_o, hid_o, du_o, out_o, keep, give, sem, out_sem = refs[26:]
+    ctx_o, a2_o, dm_o, hid_o, du_o, out_o, keep, give, query, sem, out_sem = refs[26:]
     rows, width = tok.shape
     groups, hw = hid_o.shape[0], hid_o.shape[2]
+    s0, s1, s2, s3 = [st.at[k] for k in range(4)]
+    moved = load([(near_h, near), (tok_h, tok), (cot_h, cot)] + [(h, st.at[k]) for k, h in enumerate((h0, h1, h2, h3))], sem.at[4])
     pr = hw // 8
     orow = bufs[0].shape[1] - 2 * pr
     core = meta[2]
@@ -268,6 +295,8 @@
         sent[-1].start()
 
     length, base = meta[0], meta[1]
+    pull = pltpu.make_async_copy(qkv_h.at[:, pl.ds(HALO, rows), pl.ds(0, PAIR)], query, sem.at[3])
+    pull.start()
     copies = fetch_pieces(meta, bufs, 2 * pr, orow, wout_o, sem.at[0])
     later = fetch_pieces(meta, bufs, 0, pr, w_in, sem.at[1])
     last = fetch_pieces(meta, bufs, pr, pr, w_down, sem.at[2])
@@ -276,14 +305,15 @@
     ones = same_head().astype(f32).astype(bf16)
     gs = range(groups)
     cols = [slice(g * PAIR, (g + 1) * PAIR) for g in gs]
+    for c in moved:
+        c.wait()
     states = [unpack_state((s0, s1, s2, s3), g) for g in gs]
     s1b, s2b = [two(st[0]) for st in states], [two(st[1]) for st in states]
     cr = 128
 
     def far_chunk(i, _):
         at = pl.ds(pl.multiple_of(i * cr, cr), cr)
-        q_at = pl.ds(pl.multiple_of(i * cr + HALO, HALO), cr)
-        q = [qkv[g, q_at, 0:PAIR].astype(f32) for g in gs]
+        q = [query[g, at, :].astype(f32) for g in gs]
         ph = [phi(q[g])[0] for g in gs]
         ph2 = [two(ph[g]) for g in gs]
         th2 = [two(jnp.tanh(q[g])) for g in gs]
@@ -303,6 +333,7 @@
         dm_o[at, :] = (cot[at, :].astype(f32) * (pos < length).astype(f32)).astype(bf16)
         return 0
 
+    pull.wait()
     lax.fori_loop(0, rows // cr, far_chunk, 0)
     for c in copies:
         c.wait()
@@ -364,14 +395,15 @@
     head_o[...] = do_o[0:EDGE, :]
     tail_o[...] = do_o[rows - EDGE :, :]
     send(out_o, out_h)
+    send(wout_o, wout_h)
     send(acc, dx2_h)
     ng_o[0:1, :] = dg
     ng_o[1:2, :] = db
     dctx_o[...] = dot_nt(do_o[...], wout).astype(bf16)
+    send(dctx_o, dctx_h)
 
     def far_back(i, carry):
         at = pl.ds(pl.multiple_of(i * cr, cr), cr)
-        q_at = pl.ds(pl.multiple_of(i * cr + HALO, HALO), cr)
         dc = [dctx_o[at, cols[g]] for g in gs]
         dcf = [dc[g].astype(f32) for g in gs]
         rec = [inv[at, cols[g]] for g in gs]
@@ -384,7 +416,7 @@
             dnum[at, cols[g]] = dn[g]
             dden = -dots[g] * rec[g]
             out.append(carry[g] + jnp.sum(phq[at, cols[g]].astype(f32) * dden, axis=0, keepdims=True))
-            slope = phi(qkv[g, q_at, 0:PAIR].astype(f32))[1]
+            slope = phi(query[g, at, :].astype(f32))[1]
             th = thq[at, cols[g]].astype(f32)
             da2[at, cols[g]] = (dph[g] + dden * states[g][2]) * slope + dth[g] * rlen * (1.0 - th * th)
         return tuple(out)
@@ -415,10 +447,14 @@
 
 
 def near_back_body(
-    meta, qkv, dctx, do_l, do_r, wout_h, dqf_h, dq_o, dk_o, dv_o, dce, dqe, dke, dve, wout, dqf, sem,
+    meta, qkv_h, dctx_h, do_l, do_r, wout_h, dqf_h, dq_o, dk_o, dv_o, dce, dqe, dke, dve, wout, dqf, qkv, sem,
 ):
+    pull = pltpu.make_async_copy(qkv_h, qkv, sem.at[2])
+    pull.start()
     groups = qkv.shape[0]
-    rows = dctx.shape[0]
+    rows, width = dctx_h.shape
+    third = pltpu.make_async_copy(dctx_h, dce.at[pl.ds(EDGE, rows), :], sem.at[3])
+    third.start()
     length, base = meta[0], meta[1]
     band, diag, lane = band_parts()
     first = pltpu.make_async_copy(wout_h, wout, sem.at[0])
@@ -426,12 +462,13 @@
     second = pltpu.make_async_copy(dqf_h, dqf, sem.at[1])
     second.start()
     first.wait()
-    w = wout[...].reshape(dctx.shape[1], -1)
+    w = wout[...].reshape(width, -1)
     dce[0:EDGE, :] = dot_nt(do_l[...], w).astype(bf16)
-    dce[EDGE : EDGE + rows, :] = dctx[...]
     dce[EDGE + rows :, :] = dot_nt(do_r[...], w).astype(bf16)
     dke[...] = jnp.zeros(dke.shape, f32)
     dve[...] = jnp.zeros(dve.shape, f32)
+    pull.wait()
+    third.wait()
 
     def block(b, _):
         at = b * QB
@@ -466,7 +503,14 @@
     dv_o[...] = dve[HALO : HALO + rows, :]
 
 
-def proj_body(meta, qkv, dq, dkn, dvn, s0, s1, s2, s3, a1e, dproj_h, keep_o, give_o, dproj, flat, pseudo, sem):
+def proj_body(
+    meta, qkv_h, dq, dkn, dvn, s0, s1, s2, s3, a1e_h, dproj_h, keep_o, give_o, dproj, flat, pseudo, qkv, a1e, sem, in_sem,
+):
+    rows = dq.shape[0]
+    other = pltpu.make_async_copy(a1e_h.at[pl.ds(HALO, rows), :], a1e, in_sem.at[1])
+    other.start()
+    pull = pltpu.make_async_copy(qkv_h, qkv, in_sem.at[0])
+    pull.start()
     groups = qkv.shape[0]
     rows, width = dq.shape
     length, base, core = meta[0], meta[1], meta[2]
@@ -497,12 +541,14 @@
             dproj[g, at, 2 * PAIR :] = (dvn[at, cols[g]] + dv[g]).astype(bf16)
         return 0
 
+    pull.wait()
     lax.fori_loop(0, rows // cr, far_chunk, 0)
     out = pltpu.make_async_copy(dproj, dproj_h, sem)
     out.start()
+    other.wait()
     n_flat = 3 * width
     for g in gs:
-        grad = dot_tn(a1e[HALO : HALO + rows, :], dproj[g])
+        grad = dot_tn(a1e[...], dproj[g])
         for part in range(3):
             flat[pl.ds(part, width, stride=3), :] = grad[:, part * PAIR : (part + 1) * PAIR]
         for j in range(4):
@@ -547,6 +593,30 @@
             at = k * (width // 128) + j
             ngs[at : at + 1, :] = val[:, j * 128 : (j + 1) * 128]
     ng_o[...] = ngs[...]
+
+
+def halve_body(bit, own, got, give_o, keep_o):
+    groups, _, n = give_o.shape
+    out = pl.ds(pl.multiple_of((1 - bit[0]) * n, 128), n)
+    stay = pl.ds(pl.multiple_of(bit[0] * n, 128), n)
+    for g in range(groups):
+        give_o[g] = (own[g, :, out].astype(f32) + got[g, :, out].astype(f32)).astype(bf16)
+    for g in range(groups):
+        keep_o[g] = own[g, :, stay].astype(f32) + got[g, :, stay].astype(f32)
+
+
+def total_body(meta, keep, got, *outs):
+    for m, out in enumerate(outs):
+        g = meta[3] ^ m
+        out[0] = (keep[g] + got[g].astype(f32)).astype(bf16)
+
+
+def total_q_body(meta, keep, got, ng, *outs):
+    n = keep.shape[1]
+    for m, out in enumerate(outs):
+        g = meta[3] ^ m
+        out[0, 0:n, :] = keep[g] + got[g].astype(f32)
+        out[0, n:, :] = ng[...]
 
 
 def slices_body(where, master, first, second, out_h, held, parts, sem, out_sem):
@@ -578,12 +648,15 @@
 
 
 def pieces_body(first, count, owners, slots, *refs):
-    parts, st, piece_o, w_o, norms = refs[:count], refs[count], refs[count + 1], refs[count + 2], refs[count + 3 :]
+    parts, (st, piece_o, w_o) = refs[:count], refs[count:]
     n = piece_o.shape[0]
     src = [(r, s) for r in parts for s in range(r.shape[0])]
     piece_o[...] = sum(r[s, 0:n, :].astype(f32) for r, s in src)
-    if norms:
-        norms[0][...] = sum(r[s, n:, :] for r, s in src)
+    if w_o.shape[0] > n:
+        hi, lo = two(sum(r[s, n:, :] for r, s in src))
+        k = hi.shape[0]
+        w_o[n : 2 * n, :] = piece_o[...].astype(bf16)
+        w_o[2 * n : 2 * n + k, :], w_o[2 * n + k :, :] = hi, lo
 
     def pair(i, _):
         new = []
@@ -599,52 +672,80 @@
     lax.fori_loop(0, n // 16, pair, 0, unroll=4)
 
 
-def route_body(blocks, pq, pm, ng, send_o):
-    nq = pq.shape[0] // 8
+def route_body(first, blocks, piece, send_o):
     dests, per, _ = send_o.shape
-    k_ng = ng.shape[0]
-    caps = (per - 2 * k_ng) // 8
-    hi, lo = two(ng[...])
+    caps = per // 8
 
     def dest(d, _):
         for r in range(0, caps, 2):
-            both = []
-            for k in range(2):
-                b = blocks[d * caps + r + k]
-                x = pq[pl.ds(pl.multiple_of(jnp.minimum(b, nq - 1) * 8, 8), 8), :]
-                y = pm[pl.ds(pl.multiple_of(jnp.maximum(b - nq, 0) * 8, 8), 8), :]
-                both.append(jnp.where(jnp.full((8, 128), b, jnp.int32) < nq, x, y))
+            at = [jnp.maximum(blocks[d * caps + r + k] - first, 0) * 8 for k in range(2)]
+            both = [piece[pl.ds(pl.multiple_of(a, 8), 8), :] for a in at]
             send_o[d, r * 8 : r * 8 + 16, :] = jnp.concatenate(both, axis=0).astype(bf16)
-        send_o[d, caps * 8 : caps * 8 + k_ng, :], send_o[d, caps * 8 + k_ng :, :] = hi, lo
         return 0
 
     lax.fori_loop(0, dests, dest, 0)
 
 
-def adam_body(filled, sources, recv, master, first, second, f_o, s_o, m_o, ng_o, two, grad):
+def owner_body(
+    meta, counts, blocks, recv_h, master_h, first_h, second_h, gains, biases, n_first, n_second, *refs
+):
+    bufs, (f_o, s_o, m_o, q_o, nf_o, ns_o, np_o) = refs[:8], refs[8:15]
+    held, later, early, parts, grad, flat, total, recv, master, first, second, sem, sems = refs[15:]
+    moved = load([(recv_h, recv), (master_h, master), (first_h, first), (second_h, second)], sems)
+    collect(meta, bufs, held, sem)
+    for c in moved:
+        c.wait()
     caps, br, _ = master.shape
+    n = q_o.shape[0] * q_o.shape[1] // (128 * 64)
+    k_ng = total.shape[0]
+    for p in range(8):
+        later[p] = recv[meta[9 + p]].astype(f32)
+        early[p] = held[p, n * 8 : n * 16, :].astype(f32)
+    total[...] = sum(
+        held[p, n * 16 : n * 16 + k_ng, :].astype(f32) + held[p, n * 16 + k_ng :, :].astype(f32) for p in range(8)
+    )
+    start = meta[8] * caps
+
+    def pick(r, _):
+        b = blocks[start + r]
+        old = pl.ds(pl.multiple_of(jnp.minimum(b, n - 1) * 8, 8), 8)
+        new = pl.ds(pl.multiple_of(r * 8, 8), 8)
+        is_q = jnp.full((8, 128), b, jnp.int32) < n
+        for p in range(8):
+            parts[p % 4, r, p // 4] = jnp.where(is_q, early[p, old, :], later[p, new, :])
+        return 0
+
+    lax.fori_loop(0, caps, pick, 0, unroll=2)
     for j in range(4):
-        for c in range(2):
-            two[:, c] = recv[sources[c * 4 + j], 0 : caps * 8, :].astype(f32).reshape(caps, 8, 128)
-        grad[pl.ds(j, caps * 16, stride=4), :] = two[...].reshape(caps * 16, 128)
-
-    def add(s, tot):
-        part = recv[s, caps * 8 :, :].astype(f32)
-        return tot + (part[: part.shape[0] // 2] + part[part.shape[0] // 2 :])
-
-    ng_o[...] = lax.fori_loop(0, recv.shape[0], add, jnp.zeros(ng_o.shape, f32))
+        grad[pl.ds(j, caps * 16, stride=4), :] = parts[j].reshape(caps * 16, 128)
 
     def slot(r, _):
         g = grad[pl.ds(pl.multiple_of(r * br, br), br), :]
         m_old, f_old, s_old = master[r], first[r], second[r]
         fn, sn, mn = adam(g, m_old, f_old, s_old)
-        keep = jnp.full(g.shape, filled[r], jnp.int32) > 0
+        keep = jnp.full(g.shape, counts[start + r], jnp.int32) > 0
         f_o[r] = jnp.where(keep, fn, f_old)
         s_o[r] = jnp.where(keep, sn, s_old)
         m_o[r] = jnp.where(keep, mn, m_old)
         return 0
 
     lax.fori_loop(0, caps, slot, 0, unroll=2)
+    rows = q_o.shape[0]
+    for j in range(4):
+        flat[pl.ds(j, n * 16, stride=4), :] = columns(held, j, 0, n * 8)
+    for part in range(3):
+        q_o[:, part * 128 : (part + 1) * 128] = flat[pl.ds(part, rows, stride=3), :].astype(bf16)
+    corr_one = 1.0 - beta_one**STEP
+    corr_two = 1.0 - beta_two**STEP
+    per = n_first.shape[1] // 128
+    for k in range(4):
+        old = (biases if k % 2 else gains)[k // 2 : k // 2 + 1, :]
+        g = jnp.concatenate([total[k * per + j : k * per + j + 1, :] for j in range(per)], axis=1)
+        fn = beta_one * n_first[k : k + 1, :] + (1.0 - beta_one) * g
+        sn = beta_two * n_second[k : k + 1, :] + (1.0 - beta_two) * g * g
+        nf_o[k : k + 1, :] = fn
+        ns_o[k : k + 1, :] = sn
+        np_o[k : k + 1, :] = old - norm_rate * (fn / corr_one / (jnp.sqrt(sn / corr_two) + adam_epsilon))
 
 
 def collect(meta, bufs, held, sem):
@@ -670,17 +771,6 @@
         for j in range(4):
             ref[:, j * 128 : (j + 1) * 128] = columns(held, j, lo, n).astype(bf16)
         lo += n
-
-
-def place_qkv_body(meta, *refs):
-    bufs, (q_o, held, flat, sem) = refs[:8], refs[8:]
-    collect(meta, bufs, held, sem)
-    n = held.shape[1]
-    rows = q_o.shape[0]
-    for j in range(4):
-        flat[pl.ds(j, 2 * n, stride=4), :] = columns(held, j, 0, n)
-    for part in range(3):
-        q_o[:, part * 128 : (part + 1) * 128] = flat[pl.ds(part, rows, stride=3), :].astype(bf16)
 
 
 def per_device(
@@ -721,7 +811,10 @@
     o0, o1 = bit_of(me, 1 - core, 0), bit_of(me, 1 - core, 1)
     length = lengths[0]
     base = zi * rows
-    ids = [length, base, core, zi, q0, q1, o0, o1]
+    ids = [length, base, core, zi, q0, q1, o0, o1, me]
+    ids += [
+        me - (me & 7) + c + ((j >> 1) << order[c][0]) + ((j & 1) << order[c][1]) for c in range(2) for j in range(4)
+    ]
     meta = jnp.stack(ids).astype(jnp.int32)
 
     def after(x, *deps):
@@ -742,20 +835,24 @@
     mm = 2 * rows * width
     qkv_z = over_mp(part_of(w_qkv, 4, core * 2 + q0))
     left, right = from_mp(tok[rows - HALO :], 1), from_mp(tok[:HALO], -1)
+    ffn_piece = jnp.concatenate([part_of(w, 8, mine) for w in (w_in, w_down, w_out)], axis=0)
+    qkv_z = after(qkv_z, left, right, ffn_piece)
     qkv_bufs = [qkv_z, swap(qkv_z, 0)]
-    ffn_piece = jnp.concatenate([part_of(w, 8, mine) for w in (w_in, w_down, w_out)], axis=0)
     ffn_z = over_mp(after(ffn_piece, qkv_z))
-    [a1e] = call(norm_body, [((ext, width), bf16)], [VM] * 5, [], 4 * mm, 1 << 20, 16)(
+    [a1e] = call(norm_body, [((ext, width), bf16)], [VM] * 5,
+        [pltpu.VMEM((ext, width), bf16), pltpu.SemaphoreType.DMA], 4 * mm, 1 << 20, 16, (HB,),
+    )(
         tok, left, right, norm_gains, norm_biases
     )
     qkv_bufs = both_cores([qkv_bufs[0], after(qkv_bufs[1], a1e)])
+    all_qkv = pltpu.VMEM((groups, ext, 3 * PAIR), bf16)
     proj_w = pltpu.VMEM((groups, width, 3 * PAIR), bf16)
     qkv, state = call(
         qkv_body,
         [((groups, ext, 3 * PAIR), bf16), ((groups, STATE, PAIR), bf16)],
-        [SM, VM] + [HB] * 4,
-        [proj_w, pltpu.SemaphoreType.DMA],
-        2 * ext * width * 3 * width, 6 << 20, 20,
+        [SM] + [HB] * 5,
+        [proj_w, all_qkv, pltpu.VMEM((ext, width), bf16), pltpu.SemaphoreType.DMA, pltpu.SemaphoreType.DMA],
+        2 * ext * width * 3 * width, 6 << 20, 20, (HB, VM),
     )(meta, after(a1e, ffn_z), *qkv_bufs)
     states = all_states(state)
     ffn_z = after(ffn_z, a1e, qkv_bufs[1])
@@ -775,11 +872,20 @@
         ],
         1 << 20, 4 << 20, 12, (HB,),
     )(*flat_state)
+    blocks = owners.shape[0]
+    earlier = jnp.arange(blocks)[None, :] < jnp.arange(blocks)[:, None]
+    alike = owners[None, :] == owners[:, None]
+    slot = jnp.sum((earlier & alike).astype(jnp.int32), axis=1)
+    slot_rows = owners * capacity + slot
+    hit = slot_rows[None, :] == jnp.arange(ndp * capacity, dtype=jnp.int32)[:, None]
+    held = jnp.sum(jnp.where(hit, jnp.arange(blocks, dtype=jnp.int32)[None, :], 0), axis=1)
+    counts = jnp.sum(hit.astype(jnp.int32), axis=1)
     [near] = call(
-        near_body, [((rows, width), f32)], [SM, VM], [], mm * 1024, 12 << 20, 16,
-    )(meta, after(qkv, parts, ffn_bufs[1], ffn_bufs[2], *states))
+        near_body, [((rows, width), f32)], [SM, HB],
+        [all_qkv, pltpu.VMEM((rows, width), f32), pltpu.SemaphoreType.DMA], mm * 1024, 12 << 20, 16, (HB,),
+    )(meta, after(qkv, parts, slot, held, counts, ffn_bufs[1], ffn_bufs[2], *states))
     ffn_bufs = both_cores(ffn_bufs)
-    held_state = exchange(after(parts, ffn_bufs[3]), "dp")
+    held_state = exchange(after(parts, ffn_bufs[3], near), "dp")
 
     hid_w = w_in.shape[1]
     big = pltpu.VMEM((rows, width), f32)
@@ -788,60 +894,71 @@
     wide = pltpu.VMEM((groups, rows, hid_w), f32)
     half = pltpu.VMEM((groups, n_m, width), bf16)
     four = pltpu.VMEM((groups, rows, hid_w), bf16)
-    (outputs, do, head, tail, dx2, dctx, dqf, dstate, ng2, wout, grad_m, give_m) = call(
+    (outputs, head, tail, dx2, dctx, dqf, dstate, ng2, wout, grad_m, give_m) = call(
         main_body,
         [
-            ((rows, width), bf16), ((rows, width), bf16), ((EDGE, width), bf16), ((EDGE, width), bf16),
+            ((rows, width), bf16), ((EDGE, width), bf16), ((EDGE, width), bf16),
             ((rows, width), f32), ((rows, width), bf16), ((rows, width), f32), ((groups, STATE, PAIR), bf16), ((2, width), f32),
             ((groups,) + w_out.shape, bf16), ((groups, n_m, width), bf16), ((groups, n_m, width), bf16),
         ],
-        [SM] + [VM] * 10 + [HB] * 8,
+        [SM] + [HB] * 8 + [VM] * 2 + [HB] * 8,
         [
+            low, low, pltpu.VMEM((groups,) + w_out.shape, bf16), big, low, low,
+            pltpu.VMEM((4, groups, STATE, PAIR), bf16),
             pltpu.VMEM((groups, width, hid_w), bf16), pltpu.VMEM((groups, hid_w, width), bf16),
             big, big, pltpu.VMEM((rows, 128), f32), wide, wide, big, big, big, big,
             low, low, low, low, low, low, four, four, low, half, half,
-            pltpu.SemaphoreType.DMA((3,)), pltpu.SemaphoreType.DMA,
+            pltpu.VMEM((groups, rows, PAIR), bf16), pltpu.SemaphoreType.DMA((5,)), pltpu.SemaphoreType.DMA,
         ],
         mm * hid_w * groups * 6, 24 << 20, 44,
-        (HB, VM, VM, VM, HB, VM, HB, VM, VM, VM, HB, HB),
+        (HB, VM, VM, HB, HB, HB, VM, VM, HB, HB, HB),
     )(meta, near, qkv, *states, tok, cot, norm_gains, norm_biases, *ffn_bufs)
 
     head, tail, dstate, give_m, _ = lax.optimization_barrier((head, tail, dstate, give_m, held_state))
-    dstates = all_states(dstate)
     do_l, do_r = from_mp(tail, 1), from_mp(head, -1)
+    late = after(dstate, do_l, do_r)
+    dstates = [dstate, swap_mp(dstate, 1)] + [swap_mp(late, m) for m in range(2, groups)]
+
+    bits = [bit_of(me, core, s).astype(jnp.int32).reshape(1) for s in range(2)]
 
     def halve(own, got, s):
-        n = own.shape[-1] // 2
-        bit = bit_of(me, core, s)
-
-        def half(at, own, got):
-            a = lax.dynamic_slice_in_dim(own, at * n, n, own.ndim - 1).astype(f32)
-            return a + lax.dynamic_slice_in_dim(got, at * n, n, own.ndim - 1).astype(f32)
-
-        give = half(1 - bit, own, got).astype(bf16)
-        own, got = after(own, give), after(got, give)
-        return give, half(bit, own, got)
-
-    def finish(keep, got, extra=None):
-        tot = keep + got.astype(f32)
+        shape = own.shape[:-1] + (own.shape[-1] // 2,)
+        return call(
+            halve_body, [(shape, bf16), (shape, f32)], [SM, VM, VM], [], 1 << 20, 4 << 20, 16,
+        )(bits[s], own, got)
+
+    def rest_of(keep, got):
         for s in range(2, nbits - 1):
-            tot = tot.astype(bf16).astype(f32) + swap(tot.astype(bf16), s).astype(f32)
-        if extra is None:
-            return [exchange(tot.astype(bf16), "mp")]
-        msg = jnp.concatenate([tot, jnp.broadcast_to(extra, (groups,) + extra.shape)], axis=1)
-        part = [lax.dynamic_slice_in_dim(msg, zi ^ m, 1, 0) for m in range(groups)]
-        return part[:1] + [swap_mp(part[m], m) for m in range(1, groups)]
+            tot = (keep + got.astype(f32)).astype(bf16)
+            keep, got = tot.astype(f32), swap(tot, s)
+        return keep, got
+
+    def finish_m(keep, got):
+        part = call(
+            total_body, [((1,) + keep.shape[1:], bf16)] * groups, [SM, VM, VM], [], 1 << 20, 2 << 20, 12,
+        )(meta, *rest_of(keep, got))
+        return [part[0]] + [swap_mp(part[m], m) for m in range(1, groups)]
+
+    def finish_q(keep, got, extra):
+        keep, got = rest_of(keep, got)
+        for s in range(2, nbits - 1):
+            extra = extra + swap(extra, s)
+        shape = (1, keep.shape[1] + extra.shape[0], keep.shape[2])
+        part = call(
+            total_q_body, [(shape, f32)] * groups, [SM, VM, VM, VM], [], 1 << 20, 2 << 20, 12,
+        )(meta, keep, got, extra)
+        return [part[0]] + [swap_mp(part[m], m) for m in range(1, groups)]
 
     give_m, keep_m = halve(grad_m, after(swap_core(give_m), do_l, do_r, dstates[1]), 0)
     got_m = swap(give_m, 0)
     dq, dkn, dvn = call(
         near_back_body,
         [((rows, width), bf16), ((rows, width), f32), ((rows, width), f32)],
-        [SM] + [VM] * 4 + [HB] * 2,
+        [SM, HB, HB] + [VM] * 2 + [HB] * 2,
         [
             pltpu.VMEM((rows + 2 * EDGE, width), bf16), pltpu.VMEM((rows + 2 * EDGE, width), f32),
             pltpu.VMEM((ext, width), f32), pltpu.VMEM((ext, width), f32),
-            pltpu.VMEM(wout.shape, bf16), big, pltpu.SemaphoreType.DMA((2,)),
+            pltpu.VMEM(wout.shape, bf16), big, all_qkv, pltpu.SemaphoreType.DMA((4,)),
         ],
         mm * 2048, 24 << 20, 20,
     )(meta, qkv, after(dctx, give_m), do_l, do_r, wout, dqf)
@@ -850,14 +967,15 @@
     dproj, grad_q, give_q = call(
         proj_body,
         [((groups, rows, 3 * PAIR), bf16), ((groups, n_q, width), f32), ((groups, n_q, width), f32)],
-        [SM] + [VM] * 9,
+        [SM, HB] + [VM] * 7 + [HB],
         [
             pltpu.VMEM((groups, rows, 3 * PAIR), bf16), pltpu.VMEM((3 * width, 128), f32),
-            pltpu.VMEM((2 * n_q, width), f32), pltpu.SemaphoreType.DMA,
+            pltpu.VMEM((2 * n_q, width), f32), all_qkv, low,
+            pltpu.SemaphoreType.DMA, pltpu.SemaphoreType.DMA((2,)),
         ],
         mm * 3 * width, 24 << 20, 20, (HB, VM, VM),
     )(meta, qkv, dq, dkn, dvn, *dstates, a1e)
-    got_q = swap_core(give_q)
+    got_q = swap_core(after(give_q, got_m))
     give_m, keep_m = halve(keep_m, after(got_m, give_q), 1)
     got_m = swap(give_m, 1)
     give_q, keep_q = halve(grad_q, got_q, 0)
@@ -872,83 +990,59 @@
         ],
         mm * 3 * width, 8 << 20, 16,
     )(meta, after(dproj, give_q), tok, dx2, norm_gains, ng2, *qkv_bufs)
-    z_m = finish(keep_m, after(got_m, give_q))
+    z_m = finish_m(keep_m, after(got_m, give_q, ng, got_q))
     give_q, keep_q = halve(keep_q, after(got_q, ng), 1)
     got_q = swap(give_q, 1)
-    z_m = [after(z_m[0], give_q)]
-
-
-    blocks = owners.shape[0]
-    earlier = jnp.arange(blocks)[None, :] < jnp.arange(blocks)[:, None]
-    alike = owners[None, :] == owners[:, None]
-    slot = jnp.sum((earlier & alike).astype(jnp.int32), axis=1)
-    slot_rows = owners * capacity + slot
-    hit = slot_rows[None, :] == jnp.arange(ndp * capacity, dtype=jnp.int32)[:, None]
-    held = jnp.sum(jnp.where(hit, jnp.arange(blocks, dtype=jnp.int32)[None, :], 0), axis=1)
-    filled = lax.dynamic_slice_in_dim(
-        jnp.sum(hit.astype(jnp.int32), axis=1), me * capacity, capacity, 0
-    )
+    z_m[0] = after(z_m[0], give_q)
+
     nb_q = n_q * 2 // 16
 
-    def updated(z, n, first, extra=()):
+    def updated(z, n, first, extra):
         return call(
             functools.partial(pieces_body, first, len(z)),
-            [((n, 128), f32), ((n, 128), bf16)] + list(extra),
+            [((n, 128), f32), ((n + extra, 128), bf16)],
             [SM, SM] + [VM] * (len(z) + 1), [], 1 << 20, 4 << 20, 20,
         )(owners, slot, *z, held_state)
 
-    def everywhere(piece):
+    def everywhere(piece, *first):
         x, y = swap(piece, 0), swap(piece, 1)
-        return both_cores([piece, x, y, swap(x, 1)])
-
-    piece_m, fresh_m = updated(z_m, n_m, nb_q)
+        return both_cores([piece, x, y, swap(after(x, *first), 1)])
+
+    piece_m, fresh_m = updated(z_m, n_m, nb_q, 0)
+    [send] = call(
+        functools.partial(route_body, nb_q), [((ndp, capacity * 8, 128), bf16)], [SM, VM], [],
+        1 << 20, 4 << 20, 16,
+    )(held, piece_m)
+    recv = exchange(send, "dp")
     m_bufs = everywhere(fresh_m)
-    z_q = finish(keep_q, after(got_q, fresh_m), ng)
-    z_q[0] = after(z_q[0], m_bufs[1], m_bufs[2])
-    piece_q, fresh_q, ng_z = updated(z_q, n_q, 0, [((n_ng, 128), f32)])
-    q_bufs = everywhere(fresh_q)
-    [send] = call(
-        route_body, [((ndp, capacity * 8 + 2 * n_ng, 128), bf16)], [SM, VM, VM, VM], [], 1 << 20, 4 << 20, 16,
-    )(held, piece_q, piece_m, ng_z)
-    recv = exchange(send, "dp")
-    high = me - (me & 7)
-    sources = jnp.stack(
-        [
-            high + c + ((j >> 1) << order[c][0]) + ((j & 1) << order[c][1])
-            for c in range(2)
-            for j in range(4)
-        ]
-    ).astype(jnp.int32)
-    state_shape = (capacity, block_rows, 128)
-    first_new, second_new, master_new, norm_sum = call(
-        adam_body,
-        [(state_shape, f32)] * 3 + [((n_ng, 128), f32)],
-        [SM, SM] + [VM] * 4,
-        [pltpu.VMEM((capacity, 2, 8, 128), f32), pltpu.VMEM((capacity * block_rows, 128), f32)],
-        1 << 20, 8 << 20, 20,
-    )(filled, sources, recv, master, first_moment, second_moment)
+    z_q = finish_q(keep_q, after(got_q, fresh_m), ng)
+    z_q[0] = after(z_q[0], *m_bufs[1:4])
+    _, fresh_q = updated(z_q, n_q, 0, n_q + 2 * n_ng)
     new_out, new_in, new_down = call(
         place_body, [(w_out.shape, bf16), (w_in.shape, bf16), (w_down.shape, bf16)],
         [SM] + [HB] * 8, [pltpu.VMEM((8, n_m, 128), bf16), pltpu.SemaphoreType.DMA],
         1 << 20, 4 << 20, 16,
     )(meta, *m_bufs)
-    [new_qkv] = call(
-        place_qkv_body, [(w_qkv.shape, bf16)], [SM] + [HB] * 8,
+    q_bufs = everywhere(fresh_q, new_down)
+    state_shape = (capacity, block_rows, 128)
+    norm_shape = (4, width)
+    n_held = fresh_q.shape[0]
+    (first_new, second_new, master_new, new_qkv, norm_first_new, norm_second_new, norm_new) = call(
+        owner_body,
+        [(state_shape, f32)] * 3 + [(w_qkv.shape, bf16)] + [(norm_shape, f32)] * 3,
+        [SM] * 3 + [HB] * 4 + [VM] * 4 + [HB] * 8,
         [
-            pltpu.VMEM((8, n_q, 128), bf16), pltpu.VMEM((w_qkv.size // 128, 128), f32),
-            pltpu.SemaphoreType.DMA,
+            pltpu.VMEM((8, n_held, 128), bf16), pltpu.VMEM((8, capacity * 8, 128), f32),
+            pltpu.VMEM((8, n_q, 128), f32), pltpu.VMEM((4, capacity, 2, 8, 128), f32),
+            pltpu.VMEM((capacity * block_rows, 128), f32), pltpu.VMEM((w_qkv.size // 128, 128), f32),
+            pltpu.VMEM((n_ng, 128), f32), pltpu.VMEM((ndp, capacity * 8, 128), bf16),
+            pltpu.VMEM(state_shape, f32), pltpu.VMEM(state_shape, f32), pltpu.VMEM(state_shape, f32),
+            pltpu.SemaphoreType.DMA, pltpu.SemaphoreType.DMA,
         ],
-        1 << 20, 2 << 20, 16,
-    )(meta, *q_bufs)
-
-    corr_one = 1.0 - beta_one**STEP
-    corr_two = 1.0 - beta_two**STEP
-    norm_grad = norm_sum.reshape(4, width)
-    norm_params = jnp.stack([norm_gains[0], norm_biases[0], norm_gains[1], norm_biases[1]])
-    norm_first_new = beta_one * norm_first + (1.0 - beta_one) * norm_grad
-    norm_second_new = beta_two * norm_second + (1.0 - beta_two) * norm_grad * norm_grad
-    norm_new = norm_params - norm_rate * (
-        norm_first_new / corr_one / (jnp.sqrt(norm_second_new / corr_two) + adam_epsilon)
+        1 << 20, 8 << 20, 24,
+    )(
+        meta, counts, held, recv, master, first_moment, second_moment,
+        norm_gains, norm_biases, norm_first, norm_second, *q_bufs,
     )
     return (
         outputs[None], tokens_grad[None], first_new, second_new, master_new,

time: 226 us -> 212 us (0.938)
  other arithmetic: 18.1 us -> 0.49 us
  Pallas kernels: 62.1 us -> 71.7 us
  starting transfers between devices: 70.9 us -> 66.8 us
  local copies, waits for them, and re-layouts: 12.6 us -> 9.07 us
    ppermute x15 -> x18, waiting for transfers between devices: 23.2 us -> 36.7 us  [swap_mp(): return lax.ppermute(x, 'mp', [(i, i ^ mask) for i in range(groups)])]
    convert_element_type x5 -> x0, other arithmetic: 11.2 us -> none  [the longest x4 8.6 us: halve(): give = half(1 - bit, own, got).astype(bf16)]
    pallas_call x14 -> x19, Pallas kernels: 62.1 us -> 71.7 us  [fixed(): run(*[pltpu.with_memory_space_constraint(x, pltpu.HBM) if spec is HB else...]
    ppermute x14, waiting for transfers between devices: 20.1 us -> 10.8 us  [swap(): lax.ppermute(x, 'dp', [(i, i ^ 1 << order[i & 1][s]) for i in range(ndp)])]
    ppermute x4, waiting for transfers between devices: 12.7 us -> 4.37 us  [from_mp(): lax.ppermute(x, 'mp', [(i, i + step) for i in range(groups) if 0 <= i + s...]
    ppermute x16, waiting for transfers between devices: 0.82 us -> 6.62 us  [swap_core(): return lax.ppermute(x, 'dp', [(i, i ^ 1) for i in range(ndp)])]
    add x3 -> x0, other arithmetic: 5.72 us -> none  [the longest x2 4.64 us: half(): a + lax.dynamic_slice_in_dim(got, at * n, n, own.ndim - 1).astype(f32)]
    all_to_all x3 -> x2, starting transfers between devices: 12.4 us -> 7.89 us  [exchange(): return lax.all_to_all(x, axis, 0, 0, tiled=True)]
  transfers between devices with their start and end apart: 52 -> 54, of which waited for: 13 -> 23; matrix products, arithmetic and copies ran while one was open for 7% -> 1% of each run, Pallas kernels for 25% -> 31%
where the time goes in v4:
time: 212 us; the launch traced here: 211 us
  Pallas kernels  71.7 us (34%)
  starting transfers between devices  66.8 us (32%)
  waiting for transfers between devices  61.1 us (29%)
  local copies, waits for them, and re-layouts  9.07 us (4%)
  between operations  2.2 us (1%)
    pallas_call x19, Pallas kernels, fixed(): run(*[pltpu.with_memory_space_constraint(x, pltpu.HBM) if spec is HB else...  71.7 us
    ppermute x18, waiting for transfers between devices, swap_mp(): return lax.ppermute(x, 'mp', [(i, i ^ mask) for i in range(groups)])  36.7 us
    ppermute x18, starting transfers between devices, swap_mp(): return lax.ppermute(x, 'mp', [(i, i ^ mask) for i in range(groups)])  27.5 us
    ppermute x14, starting transfers between devices, swap(): lax.ppermute(x, 'dp', [(i, i ^ 1 << order[i & 1][s]) for i in range(ndp)])  17.6 us
    ppermute x4, starting transfers between devices, from_mp(): lax.ppermute(x, 'mp', [(i, i + step) for i in range(groups) if 0 <= i + s...  11 us
    ppermute x14, waiting for transfers between devices, swap(): lax.ppermute(x, 'dp', [(i, i ^ 1 << order[i & 1][s]) for i in range(ndp)])  10.8 us
    all_to_all x2, starting transfers between devices, exchange(): return lax.all_to_all(x, axis, 0, 0, tiled=True)  7.89 us
    ppermute x16, waiting for transfers between devices, swap_core(): return lax.ppermute(x, 'dp', [(i, i ^ 1) for i in range(ndp)])  6.62 us
  transfers between devices with their start and end apart: 54, of which 23 were waited for; matrix products, arithmetic and copies ran while one was open for 1% of the time, Pallas kernels for 31%

profile of v4, /device:TPU:0, one launch (start us, length us, event | category | flops | bytes accessed | tf_op | source)
XLA Modules:
  0.0 211.5 jit_solution(18373778179323984751)
XLA Ops:
  1.7 4.1 %collective-permute-start.3 = (bf16[128,384]{1,0:T(8,128)(2,1)S(1)}, bf16[128,384]{1,0:T(8,128)(2,1)S(1)}, u32[]{:S(2)}, u32[]{:S(2)}) collective-permute-start(bf16[128,384]{1,0:T(8,128)(2,1)S(1)} %constant_dynamic-slice_fusion), channel_id=1, source_target_pairs={{0,2},{1,3},{2,0},{3,1},{4,6},{5,7},{6,4},{7,5},{8,10},{9,11},{10,... | collective-permute-start | bytes 294920 | tf_op jit(solution)/shard_map/ppermute | solution.py:802
  9.5 4.5 %collective-permute-start = (bf16[64,512]{1,0:T(8,128)(2,1)S(1)}, bf16[64,512]{1,0:T(8,128)(2,1)S(1)}, u32[]{:S(2)}, u32[]{:S(2)}) collective-permute-start(bf16[64,512]{1,0:T(8,128)(2,1)S(1)} %get-tuple-element.163), channel_id=1, source_target_pairs={{0,1},{1,2},{2,3},{4,5},{5,6},{6,7},{8,9},{9,10},{10,11},{12,13},{... | collective-permute-start | bytes 196616 | tf_op jit(solution)/shard_map/ppermute | solution.py:799
  17.7 3.5 %collective-permute-start.7 = (bf16[144,512]{1,0:T(8,128)(2,1)S(1)}, bf16[144,512]{1,0:T(8,128)(2,1)S(1)}, u32[]{:S(2)}, u32[]{:S(2)}) collective-permute-start(bf16[144,512]{1,0:T(8,128)(2,1)S(1)} %pad_maximum_fusion.2), channel_id=1, source_target_pairs={{0,3},{1,2},{2,1},{3,0},{4,7},{5,6},{6,5},{7,4},{8,11},{9,10},{10,... | collective-permute-start | bytes 442376 | tf_op jit(solution)/shard_map/ppermute | solution.py:802
  26.3 6.6 %collective-permute-done.6 = bf16[144,512]{1,0:T(8,128)(2,1)S(1)} collective-permute-done((bf16[144,512]{1,0:T(8,128)(2,1)S(1)}, bf16[144,512]{1,0:T(8,128)(2,1)S(1)}, u32[]{:S(2)}, u32[]{:S(2)}) %collective-permute-start.6) | collective-permute-done | bytes 147488 | tf_op jit(solution)/shard_map/ppermute | solution.py:802
  37.4 5.3 %shard_map.239 = (bf16[4,640,384]{2,1,0:T(8,128)(2,1)}, bf16[4,144,128]{2,1,0:T(8,128)(2,1)S(1)}) custom-call(s32[17]{0:T(128)S(1)} %stack.97.meta, bf16[640,512]{1,0:T(8,128)(2,1)} %shard_map.238.a1e_h, bf16[4,128,384]{2,1,0:T(8,128)(2,1)} %copy-done.12, bf16[4,128,384]{2,1,0:T(8,128)(2,1)} %copy-done.15, bf16[4,128,384]{2,1,0:T(8,128)(2,1)} %copy-done.16, ...), custom_call_target="tpu_custom_call" | custom-call | flops 1006632960 | bytes 6291456 | tf_op jit(solution)/shard_map/pallas_call | solution.py:54
  42.7 2.7 %collective-permute-start.15 = (bf16[4,144,128]{2,1,0:T(8,128)(2,1)S(1)}, bf16[4,144,128]{2,1,0:T(8,128)(2,1)S(1)}, u32[]{:S(2)}, u32[]{:S(2)}) collective-permute-start(bf16[4,144,128]{2,1,0:T(8,128)(2,1)S(1)} %get-tuple-element.92.h0), channel_id=1, source_target_pairs={{0,3},{1,2},{2,1},{3,0},{4,7},{5,6},{6,5},{7,4},{8,11},{9,10},{10,... | collective-permute-start | bytes 442376 | tf_op jit(solution)/shard_map/ppermute | solution.py:802
  47.1 4.2 %collective-permute-done.15.h3 = bf16[4,144,128]{2,1,0:T(8,128)(2,1)S(1)} collective-permute-done((bf16[4,144,128]{2,1,0:T(8,128)(2,1)S(1)}, bf16[4,144,128]{2,1,0:T(8,128)(2,1)S(1)}, u32[]{:S(2)}, u32[]{:S(2)}) %collective-permute-start.15) | collective-permute-done | bytes 147488 | tf_op jit(solution)/shard_map/ppermute | solution.py:802
  51.3 5.4 %collective-permute-done.14.h2 = bf16[4,144,128]{2,1,0:T(8,128)(2,1)S(1)} collective-permute-done((bf16[4,144,128]{2,1,0:T(8,128)(2,1)S(1)}, bf16[4,144,128]{2,1,0:T(8,128)(2,1)S(1)}, u32[]{:S(2)}, u32[]{:S(2)}) %collective-permute-start.14) | collective-permute-done | bytes 147488 | tf_op jit(solution)/shard_map/ppermute | solution.py:802
  58.4 2.6 %shard_map.240 = f32[8,3,192,128]{3,2,1,0:T(8,128)} custom-call(f32[1536,128]{1,0:T(8,128)} %bitcast.39, f32[1536,128]{1,0:T(8,128)} %bitcast.40, f32[1536,128]{1,0:T(8,128)} %bitcast.41), custom_call_target="tpu_custom_call" | custom-call | flops 1048576 | bytes 4194304 | tf_op jit(solution)/shard_map/pallas_call | solution.py:54
  61.3 6.3 %shard_map.241.near_h = f32[512,512]{1,0:T(8,128)} custom-call(s32[17]{0:T(128)S(1)} %stack.97.meta, bf16[4,640,384]{2,1,0:T(8,128)(2,1)} %get-tuple-element.93.qkv_h), custom_call_target="tpu_custom_call" | custom-call | flops 536870912 | bytes 12582912 | tf_op jit(solution)/shard_map/pallas_call | solution.py:54
  68.5 3.8 %all-to-all-start = ((f32[8,3,192,128]{3,2,1,0:T(8,128)}), f32[8,3,192,128]{3,2,1,0:T(8,128)S(1)}, u32[]{:S(2)}, u32[]{:S(2)}) async-start(f32[8,3,192,128]{3,2,1,0:T(8,128)} %shard_map.240), calls=%async_computation | async-start | bytes 4718592 | tf_op jit(solution)/shard_map/all_to_all | solution.py:805
  78.0 20.8 %shard_map.242 = (bf16[512,512]{1,0:T(8,128)(2,1)}, bf16[32,512]{1,0:T(8,128)(2,1)S(1)}, bf16[32,512]{1,0:T(8,128)(2,1)S(1)}, f32[512,512]{1,0:T(8,128)}, bf16[5...) custom-call(s32[17]{0:T(128)S(1)} %stack.97.meta, ...), custom_call_target="tpu_custom_call" | custom-call | flops 6442450944 | bytes 25165824 | tf_op jit(solution)/shard_map/pallas_call | solution.py:54
  98.8 2.7 %all-to-all-done.refs_4_ = f32[8,3,192,128]{3,2,1,0:T(8,128)S(1)} async-done(((f32[8,3,192,128]{3,2,1,0:T(8,128)}), f32[8,3,192,128]{3,2,1,0:T(8,128)S(1)}, u32[]{:S(2)}, u32[]{:S(2)}) %all-to-all-start) | async-done | bytes 2359328 | tf_op jit(solution)/shard_map/all_to_all | solution.py:805
  101.7 3.7 %collective-permute-start.22 = (bf16[32,512]{1,0:T(8,128)(2,1)S(1)}, bf16[32,512]{1,0:T(8,128)(2,1)S(1)}, u32[]{:S(2)}, u32[]{:S(2)}) collective-permute-start(bf16[32,512]{1,0:T(8,128)(2,1)S(1)} %get-tuple-element.104), channel_id=1, source_target_pairs={{0,1},{1,2},{2,3},{4,5},{5,6},{6,7},{8,9},{9,10},{10,11},{12,13},{... | collective-permute-start | bytes 98312 | tf_op jit(solution)/shard_map/ppermute | solution.py:799
  107.0 4.2 %collective-permute-done.23.do_r = bf16[32,512]{1,0:T(8,128)(2,1)S(1)} collective-permute-done((bf16[32,512]{1,0:T(8,128)(2,1)S(1)}, bf16[32,512]{1,0:T(8,128)(2,1)S(1)}, u32[]{:S(2)}, u32[]{:S(2)}) %collective-permute-start.23) | collective-permute-done | bytes 32800 | tf_op jit(solution)/shard_map/ppermute | solution.py:799
  114.0 2.5 %collective-permute-start.25 = (bf16[4,144,128]{2,1,0:T(8,128)(2,1)S(1)}, bf16[4,144,128]{2,1,0:T(8,128)(2,1)S(1)}, u32[]{:S(2)}, u32[]{:S(2)}) collective-permute-start(bf16[4,144,128]{2,1,0:T(8,128)(2,1)S(1)} %get-tuple-element.115.s0), channel_id=1, source_target_pairs={{0,2},{1,3},{2,0},{3,1},{4,6},{5,7},{6,4},{7,5},{8,10},{9,11},{10,... | collective-permute-start | bytes 442376 | tf_op jit(solution)/shard_map/ppermute | solution.py:802
  116.6 6.9 %shard_map.244 = (bf16[512,512]{1,0:T(8,128)(2,1)S(1)}, f32[512,512]{1,0:T(8,128)S(1)}, f32[512,512]{1,0:T(8,128)S(1)}) custom-call(s32[17]{0:T(128)S(1)} %stack.97.meta, bf16[4,640,384]{2,1,0:T(8,128)(2,1)} %get-tuple-element.93.qkv_h, bf16[512,512]{1,0:T(8,128)(2,1)} %get-tuple-element.109.dctx_h, bf16[32,512]{1,0:T(8,128)(2,1)S(1)} %collective-permute-done.22.do_l, ...), custom_call_target="tpu_custom_call" | custom-call | flops 1073741824 | bytes 25165824 | tf_op jit(solution)/shard_map/pallas_call | solution.py:54
  123.5 4.8 %collective-permute-done.25.s2 = bf16[4,144,128]{2,1,0:T(8,128)(2,1)S(1)} collective-permute-done((bf16[4,144,128]{2,1,0:T(8,128)(2,1)S(1)}, bf16[4,144,128]{2,1,0:T(8,128)(2,1)S(1)}, u32[]{:S(2)}, u32[]{:S(2)}) %collective-permute-start.25) | collective-permute-done | bytes 147488 | tf_op jit(solution)/shard_map/ppermute | solution.py:802
  128.3 5.6 %shard_map.245 = (bf16[4,512,384]{2,1,0:T(8,128)(2,1)}, f32[4,192,512]{2,1,0:T(8,128)S(1)}, f32[4,192,512]{2,1,0:T(8,128)S(1)}) custom-call(s32[17]{0:T(128)S(1)} %stack.97.meta, bf16[4,640,384]{2,1,0:T(8,128)(2,1)} %get-tuple-element.93.qkv_h, bf16[512,512]{1,0:T(8,128)(2,1)S(1)} %get-tuple-element.112.dq, f32[512,512]{1,0:T(8,128)S(1)} %get-tuple-element.113.dkn, ...), custom_call_target="tpu_custom_call" | custom-call | flops 805306368 | bytes 25165824 | tf_op jit(solution)/shard_map/pallas_call | solution.py:54
  138.2 7.1 %shard_map.247 = (f32[512,512]{1,0:T(8,128)}, f32[16,128]{1,0:T(8,128)S(1)}) custom-call(s32[17]{0:T(128)S(1)} %stack.97.meta, bf16[4,512,384]{2,1,0:T(8,128)(2,1)} %get-tuple-element.121.dproj_h, bf16[512,512]{1,0:T(8,128)(2,1)S(1)} %bitcast.38, f32[512,512]{1,0:T(8,128)} %get-tuple-element.122.dx2_h, f32[2,512]{1,0:T(2,128)S(1)} %copy-done.6, ...), custom_call_target="tpu_custom_call" | custom-call | flops 805306368 | bytes 8388608 | tf_op jit(solution)/shard_map/pallas_call | solution.py:54
  145.3 2.5 %collective-permute-done.29.got = bf16[4,576,128]{2,1,0:T(8,128)(2,1)S(1)} collective-permute-done((bf16[4,576,128]{2,1,0:T(8,128)(2,1)S(1)}, bf16[4,576,128]{2,1,0:T(8,128)(2,1)S(1)}, u32[]{:S(2)}, u32[]{:S(2)}) %collective-permute-start.29) | collective-permute-done | bytes 589856 | tf_op jit(solution)/shard_map/ppermute | solution.py:793
  150.4 2.6 %collective-permute-start.33 = (bf16[1,576,128]{2,1,0:T(8,128)(2,1)S(1)}, bf16[1,576,128]{2,1,0:T(8,128)(2,1)S(1)}, u32[]{:S(2)}, u32[]{:S(2)}) collective-permute-start(bf16[1,576,128]{2,1,0:T(8,128)(2,1)S(1)} %get-tuple-element.138), channel_id=1, source_target_pairs={{0,3},{1,2},{2,1},{3,0},{4,7},{5,6},{6,5},{7,4},{8,11},{9,10},{10,... | collective-permute-start | bytes 442376 | tf_op jit(solution)/shard_map/ppermute | solution.py:802
  156.4 6.3 %collective-permute-done.32.refs_2_ = bf16[1,576,128]{2,1,0:T(8,128)(2,1)S(1)} collective-permute-done((bf16[1,576,128]{2,1,0:T(8,128)(2,1)S(1)}, bf16[1,576,128]{2,1,0:T(8,128)(2,1)S(1)}, u32[]{:S(2)}, u32[]{:S(2)}) %collective-permute-start.32) | collective-permute-done | bytes 147488 | tf_op jit(solution)/shard_map/ppermute | solution.py:802
  165.7 3.9 %collective-permute-done.35.refs_1_ = bf16[576,128]{1,0:T(8,128)(2,1)} collective-permute-done((bf16[576,128]{1,0:T(8,128)(2,1)S(1)}, bf16[576,128]{1,0:T(8,128)(2,1)}, u32[]{:S(2)}, u32[]{:S(2)}) %collective-permute-start.35) | collective-permute-done | bytes 147488 | tf_op jit(solution)/shard_map/ppermute | solution.py:793
  171.7 3.5 %collective-permute-start.38 = (f32[1,208,128]{2,1,0:T(8,128)S(1)}, f32[1,208,128]{2,1,0:T(8,128)S(1)}, u32[]{:S(2)}, u32[]{:S(2)}) collective-permute-start(f32[1,208,128]{2,1,0:T(8,128)S(1)} %get-tuple-element.145), channel_id=1, source_target_pairs={{0,1},{1,0},{2,3},{3,2},{4,5},{5,4},{6,7},{7,6},{8,9},{9,8},{10,11... | collective-permute-start | bytes 319496 | tf_op jit(solution)/shard_map/ppermute | solution.py:802
  175.1 2.4 %collective-permute-start.40 = (f32[1,208,128]{2,1,0:T(8,128)}, f32[1,208,128]{2,1,0:T(8,128)S(1)}, u32[]{:S(2)}, u32[]{:S(2)}) collective-permute-start(f32[1,208,128]{2,1,0:T(8,128)} %get-tuple-element.147), channel_id=1, source_target_pairs={{0,3},{1,2},{2,1},{3,0},{4,7},{5,6},{6,5},{7,4},{8,11},{9,10},{10,... | collective-permute-start | bytes 319496 | tf_op jit(solution)/shard_map/ppermute | solution.py:802
  177.5 2.4 %collective-permute-done.38.refs_1_ = f32[1,208,128]{2,1,0:T(8,128)S(1)} collective-permute-done((f32[1,208,128]{2,1,0:T(8,128)S(1)}, f32[1,208,128]{2,1,0:T(8,128)S(1)}, u32[]{:S(2)}, u32[]{:S(2)}) %collective-permute-start.38) | collective-permute-done | bytes 106528 | tf_op jit(solution)/shard_map/ppermute | solution.py:802
  179.9 3.5 %collective-permute-done.39.refs_2_ = f32[1,208,128]{2,1,0:T(8,128)S(1)} collective-permute-done((f32[1,208,128]{2,1,0:T(8,128)S(1)}, f32[1,208,128]{2,1,0:T(8,128)S(1)}, u32[]{:S(2)}, u32[]{:S(2)}) %collective-permute-start.39) | collective-permute-done | bytes 106528 | tf_op jit(solution)/shard_map/ppermute | solution.py:802
  185.6 4.1 %all-to-all-start.1 = ((bf16[8,192,128]{2,1,0:T(8,128)(2,1)}), bf16[8,192,128]{2,1,0:T(8,128)(2,1)}, u32[]{:S(2)}, u32[]{:S(2)}) async-start(bf16[8,192,128]{2,1,0:T(8,128)(2,1)} %shard_map.252), calls=%async_computation.1 | async-start | bytes 786432 | tf_op jit(solution)/shard_map/all_to_all | solution.py:805
  194.5 3.1 %shard_map.255 = (bf16[128,512]{1,0:T(8,128)(2,1)}, bf16[512,512]{1,0:T(8,128)(2,1)}, bf16[512,512]{1,0:T(8,128)(2,1)}) custom-call(s32[17]{0:T(128)S(1)} %stack.97.meta, bf16[576,128]{1,0:T(8,128)(2,1)} %copy-done.4, bf16[576,128]{1,0:T(8,128)(2,1)} %collective-permute-done.35.refs_1_, bf16[576,128]{1,0:T(8,128)(2,1)} %collective-permute-done.36.refs_2_, ...), custom_call_target="tpu_custom_call" | custom-call | flops 1048576 | bytes 4194304 | tf_op jit(solution)/shard_map/pallas_call | solution.py:54
  201.4 2.6 %collective-permute-done.47.refs_3_ = bf16[416,128]{1,0:T(8,128)(2,1)S(1)} collective-permute-done((bf16[416,128]{1,0:T(8,128)(2,1)S(1)}, bf16[416,128]{1,0:T(8,128)(2,1)S(1)}, u32[]{:S(2)}, u32[]{:S(2)}) %collective-permute-start.47) | collective-permute-done | bytes 106528 | tf_op jit(solution)/shard_map/ppermute | solution.py:793
  206.0 5.3 %shard_map.256 = (f32[24,64,128]{2,1,0:T(8,128)}, f32[24,64,128]{2,1,0:T(8,128)}, f32[24,64,128]{2,1,0:T(8,128)}, bf16[512,384]{1,0:T(8,128)(2,1)}, f32[4,512]{1...) custom-call(s32[17]{0:T(128)S(1)} %stack.97.meta, s32[192]{0:T(256)S(1)} %get-tuple-element.160.counts, ...), custom_call_target="tpu_custom_call" | custom-call | flops 1048576 | bytes 8388608 | tf_op jit(solution)/shard_map/pallas_call | solution.py:54
  (175 shorter events, 59.9 us)
Async XLA Ops:
  1.7 14.1 %collective-permute-start.3 = (bf16[128,384]{1,0:T(8,128)(2,1)S(1)}, bf16[128,384]{1,0:T(8,128)(2,1)S(1)}, u32[]{:S(2)}, u32[]{:S(2)}) collective-permute-start(bf16[128,384]{1,0:T(8,128)(2,1)S(1)} %constant_dynamic-slice_fusion), channel_id=1, source_target_pairs={{0,2},{1,3},{2,0},{3,1},{4,6},{5,7},{6,4},{7,5},{8,10},{9,11},{10,... | collective-permute-start | bytes 294920 | tf_op jit(solution)/shard_map/ppermute | solution.py:802
  5.8 10.0 %collective-permute-start.2 = (bf16[128,384]{1,0:T(8,128)(2,1)S(1)}, bf16[128,384]{1,0:T(8,128)(2,1)S(1)}, u32[]{:S(2)}, u32[]{:S(2)}) collective-permute-start(bf16[128,384]{1,0:T(8,128)(2,1)S(1)} %constant_dynamic-slice_fusion), channel_id=1, source_target_pairs={{0,1},{1,0},{2,3},{3,2},{4,5},{5,4},{6,7},{7,6},{8,9},{9,8},{10,11... | collective-permute-start | bytes 294920 | tf_op jit(solution)/shard_map/ppermute | solution.py:802
  17.7 8.7 %collective-permute-start.7 = (bf16[144,512]{1,0:T(8,128)(2,1)S(1)}, bf16[144,512]{1,0:T(8,128)(2,1)S(1)}, u32[]{:S(2)}, u32[]{:S(2)}) collective-permute-start(bf16[144,512]{1,0:T(8,128)(2,1)S(1)} %pad_maximum_fusion.2), channel_id=1, source_target_pairs={{0,3},{1,2},{2,1},{3,0},{4,7},{5,6},{6,5},{7,4},{8,11},{9,10},{10,... | collective-permute-start | bytes 442376 | tf_op jit(solution)/shard_map/ppermute | solution.py:802
  21.2 11.8 %collective-permute-start.6 = (bf16[144,512]{1,0:T(8,128)(2,1)S(1)}, bf16[144,512]{1,0:T(8,128)(2,1)S(1)}, u32[]{:S(2)}, u32[]{:S(2)}) collective-permute-start(bf16[144,512]{1,0:T(8,128)(2,1)S(1)} %pad_maximum_fusion.2), channel_id=1, source_target_pairs={{0,2},{1,3},{2,0},{3,1},{4,6},{5,7},{6,4},{7,5},{8,10},{9,11},{10,... | collective-permute-start | bytes 442376 | tf_op jit(solution)/shard_map/ppermute | solution.py:802
  21.5 11.4 %collective-permute-start.5 = (bf16[144,512]{1,0:T(8,128)(2,1)S(1)}, bf16[144,512]{1,0:T(8,128)(2,1)S(1)}, u32[]{:S(2)}, u32[]{:S(2)}) collective-permute-start(bf16[144,512]{1,0:T(8,128)(2,1)S(1)} %pad_maximum_fusion.2), channel_id=1, source_target_pairs={{0,1},{1,0},{2,3},{3,2},{4,5},{5,4},{6,7},{7,6},{8,9},{9,8},{10,11... | collective-permute-start | bytes 442376 | tf_op jit(solution)/shard_map/ppermute | solution.py:802
  24.0 11.9 %collective-permute-start.9 = (bf16[4,128,384]{2,1,0:T(8,128)(2,1)S(1)}, bf16[4,128,384]{2,1,0:T(8,128)(2,1)S(1)}, u32[]{:S(2)}, u32[]{:S(2)}) collective-permute-start(bf16[4,128,384]{2,1,0:T(8,128)(2,1)S(1)} %pad_maximum_fusion.1.refs_0_), channel_id=1, source_target_pairs={{0,4},{4,0},{8,12},{12,8},{16,20},{20,16},{24,28},{28,24},{1,5},{5... | collective-permute-start | bytes 1179656 | tf_op jit(solution)/shard_map/ppermute | solution.py:796
  24.1 11.8 %collective-permute-start.10 = (bf16[4,128,384]{2,1,0:T(8,128)(2,1)S(1)}, bf16[4,128,384]{2,1,0:T(8,128)(2,1)S(1)}, u32[]{:S(2)}, u32[]{:S(2)}) collective-permute-start(bf16[4,128,384]{2,1,0:T(8,128)(2,1)S(1)} %collective-permute-done.8.refs_1_), channel_id=1, source_target_pairs={{0,4},{4,0},{8,12},{12,8},{16,20},{20,16},{24,28},{28,24},{1,5},{5... | collective-permute-start | bytes 1179656 | tf_op jit(solution)/shard_map/ppermute | solution.py:796
  33.0 23.7 %collective-permute-start.12 = (bf16[4,144,512]{2,1,0:T(8,128)(2,1)S(1)}, bf16[4,144,512]{2,1,0:T(8,128)(2,1)S(1)}, u32[]{:S(2)}, u32[]{:S(2)}) collective-permute-start(bf16[4,144,512]{2,1,0:T(8,128)(2,1)S(1)} %pad_maximum_fusion.refs_0_), channel_id=1, source_target_pairs={{0,16},{4,12},{8,24},{12,4},{16,0},{20,28},{24,8},{28,20},{1,17},{... | collective-permute-start | bytes 1769480 | tf_op jit(solution)/shard_map/ppermute | solution.py:793
  33.6 23.1 %collective-permute-start.11 = (bf16[4,144,512]{2,1,0:T(8,128)(2,1)S(1)}, bf16[4,144,512]{2,1,0:T(8,128)(2,1)}, u32[]{:S(2)}, u32[]{:S(2)}) collective-permute-start(bf16[4,144,512]{2,1,0:T(8,128)(2,1)S(1)} %pad_maximum_fusion.refs_0_), channel_id=1, source_target_pairs={{0,8},{4,20},{8,0},{12,28},{16,24},{20,4},{24,16},{28,12},{1,9},{5... | collective-permute-start | bytes 1769480 | tf_op jit(solution)/shard_map/ppermute | solution.py:793
  42.7 8.6 %collective-permute-start.15 = (bf16[4,144,128]{2,1,0:T(8,128)(2,1)S(1)}, bf16[4,144,128]{2,1,0:T(8,128)(2,1)S(1)}, u32[]{:S(2)}, u32[]{:S(2)}) collective-permute-start(bf16[4,144,128]{2,1,0:T(8,128)(2,1)S(1)} %get-tuple-element.92.h0), channel_id=1, source_target_pairs={{0,3},{1,2},{2,1},{3,0},{4,7},{5,6},{6,5},{7,4},{8,11},{9,10},{10,... | collective-permute-start | bytes 442376 | tf_op jit(solution)/shard_map/ppermute | solution.py:802
  45.4 11.3 %collective-permute-start.14 = (bf16[4,144,128]{2,1,0:T(8,128)(2,1)S(1)}, bf16[4,144,128]{2,1,0:T(8,128)(2,1)S(1)}, u32[]{:S(2)}, u32[]{:S(2)}) collective-permute-start(bf16[4,144,128]{2,1,0:T(8,128)(2,1)S(1)} %get-tuple-element.92.h0), channel_id=1, source_target_pairs={{0,2},{1,3},{2,0},{3,1},{4,6},{5,7},{6,4},{7,5},{8,10},{9,11},{10,... | collective-permute-start | bytes 442376 | tf_op jit(solution)/shard_map/ppermute | solution.py:802
  45.4 11.3 %collective-permute-start.13 = (bf16[4,144,128]{2,1,0:T(8,128)(2,1)S(1)}, bf16[4,144,128]{2,1,0:T(8,128)(2,1)S(1)}, u32[]{:S(2)}, u32[]{:S(2)}) collective-permute-start(bf16[4,144,128]{2,1,0:T(8,128)(2,1)S(1)} %get-tuple-element.92.h0), channel_id=1, source_target_pairs={{0,1},{1,0},{2,3},{3,2},{4,5},{5,4},{6,7},{7,6},{8,9},{9,8},{10,11... | collective-permute-start | bytes 442376 | tf_op jit(solution)/shard_map/ppermute | solution.py:802
  56.7 10.9 %collective-permute-start.16 = (bf16[4,144,512]{2,1,0:T(8,128)(2,1)}, bf16[4,144,512]{2,1,0:T(8,128)(2,1)S(1)}, u32[]{:S(2)}, u32[]{:S(2)}) collective-permute-start(bf16[4,144,512]{2,1,0:T(8,128)(2,1)} %collective-permute-done.11.refs_1_), channel_id=1, source_target_pairs={{0,16},{4,12},{8,24},{12,4},{16,0},{20,28},{24,8},{28,20},{1,17},{... | collective-permute-start | bytes 1769480 | tf_op jit(solution)/shard_map/ppermute | solution.py:793
  68.5 33.0 %all-to-all-start = ((f32[8,3,192,128]{3,2,1,0:T(8,128)}), f32[8,3,192,128]{3,2,1,0:T(8,128)S(1)}, u32[]{:S(2)}, u32[]{:S(2)}) async-start(f32[8,3,192,128]{3,2,1,0:T(8,128)} %shard_map.240), calls=%async_computation | async-start | bytes 4718592 | tf_op jit(solution)/shard_map/all_to_all | solution.py:805
  101.5 9.7 %collective-permute-start.21 = (bf16[4,576,512]{2,1,0:T(8,128)(2,1)}, bf16[4,576,512]{2,1,0:T(8,128)(2,1)S(1)}, u32[]{:S(2)}, u32[]{:S(2)}) collective-permute-start(bf16[4,576,512]{2,1,0:T(8,128)(2,1)} %get-tuple-element.103), channel_id=1, source_target_pairs={{0,4},{4,0},{8,12},{12,8},{16,20},{20,16},{24,28},{28,24},{1,5},{5... | collective-permute-start | bytes 7077896 | tf_op jit(solution)/shard_map/ppermute | solution.py:796
  101.5 9.7 %collective-permute-start.24 = (bf16[4,144,128]{2,1,0:T(8,128)(2,1)S(1)}, bf16[4,144,128]{2,1,0:T(8,128)(2,1)S(1)}, u32[]{:S(2)}, u32[]{:S(2)}) collective-permute-start(bf16[4,144,128]{2,1,0:T(8,128)(2,1)S(1)} %get-tuple-element.115.s0), channel_id=1, source_target_pairs={{0,1},{1,0},{2,3},{3,2},{4,5},{5,4},{6,7},{7,6},{8,9},{9,8},{10,11... | collective-permute-start | bytes 442376 | tf_op jit(solution)/shard_map/ppermute | solution.py:802
  113.4 20.4 %collective-permute-start.27 = (bf16[4,576,256]{2,1,0:T(8,128)(2,1)S(1)}, bf16[4,576,256]{2,1,0:T(8,128)(2,1)S(1)}, u32[]{:S(2)}, u32[]{:S(2)}) collective-permute-start(bf16[4,576,256]{2,1,0:T(8,128)(2,1)S(1)} %get-tuple-element.108), channel_id=1, source_target_pairs={{0,8},{4,20},{8,0},{12,28},{16,24},{20,4},{24,16},{28,12},{1,9},{5... | collective-permute-start | bytes 3538952 | tf_op jit(solution)/shard_map/ppermute | solution.py:793
  114.0 9.4 %collective-permute-start.26 = (bf16[4,144,128]{2,1,0:T(8,128)(2,1)S(1)}, bf16[4,144,128]{2,1,0:T(8,128)(2,1)S(1)}, u32[]{:S(2)}, u32[]{:S(2)}) collective-permute-start(bf16[4,144,128]{2,1,0:T(8,128)(2,1)S(1)} %get-tuple-element.115.s0), channel_id=1, source_target_pairs={{0,3},{1,2},{2,1},{3,0},{4,7},{5,6},{6,5},{7,4},{8,11},{9,10},{10,... | collective-permute-start | bytes 442376 | tf_op jit(solution)/shard_map/ppermute | solution.py:802
  114.0 14.2 %collective-permute-start.25 = (bf16[4,144,128]{2,1,0:T(8,128)(2,1)S(1)}, bf16[4,144,128]{2,1,0:T(8,128)(2,1)S(1)}, u32[]{:S(2)}, u32[]{:S(2)}) collective-permute-start(bf16[4,144,128]{2,1,0:T(8,128)(2,1)S(1)} %get-tuple-element.115.s0), channel_id=1, source_target_pairs={{0,2},{1,3},{2,0},{3,1},{4,6},{5,7},{6,4},{7,5},{8,10},{9,11},{10,... | collective-permute-start | bytes 442376 | tf_op jit(solution)/shard_map/ppermute | solution.py:802
  134.2 13.7 %collective-permute-start.29 = (bf16[4,576,128]{2,1,0:T(8,128)(2,1)S(1)}, bf16[4,576,128]{2,1,0:T(8,128)(2,1)S(1)}, u32[]{:S(2)}, u32[]{:S(2)}) collective-permute-start(bf16[4,576,128]{2,1,0:T(8,128)(2,1)S(1)} %get-tuple-element.128), channel_id=1, source_target_pairs={{0,16},{4,12},{8,24},{12,4},{16,0},{20,28},{24,8},{28,20},{1,17},{... | collective-permute-start | bytes 1769480 | tf_op jit(solution)/shard_map/ppermute | solution.py:793
  137.5 10.3 %collective-permute-start.30 = (bf16[4,192,256]{2,1,0:T(8,128)(2,1)S(1)}, bf16[4,192,256]{2,1,0:T(8,128)(2,1)S(1)}, u32[]{:S(2)}, u32[]{:S(2)}) collective-permute-start(bf16[4,192,256]{2,1,0:T(8,128)(2,1)S(1)} %get-tuple-element.120), channel_id=1, source_target_pairs={{0,8},{4,20},{8,0},{12,28},{16,24},{20,4},{24,16},{28,12},{1,9},{5... | collective-permute-start | bytes 1179656 | tf_op jit(solution)/shard_map/ppermute | solution.py:793
  148.6 14.0 %collective-permute-start.32 = (bf16[1,576,128]{2,1,0:T(8,128)(2,1)S(1)}, bf16[1,576,128]{2,1,0:T(8,128)(2,1)S(1)}, u32[]{:S(2)}, u32[]{:S(2)}) collective-permute-start(bf16[1,576,128]{2,1,0:T(8,128)(2,1)S(1)} %get-tuple-element.137), channel_id=1, source_target_pairs={{0,2},{1,3},{2,0},{3,1},{4,6},{5,7},{6,4},{7,5},{8,10},{9,11},{10,... | collective-permute-start | bytes 442376 | tf_op jit(solution)/shard_map/ppermute | solution.py:802
  150.4 12.3 %collective-permute-start.33 = (bf16[1,576,128]{2,1,0:T(8,128)(2,1)S(1)}, bf16[1,576,128]{2,1,0:T(8,128)(2,1)S(1)}, u32[]{:S(2)}, u32[]{:S(2)}) collective-permute-start(bf16[1,576,128]{2,1,0:T(8,128)(2,1)S(1)} %get-tuple-element.138), channel_id=1, source_target_pairs={{0,3},{1,2},{2,1},{3,0},{4,7},{5,6},{6,5},{7,4},{8,11},{9,10},{10,... | collective-permute-start | bytes 442376 | tf_op jit(solution)/shard_map/ppermute | solution.py:802
  153.1 17.4 %collective-permute-start.34 = (bf16[4,192,128]{2,1,0:T(8,128)(2,1)S(1)}, bf16[4,192,128]{2,1,0:T(8,128)(2,1)S(1)}, u32[]{:S(2)}, u32[]{:S(2)}) collective-permute-start(bf16[4,192,128]{2,1,0:T(8,128)(2,1)S(1)} %get-tuple-element.134), channel_id=1, source_target_pairs={{0,16},{4,12},{8,24},{12,4},{16,0},{20,28},{24,8},{28,20},{1,17},{... | collective-permute-start | bytes 589832 | tf_op jit(solution)/shard_map/ppermute | solution.py:793
  164.3 13.2 %collective-permute-start.36 = (bf16[576,128]{1,0:T(8,128)(2,1)S(1)}, bf16[576,128]{1,0:T(8,128)(2,1)}, u32[]{:S(2)}, u32[]{:S(2)}) collective-permute-start(bf16[576,128]{1,0:T(8,128)(2,1)S(1)} %get-tuple-element.141.refs_0_), channel_id=1, source_target_pairs={{0,16},{4,12},{8,24},{12,4},{16,0},{20,28},{24,8},{28,20},{1,17},{... | collective-permute-start | bytes 442376 | tf_op jit(solution)/shard_map/ppermute | solution.py:793
  169.7 13.7 %collective-permute-start.37 = (bf16[576,128]{1,0:T(8,128)(2,1)}, bf16[576,128]{1,0:T(8,128)(2,1)}, u32[]{:S(2)}, u32[]{:S(2)}) collective-permute-start(bf16[576,128]{1,0:T(8,128)(2,1)} %collective-permute-done.35.refs_1_), channel_id=1, source_target_pairs={{0,16},{4,12},{8,24},{12,4},{16,0},{20,28},{24,8},{28,20},{1,17},{... | collective-permute-start | bytes 442376 | tf_op jit(solution)/shard_map/ppermute | solution.py:793
  175.1 14.6 %collective-permute-start.40 = (f32[1,208,128]{2,1,0:T(8,128)}, f32[1,208,128]{2,1,0:T(8,128)S(1)}, u32[]{:S(2)}, u32[]{:S(2)}) collective-permute-start(f32[1,208,128]{2,1,0:T(8,128)} %get-tuple-element.147), channel_id=1, source_target_pairs={{0,3},{1,2},{2,1},{3,0},{4,7},{5,6},{6,5},{7,4},{8,11},{9,10},{10,... | collective-permute-start | bytes 319496 | tf_op jit(solution)/shard_map/ppermute | solution.py:802
  177.5 15.5 %collective-permute-start.43 = (bf16[576,128]{1,0:T(8,128)(2,1)S(1)}, bf16[576,128]{1,0:T(8,128)(2,1)}, u32[]{:S(2)}, u32[]{:S(2)}) collective-permute-start(bf16[576,128]{1,0:T(8,128)(2,1)S(1)} %get-tuple-element.141.refs_0_), channel_id=1, source_target_pairs={{0,4},{4,0},{8,12},{12,8},{16,20},{20,16},{24,28},{28,24},{1,5},{5... | collective-permute-start | bytes 442376 | tf_op jit(solution)/shard_map/ppermute | solution.py:796
  179.9 14.5 %collective-permute-start.44 = (bf16[576,128]{1,0:T(8,128)(2,1)}, bf16[576,128]{1,0:T(8,128)(2,1)}, u32[]{:S(2)}, u32[]{:S(2)}) collective-permute-start(bf16[576,128]{1,0:T(8,128)(2,1)} %collective-permute-done.35.refs_1_), channel_id=1, source_target_pairs={{0,4},{4,0},{8,12},{12,8},{16,20},{20,16},{24,28},{28,24},{1,5},{5... | collective-permute-start | bytes 442376 | tf_op jit(solution)/shard_map/ppermute | solution.py:796
  183.4 11.1 %collective-permute-start.45 = (bf16[576,128]{1,0:T(8,128)(2,1)}, bf16[576,128]{1,0:T(8,128)(2,1)}, u32[]{:S(2)}, u32[]{:S(2)}) collective-permute-start(bf16[576,128]{1,0:T(8,128)(2,1)} %collective-permute-done.36.refs_2_), channel_id=1, source_target_pairs={{0,4},{4,0},{8,12},{12,8},{16,20},{20,16},{24,28},{28,24},{1,5},{5... | collective-permute-start | bytes 442376 | tf_op jit(solution)/shard_map/ppermute | solution.py:796
  183.4 11.1 %collective-permute-start.46 = (bf16[576,128]{1,0:T(8,128)(2,1)}, bf16[576,128]{1,0:T(8,128)(2,1)}, u32[]{:S(2)}, u32[]{:S(2)}) collective-permute-start(bf16[576,128]{1,0:T(8,128)(2,1)} %collective-permute-done.37.refs_3_), channel_id=1, source_target_pairs={{0,4},{4,0},{8,12},{12,8},{16,20},{20,16},{24,28},{28,24},{1,5},{5... | collective-permute-start | bytes 442376 | tf_op jit(solution)/shard_map/ppermute | solution.py:796
  185.6 18.4 %all-to-all-start.1 = ((bf16[8,192,128]{2,1,0:T(8,128)(2,1)}), bf16[8,192,128]{2,1,0:T(8,128)(2,1)}, u32[]{:S(2)}, u32[]{:S(2)}) async-start(bf16[8,192,128]{2,1,0:T(8,128)(2,1)} %shard_map.252), calls=%async_computation.1 | async-start | bytes 786432 | tf_op jit(solution)/shard_map/all_to_all | solution.py:805
  (56 other events, 394.8 us)

commit v5 on v4

--- a/solution.py
+++ b/solution.py
@@ -275,8 +275,8 @@
 
 def main_body(meta, near_h, qkv_h, h0, h1, h2, h3, tok_h, cot_h, gains, biases, *refs):
     bufs, refs = refs[:8], refs[8:]
-    out_h, head_o, tail_o, dx2_h, dctx_h, dqf_h, dst_o, ng_o, wout_h, keep_h, give_h = refs[:11]
-    refs = refs[11:]
+    out_h, dst_o, far_o, dx2_h, dctx_h, dqf_h, ng_o, wout_h, keep_h, give_h = refs[:10]
+    refs = refs[10:]
     do_o, dctx_o, wout_o, near, tok, cot, st = refs[:7]
     refs = (None,) * 5 + refs
     w_in, w_down, x2, xhat, rs, u, dh, acc, da2, far1, inv, dnum, phq, thq = refs[12:26]
@@ -392,8 +392,12 @@
 
     zero = jnp.zeros((1, width), f32)
     dg, db = lax.fori_loop(0, rows // 64, back_chunk, (zero, zero))
-    head_o[...] = do_o[0:EDGE, :]
-    tail_o[...] = do_o[rows - EDGE :, :]
+    even = jnp.full((EDGE, width), meta[3] & 1, jnp.int32) == 0
+    head, tail = do_o[0:EDGE, :].astype(f32), do_o[rows - EDGE :, :].astype(f32)
+    near_edge, far_edge = jnp.where(even, tail, head).astype(bf16), jnp.where(even, head, tail).astype(bf16)
+    for g in gs:
+        dst_o[g, STATE:, :] = near_edge[:, cols[g]]
+        far_o[g, STATE:, :] = far_edge[:, cols[g]]
     send(out_o, out_h)
     send(wout_o, wout_h)
     send(acc, dx2_h)
@@ -426,7 +430,10 @@
     for g in gs:
         d1 = dot_tn(phq[:, cols[g]], dnum[:, cols[g]])
         d2 = dot_tn(thq[:, cols[g]], dctx_o[:, cols[g]]) * rlen
-        dst_o[g, :PAIR, :], dst_o[g, PAIR:, :] = pack_state(d1, d2, dz[g])
+        both, low = pack_state(d1, d2, dz[g])
+        for ref in (dst_o, far_o):
+            ref[g, :PAIR, :] = both
+            ref[g, PAIR:STATE, :] = low
     send(da2, dqf_h)
     n_out = ctx_o.shape[1] // groups
 
@@ -447,7 +454,7 @@
 
 
 def near_back_body(
-    meta, qkv_h, dctx_h, do_l, do_r, wout_h, dqf_h, dq_o, dk_o, dv_o, dce, dqe, dke, dve, wout, dqf, qkv, sem,
+    meta, qkv_h, dctx_h, one, three, wout_h, dqf_h, dq_o, dk_o, dv_o, dce, dqe, dke, dve, wout, dqf, qkv, sem,
 ):
     pull = pltpu.make_async_copy(qkv_h, qkv, sem.at[2])
     pull.start()
@@ -463,8 +470,16 @@
     second.start()
     first.wait()
     w = wout[...].reshape(width, -1)
-    dce[0:EDGE, :] = dot_nt(do_l[...], w).astype(bf16)
-    dce[EDGE + rows :, :] = dot_nt(do_r[...], w).astype(bf16)
+    z = meta[3]
+    odd = jnp.full((EDGE, width), z & 1, jnp.int32) == 1
+    side = [
+        jnp.concatenate([ref[g, STATE:, :] for g in range(groups)], axis=1).astype(f32) for ref in (one, three)
+    ]
+    last_z = meta[17] - 1
+    do_l = jnp.where(odd, side[0], side[1]) * (z > 0).astype(f32)
+    do_r = jnp.where(odd, side[1], side[0]) * (z < last_z).astype(f32)
+    dce[0:EDGE, :] = dot_nt(do_l.astype(bf16), w).astype(bf16)
+    dce[EDGE + rows :, :] = dot_nt(do_r.astype(bf16), w).astype(bf16)
     dke[...] = jnp.zeros(dke.shape, f32)
     dve[...] = jnp.zeros(dve.shape, f32)
     pull.wait()
@@ -612,11 +627,12 @@
 
 
 def total_q_body(meta, keep, got, ng, *outs):
-    n = keep.shape[1]
+    n, k = keep.shape[1], ng.shape[0]
+    hi, lo = two(ng[...])
     for m, out in enumerate(outs):
         g = meta[3] ^ m
-        out[0, 0:n, :] = keep[g] + got[g].astype(f32)
-        out[0, n:, :] = ng[...]
+        out[0, 0:n, :] = (keep[g] + got[g].astype(f32)).astype(bf16)
+        out[0, n : n + k, :], out[0, n + k :, :] = hi, lo
 
 
 def slices_body(where, master, first, second, out_h, held, parts, sem, out_sem):
@@ -648,15 +664,16 @@
 
 
 def pieces_body(first, count, owners, slots, *refs):
-    parts, (st, piece_o, w_o) = refs[:count], refs[count:]
+    parts, (st, w_o, piece_o) = refs[:count], refs[count:]
     n = piece_o.shape[0]
     src = [(r, s) for r in parts for s in range(r.shape[0])]
     piece_o[...] = sum(r[s, 0:n, :].astype(f32) for r, s in src)
-    if w_o.shape[0] > n:
-        hi, lo = two(sum(r[s, n:, :] for r, s in src))
-        k = hi.shape[0]
-        w_o[n : 2 * n, :] = piece_o[...].astype(bf16)
-        w_o[2 * n : 2 * n + k, :], w_o[2 * n + k :, :] = hi, lo
+    w_o[n : 2 * n, :] = piece_o[...].astype(bf16)
+    if w_o.shape[0] > 2 * n:
+        k = (parts[0].shape[1] - n) // 2
+        w_o[2 * n : 3 * n, :] = two(piece_o[...])[1]
+        norms = sum(r[s, n : n + k, :].astype(f32) + r[s, n + k :, :].astype(f32) for r, s in src)
+        w_o[3 * n : 3 * n + k, :], w_o[3 * n + k :, :] = two(norms)
 
     def pair(i, _):
         new = []
@@ -672,26 +689,12 @@
     lax.fori_loop(0, n // 16, pair, 0, unroll=4)
 
 
-def route_body(first, blocks, piece, send_o):
-    dests, per, _ = send_o.shape
-    caps = per // 8
-
-    def dest(d, _):
-        for r in range(0, caps, 2):
-            at = [jnp.maximum(blocks[d * caps + r + k] - first, 0) * 8 for k in range(2)]
-            both = [piece[pl.ds(pl.multiple_of(a, 8), 8), :] for a in at]
-            send_o[d, r * 8 : r * 8 + 16, :] = jnp.concatenate(both, axis=0).astype(bf16)
-        return 0
-
-    lax.fori_loop(0, dests, dest, 0)
-
-
 def owner_body(
-    meta, counts, blocks, recv_h, master_h, first_h, second_h, gains, biases, n_first, n_second, *refs
+    meta, counts, blocks, later_h, master_h, first_h, second_h, gains, biases, n_first, n_second, *refs
 ):
     bufs, (f_o, s_o, m_o, q_o, nf_o, ns_o, np_o) = refs[:8], refs[8:15]
-    held, later, early, parts, grad, flat, total, recv, master, first, second, sem, sems = refs[15:]
-    moved = load([(recv_h, recv), (master_h, master), (first_h, first), (second_h, second)], sems)
+    held, early, parts, grad, flat, total, master, first, second, sem, sems = refs[15:]
+    moved = load([(later_h, parts), (master_h, master), (first_h, first), (second_h, second)], sems)
     collect(meta, bufs, held, sem)
     for c in moved:
         c.wait()
@@ -699,20 +702,18 @@
     n = q_o.shape[0] * q_o.shape[1] // (128 * 64)
     k_ng = total.shape[0]
     for p in range(8):
-        later[p] = recv[meta[9 + p]].astype(f32)
-        early[p] = held[p, n * 8 : n * 16, :].astype(f32)
+        early[p] = held[p, n * 8 : n * 16, :].astype(f32) + held[p, n * 16 : n * 24, :].astype(f32)
     total[...] = sum(
-        held[p, n * 16 : n * 16 + k_ng, :].astype(f32) + held[p, n * 16 + k_ng :, :].astype(f32) for p in range(8)
+        held[p, n * 24 : n * 24 + k_ng, :].astype(f32) + held[p, n * 24 + k_ng :, :].astype(f32) for p in range(8)
     )
     start = meta[8] * caps
 
     def pick(r, _):
         b = blocks[start + r]
         old = pl.ds(pl.multiple_of(jnp.minimum(b, n - 1) * 8, 8), 8)
-        new = pl.ds(pl.multiple_of(r * 8, 8), 8)
         is_q = jnp.full((8, 128), b, jnp.int32) < n
         for p in range(8):
-            parts[p % 4, r, p // 4] = jnp.where(is_q, early[p, old, :], later[p, new, :])
+            parts[p % 4, r, p // 4] = jnp.where(is_q, early[p, old, :], parts[p % 4, r, p // 4])
         return 0
 
     lax.fori_loop(0, caps, pick, 0, unroll=2)
@@ -762,15 +763,31 @@
     return jnp.concatenate([even, odd], axis=1).reshape(2 * n, 128)
 
 
-def place_body(meta, *refs):
-    bufs, outs, (held, sem) = refs[:8], refs[8:11], refs[11:]
+def place_body(first, meta, blocks, *refs):
+    bufs, outs, (parts_h, held, grads, parts, sem) = refs[:8], refs[8:11], refs[11:]
     collect(meta, bufs, held, sem)
+    half = held.shape[1] // 2
+    for p in range(8):
+        grads[p] = held[p, half:, :].astype(f32)
+    caps = parts.shape[1]
+
+    def pick(r, _):
+        b = jnp.maximum(blocks[meta[8] * caps + r] - first, 0)
+        at = pl.ds(pl.multiple_of(b * 8, 8), 8)
+        for p in range(8):
+            parts[p % 4, r, p // 4] = grads[p, at, :]
+        return 0
+
+    lax.fori_loop(0, caps, pick, 0, unroll=2)
+    out = pltpu.make_async_copy(parts, parts_h, sem)
+    out.start()
     lo = 0
     for ref in outs:
         n = ref.shape[0] // 2
         for j in range(4):
             ref[:, j * 128 : (j + 1) * 128] = columns(held, j, lo, n).astype(bf16)
         lo += n
+    out.wait()
 
 
 def per_device(
@@ -815,13 +832,14 @@
     ids += [
         me - (me & 7) + c + ((j >> 1) << order[c][0]) + ((j & 1) << order[c][1]) for c in range(2) for j in range(4)
     ]
+    ids.append(jnp.int32(groups))
     meta = jnp.stack(ids).astype(jnp.int32)
 
     def after(x, *deps):
         return lax.optimization_barrier((x,) + deps)[0]
 
     def over_mp(piece):
-        return jnp.stack([piece] + [swap_mp(piece, m) for m in range(1, groups)])
+        return [piece] + [swap_mp(piece, m) for m in range(1, groups)]
 
     def both_cores(bufs):
         return bufs + [swap_core(b) for b in bufs]
@@ -836,13 +854,27 @@
     qkv_z = over_mp(part_of(w_qkv, 4, core * 2 + q0))
     left, right = from_mp(tok[rows - HALO :], 1), from_mp(tok[:HALO], -1)
     ffn_piece = jnp.concatenate([part_of(w, 8, mine) for w in (w_in, w_down, w_out)], axis=0)
-    qkv_z = after(qkv_z, left, right, ffn_piece)
+    qkv_z = after(jnp.stack(qkv_z), left, right, ffn_piece)
+    ffn_z = jnp.stack(over_mp(after(ffn_piece, qkv_z)))
     qkv_bufs = [qkv_z, swap(qkv_z, 0)]
-    ffn_z = over_mp(after(ffn_piece, qkv_z))
+    capacity, block_rows = master.shape[0], master.shape[1]
+    where = [[[] for _ in range(4)] for _ in range(2)]
+    for d in range(ndp):
+        b = order[d & 1]
+        where[d & 1][2 * ((d >> b[0]) & 1) + ((d >> b[1]) & 1)].append(d)
+    flat_state = [x.reshape(capacity * block_rows, 128) for x in (master, first_moment, second_moment)]
+    [parts] = call(
+        functools.partial(slices_body, where), [((ndp, 3, capacity * 8, 128), f32)], [HB] * 3,
+        [
+            pltpu.VMEM((3, capacity * block_rows, 128), f32), pltpu.VMEM((3, 2, 4, capacity * 8, 128), f32),
+            pltpu.SemaphoreType.DMA((3,)), pltpu.SemaphoreType.DMA,
+        ],
+        1 << 20, 4 << 20, 12, (HB,),
+    )(*flat_state)
     [a1e] = call(norm_body, [((ext, width), bf16)], [VM] * 5,
         [pltpu.VMEM((ext, width), bf16), pltpu.SemaphoreType.DMA], 4 * mm, 1 << 20, 16, (HB,),
     )(
-        tok, left, right, norm_gains, norm_biases
+        after(tok, parts), left, right, norm_gains, norm_biases
     )
     qkv_bufs = both_cores([qkv_bufs[0], after(qkv_bufs[1], a1e)])
     all_qkv = pltpu.VMEM((groups, ext, 3 * PAIR), bf16)
@@ -858,20 +890,6 @@
     ffn_z = after(ffn_z, a1e, qkv_bufs[1])
     ffn_x, ffn_y = swap(ffn_z, 0), swap(ffn_z, 1)
     ffn_bufs = [ffn_z, ffn_x, ffn_y, swap(after(ffn_x, ffn_y, *states), 1)]
-    capacity, block_rows = master.shape[0], master.shape[1]
-    where = [[[] for _ in range(4)] for _ in range(2)]
-    for d in range(ndp):
-        b = order[d & 1]
-        where[d & 1][2 * ((d >> b[0]) & 1) + ((d >> b[1]) & 1)].append(d)
-    flat_state = [x.reshape(capacity * block_rows, 128) for x in (master, first_moment, second_moment)]
-    [parts] = call(
-        functools.partial(slices_body, where), [((ndp, 3, capacity * 8, 128), f32)], [HB] * 3,
-        [
-            pltpu.VMEM((3, capacity * block_rows, 128), f32), pltpu.VMEM((3, 2, 4, capacity * 8, 128), f32),
-            pltpu.SemaphoreType.DMA((3,)), pltpu.SemaphoreType.DMA,
-        ],
-        1 << 20, 4 << 20, 12, (HB,),
-    )(*flat_state)
     blocks = owners.shape[0]
     earlier = jnp.arange(blocks)[None, :] < jnp.arange(blocks)[:, None]
     alike = owners[None, :] == owners[:, None]
@@ -883,7 +901,7 @@
     [near] = call(
         near_body, [((rows, width), f32)], [SM, HB],
         [all_qkv, pltpu.VMEM((rows, width), f32), pltpu.SemaphoreType.DMA], mm * 1024, 12 << 20, 16, (HB,),
-    )(meta, after(qkv, parts, slot, held, counts, ffn_bufs[1], ffn_bufs[2], *states))
+    )(meta, after(qkv, slot, held, counts, ffn_bufs[1], ffn_bufs[2], *states))
     ffn_bufs = both_cores(ffn_bufs)
     held_state = exchange(after(parts, ffn_bufs[3], near), "dp")
 
@@ -894,11 +912,11 @@
     wide = pltpu.VMEM((groups, rows, hid_w), f32)
     half = pltpu.VMEM((groups, n_m, width), bf16)
     four = pltpu.VMEM((groups, rows, hid_w), bf16)
-    (outputs, head, tail, dx2, dctx, dqf, dstate, ng2, wout, grad_m, give_m) = call(
+    (outputs, dstate, dfar, dx2, dctx, dqf, ng2, wout, grad_m, give_m) = call(
         main_body,
         [
-            ((rows, width), bf16), ((EDGE, width), bf16), ((EDGE, width), bf16),
-            ((rows, width), f32), ((rows, width), bf16), ((rows, width), f32), ((groups, STATE, PAIR), bf16), ((2, width), f32),
+            ((rows, width), bf16), ((groups, STATE + EDGE, PAIR), bf16), ((groups, STATE + EDGE, PAIR), bf16),
+            ((rows, width), f32), ((rows, width), bf16), ((rows, width), f32), ((2, width), f32),
             ((groups,) + w_out.shape, bf16), ((groups, n_m, width), bf16), ((groups, n_m, width), bf16),
         ],
         [SM] + [HB] * 8 + [VM] * 2 + [HB] * 8,
@@ -911,13 +929,11 @@
             pltpu.VMEM((groups, rows, PAIR), bf16), pltpu.SemaphoreType.DMA((5,)), pltpu.SemaphoreType.DMA,
         ],
         mm * hid_w * groups * 6, 24 << 20, 44,
-        (HB, VM, VM, HB, HB, HB, VM, VM, HB, HB, HB),
+        (HB, VM, VM, HB, HB, HB, VM, HB, HB, HB),
     )(meta, near, qkv, *states, tok, cot, norm_gains, norm_biases, *ffn_bufs)
 
-    head, tail, dstate, give_m, _ = lax.optimization_barrier((head, tail, dstate, give_m, held_state))
-    do_l, do_r = from_mp(tail, 1), from_mp(head, -1)
-    late = after(dstate, do_l, do_r)
-    dstates = [dstate, swap_mp(dstate, 1)] + [swap_mp(late, m) for m in range(2, groups)]
+    dstate, dfar, give_m, _ = lax.optimization_barrier((dstate, dfar, give_m, held_state))
+    dstates = [dstate, swap_mp(dstate, 1), swap_mp(dstate, 2), swap_mp(dfar, 3)]
 
     bits = [bit_of(me, core, s).astype(jnp.int32).reshape(1) for s in range(2)]
 
@@ -933,23 +949,24 @@
             keep, got = tot.astype(f32), swap(tot, s)
         return keep, got
 
-    def finish_m(keep, got):
-        part = call(
+    def to_groups(part):
+        return [part[0]] + [swap_mp(part[m], m) for m in range(1, groups)]
+
+    def total_m(keep, got):
+        return call(
             total_body, [((1,) + keep.shape[1:], bf16)] * groups, [SM, VM, VM], [], 1 << 20, 2 << 20, 12,
         )(meta, *rest_of(keep, got))
-        return [part[0]] + [swap_mp(part[m], m) for m in range(1, groups)]
-
-    def finish_q(keep, got, extra):
+
+    def total_q(keep, got, extra):
         keep, got = rest_of(keep, got)
         for s in range(2, nbits - 1):
             extra = extra + swap(extra, s)
-        shape = (1, keep.shape[1] + extra.shape[0], keep.shape[2])
-        part = call(
-            total_q_body, [(shape, f32)] * groups, [SM, VM, VM, VM], [], 1 << 20, 2 << 20, 12,
+        shape = (1, keep.shape[1] + 2 * extra.shape[0], keep.shape[2])
+        return call(
+            total_q_body, [(shape, bf16)] * groups, [SM, VM, VM, VM], [], 1 << 20, 2 << 20, 12,
         )(meta, keep, got, extra)
-        return [part[0]] + [swap_mp(part[m], m) for m in range(1, groups)]
-
-    give_m, keep_m = halve(grad_m, after(swap_core(give_m), do_l, do_r, dstates[1]), 0)
+
+    give_m, keep_m = halve(grad_m, after(swap_core(give_m), dstates[1], dstates[3]), 0)
     got_m = swap(give_m, 0)
     dq, dkn, dvn = call(
         near_back_body,
@@ -961,7 +978,7 @@
             pltpu.VMEM(wout.shape, bf16), big, all_qkv, pltpu.SemaphoreType.DMA((4,)),
         ],
         mm * 2048, 24 << 20, 20,
-    )(meta, qkv, after(dctx, give_m), do_l, do_r, wout, dqf)
+    )(meta, qkv, after(dctx, give_m), dstates[1], dstates[3], wout, dqf)
     n_q = w_qkv.size // width // 2
     n_ng = 4 * width // 128
     dproj, grad_q, give_q = call(
@@ -990,40 +1007,45 @@
         ],
         mm * 3 * width, 8 << 20, 16,
     )(meta, after(dproj, give_q), tok, dx2, norm_gains, ng2, *qkv_bufs)
-    z_m = finish_m(keep_m, after(got_m, give_q, ng, got_q))
     give_q, keep_q = halve(keep_q, after(got_q, ng), 1)
+    z_m = to_groups(total_m(keep_m, after(got_m, give_q)))
     got_q = swap(give_q, 1)
-    z_m[0] = after(z_m[0], give_q)
-
     nb_q = n_q * 2 // 16
 
     def updated(z, n, first, extra):
         return call(
             functools.partial(pieces_body, first, len(z)),
-            [((n, 128), f32), ((n + extra, 128), bf16)],
-            [SM, SM] + [VM] * (len(z) + 1), [], 1 << 20, 4 << 20, 20,
-        )(owners, slot, *z, held_state)
+            [((2 * n + extra, 128), bf16)],
+            [SM, SM] + [VM] * (len(z) + 1), [pltpu.VMEM((n, 128), f32)], 1 << 20, 4 << 20, 20,
+        )(owners, slot, *z, held_state)[0]
 
     def everywhere(piece, *first):
         x, y = swap(piece, 0), swap(piece, 1)
         return both_cores([piece, x, y, swap(after(x, *first), 1)])
 
-    piece_m, fresh_m = updated(z_m, n_m, nb_q, 0)
-    [send] = call(
-        functools.partial(route_body, nb_q), [((ndp, capacity * 8, 128), bf16)], [SM, VM], [],
-        1 << 20, 4 << 20, 16,
-    )(held, piece_m)
-    recv = exchange(send, "dp")
-    m_bufs = everywhere(fresh_m)
-    z_q = finish_q(keep_q, after(got_q, fresh_m), ng)
-    z_q[0] = after(z_q[0], *m_bufs[1:4])
-    _, fresh_q = updated(z_q, n_q, 0, n_q + 2 * n_ng)
-    new_out, new_in, new_down = call(
-        place_body, [(w_out.shape, bf16), (w_in.shape, bf16), (w_down.shape, bf16)],
-        [SM] + [HB] * 8, [pltpu.VMEM((8, n_m, 128), bf16), pltpu.SemaphoreType.DMA],
-        1 << 20, 4 << 20, 16,
-    )(meta, *m_bufs)
-    q_bufs = everywhere(fresh_q, new_down)
+    part_q = total_q(keep_q, got_q, ng)
+    z_q = to_groups(part_q)
+    z_m[0] = after(z_m[0], part_q[0])
+    fresh_m = updated(z_m, n_m, nb_q, 0)
+    m_x, m_y = swap(fresh_m, 0), swap(fresh_m, 1)
+    z_q[0] = after(z_q[0], m_x, m_y)
+    fresh_q = updated(z_q, n_q, 0, n_q + 2 * n_ng)
+    q_x, q_y = swap(fresh_q, 0), swap(fresh_q, 1)
+    m_bufs = both_cores([fresh_m, m_x, m_y, swap(after(m_x, fresh_q), 1)])
+    part_shape = (4, capacity, 2, 8, 128)
+    new_out, new_in, new_down, later = call(
+        functools.partial(place_body, nb_q),
+        [(w_out.shape, bf16), (w_in.shape, bf16), (w_down.shape, bf16), (part_shape, f32)],
+        [SM, SM] + [HB] * 8,
+        [
+            pltpu.VMEM((8, 2 * n_m, 128), bf16), pltpu.VMEM((8, n_m, 128), f32), pltpu.VMEM(part_shape, f32),
+            pltpu.SemaphoreType.DMA,
+        ],
+        1 << 20, 4 << 20, 16, (VM, VM, VM, HB),
+    )(meta, held, *m_bufs)
+    q_z = swap(after(q_x, q_y, m_bufs[3]), 1)
+    q_bufs = [fresh_q, q_x, q_y, q_z]
+    q_bufs += [swap_core(b) for b in q_bufs[:3]] + [swap_core(after(q_z, new_down))]
     state_shape = (capacity, block_rows, 128)
     norm_shape = (4, width)
     n_held = fresh_q.shape[0]
@@ -1032,16 +1054,15 @@
         [(state_shape, f32)] * 3 + [(w_qkv.shape, bf16)] + [(norm_shape, f32)] * 3,
         [SM] * 3 + [HB] * 4 + [VM] * 4 + [HB] * 8,
         [
-            pltpu.VMEM((8, n_held, 128), bf16), pltpu.VMEM((8, capacity * 8, 128), f32),
-            pltpu.VMEM((8, n_q, 128), f32), pltpu.VMEM((4, capacity, 2, 8, 128), f32),
+            pltpu.VMEM((8, n_held, 128), bf16), pltpu.VMEM((8, n_q, 128), f32), pltpu.VMEM(part_shape, f32),
             pltpu.VMEM((capacity * block_rows, 128), f32), pltpu.VMEM((w_qkv.size // 128, 128), f32),
-            pltpu.VMEM((n_ng, 128), f32), pltpu.VMEM((ndp, capacity * 8, 128), bf16),
+            pltpu.VMEM((n_ng, 128), f32),
             pltpu.VMEM(state_shape, f32), pltpu.VMEM(state_shape, f32), pltpu.VMEM(state_shape, f32),
             pltpu.SemaphoreType.DMA, pltpu.SemaphoreType.DMA,
         ],
         1 << 20, 8 << 20, 24,
     )(
-        meta, counts, held, recv, master, first_moment, second_moment,
+        meta, counts, held, later, master, first_moment, second_moment,
         norm_gains, norm_biases, norm_first, norm_second, *q_bufs,
     )
     return (

time: 212 us -> 201 us (0.948)
  starting transfers between devices: 66.8 us -> 55.1 us
    ppermute x4 -> x2, starting transfers between devices: 11 us -> 5.84 us  [from_mp(): lax.ppermute(x, 'mp', [(i, i + step) for i in range(groups) if 0 <= i + s...]
    ppermute x18, waiting for transfers between devices: 36.7 us -> 41 us  [swap_mp(): return lax.ppermute(x, 'mp', [(i, i ^ mask) for i in range(groups)])]
    ppermute x4 -> x2, waiting for transfers between devices: 4.37 us -> 0.09 us  [from_mp(): lax.ppermute(x, 'mp', [(i, i + step) for i in range(groups) if 0 <= i + s...]
    all_to_all x2 -> x1, starting transfers between devices: 7.89 us -> 3.94 us  [exchange(): return lax.all_to_all(x, axis, 0, 0, tiled=True)]
    ppermute x14, starting transfers between devices: 17.6 us -> 14.1 us  [swap(): lax.ppermute(x, 'dp', [(i, i ^ 1 << order[i & 1][s]) for i in range(ndp)])]
    pallas_call x19 -> x18, Pallas kernels: 71.7 us -> 70.6 us  [fixed(): run(*[pltpu.with_memory_space_constraint(x, pltpu.HBM) if spec is HB else...]
    unnamed x68 -> x80, local copies, waits for them, and re-layouts: 6.46 us -> 6.64 us
  transfers between devices with their start and end apart: 54 -> 51, of which waited for: 23 -> 23; matrix products, arithmetic and copies ran while one was open for 1% -> 2% of each run, Pallas kernels for 31% -> 31%
where the time goes in v5:
time: 201 us; the launch traced here: 200 us
  Pallas kernels  70.6 us (35%)
  waiting for transfers between devices  62.2 us (31%)
  starting transfers between devices  55.1 us (27%)
  local copies, waits for them, and re-layouts  9.26 us (5%)
  between operations  2.18 us (1%)
    pallas_call x18, Pallas kernels, fixed(): run(*[pltpu.with_memory_space_constraint(x, pltpu.HBM) if spec is HB else...  70.6 us
    ppermute x18, waiting for transfers between devices, swap_mp(): return lax.ppermute(x, 'mp', [(i, i ^ mask) for i in range(groups)])  41 us
    ppermute x18, starting transfers between devices, swap_mp(): return lax.ppermute(x, 'mp', [(i, i ^ mask) for i in range(groups)])  27.7 us
    ppermute x14, starting transfers between devices, swap(): lax.ppermute(x, 'dp', [(i, i ^ 1 << order[i & 1][s]) for i in range(ndp)])  14.1 us
    ppermute x14, waiting for transfers between devices, swap(): lax.ppermute(x, 'dp', [(i, i ^ 1 << order[i & 1][s]) for i in range(ndp)])  11.4 us
    ppermute x16, waiting for transfers between devices, swap_core(): return lax.ppermute(x, 'dp', [(i, i ^ 1) for i in range(ndp)])  7.09 us
    unnamed x80, local copies, waits for them, and re-layouts  6.64 us
    ppermute x2, starting transfers between devices, from_mp(): lax.ppermute(x, 'mp', [(i, i + step) for i in range(groups) if 0 <= i + s...  5.84 us
  transfers between devices with their start and end apart: 51, of which 23 were waited for; matrix products, arithmetic and copies ran while one was open for 2% of the time, Pallas kernels for 31%

profile of v5, /device:TPU:0, one launch (start us, length us, event | category | flops | bytes accessed | tf_op | source)
XLA Modules:
  0.0 199.9 jit_solution(9917136709448194095)
XLA Ops:
  1.7 4.1 %collective-permute-start.3 = (bf16[128,384]{1,0:T(8,128)(2,1)S(1)}, bf16[128,384]{1,0:T(8,128)(2,1)S(1)}, u32[]{:S(2)}, u32[]{:S(2)}) collective-permute-start(bf16[128,384]{1,0:T(8,128)(2,1)S(1)} %constant_dynamic-slice_fusion), channel_id=1, source_target_pairs={{0,2},{1,3},{2,0},{3,1},{4,6},{5,7},{6,4},{7,5},{8,10},{9,11},{10,... | collective-permute-start | bytes 294920 | tf_op jit(solution)/shard_map/ppermute | solution.py:819
  9.5 4.5 %collective-permute-start = (bf16[64,512]{1,0:T(8,128)(2,1)S(1)}, bf16[64,512]{1,0:T(8,128)(2,1)S(1)}, u32[]{:S(2)}, u32[]{:S(2)}) collective-permute-start(bf16[64,512]{1,0:T(8,128)(2,1)S(1)} %get-tuple-element.157), channel_id=1, source_target_pairs={{0,1},{1,2},{2,3},{4,5},{5,6},{6,7},{8,9},{9,10},{10,11},{12,13},{... | collective-permute-start | bytes 196616 | tf_op jit(solution)/shard_map/ppermute | solution.py:816
  17.7 3.5 %collective-permute-start.7 = (bf16[144,512]{1,0:T(8,128)(2,1)S(1)}, bf16[144,512]{1,0:T(8,128)(2,1)S(1)}, u32[]{:S(2)}, u32[]{:S(2)}) collective-permute-start(bf16[144,512]{1,0:T(8,128)(2,1)S(1)} %pad_maximum_fusion.2), channel_id=1, source_target_pairs={{0,3},{1,2},{2,1},{3,0},{4,7},{5,6},{6,5},{7,4},{8,11},{9,10},{10,... | collective-permute-start | bytes 442376 | tf_op jit(solution)/shard_map/ppermute | solution.py:819
  22.1 2.6 %shard_map.238 = f32[8,3,192,128]{3,2,1,0:T(8,128)} custom-call(f32[1536,128]{1,0:T(8,128)} %bitcast.39, f32[1536,128]{1,0:T(8,128)} %bitcast.40, f32[1536,128]{1,0:T(8,128)} %bitcast.41), custom_call_target="tpu_custom_call" | custom-call | flops 1048576 | bytes 4194304 | tf_op jit(solution)/shard_map/pallas_call | solution.py:54
  24.7 1.9 shard_map.239.a1e_h
  27.2 5.7 %collective-permute-done.6 = bf16[144,512]{1,0:T(8,128)(2,1)S(1)} collective-permute-done((bf16[144,512]{1,0:T(8,128)(2,1)S(1)}, bf16[144,512]{1,0:T(8,128)(2,1)S(1)}, u32[]{:S(2)}, u32[]{:S(2)}) %collective-permute-start.6) | collective-permute-done | bytes 147488 | tf_op jit(solution)/shard_map/ppermute | solution.py:819
  37.4 5.3 %shard_map.240 = (bf16[4,640,384]{2,1,0:T(8,128)(2,1)}, bf16[4,144,128]{2,1,0:T(8,128)(2,1)S(1)}) custom-call(s32[18]{0:T(128)S(1)} %stack.97.meta, bf16[640,512]{1,0:T(8,128)(2,1)} %shard_map.239.a1e_h, bf16[4,128,384]{2,1,0:T(8,128)(2,1)} %copy-done.12, bf16[4,128,384]{2,1,0:T(8,128)(2,1)} %copy-done.15, bf16[4,128,384]{2,1,0:T(8,128)(2,1)} %copy-done.16, ...), custom_call_target="tpu_custom_call" | custom-call | flops 1006632960 | bytes 6291456 | tf_op jit(solution)/shard_map/pallas_call | solution.py:54
  42.7 2.7 %collective-permute-start.15 = (bf16[4,144,128]{2,1,0:T(8,128)(2,1)S(1)}, bf16[4,144,128]{2,1,0:T(8,128)(2,1)S(1)}, u32[]{:S(2)}, u32[]{:S(2)}) collective-permute-start(bf16[4,144,128]{2,1,0:T(8,128)(2,1)S(1)} %get-tuple-element.90.h0), channel_id=1, source_target_pairs={{0,3},{1,2},{2,1},{3,0},{4,7},{5,6},{6,5},{7,4},{8,11},{9,10},{10,... | collective-permute-start | bytes 442376 | tf_op jit(solution)/shard_map/ppermute | solution.py:819
  47.1 4.2 %collective-permute-done.15.h3 = bf16[4,144,128]{2,1,0:T(8,128)(2,1)S(1)} collective-permute-done((bf16[4,144,128]{2,1,0:T(8,128)(2,1)S(1)}, bf16[4,144,128]{2,1,0:T(8,128)(2,1)S(1)}, u32[]{:S(2)}, u32[]{:S(2)}) %collective-permute-start.15) | collective-permute-done | bytes 147488 | tf_op jit(solution)/shard_map/ppermute | solution.py:819
  51.3 5.4 %collective-permute-done.14.h2 = bf16[4,144,128]{2,1,0:T(8,128)(2,1)S(1)} collective-permute-done((bf16[4,144,128]{2,1,0:T(8,128)(2,1)S(1)}, bf16[4,144,128]{2,1,0:T(8,128)(2,1)S(1)}, u32[]{:S(2)}, u32[]{:S(2)}) %collective-permute-start.14) | collective-permute-done | bytes 147488 | tf_op jit(solution)/shard_map/ppermute | solution.py:819
  58.7 6.3 %shard_map.241.near_h = f32[512,512]{1,0:T(8,128)} custom-call(s32[18]{0:T(128)S(1)} %stack.97.meta, bf16[4,640,384]{2,1,0:T(8,128)(2,1)} %get-tuple-element.91.qkv_h), custom_call_target="tpu_custom_call" | custom-call | flops 536870912 | bytes 12582912 | tf_op jit(solution)/shard_map/pallas_call | solution.py:54
  65.1 2.0 collective-permute-done.16.refs_3_
  67.0 3.9 %all-to-all-start = ((f32[8,3,192,128]{3,2,1,0:T(8,128)}), f32[8,3,192,128]{3,2,1,0:T(8,128)S(1)}, u32[]{:S(2)}, u32[]{:S(2)}) async-start(f32[8,3,192,128]{3,2,1,0:T(8,128)} %shard_map.238), calls=%async_computation | async-start | bytes 4718592 | tf_op jit(solution)/shard_map/all_to_all | solution.py:822
  76.7 20.9 %shard_map.242 = (bf16[512,512]{1,0:T(8,128)(2,1)}, bf16[4,176,128]{2,1,0:T(8,128)(2,1)S(1)}, bf16[4,176,128]{2,1,0:T(8,128)(2,1)S(1)}, f32[512,512]{1,0:T(8,128...) custom-call(s32[18]{0:T(128)S(1)} %stack.97.meta, ...), custom_call_target="tpu_custom_call" | custom-call | flops 6442450944 | bytes 25165824 | tf_op jit(solution)/shard_map/pallas_call | solution.py:54
  97.6 2.6 %all-to-all-done.refs_4_ = f32[8,3,192,128]{3,2,1,0:T(8,128)S(1)} async-done(((f32[8,3,192,128]{3,2,1,0:T(8,128)}), f32[8,3,192,128]{3,2,1,0:T(8,128)S(1)}, u32[]{:S(2)}, u32[]{:S(2)}) %all-to-all-start) | async-done | bytes 2359328 | tf_op jit(solution)/shard_map/all_to_all | solution.py:822
  100.2 1.8 collective-permute-start.23
  102.0 7.4 %collective-permute-done.23.three.s3 = bf16[4,176,128]{2,1,0:T(8,128)(2,1)S(1)} collective-permute-done((bf16[4,176,128]{2,1,0:T(8,128)(2,1)S(1)}, bf16[4,176,128]{2,1,0:T(8,128)(2,1)S(1)}, u32[]{:S(2)}, u32[]{:S(2)}) %collective-permute-start.23) | collective-permute-done | bytes 180256 | tf_op jit(solution)/shard_map/ppermute | solution.py:819
  109.4 3.1 %collective-permute-done.22.one.s1 = bf16[4,176,128]{2,1,0:T(8,128)(2,1)S(1)} collective-permute-done((bf16[4,176,128]{2,1,0:T(8,128)(2,1)S(1)}, bf16[4,176,128]{2,1,0:T(8,128)(2,1)S(1)}, u32[]{:S(2)}, u32[]{:S(2)}) %collective-permute-start.22) | collective-permute-done | bytes 180256 | tf_op jit(solution)/shard_map/ppermute | solution.py:819
  116.2 6.9 %shard_map.244 = (bf16[512,512]{1,0:T(8,128)(2,1)S(1)}, f32[512,512]{1,0:T(8,128)S(1)}, f32[512,512]{1,0:T(8,128)S(1)}) custom-call(s32[18]{0:T(128)S(1)} %stack.97.meta, bf16[4,640,384]{2,1,0:T(8,128)(2,1)} %get-tuple-element.91.qkv_h, bf16[512,512]{1,0:T(8,128)(2,1)} %get-tuple-element.105.dctx_h, bf16[4,176,128]{2,1,0:T(8,128)(2,1)S(1)} %collective-permute-done.22.one.s1, ...), custom_call_target="tpu_custom_call" | custom-call | flops 1073741824 | bytes 25165824 | tf_op jit(solution)/shard_map/pallas_call | solution.py:54
  123.1 2.7 %collective-permute-done.24.s2 = bf16[4,176,128]{2,1,0:T(8,128)(2,1)S(1)} collective-permute-done((bf16[4,176,128]{2,1,0:T(8,128)(2,1)S(1)}, bf16[4,176,128]{2,1,0:T(8,128)(2,1)S(1)}, u32[]{:S(2)}, u32[]{:S(2)}) %collective-permute-start.24) | collective-permute-done | bytes 180256 | tf_op jit(solution)/shard_map/ppermute | solution.py:819
  125.7 5.5 %shard_map.245 = (bf16[4,512,384]{2,1,0:T(8,128)(2,1)}, f32[4,192,512]{2,1,0:T(8,128)S(1)}, f32[4,192,512]{2,1,0:T(8,128)S(1)}) custom-call(s32[18]{0:T(128)S(1)} %stack.97.meta, bf16[4,640,384]{2,1,0:T(8,128)(2,1)} %get-tuple-element.91.qkv_h, bf16[512,512]{1,0:T(8,128)(2,1)S(1)} %get-tuple-element.108.dq, f32[512,512]{1,0:T(8,128)S(1)} %get-tuple-element.109.dkn, ...), custom_call_target="tpu_custom_call" | custom-call | flops 805306368 | bytes 25165824 | tf_op jit(solution)/shard_map/pallas_call | solution.py:54
  135.6 7.1 %shard_map.247 = (f32[512,512]{1,0:T(8,128)}, f32[16,128]{1,0:T(8,128)S(1)}) custom-call(s32[18]{0:T(128)S(1)} %stack.97.meta, bf16[4,512,384]{2,1,0:T(8,128)(2,1)} %get-tuple-element.116.dproj_h, bf16[512,512]{1,0:T(8,128)(2,1)S(1)} %bitcast.38, f32[512,512]{1,0:T(8,128)} %get-tuple-element.117.dx2_h, f32[2,512]{1,0:T(2,128)S(1)} %copy-done.6, ...), custom_call_target="tpu_custom_call" | custom-call | flops 805306368 | bytes 8388608 | tf_op jit(solution)/shard_map/pallas_call | solution.py:54
  142.7 2.5 %collective-permute-done.28.got = bf16[4,192,256]{2,1,0:T(8,128)(2,1)S(1)} collective-permute-done((bf16[4,192,256]{2,1,0:T(8,128)(2,1)S(1)}, bf16[4,192,256]{2,1,0:T(8,128)(2,1)S(1)}, u32[]{:S(2)}, u32[]{:S(2)}) %collective-permute-start.28) | collective-permute-done | bytes 393248 | tf_op jit(solution)/shard_map/ppermute | solution.py:810
  147.6 2.6 %collective-permute-start.31 = (bf16[1,576,128]{2,1,0:T(8,128)(2,1)S(1)}, bf16[1,576,128]{2,1,0:T(8,128)(2,1)S(1)}, u32[]{:S(2)}, u32[]{:S(2)}) collective-permute-start(bf16[1,576,128]{2,1,0:T(8,128)(2,1)S(1)} %get-tuple-element.134), channel_id=1, source_target_pairs={{0,2},{1,3},{2,0},{3,1},{4,6},{5,7},{6,4},{7,5},{8,10},{9,11},{10,... | collective-permute-start | bytes 442376 | tf_op jit(solution)/shard_map/ppermute | solution.py:819
  150.2 1.8 collective-permute-start.32
  152.6 2.0 %collective-permute-done.30.refs_1_ = bf16[1,576,128]{2,1,0:T(8,128)(2,1)S(1)} collective-permute-done((bf16[1,576,128]{2,1,0:T(8,128)(2,1)S(1)}, bf16[1,576,128]{2,1,0:T(8,128)(2,1)S(1)}, u32[]{:S(2)}, u32[]{:S(2)}) %collective-permute-start.30) | collective-permute-done | bytes 147488 | tf_op jit(solution)/shard_map/ppermute | solution.py:819
  154.6 6.7 %collective-permute-done.31.refs_2_ = bf16[1,576,128]{2,1,0:T(8,128)(2,1)S(1)} collective-permute-done((bf16[1,576,128]{2,1,0:T(8,128)(2,1)S(1)}, bf16[1,576,128]{2,1,0:T(8,128)(2,1)S(1)}, u32[]{:S(2)}, u32[]{:S(2)}) %collective-permute-start.31) | collective-permute-done | bytes 147488 | tf_op jit(solution)/shard_map/ppermute | solution.py:819
  164.2 3.7 %collective-permute-start.35 = (bf16[1,224,128]{2,1,0:T(8,128)(2,1)S(1)}, bf16[1,224,128]{2,1,0:T(8,128)(2,1)S(1)}, u32[]{:S(2)}, u32[]{:S(2)}) collective-permute-start(bf16[1,224,128]{2,1,0:T(8,128)(2,1)S(1)} %get-tuple-element.137), channel_id=1, source_target_pairs={{0,1},{1,0},{2,3},{3,2},{4,5},{5,4},{6,7},{7,6},{8,9},{9,8},{10,11... | collective-permute-start | bytes 172040 | tf_op jit(solution)/shard_map/ppermute | solution.py:819
  171.1 3.8 %collective-permute-done.36.refs_2_ = bf16[1,224,128]{2,1,0:T(8,128)(2,1)S(1)} collective-permute-done((bf16[1,224,128]{2,1,0:T(8,128)(2,1)S(1)}, bf16[1,224,128]{2,1,0:T(8,128)(2,1)S(1)}, u32[]{:S(2)}, u32[]{:S(2)}) %collective-permute-start.36) | collective-permute-done | bytes 57376 | tf_op jit(solution)/shard_map/ppermute | solution.py:819
  178.6 6.0 %collective-permute-done.44.refs_2_ = bf16[608,128]{1,0:T(8,128)(2,1)S(1)} collective-permute-done((bf16[608,128]{1,0:T(8,128)(2,1)S(1)}, bf16[608,128]{1,0:T(8,128)(2,1)S(1)}, u32[]{:S(2)}, u32[]{:S(2)}) %collective-permute-start.44) | collective-permute-done | bytes 155680 | tf_op jit(solution)/shard_map/ppermute | solution.py:810
  187.6 4.5 %shard_map.254 = (bf16[128,512]{1,0:T(8,128)(2,1)}, bf16[512,512]{1,0:T(8,128)(2,1)}, bf16[512,512]{1,0:T(8,128)(2,1)}, f32[4,24,2,8,128]{4,3,2,1,0:T(8,128)}) custom-call(s32[18]{0:T(128)S(1)} %stack.97.meta, s32[192]{0:T(256)S(1)} %get-tuple-element.155.blocks, bf16[1152,128]{1,0:T(8,128)(2,1)} %copy-done.4, bf16[1152,128]{1,0:T(8,128)(2,1)} %copy-done.19, ...), custom_call_target="tpu_custom_call" | custom-call | flops 1048576 | bytes 4194304 | tf_op jit(solution)/shard_map/pallas_call | solution.py:54
  194.2 5.4 %shard_map.255 = (f32[24,64,128]{2,1,0:T(8,128)}, f32[24,64,128]{2,1,0:T(8,128)}, f32[24,64,128]{2,1,0:T(8,128)}, bf16[512,384]{1,0:T(8,128)(2,1)}, f32[4,512]{1...) custom-call(s32[18]{0:T(128)S(1)} %stack.97.meta, s32[192]{0:T(256)S(1)} %get-tuple-element.154.counts, ...), custom_call_target="tpu_custom_call" | custom-call | flops 1048576 | bytes 8388608 | tf_op jit(solution)/shard_map/pallas_call | solution.py:54
  (180 shorter events, 48.6 us)
Async XLA Ops:
  1.7 14.1 %collective-permute-start.3 = (bf16[128,384]{1,0:T(8,128)(2,1)S(1)}, bf16[128,384]{1,0:T(8,128)(2,1)S(1)}, u32[]{:S(2)}, u32[]{:S(2)}) collective-permute-start(bf16[128,384]{1,0:T(8,128)(2,1)S(1)} %constant_dynamic-slice_fusion), channel_id=1, source_target_pairs={{0,2},{1,3},{2,0},{3,1},{4,6},{5,7},{6,4},{7,5},{8,10},{9,11},{10,... | collective-permute-start | bytes 294920 | tf_op jit(solution)/shard_map/ppermute | solution.py:819
  5.8 10.0 %collective-permute-start.2 = (bf16[128,384]{1,0:T(8,128)(2,1)S(1)}, bf16[128,384]{1,0:T(8,128)(2,1)S(1)}, u32[]{:S(2)}, u32[]{:S(2)}) collective-permute-start(bf16[128,384]{1,0:T(8,128)(2,1)S(1)} %constant_dynamic-slice_fusion), channel_id=1, source_target_pairs={{0,1},{1,0},{2,3},{3,2},{4,5},{5,4},{6,7},{7,6},{8,9},{9,8},{10,11... | collective-permute-start | bytes 294920 | tf_op jit(solution)/shard_map/ppermute | solution.py:819
  7.3 8.4 %collective-permute-start.4 = (bf16[128,384]{1,0:T(8,128)(2,1)S(1)}, bf16[128,384]{1,0:T(8,128)(2,1)S(1)}, u32[]{:S(2)}, u32[]{:S(2)}) collective-permute-start(bf16[128,384]{1,0:T(8,128)(2,1)S(1)} %constant_dynamic-slice_fusion), channel_id=1, source_target_pairs={{0,3},{1,2},{2,1},{3,0},{4,7},{5,6},{6,5},{7,4},{8,11},{9,10},{10,... | collective-permute-start | bytes 294920 | tf_op jit(solution)/shard_map/ppermute | solution.py:819
  8.2 7.7 %collective-permute-start.1 = (bf16[64,512]{1,0:T(8,128)(2,1)S(1)}, bf16[64,512]{1,0:T(8,128)(2,1)S(1)}, u32[]{:S(2)}, u32[]{:S(2)}) collective-permute-start(bf16[64,512]{1,0:T(8,128)(2,1)S(1)} %get-tuple-element.156), channel_id=1, source_target_pairs={{1,0},{2,1},{3,2},{5,4},{6,5},{7,6},{9,8},{10,9},{11,10},{13,12},{... | collective-permute-start | bytes 196616 | tf_op jit(solution)/shard_map/ppermute | solution.py:816
  16.0 10.8 %collective-permute-start.8 = (bf16[4,128,384]{2,1,0:T(8,128)(2,1)S(1)}, bf16[4,128,384]{2,1,0:T(8,128)(2,1)S(1)}, u32[]{:S(2)}, u32[]{:S(2)}) collective-permute-start(bf16[4,128,384]{2,1,0:T(8,128)(2,1)S(1)} %pad_maximum_fusion.1.refs_0_), channel_id=1, source_target_pairs={{0,8},{4,20},{8,0},{12,28},{16,24},{20,4},{24,16},{28,12},{1,9},{5... | collective-permute-start | bytes 1179656 | tf_op jit(solution)/shard_map/ppermute | solution.py:810
  17.7 9.5 %collective-permute-start.7 = (bf16[144,512]{1,0:T(8,128)(2,1)S(1)}, bf16[144,512]{1,0:T(8,128)(2,1)S(1)}, u32[]{:S(2)}, u32[]{:S(2)}) collective-permute-start(bf16[144,512]{1,0:T(8,128)(2,1)S(1)} %pad_maximum_fusion.2), channel_id=1, source_target_pairs={{0,3},{1,2},{2,1},{3,0},{4,7},{5,6},{6,5},{7,4},{8,11},{9,10},{10,... | collective-permute-start | bytes 442376 | tf_op jit(solution)/shard_map/ppermute | solution.py:819
  21.2 11.8 %collective-permute-start.6 = (bf16[144,512]{1,0:T(8,128)(2,1)S(1)}, bf16[144,512]{1,0:T(8,128)(2,1)S(1)}, u32[]{:S(2)}, u32[]{:S(2)}) collective-permute-start(bf16[144,512]{1,0:T(8,128)(2,1)S(1)} %pad_maximum_fusion.2), channel_id=1, source_target_pairs={{0,2},{1,3},{2,0},{3,1},{4,6},{5,7},{6,4},{7,5},{8,10},{9,11},{10,... | collective-permute-start | bytes 442376 | tf_op jit(solution)/shard_map/ppermute | solution.py:819
  21.5 11.4 %collective-permute-start.5 = (bf16[144,512]{1,0:T(8,128)(2,1)S(1)}, bf16[144,512]{1,0:T(8,128)(2,1)S(1)}, u32[]{:S(2)}, u32[]{:S(2)}) collective-permute-start(bf16[144,512]{1,0:T(8,128)(2,1)S(1)} %pad_maximum_fusion.2), channel_id=1, source_target_pairs={{0,1},{1,0},{2,3},{3,2},{4,5},{5,4},{6,7},{7,6},{8,9},{9,8},{10,11... | collective-permute-start | bytes 442376 | tf_op jit(solution)/shard_map/ppermute | solution.py:819
  26.6 9.2 %collective-permute-start.9 = (bf16[4,128,384]{2,1,0:T(8,128)(2,1)S(1)}, bf16[4,128,384]{2,1,0:T(8,128)(2,1)S(1)}, u32[]{:S(2)}, u32[]{:S(2)}) collective-permute-start(bf16[4,128,384]{2,1,0:T(8,128)(2,1)S(1)} %pad_maximum_fusion.1.refs_0_), channel_id=1, source_target_pairs={{0,4},{4,0},{8,12},{12,8},{16,20},{20,16},{24,28},{28,24},{1,5},{5... | collective-permute-start | bytes 1179656 | tf_op jit(solution)/shard_map/ppermute | solution.py:813
  26.7 9.2 %collective-permute-start.10 = (bf16[4,128,384]{2,1,0:T(8,128)(2,1)S(1)}, bf16[4,128,384]{2,1,0:T(8,128)(2,1)S(1)}, u32[]{:S(2)}, u32[]{:S(2)}) collective-permute-start(bf16[4,128,384]{2,1,0:T(8,128)(2,1)S(1)} %collective-permute-done.8.refs_1_), channel_id=1, source_target_pairs={{0,4},{4,0},{8,12},{12,8},{16,20},{20,16},{24,28},{28,24},{1,5},{5... | collective-permute-start | bytes 1179656 | tf_op jit(solution)/shard_map/ppermute | solution.py:813
  33.1 23.7 %collective-permute-start.12 = (bf16[4,144,512]{2,1,0:T(8,128)(2,1)S(1)}, bf16[4,144,512]{2,1,0:T(8,128)(2,1)S(1)}, u32[]{:S(2)}, u32[]{:S(2)}) collective-permute-start(bf16[4,144,512]{2,1,0:T(8,128)(2,1)S(1)} %pad_maximum_fusion.refs_0_), channel_id=1, source_target_pairs={{0,16},{4,12},{8,24},{12,4},{16,0},{20,28},{24,8},{28,20},{1,17},{... | collective-permute-start | bytes 1769480 | tf_op jit(solution)/shard_map/ppermute | solution.py:810
  33.6 23.1 %collective-permute-start.11 = (bf16[4,144,512]{2,1,0:T(8,128)(2,1)S(1)}, bf16[4,144,512]{2,1,0:T(8,128)(2,1)}, u32[]{:S(2)}, u32[]{:S(2)}) collective-permute-start(bf16[4,144,512]{2,1,0:T(8,128)(2,1)S(1)} %pad_maximum_fusion.refs_0_), channel_id=1, source_target_pairs={{0,8},{4,20},{8,0},{12,28},{16,24},{20,4},{24,16},{28,12},{1,9},{5... | collective-permute-start | bytes 1769480 | tf_op jit(solution)/shard_map/ppermute | solution.py:810
  42.7 8.7 %collective-permute-start.15 = (bf16[4,144,128]{2,1,0:T(8,128)(2,1)S(1)}, bf16[4,144,128]{2,1,0:T(8,128)(2,1)S(1)}, u32[]{:S(2)}, u32[]{:S(2)}) collective-permute-start(bf16[4,144,128]{2,1,0:T(8,128)(2,1)S(1)} %get-tuple-element.90.h0), channel_id=1, source_target_pairs={{0,3},{1,2},{2,1},{3,0},{4,7},{5,6},{6,5},{7,4},{8,11},{9,10},{10,... | collective-permute-start | bytes 442376 | tf_op jit(solution)/shard_map/ppermute | solution.py:819
  45.4 11.3 %collective-permute-start.14 = (bf16[4,144,128]{2,1,0:T(8,128)(2,1)S(1)}, bf16[4,144,128]{2,1,0:T(8,128)(2,1)S(1)}, u32[]{:S(2)}, u32[]{:S(2)}) collective-permute-start(bf16[4,144,128]{2,1,0:T(8,128)(2,1)S(1)} %get-tuple-element.90.h0), channel_id=1, source_target_pairs={{0,2},{1,3},{2,0},{3,1},{4,6},{5,7},{6,4},{7,5},{8,10},{9,11},{10,... | collective-permute-start | bytes 442376 | tf_op jit(solution)/shard_map/ppermute | solution.py:819
  45.4 11.3 %collective-permute-start.13 = (bf16[4,144,128]{2,1,0:T(8,128)(2,1)S(1)}, bf16[4,144,128]{2,1,0:T(8,128)(2,1)S(1)}, u32[]{:S(2)}, u32[]{:S(2)}) collective-permute-start(bf16[4,144,128]{2,1,0:T(8,128)(2,1)S(1)} %get-tuple-element.90.h0), channel_id=1, source_target_pairs={{0,1},{1,0},{2,3},{3,2},{4,5},{5,4},{6,7},{7,6},{8,9},{9,8},{10,11... | collective-permute-start | bytes 442376 | tf_op jit(solution)/shard_map/ppermute | solution.py:819
  56.8 10.3 %collective-permute-start.16 = (bf16[4,144,512]{2,1,0:T(8,128)(2,1)}, bf16[4,144,512]{2,1,0:T(8,128)(2,1)}, u32[]{:S(2)}, u32[]{:S(2)}) collective-permute-start(bf16[4,144,512]{2,1,0:T(8,128)(2,1)} %collective-permute-done.11.refs_1_), channel_id=1, source_target_pairs={{0,16},{4,12},{8,24},{12,4},{16,0},{20,28},{24,8},{28,20},{1,17},{... | collective-permute-start | bytes 1769480 | tf_op jit(solution)/shard_map/ppermute | solution.py:810
  67.0 33.1 %all-to-all-start = ((f32[8,3,192,128]{3,2,1,0:T(8,128)}), f32[8,3,192,128]{3,2,1,0:T(8,128)S(1)}, u32[]{:S(2)}, u32[]{:S(2)}) async-start(f32[8,3,192,128]{3,2,1,0:T(8,128)} %shard_map.238), calls=%async_computation | async-start | bytes 4718592 | tf_op jit(solution)/shard_map/all_to_all | solution.py:822
  100.2 12.3 %collective-permute-start.21 = (bf16[4,576,512]{2,1,0:T(8,128)(2,1)}, bf16[4,576,512]{2,1,0:T(8,128)(2,1)S(1)}, u32[]{:S(2)}, u32[]{:S(2)}) collective-permute-start(bf16[4,576,512]{2,1,0:T(8,128)(2,1)} %get-tuple-element.100), channel_id=1, source_target_pairs={{0,4},{4,0},{8,12},{12,8},{16,20},{20,16},{24,28},{28,24},{1,5},{5... | collective-permute-start | bytes 7077896 | tf_op jit(solution)/shard_map/ppermute | solution.py:813
  100.2 9.2 %collective-permute-start.23 = (bf16[4,176,128]{2,1,0:T(8,128)(2,1)S(1)}, bf16[4,176,128]{2,1,0:T(8,128)(2,1)S(1)}, u32[]{:S(2)}, u32[]{:S(2)}) collective-permute-start(bf16[4,176,128]{2,1,0:T(8,128)(2,1)S(1)} %get-tuple-element.102), channel_id=1, source_target_pairs={{0,3},{1,2},{2,1},{3,0},{4,7},{5,6},{6,5},{7,4},{8,11},{9,10},{10,... | collective-permute-start | bytes 540680 | tf_op jit(solution)/shard_map/ppermute | solution.py:819
  102.0 10.5 %collective-permute-start.22 = (bf16[4,176,128]{2,1,0:T(8,128)(2,1)S(1)}, bf16[4,176,128]{2,1,0:T(8,128)(2,1)S(1)}, u32[]{:S(2)}, u32[]{:S(2)}) collective-permute-start(bf16[4,176,128]{2,1,0:T(8,128)(2,1)S(1)} %get-tuple-element.101.s0), channel_id=1, source_target_pairs={{0,1},{1,0},{2,3},{3,2},{4,5},{5,4},{6,7},{7,6},{8,9},{9,8},{10,11... | collective-permute-start | bytes 540680 | tf_op jit(solution)/shard_map/ppermute | solution.py:819
  114.7 16.5 %collective-permute-start.25 = (bf16[4,576,256]{2,1,0:T(8,128)(2,1)S(1)}, bf16[4,576,256]{2,1,0:T(8,128)(2,1)S(1)}, u32[]{:S(2)}, u32[]{:S(2)}) collective-permute-start(bf16[4,576,256]{2,1,0:T(8,128)(2,1)S(1)} %get-tuple-element.104), channel_id=1, source_target_pairs={{0,8},{4,20},{8,0},{12,28},{16,24},{20,4},{24,16},{28,12},{1,9},{5... | collective-permute-start | bytes 3538952 | tf_op jit(solution)/shard_map/ppermute | solution.py:810
  115.2 10.5 %collective-permute-start.24 = (bf16[4,176,128]{2,1,0:T(8,128)(2,1)S(1)}, bf16[4,176,128]{2,1,0:T(8,128)(2,1)S(1)}, u32[]{:S(2)}, u32[]{:S(2)}) collective-permute-start(bf16[4,176,128]{2,1,0:T(8,128)(2,1)S(1)} %get-tuple-element.101.s0), channel_id=1, source_target_pairs={{0,2},{1,3},{2,0},{3,1},{4,6},{5,7},{6,4},{7,5},{8,10},{9,11},{10,... | collective-permute-start | bytes 540680 | tf_op jit(solution)/shard_map/ppermute | solution.py:819
  131.5 15.3 %collective-permute-start.27 = (bf16[4,576,128]{2,1,0:T(8,128)(2,1)S(1)}, bf16[4,576,128]{2,1,0:T(8,128)(2,1)S(1)}, u32[]{:S(2)}, u32[]{:S(2)}) collective-permute-start(bf16[4,576,128]{2,1,0:T(8,128)(2,1)S(1)} %get-tuple-element.123), channel_id=1, source_target_pairs={{0,16},{4,12},{8,24},{12,4},{16,0},{20,28},{24,8},{28,20},{1,17},{... | collective-permute-start | bytes 1769480 | tf_op jit(solution)/shard_map/ppermute | solution.py:810
  134.9 10.3 %collective-permute-start.28 = (bf16[4,192,256]{2,1,0:T(8,128)(2,1)S(1)}, bf16[4,192,256]{2,1,0:T(8,128)(2,1)S(1)}, u32[]{:S(2)}, u32[]{:S(2)}) collective-permute-start(bf16[4,192,256]{2,1,0:T(8,128)(2,1)S(1)} %get-tuple-element.115), channel_id=1, source_target_pairs={{0,8},{4,20},{8,0},{12,28},{16,24},{20,4},{24,16},{28,12},{1,9},{5... | collective-permute-start | bytes 1179656 | tf_op jit(solution)/shard_map/ppermute | solution.py:810
  147.6 13.7 %collective-permute-start.31 = (bf16[1,576,128]{2,1,0:T(8,128)(2,1)S(1)}, bf16[1,576,128]{2,1,0:T(8,128)(2,1)S(1)}, u32[]{:S(2)}, u32[]{:S(2)}) collective-permute-start(bf16[1,576,128]{2,1,0:T(8,128)(2,1)S(1)} %get-tuple-element.134), channel_id=1, source_target_pairs={{0,2},{1,3},{2,0},{3,1},{4,6},{5,7},{6,4},{7,5},{8,10},{9,11},{10,... | collective-permute-start | bytes 442376 | tf_op jit(solution)/shard_map/ppermute | solution.py:819
  150.2 11.1 %collective-permute-start.32 = (bf16[1,576,128]{2,1,0:T(8,128)(2,1)S(1)}, bf16[1,576,128]{2,1,0:T(8,128)(2,1)S(1)}, u32[]{:S(2)}, u32[]{:S(2)}) collective-permute-start(bf16[1,576,128]{2,1,0:T(8,128)(2,1)S(1)} %get-tuple-element.135), channel_id=1, source_target_pairs={{0,3},{1,2},{2,1},{3,0},{4,7},{5,6},{6,5},{7,4},{8,11},{9,10},{10,... | collective-permute-start | bytes 442376 | tf_op jit(solution)/shard_map/ppermute | solution.py:819
  162.6 8.5 %collective-permute-start.34 = (bf16[1152,128]{1,0:T(8,128)(2,1)S(1)}, bf16[1152,128]{1,0:T(8,128)(2,1)S(1)}, u32[]{:S(2)}, u32[]{:S(2)}) collective-permute-start(bf16[1152,128]{1,0:T(8,128)(2,1)S(1)} %shard_map.252.refs_0_), channel_id=1, source_target_pairs={{0,16},{4,12},{8,24},{12,4},{16,0},{20,28},{24,8},{28,20},{1,17},{... | collective-permute-start | bytes 884744 | tf_op jit(solution)/shard_map/ppermute | solution.py:810
  163.5 7.6 %collective-permute-start.33 = (bf16[1152,128]{1,0:T(8,128)(2,1)S(1)}, bf16[1152,128]{1,0:T(8,128)(2,1)S(1)}, u32[]{:S(2)}, u32[]{:S(2)}) collective-permute-start(bf16[1152,128]{1,0:T(8,128)(2,1)S(1)} %shard_map.252.refs_0_), channel_id=1, source_target_pairs={{0,8},{4,20},{8,0},{12,28},{16,24},{20,4},{24,16},{28,12},{1,9},{5... | collective-permute-start | bytes 884744 | tf_op jit(solution)/shard_map/ppermute | solution.py:810
  175.6 9.0 %collective-permute-start.38 = (bf16[1152,128]{1,0:T(8,128)(2,1)S(1)}, bf16[1152,128]{1,0:T(8,128)(2,1)S(1)}, u32[]{:S(2)}, u32[]{:S(2)}) collective-permute-start(bf16[1152,128]{1,0:T(8,128)(2,1)S(1)} %collective-permute-done.33.refs_1_), channel_id=1, source_target_pairs={{0,16},{4,12},{8,24},{12,4},{16,0},{20,28},{24,8},{28,20},{1,17},{... | collective-permute-start | bytes 884744 | tf_op jit(solution)/shard_map/ppermute | solution.py:810
  176.0 8.6 %collective-permute-start.44 = (bf16[608,128]{1,0:T(8,128)(2,1)S(1)}, bf16[608,128]{1,0:T(8,128)(2,1)S(1)}, u32[]{:S(2)}, u32[]{:S(2)}) collective-permute-start(bf16[608,128]{1,0:T(8,128)(2,1)S(1)} %shard_map.253.refs_0_), channel_id=1, source_target_pairs={{0,16},{4,12},{8,24},{12,4},{16,0},{20,28},{24,8},{28,20},{1,17},{... | collective-permute-start | bytes 466952 | tf_op jit(solution)/shard_map/ppermute | solution.py:810
  177.7 7.4 %collective-permute-start.43 = (bf16[608,128]{1,0:T(8,128)(2,1)S(1)}, bf16[608,128]{1,0:T(8,128)(2,1)S(1)}, u32[]{:S(2)}, u32[]{:S(2)}) collective-permute-start(bf16[608,128]{1,0:T(8,128)(2,1)S(1)} %shard_map.253.refs_0_), channel_id=1, source_target_pairs={{0,8},{4,20},{8,0},{12,28},{16,24},{20,4},{24,16},{28,12},{1,9},{5... | collective-permute-start | bytes 466952 | tf_op jit(solution)/shard_map/ppermute | solution.py:810
  178.1 7.3 %collective-permute-start.41 = (bf16[1152,128]{1,0:T(8,128)(2,1)S(1)}, bf16[1152,128]{1,0:T(8,128)(2,1)S(1)}, u32[]{:S(2)}, u32[]{:S(2)}) collective-permute-start(bf16[1152,128]{1,0:T(8,128)(2,1)S(1)} %collective-permute-done.34.refs_2_), channel_id=1, source_target_pairs={{0,4},{4,0},{8,12},{12,8},{16,20},{20,16},{24,28},{28,24},{1,5},{5... | collective-permute-start | bytes 884744 | tf_op jit(solution)/shard_map/ppermute | solution.py:813
  (59 other events, 422.0 us)

commit v6 on v5

--- a/solution.py
+++ b/solution.py
@@ -341,16 +341,16 @@
     x2[...] = dot(ctx_o[...], wout)
 
     def norm_chunk(i, _):
-        at = pl.ds(pl.multiple_of(i * 64, 64), 64)
+        at = pl.ds(pl.multiple_of(i * 128, 128), 128)
         val = x2[at, :] + tok[at, :].astype(f32)
         x2[at, :] = val
         xh, rstd = normalize(val)
         xhat[at, :] = xh
-        rs[at, :] = jnp.broadcast_to(rstd, (64, 128))
+        rs[at, :] = jnp.broadcast_to(rstd, (128, 128))
         a2_o[at, :] = (xh * gain + bias).astype(bf16)
         return 0
 
-    lax.fori_loop(0, rows // 64, norm_chunk, 0)
+    lax.fori_loop(0, rows // 128, norm_chunk, 0)
     for c in later + last:
         c.wait()
     for g in gs:
@@ -375,7 +375,7 @@
 
     def back_chunk(i, carry):
         dg, db = carry
-        at = pl.ds(pl.multiple_of(i * 64, 64), 64)
+        at = pl.ds(pl.multiple_of(i * 128, 128), 128)
         out_o[at, :] = (x2[at, :] + acc[at, :]).astype(bf16)
         xh = xhat[at, :]
         rstd = rs[at, 0:1]
@@ -391,7 +391,7 @@
         return dg, db
 
     zero = jnp.zeros((1, width), f32)
-    dg, db = lax.fori_loop(0, rows // 64, back_chunk, (zero, zero))
+    dg, db = lax.fori_loop(0, rows // 128, back_chunk, (zero, zero))
     even = jnp.full((EDGE, width), meta[3] & 1, jnp.int32) == 0
     head, tail = do_o[0:EDGE, :].astype(f32), do_o[rows - EDGE :, :].astype(f32)
     near_edge, far_edge = jnp.where(even, tail, head).astype(bf16), jnp.where(even, head, tail).astype(bf16)
@@ -646,12 +646,28 @@
         for j in range(4):
             val = held[t, pl.ds(j, caps * 16, stride=4), :].reshape(caps, 2, 8, 128)
             for c in range(2):
-                parts[t, c, j] = val[:, c].reshape(caps * 8, 128)
-                for d in where[c][j]:
-                    sent.append(pltpu.make_async_copy(parts.at[t, c, j], out_h.at[d, t], out_sem))
-                    sent[-1].start()
+                hi, lo = two(val[:, c].reshape(caps * 8, 128))
+                for k, part in ((0, hi), (1, lo)) if t == 0 else ((t + 1, hi),):
+                    parts[k, c, j] = part
+                    for d in where[c][j]:
+                        sent.append(pltpu.make_async_copy(parts.at[k, c, j], out_h.at[d, k], out_sem))
+                        sent[-1].start()
     for c in sent:
         c.wait()
+
+
+def widen_body(recv_h, st_o, recv, sem):
+    copies = load([(recv_h.at[d], recv.at[d]) for d in range(recv.shape[0])], sem)
+    for c in copies:
+        c.wait()
+
+    def owner(d, _):
+        st_o[d, 0] = recv[d, 0].astype(f32) + recv[d, 1].astype(f32)
+        st_o[d, 1] = recv[d, 2].astype(f32)
+        st_o[d, 2] = recv[d, 3].astype(f32)
+        return 0
+
+    lax.fori_loop(0, recv.shape[0], owner, 0)
 
 
 def adam(g, m_old, f_old, s_old):
@@ -864,9 +880,9 @@
         where[d & 1][2 * ((d >> b[0]) & 1) + ((d >> b[1]) & 1)].append(d)
     flat_state = [x.reshape(capacity * block_rows, 128) for x in (master, first_moment, second_moment)]
     [parts] = call(
-        functools.partial(slices_body, where), [((ndp, 3, capacity * 8, 128), f32)], [HB] * 3,
+        functools.partial(slices_body, where), [((ndp, 4, capacity * 8, 128), bf16)], [HB] * 3,
         [
-            pltpu.VMEM((3, capacity * block_rows, 128), f32), pltpu.VMEM((3, 2, 4, capacity * 8, 128), f32),
+            pltpu.VMEM((3, capacity * block_rows, 128), f32), pltpu.VMEM((4, 2, 4, capacity * 8, 128), bf16),
             pltpu.SemaphoreType.DMA((3,)), pltpu.SemaphoreType.DMA,
         ],
         1 << 20, 4 << 20, 12, (HB,),
@@ -889,6 +905,7 @@
     states = all_states(state)
     ffn_z = after(ffn_z, a1e, qkv_bufs[1])
     ffn_x, ffn_y = swap(ffn_z, 0), swap(ffn_z, 1)
+    ffn_oth = [swap_core(b) for b in (ffn_z, ffn_x, ffn_y)]
     ffn_bufs = [ffn_z, ffn_x, ffn_y, swap(after(ffn_x, ffn_y, *states), 1)]
     blocks = owners.shape[0]
     earlier = jnp.arange(blocks)[None, :] < jnp.arange(blocks)[:, None]
@@ -901,8 +918,8 @@
     [near] = call(
         near_body, [((rows, width), f32)], [SM, HB],
         [all_qkv, pltpu.VMEM((rows, width), f32), pltpu.SemaphoreType.DMA], mm * 1024, 12 << 20, 16, (HB,),
-    )(meta, after(qkv, slot, held, counts, ffn_bufs[1], ffn_bufs[2], *states))
-    ffn_bufs = both_cores(ffn_bufs)
+    )(meta, after(qkv, slot, held, counts, *ffn_oth, *states))
+    ffn_bufs = ffn_bufs + ffn_oth + [swap_core(ffn_bufs[3])]
     held_state = exchange(after(parts, ffn_bufs[3], near), "dp")
 
     hid_w = w_in.shape[1]
@@ -935,6 +952,11 @@
     dstate, dfar, give_m, _ = lax.optimization_barrier((dstate, dfar, give_m, held_state))
     dstates = [dstate, swap_mp(dstate, 1), swap_mp(dstate, 2), swap_mp(dfar, 3)]
 
+    [slot_state] = call(
+        widen_body, [((ndp, 3, capacity * 8, 128), f32)], [HB],
+        [pltpu.VMEM((ndp, 4, capacity * 8, 128), bf16), pltpu.SemaphoreType.DMA], 1 << 20, 4 << 20, 12,
+    )(held_state)
+
     bits = [bit_of(me, core, s).astype(jnp.int32).reshape(1) for s in range(2)]
 
     def halve(own, got, s):
@@ -966,7 +988,7 @@
             total_q_body, [(shape, bf16)] * groups, [SM, VM, VM, VM], [], 1 << 20, 2 << 20, 12,
         )(meta, keep, got, extra)
 
-    give_m, keep_m = halve(grad_m, after(swap_core(give_m), dstates[1], dstates[3]), 0)
+    give_m, keep_m = halve(grad_m, after(swap_core(give_m), dstates[1], dstates[3], slot_state), 0)
     got_m = swap(give_m, 0)
     dq, dkn, dvn = call(
         near_back_body,
@@ -1017,7 +1039,7 @@
             functools.partial(pieces_body, first, len(z)),
             [((2 * n + extra, 128), bf16)],
             [SM, SM] + [VM] * (len(z) + 1), [pltpu.VMEM((n, 128), f32)], 1 << 20, 4 << 20, 20,
-        )(owners, slot, *z, held_state)[0]
+        )(owners, slot, *z, slot_state)[0]
 
     def everywhere(piece, *first):
         x, y = swap(piece, 0), swap(piece, 1)

time: 201 us -> 193 us (0.960)
  waiting for transfers between devices: 62.2 us -> 50 us
  starting transfers between devices: 55.1 us -> 60.4 us
    ppermute x18, waiting for transfers between devices: 41 us -> 34.2 us  [swap_mp(): return lax.ppermute(x, 'mp', [(i, i ^ mask) for i in range(groups)])]
    ppermute x14, starting transfers between devices: 14.1 us -> 18.7 us  [swap(): lax.ppermute(x, 'dp', [(i, i ^ 1 << order[i & 1][s]) for i in range(ndp)])]
    ppermute x18, starting transfers between devices: 27.7 us -> 30.4 us  [swap_mp(): return lax.ppermute(x, 'mp', [(i, i ^ mask) for i in range(groups)])]
    all_to_all x1, waiting for transfers between devices: 2.59 us -> 0.01 us  [exchange(): return lax.all_to_all(x, axis, 0, 0, tiled=True)]
    ppermute x14, waiting for transfers between devices: 11.4 us -> 9.11 us  [swap(): lax.ppermute(x, 'dp', [(i, i ^ 1 << order[i & 1][s]) for i in range(ndp)])]
    ppermute x16, waiting for transfers between devices: 7.09 us -> 4.92 us  [swap_core(): return lax.ppermute(x, 'dp', [(i, i ^ 1) for i in range(ndp)])]
    unnamed x80 -> x78, local copies, waits for them, and re-layouts: 6.64 us -> 5.34 us
    pallas_call x18 -> x19, Pallas kernels: 70.6 us -> 71.1 us  [fixed(): run(*[pltpu.with_memory_space_constraint(x, pltpu.HBM) if spec is HB else...]
  transfers between devices with their start and end apart: 51 -> 51, of which waited for: 23 -> 20; matrix products, arithmetic and copies ran while one was open for 2% -> 2% of each run, Pallas kernels for 31% -> 33%
where the time goes in v6:
time: 193 us; the launch traced here: 192 us
  Pallas kernels  71.1 us (37%)
  starting transfers between devices  60.4 us (31%)
  waiting for transfers between devices  50 us (26%)
  local copies, waits for them, and re-layouts  7.95 us (4%)
  between operations  2.2 us (1%)
    pallas_call x19, Pallas kernels, fixed(): run(*[pltpu.with_memory_space_constraint(x, pltpu.HBM) if spec is HB else...  71.1 us
    ppermute x18, waiting for transfers between devices, swap_mp(): return lax.ppermute(x, 'mp', [(i, i ^ mask) for i in range(groups)])  34.2 us
    ppermute x18, starting transfers between devices, swap_mp(): return lax.ppermute(x, 'mp', [(i, i ^ mask) for i in range(groups)])  30.4 us
    ppermute x14, starting transfers between devices, swap(): lax.ppermute(x, 'dp', [(i, i ^ 1 << order[i & 1][s]) for i in range(ndp)])  18.7 us
    ppermute x14, waiting for transfers between devices, swap(): lax.ppermute(x, 'dp', [(i, i ^ 1 << order[i & 1][s]) for i in range(ndp)])  9.11 us
    unnamed x78, local copies, waits for them, and re-layouts  5.34 us
    ppermute x16, waiting for transfers between devices, swap_core(): return lax.ppermute(x, 'dp', [(i, i ^ 1) for i in range(ndp)])  4.92 us
    ppermute x2, starting transfers between devices, from_mp(): lax.ppermute(x, 'mp', [(i, i + step) for i in range(groups) if 0 <= i + s...  4.1 us
  transfers between devices with their start and end apart: 51, of which 20 were waited for; matrix products, arithmetic and copies ran while one was open for 2% of the time, Pallas kernels for 33%

profile of v6, /device:TPU:0, one launch (start us, length us, event | category | flops | bytes accessed | tf_op | source)
XLA Modules:
  0.0 192.1 jit_solution(5418470824635708527)
XLA Ops:
  1.7 3.1 %collective-permute-start.2 = (bf16[128,384]{1,0:T(8,128)(2,1)S(1)}, bf16[128,384]{1,0:T(8,128)(2,1)S(1)}, u32[]{:S(2)}, u32[]{:S(2)}) collective-permute-start(bf16[128,384]{1,0:T(8,128)(2,1)S(1)} %constant_dynamic-slice_fusion), channel_id=1, source_target_pairs={{0,1},{1,0},{2,3},{3,2},{4,5},{5,4},{6,7},{7,6},{8,9},{9,8},{10,11... | collective-permute-start | bytes 294920 | tf_op jit(solution)/shard_map/ppermute | solution.py:835
  4.7 2.6 %collective-permute-start.3 = (bf16[128,384]{1,0:T(8,128)(2,1)S(1)}, bf16[128,384]{1,0:T(8,128)(2,1)S(1)}, u32[]{:S(2)}, u32[]{:S(2)}) collective-permute-start(bf16[128,384]{1,0:T(8,128)(2,1)S(1)} %constant_dynamic-slice_fusion), channel_id=1, source_target_pairs={{0,2},{1,3},{2,0},{3,1},{4,6},{5,7},{6,4},{7,5},{8,10},{9,11},{10,... | collective-permute-start | bytes 294920 | tf_op jit(solution)/shard_map/ppermute | solution.py:835
  8.2 2.8 %collective-permute-start = (bf16[64,512]{1,0:T(8,128)(2,1)S(1)}, bf16[64,512]{1,0:T(8,128)(2,1)S(1)}, u32[]{:S(2)}, u32[]{:S(2)}) collective-permute-start(bf16[64,512]{1,0:T(8,128)(2,1)S(1)} %get-tuple-element.157), channel_id=1, source_target_pairs={{0,1},{1,2},{2,3},{4,5},{5,6},{6,7},{8,9},{9,10},{10,11},{12,13},{... | collective-permute-start | bytes 196616 | tf_op jit(solution)/shard_map/ppermute | solution.py:832
  15.4 1.8 collective-permute-done.1.right
  18.7 2.0 %collective-permute-start.5 = (bf16[144,512]{1,0:T(8,128)(2,1)S(1)}, bf16[144,512]{1,0:T(8,128)(2,1)S(1)}, u32[]{:S(2)}, u32[]{:S(2)}) collective-permute-start(bf16[144,512]{1,0:T(8,128)(2,1)S(1)} %pad_maximum_fusion.2), channel_id=1, source_target_pairs={{0,1},{1,0},{2,3},{3,2},{4,5},{5,4},{6,7},{7,6},{8,9},{9,8},{10,11... | collective-permute-start | bytes 442376 | tf_op jit(solution)/shard_map/ppermute | solution.py:835
  23.6 2.5 %shard_map.238 = bf16[8,4,192,128]{3,2,1,0:T(8,128)(2,1)} custom-call(f32[1536,128]{1,0:T(8,128)} %bitcast.39, f32[1536,128]{1,0:T(8,128)} %bitcast.40, f32[1536,128]{1,0:T(8,128)} %bitcast.41), custom_call_target="tpu_custom_call" | custom-call | flops 1048576 | bytes 4194304 | tf_op jit(solution)/shard_map/pallas_call | solution.py:54
  26.2 1.9 shard_map.239.a1e_h
  28.7 4.1 %collective-permute-done.6 = bf16[144,512]{1,0:T(8,128)(2,1)S(1)} collective-permute-done((bf16[144,512]{1,0:T(8,128)(2,1)S(1)}, bf16[144,512]{1,0:T(8,128)(2,1)S(1)}, u32[]{:S(2)}, u32[]{:S(2)}) %collective-permute-start.6) | collective-permute-done | bytes 147488 | tf_op jit(solution)/shard_map/ppermute | solution.py:835
  37.3 5.2 %shard_map.240 = (bf16[4,640,384]{2,1,0:T(8,128)(2,1)}, bf16[4,144,128]{2,1,0:T(8,128)(2,1)S(1)}) custom-call(s32[18]{0:T(128)S(1)} %stack.97.meta, bf16[640,512]{1,0:T(8,128)(2,1)} %shard_map.239.a1e_h, bf16[4,128,384]{2,1,0:T(8,128)(2,1)} %copy-done.13, bf16[4,128,384]{2,1,0:T(8,128)(2,1)} %copy-done.15, bf16[4,128,384]{2,1,0:T(8,128)(2,1)} %copy-done.16, ...), custom_call_target="tpu_custom_call" | custom-call | flops 1006632960 | bytes 6291456 | tf_op jit(solution)/shard_map/pallas_call | solution.py:54
  42.5 2.2 %collective-permute-start.16 = (bf16[4,144,128]{2,1,0:T(8,128)(2,1)S(1)}, bf16[4,144,128]{2,1,0:T(8,128)(2,1)S(1)}, u32[]{:S(2)}, u32[]{:S(2)}) collective-permute-start(bf16[4,144,128]{2,1,0:T(8,128)(2,1)S(1)} %get-tuple-element.90.h0), channel_id=1, source_target_pairs={{0,1},{1,0},{2,3},{3,2},{4,5},{5,4},{6,7},{7,6},{8,9},{9,8},{10,11... | collective-permute-start | bytes 442376 | tf_op jit(solution)/shard_map/ppermute | solution.py:835
  49.6 7.9 %collective-permute-done.17.h2 = bf16[4,144,128]{2,1,0:T(8,128)(2,1)S(1)} collective-permute-done((bf16[4,144,128]{2,1,0:T(8,128)(2,1)S(1)}, bf16[4,144,128]{2,1,0:T(8,128)(2,1)S(1)}, u32[]{:S(2)}, u32[]{:S(2)}) %collective-permute-start.17) | collective-permute-done | bytes 147488 | tf_op jit(solution)/shard_map/ppermute | solution.py:835
  59.4 6.3 %shard_map.241.near_h = f32[512,512]{1,0:T(8,128)} custom-call(s32[18]{0:T(128)S(1)} %stack.97.meta, bf16[4,640,384]{2,1,0:T(8,128)(2,1)} %get-tuple-element.91.qkv_h), custom_call_target="tpu_custom_call" | custom-call | flops 536870912 | bytes 12582912 | tf_op jit(solution)/shard_map/pallas_call | solution.py:54
  67.5 3.8 %all-to-all-start = ((bf16[8,4,192,128]{3,2,1,0:T(8,128)(2,1)}), bf16[8,4,192,128]{3,2,1,0:T(8,128)(2,1)S(1)}, u32[]{:S(2)}, u32[]{:S(2)}) async-start(bf16[8,4,192,128]{3,2,1,0:T(8,128)(2,1)} %shard_map.238), calls=%async_computation | async-start | bytes 3145728 | tf_op jit(solution)/shard_map/all_to_all | solution.py:838
  71.5 2.1 %collective-permute-done.20.refs_7_ = bf16[4,144,512]{2,1,0:T(8,128)(2,1)S(1)} collective-permute-done((bf16[4,144,512]{2,1,0:T(8,128)(2,1)}, bf16[4,144,512]{2,1,0:T(8,128)(2,1)S(1)}, u32[]{:S(2)}, u32[]{:S(2)}) %collective-permute-start.20) | collective-permute-done | bytes 589856 | tf_op jit(solution)/shard_map/ppermute | solution.py:829
  74.4 19.8 %shard_map.242 = (bf16[512,512]{1,0:T(8,128)(2,1)}, bf16[4,176,128]{2,1,0:T(8,128)(2,1)S(1)}, bf16[4,176,128]{2,1,0:T(8,128)(2,1)S(1)}, f32[512,512]{1,0:T(8,128...) custom-call(s32[18]{0:T(128)S(1)} %stack.97.meta, ...), custom_call_target="tpu_custom_call" | custom-call | flops 6442450944 | bytes 25165824 | tf_op jit(solution)/shard_map/pallas_call | solution.py:54
  94.5 2.1 %collective-permute-start.22 = (bf16[4,176,128]{2,1,0:T(8,128)(2,1)S(1)}, bf16[4,176,128]{2,1,0:T(8,128)(2,1)S(1)}, u32[]{:S(2)}, u32[]{:S(2)}) collective-permute-start(bf16[4,176,128]{2,1,0:T(8,128)(2,1)S(1)} %get-tuple-element.101.s0), channel_id=1, source_target_pairs={{0,1},{1,0},{2,3},{3,2},{4,5},{5,4},{6,7},{7,6},{8,9},{9,8},{10,11... | collective-permute-start | bytes 540680 | tf_op jit(solution)/shard_map/ppermute | solution.py:835
  96.6 2.6 %collective-permute-start.23 = (bf16[4,176,128]{2,1,0:T(8,128)(2,1)S(1)}, bf16[4,176,128]{2,1,0:T(8,128)(2,1)S(1)}, u32[]{:S(2)}, u32[]{:S(2)}) collective-permute-start(bf16[4,176,128]{2,1,0:T(8,128)(2,1)S(1)} %get-tuple-element.102), channel_id=1, source_target_pairs={{0,3},{1,2},{2,1},{3,0},{4,7},{5,6},{6,5},{7,4},{8,11},{9,10},{10,... | collective-permute-start | bytes 540680 | tf_op jit(solution)/shard_map/ppermute | solution.py:835
  99.1 1.9 shard_map.243.refs_4_
  101.6 6.1 %collective-permute-done.23.three.s3 = bf16[4,176,128]{2,1,0:T(8,128)(2,1)S(1)} collective-permute-done((bf16[4,176,128]{2,1,0:T(8,128)(2,1)S(1)}, bf16[4,176,128]{2,1,0:T(8,128)(2,1)S(1)}, u32[]{:S(2)}, u32[]{:S(2)}) %collective-permute-start.23) | collective-permute-done | bytes 180256 | tf_op jit(solution)/shard_map/ppermute | solution.py:835
  110.6 6.9 %shard_map.245 = (bf16[512,512]{1,0:T(8,128)(2,1)S(1)}, f32[512,512]{1,0:T(8,128)S(1)}, f32[512,512]{1,0:T(8,128)S(1)}) custom-call(s32[18]{0:T(128)S(1)} %stack.97.meta, bf16[4,640,384]{2,1,0:T(8,128)(2,1)} %get-tuple-element.91.qkv_h, bf16[512,512]{1,0:T(8,128)(2,1)} %get-tuple-element.105.dctx_h, bf16[4,176,128]{2,1,0:T(8,128)(2,1)S(1)} %collective-permute-done.22.one.s1, ...), custom_call_target="tpu_custom_call" | custom-call | flops 1073741824 | bytes 25165824 | tf_op jit(solution)/shard_map/pallas_call | solution.py:54
  119.0 5.6 %shard_map.246 = (bf16[4,512,384]{2,1,0:T(8,128)(2,1)}, f32[4,192,512]{2,1,0:T(8,128)S(1)}, f32[4,192,512]{2,1,0:T(8,128)S(1)}) custom-call(s32[18]{0:T(128)S(1)} %stack.97.meta, bf16[4,640,384]{2,1,0:T(8,128)(2,1)} %get-tuple-element.91.qkv_h, bf16[512,512]{1,0:T(8,128)(2,1)S(1)} %get-tuple-element.108.dq, f32[512,512]{1,0:T(8,128)S(1)} %get-tuple-element.109.dkn, ...), custom_call_target="tpu_custom_call" | custom-call | flops 805306368 | bytes 25165824 | tf_op jit(solution)/shard_map/pallas_call | solution.py:54
  129.9 7.1 %shard_map.248 = (f32[512,512]{1,0:T(8,128)}, f32[16,128]{1,0:T(8,128)S(1)}) custom-call(s32[18]{0:T(128)S(1)} %stack.97.meta, bf16[4,512,384]{2,1,0:T(8,128)(2,1)} %get-tuple-element.116.dproj_h, bf16[512,512]{1,0:T(8,128)(2,1)S(1)} %bitcast.38, f32[512,512]{1,0:T(8,128)} %get-tuple-element.117.dx2_h, f32[2,512]{1,0:T(2,128)S(1)} %copy-done.6, ...), custom_call_target="tpu_custom_call" | custom-call | flops 805306368 | bytes 8388608 | tf_op jit(solution)/shard_map/pallas_call | solution.py:54
  141.1 2.0 %collective-permute-start.31 = (bf16[1,576,128]{2,1,0:T(8,128)(2,1)S(1)}, bf16[1,576,128]{2,1,0:T(8,128)(2,1)S(1)}, u32[]{:S(2)}, u32[]{:S(2)}) collective-permute-start(bf16[1,576,128]{2,1,0:T(8,128)(2,1)S(1)} %get-tuple-element.134), channel_id=1, source_target_pairs={{0,2},{1,3},{2,0},{3,1},{4,6},{5,7},{6,4},{7,5},{8,10},{9,11},{10,... | collective-permute-start | bytes 442376 | tf_op jit(solution)/shard_map/ppermute | solution.py:835
  143.0 2.4 %collective-permute-start.32 = (bf16[1,576,128]{2,1,0:T(8,128)(2,1)S(1)}, bf16[1,576,128]{2,1,0:T(8,128)(2,1)S(1)}, u32[]{:S(2)}, u32[]{:S(2)}) collective-permute-start(bf16[1,576,128]{2,1,0:T(8,128)(2,1)S(1)} %get-tuple-element.135), channel_id=1, source_target_pairs={{0,3},{1,2},{2,1},{3,0},{4,7},{5,6},{6,5},{7,4},{8,11},{9,10},{10,... | collective-permute-start | bytes 442376 | tf_op jit(solution)/shard_map/ppermute | solution.py:835
  146.0 3.4 %collective-permute-done.30.refs_1_ = bf16[1,576,128]{2,1,0:T(8,128)(2,1)S(1)} collective-permute-done((bf16[1,576,128]{2,1,0:T(8,128)(2,1)S(1)}, bf16[1,576,128]{2,1,0:T(8,128)(2,1)S(1)}, u32[]{:S(2)}, u32[]{:S(2)}) %collective-permute-start.30) | collective-permute-done | bytes 147488 | tf_op jit(solution)/shard_map/ppermute | solution.py:835
  149.4 5.7 %collective-permute-done.31.refs_2_ = bf16[1,576,128]{2,1,0:T(8,128)(2,1)S(1)} collective-permute-done((bf16[1,576,128]{2,1,0:T(8,128)(2,1)S(1)}, bf16[1,576,128]{2,1,0:T(8,128)(2,1)S(1)}, u32[]{:S(2)}, u32[]{:S(2)}) %collective-permute-start.31) | collective-permute-done | bytes 147488 | tf_op jit(solution)/shard_map/ppermute | solution.py:835
  158.3 2.8 %collective-permute-start.35 = (bf16[1,224,128]{2,1,0:T(8,128)(2,1)S(1)}, bf16[1,224,128]{2,1,0:T(8,128)(2,1)S(1)}, u32[]{:S(2)}, u32[]{:S(2)}) collective-permute-start(bf16[1,224,128]{2,1,0:T(8,128)(2,1)S(1)} %get-tuple-element.137), channel_id=1, source_target_pairs={{0,1},{1,0},{2,3},{3,2},{4,5},{5,4},{6,7},{7,6},{8,9},{9,8},{10,11... | collective-permute-start | bytes 172040 | tf_op jit(solution)/shard_map/ppermute | solution.py:835
  161.5 1.9 %collective-permute-start.37 = (bf16[1,224,128]{2,1,0:T(8,128)(2,1)S(1)}, bf16[1,224,128]{2,1,0:T(8,128)(2,1)S(1)}, u32[]{:S(2)}, u32[]{:S(2)}) collective-permute-start(bf16[1,224,128]{2,1,0:T(8,128)(2,1)S(1)} %get-tuple-element.139), channel_id=1, source_target_pairs={{0,3},{1,2},{2,1},{3,0},{4,7},{5,6},{6,5},{7,4},{8,11},{9,10},{10,... | collective-permute-start | bytes 172040 | tf_op jit(solution)/shard_map/ppermute | solution.py:835
  163.4 2.1 %collective-permute-done.33.refs_1_ = bf16[1152,128]{1,0:T(8,128)(2,1)S(1)} collective-permute-done((bf16[1152,128]{1,0:T(8,128)(2,1)S(1)}, bf16[1152,128]{1,0:T(8,128)(2,1)S(1)}, u32[]{:S(2)}, u32[]{:S(2)}) %collective-permute-start.33) | collective-permute-done | bytes 294944 | tf_op jit(solution)/shard_map/ppermute | solution.py:826
  172.6 2.7 %collective-permute-done.43.refs_1_ = bf16[608,128]{1,0:T(8,128)(2,1)S(1)} collective-permute-done((bf16[608,128]{1,0:T(8,128)(2,1)S(1)}, bf16[608,128]{1,0:T(8,128)(2,1)S(1)}, u32[]{:S(2)}, u32[]{:S(2)}) %collective-permute-start.43) | collective-permute-done | bytes 155680 | tf_op jit(solution)/shard_map/ppermute | solution.py:826
  179.9 4.4 %shard_map.255 = (bf16[128,512]{1,0:T(8,128)(2,1)}, bf16[512,512]{1,0:T(8,128)(2,1)}, bf16[512,512]{1,0:T(8,128)(2,1)}, f32[4,24,2,8,128]{4,3,2,1,0:T(8,128)}) custom-call(s32[18]{0:T(128)S(1)} %stack.97.meta, s32[192]{0:T(256)S(1)} %get-tuple-element.155.blocks, bf16[1152,128]{1,0:T(8,128)(2,1)} %copy-done.4, bf16[1152,128]{1,0:T(8,128)(2,1)} %copy-done.18, ...), custom_call_target="tpu_custom_call" | custom-call | flops 1048576 | bytes 4194304 | tf_op jit(solution)/shard_map/pallas_call | solution.py:54
  186.5 5.4 %shard_map.256 = (f32[24,64,128]{2,1,0:T(8,128)}, f32[24,64,128]{2,1,0:T(8,128)}, f32[24,64,128]{2,1,0:T(8,128)}, bf16[512,384]{1,0:T(8,128)(2,1)}, f32[4,512]{1...) custom-call(s32[18]{0:T(128)S(1)} %stack.97.meta, s32[192]{0:T(256)S(1)} %get-tuple-element.154.counts, ...), custom_call_target="tpu_custom_call" | custom-call | flops 1048576 | bytes 8388608 | tf_op jit(solution)/shard_map/pallas_call | solution.py:54
  (179 shorter events, 56.9 us)
Async XLA Ops:
  1.7 12.4 %collective-permute-start.2 = (bf16[128,384]{1,0:T(8,128)(2,1)S(1)}, bf16[128,384]{1,0:T(8,128)(2,1)S(1)}, u32[]{:S(2)}, u32[]{:S(2)}) collective-permute-start(bf16[128,384]{1,0:T(8,128)(2,1)S(1)} %constant_dynamic-slice_fusion), channel_id=1, source_target_pairs={{0,1},{1,0},{2,3},{3,2},{4,5},{5,4},{6,7},{7,6},{8,9},{9,8},{10,11... | collective-permute-start | bytes 294920 | tf_op jit(solution)/shard_map/ppermute | solution.py:835
  4.7 10.5 %collective-permute-start.3 = (bf16[128,384]{1,0:T(8,128)(2,1)S(1)}, bf16[128,384]{1,0:T(8,128)(2,1)S(1)}, u32[]{:S(2)}, u32[]{:S(2)}) collective-permute-start(bf16[128,384]{1,0:T(8,128)(2,1)S(1)} %constant_dynamic-slice_fusion), channel_id=1, source_target_pairs={{0,2},{1,3},{2,0},{3,1},{4,6},{5,7},{6,4},{7,5},{8,10},{9,11},{10,... | collective-permute-start | bytes 294920 | tf_op jit(solution)/shard_map/ppermute | solution.py:835
  7.3 7.9 %collective-permute-start.4 = (bf16[128,384]{1,0:T(8,128)(2,1)S(1)}, bf16[128,384]{1,0:T(8,128)(2,1)S(1)}, u32[]{:S(2)}, u32[]{:S(2)}) collective-permute-start(bf16[128,384]{1,0:T(8,128)(2,1)S(1)} %constant_dynamic-slice_fusion), channel_id=1, source_target_pairs={{0,3},{1,2},{2,1},{3,0},{4,7},{5,6},{6,5},{7,4},{8,11},{9,10},{10,... | collective-permute-start | bytes 294920 | tf_op jit(solution)/shard_map/ppermute | solution.py:835
  8.2 7.1 %collective-permute-start = (bf16[64,512]{1,0:T(8,128)(2,1)S(1)}, bf16[64,512]{1,0:T(8,128)(2,1)S(1)}, u32[]{:S(2)}, u32[]{:S(2)}) collective-permute-start(bf16[64,512]{1,0:T(8,128)(2,1)S(1)} %get-tuple-element.157), channel_id=1, source_target_pairs={{0,1},{1,2},{2,3},{4,5},{5,6},{6,7},{8,9},{9,10},{10,11},{12,13},{... | collective-permute-start | bytes 196616 | tf_op jit(solution)/shard_map/ppermute | solution.py:832
  17.2 11.0 %collective-permute-start.8 = (bf16[4,128,384]{2,1,0:T(8,128)(2,1)S(1)}, bf16[4,128,384]{2,1,0:T(8,128)(2,1)S(1)}, u32[]{:S(2)}, u32[]{:S(2)}) collective-permute-start(bf16[4,128,384]{2,1,0:T(8,128)(2,1)S(1)} %pad_maximum_fusion.1.refs_0_), channel_id=1, source_target_pairs={{0,8},{4,20},{8,0},{12,28},{16,24},{20,4},{24,16},{28,12},{1,9},{5... | collective-permute-start | bytes 1179656 | tf_op jit(solution)/shard_map/ppermute | solution.py:826
  18.7 10.0 %collective-permute-start.5 = (bf16[144,512]{1,0:T(8,128)(2,1)S(1)}, bf16[144,512]{1,0:T(8,128)(2,1)S(1)}, u32[]{:S(2)}, u32[]{:S(2)}) collective-permute-start(bf16[144,512]{1,0:T(8,128)(2,1)S(1)} %pad_maximum_fusion.2), channel_id=1, source_target_pairs={{0,1},{1,0},{2,3},{3,2},{4,5},{5,4},{6,7},{7,6},{8,9},{9,8},{10,11... | collective-permute-start | bytes 442376 | tf_op jit(solution)/shard_map/ppermute | solution.py:835
  20.7 12.1 %collective-permute-start.6 = (bf16[144,512]{1,0:T(8,128)(2,1)S(1)}, bf16[144,512]{1,0:T(8,128)(2,1)S(1)}, u32[]{:S(2)}, u32[]{:S(2)}) collective-permute-start(bf16[144,512]{1,0:T(8,128)(2,1)S(1)} %pad_maximum_fusion.2), channel_id=1, source_target_pairs={{0,2},{1,3},{2,0},{3,1},{4,6},{5,7},{6,4},{7,5},{8,10},{9,11},{10,... | collective-permute-start | bytes 442376 | tf_op jit(solution)/shard_map/ppermute | solution.py:835
  22.2 10.6 %collective-permute-start.7 = (bf16[144,512]{1,0:T(8,128)(2,1)S(1)}, bf16[144,512]{1,0:T(8,128)(2,1)S(1)}, u32[]{:S(2)}, u32[]{:S(2)}) collective-permute-start(bf16[144,512]{1,0:T(8,128)(2,1)S(1)} %pad_maximum_fusion.2), channel_id=1, source_target_pairs={{0,3},{1,2},{2,1},{3,0},{4,7},{5,6},{6,5},{7,4},{8,11},{9,10},{10,... | collective-permute-start | bytes 442376 | tf_op jit(solution)/shard_map/ppermute | solution.py:835
  28.1 7.6 %collective-permute-start.9 = (bf16[4,128,384]{2,1,0:T(8,128)(2,1)S(1)}, bf16[4,128,384]{2,1,0:T(8,128)(2,1)S(1)}, u32[]{:S(2)}, u32[]{:S(2)}) collective-permute-start(bf16[4,128,384]{2,1,0:T(8,128)(2,1)S(1)} %pad_maximum_fusion.1.refs_0_), channel_id=1, source_target_pairs={{0,4},{4,0},{8,12},{12,8},{16,20},{20,16},{24,28},{28,24},{1,5},{5... | collective-permute-start | bytes 1179656 | tf_op jit(solution)/shard_map/ppermute | solution.py:829
  28.2 7.6 %collective-permute-start.10 = (bf16[4,128,384]{2,1,0:T(8,128)(2,1)S(1)}, bf16[4,128,384]{2,1,0:T(8,128)(2,1)S(1)}, u32[]{:S(2)}, u32[]{:S(2)}) collective-permute-start(bf16[4,128,384]{2,1,0:T(8,128)(2,1)S(1)} %collective-permute-done.8.refs_1_), channel_id=1, source_target_pairs={{0,4},{4,0},{8,12},{12,8},{16,20},{20,16},{24,28},{28,24},{1,5},{5... | collective-permute-start | bytes 1179656 | tf_op jit(solution)/shard_map/ppermute | solution.py:829
  32.9 16.1 %collective-permute-start.12 = (bf16[4,144,512]{2,1,0:T(8,128)(2,1)S(1)}, bf16[4,144,512]{2,1,0:T(8,128)(2,1)S(1)}, u32[]{:S(2)}, u32[]{:S(2)}) collective-permute-start(bf16[4,144,512]{2,1,0:T(8,128)(2,1)S(1)} %pad_maximum_fusion.refs_0_), channel_id=1, source_target_pairs={{0,8},{4,20},{8,0},{12,28},{16,24},{20,4},{24,16},{28,12},{1,9},{5... | collective-permute-start | bytes 1769480 | tf_op jit(solution)/shard_map/ppermute | solution.py:826
  34.5 15.0 %collective-permute-start.14 = (bf16[4,144,512]{2,1,0:T(8,128)(2,1)S(1)}, bf16[4,144,512]{2,1,0:T(8,128)(2,1)}, u32[]{:S(2)}, u32[]{:S(2)}) collective-permute-start(bf16[4,144,512]{2,1,0:T(8,128)(2,1)S(1)} %pad_maximum_fusion.refs_0_), channel_id=1, source_target_pairs={{0,16},{4,12},{8,24},{12,4},{16,0},{20,28},{24,8},{28,20},{1,17},{... | collective-permute-start | bytes 1769480 | tf_op jit(solution)/shard_map/ppermute | solution.py:826
  44.7 12.7 %collective-permute-start.17 = (bf16[4,144,128]{2,1,0:T(8,128)(2,1)S(1)}, bf16[4,144,128]{2,1,0:T(8,128)(2,1)S(1)}, u32[]{:S(2)}, u32[]{:S(2)}) collective-permute-start(bf16[4,144,128]{2,1,0:T(8,128)(2,1)S(1)} %get-tuple-element.90.h0), channel_id=1, source_target_pairs={{0,2},{1,3},{2,0},{3,1},{4,6},{5,7},{6,4},{7,5},{8,10},{9,11},{10,... | collective-permute-start | bytes 442376 | tf_op jit(solution)/shard_map/ppermute | solution.py:835
  46.1 11.4 %collective-permute-start.18 = (bf16[4,144,128]{2,1,0:T(8,128)(2,1)S(1)}, bf16[4,144,128]{2,1,0:T(8,128)(2,1)S(1)}, u32[]{:S(2)}, u32[]{:S(2)}) collective-permute-start(bf16[4,144,128]{2,1,0:T(8,128)(2,1)S(1)} %get-tuple-element.90.h0), channel_id=1, source_target_pairs={{0,3},{1,2},{2,1},{3,0},{4,7},{5,6},{6,5},{7,4},{8,11},{9,10},{10,... | collective-permute-start | bytes 442376 | tf_op jit(solution)/shard_map/ppermute | solution.py:835
  49.0 10.3 %collective-permute-start.11 = (bf16[4,144,512]{2,1,0:T(8,128)(2,1)S(1)}, bf16[4,144,512]{2,1,0:T(8,128)(2,1)S(1)}, u32[]{:S(2)}, u32[]{:S(2)}) collective-permute-start(bf16[4,144,512]{2,1,0:T(8,128)(2,1)S(1)} %pad_maximum_fusion.refs_0_), channel_id=1, source_target_pairs={{0,4},{4,0},{8,12},{12,8},{16,20},{20,16},{24,28},{28,24},{1,5},{5... | collective-permute-start | bytes 1769480 | tf_op jit(solution)/shard_map/ppermute | solution.py:829
  49.0 10.3 %collective-permute-start.13 = (bf16[4,144,512]{2,1,0:T(8,128)(2,1)S(1)}, bf16[4,144,512]{2,1,0:T(8,128)(2,1)S(1)}, u32[]{:S(2)}, u32[]{:S(2)}) collective-permute-start(bf16[4,144,512]{2,1,0:T(8,128)(2,1)S(1)} %collective-permute-done.12.refs_1_), channel_id=1, source_target_pairs={{0,4},{4,0},{8,12},{12,8},{16,20},{20,16},{24,28},{28,24},{1,5},{5... | collective-permute-start | bytes 1769480 | tf_op jit(solution)/shard_map/ppermute | solution.py:829
  49.5 9.9 %collective-permute-start.15 = (bf16[4,144,512]{2,1,0:T(8,128)(2,1)}, bf16[4,144,512]{2,1,0:T(8,128)(2,1)}, u32[]{:S(2)}, u32[]{:S(2)}) collective-permute-start(bf16[4,144,512]{2,1,0:T(8,128)(2,1)} %collective-permute-done.14.refs_2_), channel_id=1, source_target_pairs={{0,4},{4,0},{8,12},{12,8},{16,20},{20,16},{24,28},{28,24},{1,5},{5... | collective-permute-start | bytes 1769480 | tf_op jit(solution)/shard_map/ppermute | solution.py:829
  57.4 10.0 %collective-permute-start.19 = (bf16[4,144,512]{2,1,0:T(8,128)(2,1)S(1)}, bf16[4,144,512]{2,1,0:T(8,128)(2,1)}, u32[]{:S(2)}, u32[]{:S(2)}) collective-permute-start(bf16[4,144,512]{2,1,0:T(8,128)(2,1)S(1)} %collective-permute-done.12.refs_1_), channel_id=1, source_target_pairs={{0,16},{4,12},{8,24},{12,4},{16,0},{20,28},{24,8},{28,20},{1,17},{... | collective-permute-start | bytes 1769480 | tf_op jit(solution)/shard_map/ppermute | solution.py:826
  67.5 26.6 %all-to-all-start = ((bf16[8,4,192,128]{3,2,1,0:T(8,128)(2,1)}), bf16[8,4,192,128]{3,2,1,0:T(8,128)(2,1)S(1)}, u32[]{:S(2)}, u32[]{:S(2)}) async-start(bf16[8,4,192,128]{3,2,1,0:T(8,128)(2,1)} %shard_map.238), calls=%async_computation | async-start | bytes 3145728 | tf_op jit(solution)/shard_map/all_to_all | solution.py:838
  94.2 13.5 %collective-permute-start.21 = (bf16[4,576,512]{2,1,0:T(8,128)(2,1)}, bf16[4,576,512]{2,1,0:T(8,128)(2,1)S(1)}, u32[]{:S(2)}, u32[]{:S(2)}) collective-permute-start(bf16[4,576,512]{2,1,0:T(8,128)(2,1)} %get-tuple-element.100), channel_id=1, source_target_pairs={{0,4},{4,0},{8,12},{12,8},{16,20},{20,16},{24,28},{28,24},{1,5},{5... | collective-permute-start | bytes 7077896 | tf_op jit(solution)/shard_map/ppermute | solution.py:829
  96.6 11.2 %collective-permute-start.23 = (bf16[4,176,128]{2,1,0:T(8,128)(2,1)S(1)}, bf16[4,176,128]{2,1,0:T(8,128)(2,1)S(1)}, u32[]{:S(2)}, u32[]{:S(2)}) collective-permute-start(bf16[4,176,128]{2,1,0:T(8,128)(2,1)S(1)} %get-tuple-element.102), channel_id=1, source_target_pairs={{0,3},{1,2},{2,1},{3,0},{4,7},{5,6},{6,5},{7,4},{8,11},{9,10},{10,... | collective-permute-start | bytes 540680 | tf_op jit(solution)/shard_map/ppermute | solution.py:835
  108.2 16.4 %collective-permute-start.25 = (bf16[4,576,256]{2,1,0:T(8,128)(2,1)S(1)}, bf16[4,576,256]{2,1,0:T(8,128)(2,1)S(1)}, u32[]{:S(2)}, u32[]{:S(2)}) collective-permute-start(bf16[4,576,256]{2,1,0:T(8,128)(2,1)S(1)} %get-tuple-element.104), channel_id=1, source_target_pairs={{0,8},{4,20},{8,0},{12,28},{16,24},{20,4},{24,16},{28,12},{1,9},{5... | collective-permute-start | bytes 3538952 | tf_op jit(solution)/shard_map/ppermute | solution.py:826
  110.0 9.0 %collective-permute-start.24 = (bf16[4,176,128]{2,1,0:T(8,128)(2,1)S(1)}, bf16[4,176,128]{2,1,0:T(8,128)(2,1)S(1)}, u32[]{:S(2)}, u32[]{:S(2)}) collective-permute-start(bf16[4,176,128]{2,1,0:T(8,128)(2,1)S(1)} %get-tuple-element.101.s0), channel_id=1, source_target_pairs={{0,2},{1,3},{2,0},{3,1},{4,6},{5,7},{6,4},{7,5},{8,10},{9,11},{10,... | collective-permute-start | bytes 540680 | tf_op jit(solution)/shard_map/ppermute | solution.py:835
  124.9 15.4 %collective-permute-start.27 = (bf16[4,576,128]{2,1,0:T(8,128)(2,1)S(1)}, bf16[4,576,128]{2,1,0:T(8,128)(2,1)S(1)}, u32[]{:S(2)}, u32[]{:S(2)}) collective-permute-start(bf16[4,576,128]{2,1,0:T(8,128)(2,1)S(1)} %get-tuple-element.123), channel_id=1, source_target_pairs={{0,16},{4,12},{8,24},{12,4},{16,0},{20,28},{24,8},{28,20},{1,17},{... | collective-permute-start | bytes 1769480 | tf_op jit(solution)/shard_map/ppermute | solution.py:826
  128.3 10.3 %collective-permute-start.28 = (bf16[4,192,256]{2,1,0:T(8,128)(2,1)S(1)}, bf16[4,192,256]{2,1,0:T(8,128)(2,1)S(1)}, u32[]{:S(2)}, u32[]{:S(2)}) collective-permute-start(bf16[4,192,256]{2,1,0:T(8,128)(2,1)S(1)} %get-tuple-element.115), channel_id=1, source_target_pairs={{0,8},{4,20},{8,0},{12,28},{16,24},{20,4},{24,16},{28,12},{1,9},{5... | collective-permute-start | bytes 1179656 | tf_op jit(solution)/shard_map/ppermute | solution.py:826
  141.0 8.4 %collective-permute-start.30 = (bf16[1,576,128]{2,1,0:T(8,128)(2,1)S(1)}, bf16[1,576,128]{2,1,0:T(8,128)(2,1)S(1)}, u32[]{:S(2)}, u32[]{:S(2)}) collective-permute-start(bf16[1,576,128]{2,1,0:T(8,128)(2,1)S(1)} %get-tuple-element.133), channel_id=1, source_target_pairs={{0,1},{1,0},{2,3},{3,2},{4,5},{5,4},{6,7},{7,6},{8,9},{9,8},{10,11... | collective-permute-start | bytes 442376 | tf_op jit(solution)/shard_map/ppermute | solution.py:835
  141.1 14.0 %collective-permute-start.31 = (bf16[1,576,128]{2,1,0:T(8,128)(2,1)S(1)}, bf16[1,576,128]{2,1,0:T(8,128)(2,1)S(1)}, u32[]{:S(2)}, u32[]{:S(2)}) collective-permute-start(bf16[1,576,128]{2,1,0:T(8,128)(2,1)S(1)} %get-tuple-element.134), channel_id=1, source_target_pairs={{0,2},{1,3},{2,0},{3,1},{4,6},{5,7},{6,4},{7,5},{8,10},{9,11},{10,... | collective-permute-start | bytes 442376 | tf_op jit(solution)/shard_map/ppermute | solution.py:835
  143.0 12.1 %collective-permute-start.32 = (bf16[1,576,128]{2,1,0:T(8,128)(2,1)S(1)}, bf16[1,576,128]{2,1,0:T(8,128)(2,1)S(1)}, u32[]{:S(2)}, u32[]{:S(2)}) collective-permute-start(bf16[1,576,128]{2,1,0:T(8,128)(2,1)S(1)} %get-tuple-element.135), channel_id=1, source_target_pairs={{0,3},{1,2},{2,1},{3,0},{4,7},{5,6},{6,5},{7,4},{8,11},{9,10},{10,... | collective-permute-start | bytes 442376 | tf_op jit(solution)/shard_map/ppermute | solution.py:835
  156.2 9.3 %collective-permute-start.33 = (bf16[1152,128]{1,0:T(8,128)(2,1)S(1)}, bf16[1152,128]{1,0:T(8,128)(2,1)S(1)}, u32[]{:S(2)}, u32[]{:S(2)}) collective-permute-start(bf16[1152,128]{1,0:T(8,128)(2,1)S(1)} %shard_map.253.refs_0_), channel_id=1, source_target_pairs={{0,8},{4,20},{8,0},{12,28},{16,24},{20,4},{24,16},{28,12},{1,9},{5... | collective-permute-start | bytes 884744 | tf_op jit(solution)/shard_map/ppermute | solution.py:826
  157.5 8.0 %collective-permute-start.34 = (bf16[1152,128]{1,0:T(8,128)(2,1)S(1)}, bf16[1152,128]{1,0:T(8,128)(2,1)S(1)}, u32[]{:S(2)}, u32[]{:S(2)}) collective-permute-start(bf16[1152,128]{1,0:T(8,128)(2,1)S(1)} %shard_map.253.refs_0_), channel_id=1, source_target_pairs={{0,16},{4,12},{8,24},{12,4},{16,0},{20,28},{24,8},{28,20},{1,17},{... | collective-permute-start | bytes 884744 | tf_op jit(solution)/shard_map/ppermute | solution.py:826
  158.3 7.2 %collective-permute-start.35 = (bf16[1,224,128]{2,1,0:T(8,128)(2,1)S(1)}, bf16[1,224,128]{2,1,0:T(8,128)(2,1)S(1)}, u32[]{:S(2)}, u32[]{:S(2)}) collective-permute-start(bf16[1,224,128]{2,1,0:T(8,128)(2,1)S(1)} %get-tuple-element.137), channel_id=1, source_target_pairs={{0,1},{1,0},{2,3},{3,2},{4,5},{5,4},{6,7},{7,6},{8,9},{9,8},{10,11... | collective-permute-start | bytes 172040 | tf_op jit(solution)/shard_map/ppermute | solution.py:835
  176.8 7.6 %collective-permute-start.45 = (bf16[608,128]{1,0:T(8,128)(2,1)S(1)}, bf16[608,128]{1,0:T(8,128)(2,1)S(1)}, u32[]{:S(2)}, u32[]{:S(2)}) collective-permute-start(bf16[608,128]{1,0:T(8,128)(2,1)S(1)} %collective-permute-done.43.refs_1_), channel_id=1, source_target_pairs={{0,16},{4,12},{8,24},{12,4},{16,0},{20,28},{24,8},{28,20},{1,17},{... | collective-permute-start | bytes 466952 | tf_op jit(solution)/shard_map/ppermute | solution.py:826
  (58 other events, 425.9 us)

commit v7 on v6

--- a/solution.py
+++ b/solution.py
@@ -34,6 +34,7 @@
 VM = pl.BlockSpec(memory_space=pltpu.VMEM)
 HB = pl.BlockSpec(memory_space=pltpu.HBM)
 SM = pl.BlockSpec(memory_space=pltpu.SMEM)
+ANY = pl.BlockSpec(memory_space=pl.ANY)
 
 
 def call(body, outs, in_specs, scratch, flops, moved, vmem=48, out_specs=None):
@@ -898,7 +899,7 @@
     qkv, state = call(
         qkv_body,
         [((groups, ext, 3 * PAIR), bf16), ((groups, STATE, PAIR), bf16)],
-        [SM] + [HB] * 5,
+        [SM, HB] + [ANY] * 4,
         [proj_w, all_qkv, pltpu.VMEM((ext, width), bf16), pltpu.SemaphoreType.DMA, pltpu.SemaphoreType.DMA],
         2 * ext * width * 3 * width, 6 << 20, 20, (HB, VM),
     )(meta, after(a1e, ffn_z), *qkv_bufs)
@@ -936,7 +937,7 @@
             ((rows, width), f32), ((rows, width), bf16), ((rows, width), f32), ((2, width), f32),
             ((groups,) + w_out.shape, bf16), ((groups, n_m, width), bf16), ((groups, n_m, width), bf16),
         ],
-        [SM] + [HB] * 8 + [VM] * 2 + [HB] * 8,
+        [SM] + [HB] * 8 + [VM] * 2 + [HB] * 7 + [ANY],
         [
             low, low, pltpu.VMEM((groups,) + w_out.shape, bf16), big, low, low,
             pltpu.VMEM((4, groups, STATE, PAIR), bf16),
@@ -1058,7 +1059,7 @@
     new_out, new_in, new_down, later = call(
         functools.partial(place_body, nb_q),
         [(w_out.shape, bf16), (w_in.shape, bf16), (w_down.shape, bf16), (part_shape, f32)],
-        [SM, SM] + [HB] * 8,
+        [SM, SM] + [ANY] * 8,
         [
             pltpu.VMEM((8, 2 * n_m, 128), bf16), pltpu.VMEM((8, n_m, 128), f32), pltpu.VMEM(part_shape, f32),
             pltpu.SemaphoreType.DMA,
@@ -1074,7 +1075,7 @@
     (first_new, second_new, master_new, new_qkv, norm_first_new, norm_second_new, norm_new) = call(
         owner_body,
         [(state_shape, f32)] * 3 + [(w_qkv.shape, bf16)] + [(norm_shape, f32)] * 3,
-        [SM] * 3 + [HB] * 4 + [VM] * 4 + [HB] * 8,
+        [SM] * 3 + [HB] * 4 + [VM] * 4 + [ANY] * 8,
         [
             pltpu.VMEM((8, n_held, 128), bf16), pltpu.VMEM((8, n_q, 128), f32), pltpu.VMEM(part_shape, f32),
             pltpu.VMEM((capacity * block_rows, 128), f32), pltpu.VMEM((w_qkv.size // 128, 128), f32),

time: 193 us -> 188 us (0.974)
  local copies, waits for them, and re-layouts: 7.95 us -> 4.34 us
    unnamed x78 -> x42, local copies, waits for them, and re-layouts: 5.34 us -> 1.73 us
where the time goes in v7:
time: 188 us
  Pallas kernels  70.1 us (37%)
  starting transfers between devices  60.9 us (32%)
  waiting for transfers between devices  49.8 us (26%)
  local copies, waits for them, and re-layouts  4.34 us (2%)
  between operations  2.07 us (1%)
    pallas_call x19, Pallas kernels, fixed(): run(*[pltpu.with_memory_space_constraint(x, pltpu.HBM) if spec is HB else...  70.1 us
    ppermute x18, waiting for transfers between devices, swap_mp(): return lax.ppermute(x, 'mp', [(i, i ^ mask) for i in range(groups)])  34.2 us
    ppermute x18, starting transfers between devices, swap_mp(): return lax.ppermute(x, 'mp', [(i, i ^ mask) for i in range(groups)])  29.8 us
    ppermute x14, starting transfers between devices, swap(): lax.ppermute(x, 'dp', [(i, i ^ 1 << order[i & 1][s]) for i in range(ndp)])  18.7 us
    ppermute x14, waiting for transfers between devices, swap(): lax.ppermute(x, 'dp', [(i, i ^ 1 << order[i & 1][s]) for i in range(ndp)])  9.1 us
    ppermute x16, waiting for transfers between devices, swap_core(): return lax.ppermute(x, 'dp', [(i, i ^ 1) for i in range(ndp)])  4.68 us
    all_to_all x1, starting transfers between devices, exchange(): return lax.all_to_all(x, axis, 0, 0, tiled=True)  4.49 us
    ppermute x2, starting transfers between devices, from_mp(): lax.ppermute(x, 'mp', [(i, i + step) for i in range(groups) if 0 <= i + s...  4.1 us
  transfers between devices with their start and end apart: 51, of which 20 were waited for; matrix products, arithmetic and copies ran while one was open for 2% of the time, Pallas kernels for 33%

profile of v7, /device:TPU:0, one launch (start us, length us, event | category | flops | bytes accessed | tf_op | source)
XLA Modules:
  0.0 187.6 jit_solution(11060334063517881759)
XLA Ops:
  1.7 3.1 %collective-permute-start.2 = (bf16[128,384]{1,0:T(8,128)(2,1)S(1)}, bf16[128,384]{1,0:T(8,128)(2,1)S(1)}, u32[]{:S(2)}, u32[]{:S(2)}) collective-permute-start(bf16[128,384]{1,0:T(8,128)(2,1)S(1)} %constant_dynamic-slice_fusion), channel_id=1, source_target_pairs={{0,1},{1,0},{2,3},{3,2},{4,5},{5,4},{6,7},{7,6},{8,9},{9,8},{10,11... | collective-permute-start | bytes 294920 | tf_op jit(solution)/shard_map/ppermute | solution.py:836
  4.7 2.6 %collective-permute-start.3 = (bf16[128,384]{1,0:T(8,128)(2,1)S(1)}, bf16[128,384]{1,0:T(8,128)(2,1)S(1)}, u32[]{:S(2)}, u32[]{:S(2)}) collective-permute-start(bf16[128,384]{1,0:T(8,128)(2,1)S(1)} %constant_dynamic-slice_fusion), channel_id=1, source_target_pairs={{0,2},{1,3},{2,0},{3,1},{4,6},{5,7},{6,4},{7,5},{8,10},{9,11},{10,... | collective-permute-start | bytes 294920 | tf_op jit(solution)/shard_map/ppermute | solution.py:836
  8.2 2.8 %collective-permute-start = (bf16[64,512]{1,0:T(8,128)(2,1)S(1)}, bf16[64,512]{1,0:T(8,128)(2,1)S(1)}, u32[]{:S(2)}, u32[]{:S(2)}) collective-permute-start(bf16[64,512]{1,0:T(8,128)(2,1)S(1)} %get-tuple-element.157), channel_id=1, source_target_pairs={{0,1},{1,2},{2,3},{4,5},{5,6},{6,7},{8,9},{9,10},{10,11},{12,13},{... | collective-permute-start | bytes 196616 | tf_op jit(solution)/shard_map/ppermute | solution.py:833
  15.4 1.8 collective-permute-done.1.right
  18.7 2.0 %collective-permute-start.5 = (bf16[144,512]{1,0:T(8,128)(2,1)S(1)}, bf16[144,512]{1,0:T(8,128)(2,1)S(1)}, u32[]{:S(2)}, u32[]{:S(2)}) collective-permute-start(bf16[144,512]{1,0:T(8,128)(2,1)S(1)} %pad_maximum_fusion.2), channel_id=1, source_target_pairs={{0,1},{1,0},{2,3},{3,2},{4,5},{5,4},{6,7},{7,6},{8,9},{9,8},{10,11... | collective-permute-start | bytes 442376 | tf_op jit(solution)/shard_map/ppermute | solution.py:836
  23.6 2.5 %shard_map.238 = bf16[8,4,192,128]{3,2,1,0:T(8,128)(2,1)} custom-call(f32[1536,128]{1,0:T(8,128)} %bitcast.39, f32[1536,128]{1,0:T(8,128)} %bitcast.40, f32[1536,128]{1,0:T(8,128)} %bitcast.41), custom_call_target="tpu_custom_call" | custom-call | flops 1048576 | bytes 4194304 | tf_op jit(solution)/shard_map/pallas_call | solution.py:55
  26.2 1.9 %shard_map.239.a1e_h = bf16[640,512]{1,0:T(8,128)(2,1)} custom-call(bf16[512,512]{1,0:T(8,128)(2,1)S(1)} %bitcast.37, bf16[64,512]{1,0:T(8,128)(2,1)S(1)} %collective-permute-done.left, bf16[64,512]{1,0:T(8,128)(2,1)S(1)} %collective-permute-done.1.right, f32[2,512]{1,0:T(2,128)S(1)} %copy-done.8, f32[2,512]{1,0:T(2,128)S(1)} %copy-done.9), custom_call_target="tpu_custom_call" | custom-call | flops 2097152 | bytes 1048576 | tf_op jit(solution)/shard_map/pallas_call | solution.py:55
  28.7 4.1 %collective-permute-done.6 = bf16[144,512]{1,0:T(8,128)(2,1)S(1)} collective-permute-done((bf16[144,512]{1,0:T(8,128)(2,1)S(1)}, bf16[144,512]{1,0:T(8,128)(2,1)S(1)}, u32[]{:S(2)}, u32[]{:S(2)}) %collective-permute-start.6) | collective-permute-done | bytes 147488 | tf_op jit(solution)/shard_map/ppermute | solution.py:836
  35.8 5.6 %shard_map.240 = (bf16[4,640,384]{2,1,0:T(8,128)(2,1)}, bf16[4,144,128]{2,1,0:T(8,128)(2,1)S(1)}) custom-call(s32[18]{0:T(128)S(1)} %stack.97.meta, bf16[640,512]{1,0:T(8,128)(2,1)} %shard_map.239.a1e_h, bf16[4,128,384]{2,1,0:T(8,128)(2,1)S(1)} %pad_maximum_fusion.1.refs_0_, bf16[4,128,384]{2,1,0:T(8,128)(2,1)S(1)} %collective-permute-done.8.refs_1_, ...), custom_call_target="tpu_custom_call" | custom-call | flops 1006632960 | bytes 6291456 | tf_op jit(solution)/shard_map/pallas_call | solution.py:55
  41.5 2.2 %collective-permute-start.16 = (bf16[4,144,128]{2,1,0:T(8,128)(2,1)S(1)}, bf16[4,144,128]{2,1,0:T(8,128)(2,1)S(1)}, u32[]{:S(2)}, u32[]{:S(2)}) collective-permute-start(bf16[4,144,128]{2,1,0:T(8,128)(2,1)S(1)} %get-tuple-element.90.h0), channel_id=1, source_target_pairs={{0,1},{1,0},{2,3},{3,2},{4,5},{5,4},{6,7},{7,6},{8,9},{9,8},{10,11... | collective-permute-start | bytes 442376 | tf_op jit(solution)/shard_map/ppermute | solution.py:836
  48.5 7.9 %collective-permute-done.17.h2 = bf16[4,144,128]{2,1,0:T(8,128)(2,1)S(1)} collective-permute-done((bf16[4,144,128]{2,1,0:T(8,128)(2,1)S(1)}, bf16[4,144,128]{2,1,0:T(8,128)(2,1)S(1)}, u32[]{:S(2)}, u32[]{:S(2)}) %collective-permute-start.17) | collective-permute-done | bytes 147488 | tf_op jit(solution)/shard_map/ppermute | solution.py:836
  58.9 6.3 %shard_map.241.near_h = f32[512,512]{1,0:T(8,128)} custom-call(s32[18]{0:T(128)S(1)} %stack.97.meta, bf16[4,640,384]{2,1,0:T(8,128)(2,1)} %get-tuple-element.91.qkv_h), custom_call_target="tpu_custom_call" | custom-call | flops 536870912 | bytes 12582912 | tf_op jit(solution)/shard_map/pallas_call | solution.py:55
  65.2 1.8 collective-permute-done.19.refs_3_
  67.1 4.5 %all-to-all-start = ((bf16[8,4,192,128]{3,2,1,0:T(8,128)(2,1)}), bf16[8,4,192,128]{3,2,1,0:T(8,128)(2,1)}, u32[]{:S(2)}, u32[]{:S(2)}) async-start(bf16[8,4,192,128]{3,2,1,0:T(8,128)(2,1)} %shard_map.238), calls=%async_computation | async-start | bytes 3145728 | tf_op jit(solution)/shard_map/all_to_all | solution.py:839
  71.8 2.1 %collective-permute-done.20.refs_7_ = bf16[4,144,512]{2,1,0:T(8,128)(2,1)S(1)} collective-permute-done((bf16[4,144,512]{2,1,0:T(8,128)(2,1)}, bf16[4,144,512]{2,1,0:T(8,128)(2,1)S(1)}, u32[]{:S(2)}, u32[]{:S(2)}) %collective-permute-start.20) | collective-permute-done | bytes 589856 | tf_op jit(solution)/shard_map/ppermute | solution.py:830
  73.9 19.7 %shard_map.242 = (bf16[512,512]{1,0:T(8,128)(2,1)}, bf16[4,176,128]{2,1,0:T(8,128)(2,1)S(1)}, bf16[4,176,128]{2,1,0:T(8,128)(2,1)S(1)}, f32[512,512]{1,0:T(8,128...) custom-call(s32[18]{0:T(128)S(1)} %stack.97.meta, ...), custom_call_target="tpu_custom_call" | custom-call | flops 6442450944 | bytes 25165824 | tf_op jit(solution)/shard_map/pallas_call | solution.py:55
  95.4 2.6 %collective-permute-start.23 = (bf16[4,176,128]{2,1,0:T(8,128)(2,1)S(1)}, bf16[4,176,128]{2,1,0:T(8,128)(2,1)S(1)}, u32[]{:S(2)}, u32[]{:S(2)}) collective-permute-start(bf16[4,176,128]{2,1,0:T(8,128)(2,1)S(1)} %get-tuple-element.102), channel_id=1, source_target_pairs={{0,3},{1,2},{2,1},{3,0},{4,7},{5,6},{6,5},{7,4},{8,11},{9,10},{10,... | collective-permute-start | bytes 540680 | tf_op jit(solution)/shard_map/ppermute | solution.py:836
  98.0 1.9 %shard_map.243.refs_4_ = f32[8,3,192,128]{3,2,1,0:T(8,128)S(1)} custom-call(bf16[8,4,192,128]{3,2,1,0:T(8,128)(2,1)} %all-to-all-done.recv_h), custom_call_target="tpu_custom_call" | custom-call | flops 1048576 | bytes 4194304 | tf_op jit(solution)/shard_map/pallas_call | solution.py:55
  100.6 5.9 %collective-permute-done.23.three.s3 = bf16[4,176,128]{2,1,0:T(8,128)(2,1)S(1)} collective-permute-done((bf16[4,176,128]{2,1,0:T(8,128)(2,1)S(1)}, bf16[4,176,128]{2,1,0:T(8,128)(2,1)S(1)}, u32[]{:S(2)}, u32[]{:S(2)}) %collective-permute-start.23) | collective-permute-done | bytes 180256 | tf_op jit(solution)/shard_map/ppermute | solution.py:836
  109.4 6.9 %shard_map.245 = (bf16[512,512]{1,0:T(8,128)(2,1)S(1)}, f32[512,512]{1,0:T(8,128)S(1)}, f32[512,512]{1,0:T(8,128)S(1)}) custom-call(s32[18]{0:T(128)S(1)} %stack.97.meta, bf16[4,640,384]{2,1,0:T(8,128)(2,1)} %get-tuple-element.91.qkv_h, bf16[512,512]{1,0:T(8,128)(2,1)} %get-tuple-element.105.dctx_h, bf16[4,176,128]{2,1,0:T(8,128)(2,1)S(1)} %collective-permute-done.22.one.s1, ...), custom_call_target="tpu_custom_call" | custom-call | flops 1073741824 | bytes 25165824 | tf_op jit(solution)/shard_map/pallas_call | solution.py:55
  117.8 5.6 %shard_map.246 = (bf16[4,512,384]{2,1,0:T(8,128)(2,1)}, f32[4,192,512]{2,1,0:T(8,128)S(1)}, f32[4,192,512]{2,1,0:T(8,128)S(1)}) custom-call(s32[18]{0:T(128)S(1)} %stack.97.meta, bf16[4,640,384]{2,1,0:T(8,128)(2,1)} %get-tuple-element.91.qkv_h, bf16[512,512]{1,0:T(8,128)(2,1)S(1)} %get-tuple-element.108.dq, f32[512,512]{1,0:T(8,128)S(1)} %get-tuple-element.109.dkn, ...), custom_call_target="tpu_custom_call" | custom-call | flops 805306368 | bytes 25165824 | tf_op jit(solution)/shard_map/pallas_call | solution.py:55
  128.7 7.1 %shard_map.248 = (f32[512,512]{1,0:T(8,128)}, f32[16,128]{1,0:T(8,128)S(1)}) custom-call(s32[18]{0:T(128)S(1)} %stack.97.meta, bf16[4,512,384]{2,1,0:T(8,128)(2,1)} %get-tuple-element.116.dproj_h, bf16[512,512]{1,0:T(8,128)(2,1)S(1)} %bitcast.38, f32[512,512]{1,0:T(8,128)} %get-tuple-element.117.dx2_h, f32[2,512]{1,0:T(2,128)S(1)} %copy-done.8, ...), custom_call_target="tpu_custom_call" | custom-call | flops 805306368 | bytes 8388608 | tf_op jit(solution)/shard_map/pallas_call | solution.py:55
  139.9 2.0 %collective-permute-start.31 = (bf16[1,576,128]{2,1,0:T(8,128)(2,1)S(1)}, bf16[1,576,128]{2,1,0:T(8,128)(2,1)S(1)}, u32[]{:S(2)}, u32[]{:S(2)}) collective-permute-start(bf16[1,576,128]{2,1,0:T(8,128)(2,1)S(1)} %get-tuple-element.134), channel_id=1, source_target_pairs={{0,2},{1,3},{2,0},{3,1},{4,6},{5,7},{6,4},{7,5},{8,10},{9,11},{10,... | collective-permute-start | bytes 442376 | tf_op jit(solution)/shard_map/ppermute | solution.py:836
  141.8 2.4 %collective-permute-start.32 = (bf16[1,576,128]{2,1,0:T(8,128)(2,1)S(1)}, bf16[1,576,128]{2,1,0:T(8,128)(2,1)S(1)}, u32[]{:S(2)}, u32[]{:S(2)}) collective-permute-start(bf16[1,576,128]{2,1,0:T(8,128)(2,1)S(1)} %get-tuple-element.135), channel_id=1, source_target_pairs={{0,3},{1,2},{2,1},{3,0},{4,7},{5,6},{6,5},{7,4},{8,11},{9,10},{10,... | collective-permute-start | bytes 442376 | tf_op jit(solution)/shard_map/ppermute | solution.py:836
  144.8 3.4 %collective-permute-done.30.refs_1_ = bf16[1,576,128]{2,1,0:T(8,128)(2,1)S(1)} collective-permute-done((bf16[1,576,128]{2,1,0:T(8,128)(2,1)S(1)}, bf16[1,576,128]{2,1,0:T(8,128)(2,1)S(1)}, u32[]{:S(2)}, u32[]{:S(2)}) %collective-permute-start.30) | collective-permute-done | bytes 147488 | tf_op jit(solution)/shard_map/ppermute | solution.py:836
  148.2 5.7 %collective-permute-done.31.refs_2_ = bf16[1,576,128]{2,1,0:T(8,128)(2,1)S(1)} collective-permute-done((bf16[1,576,128]{2,1,0:T(8,128)(2,1)S(1)}, bf16[1,576,128]{2,1,0:T(8,128)(2,1)S(1)}, u32[]{:S(2)}, u32[]{:S(2)}) %collective-permute-start.31) | collective-permute-done | bytes 147488 | tf_op jit(solution)/shard_map/ppermute | solution.py:836
  157.1 2.8 %collective-permute-start.35 = (bf16[1,224,128]{2,1,0:T(8,128)(2,1)S(1)}, bf16[1,224,128]{2,1,0:T(8,128)(2,1)S(1)}, u32[]{:S(2)}, u32[]{:S(2)}) collective-permute-start(bf16[1,224,128]{2,1,0:T(8,128)(2,1)S(1)} %get-tuple-element.137), channel_id=1, source_target_pairs={{0,1},{1,0},{2,3},{3,2},{4,5},{5,4},{6,7},{7,6},{8,9},{9,8},{10,11... | collective-permute-start | bytes 172040 | tf_op jit(solution)/shard_map/ppermute | solution.py:836
  160.2 2.0 %collective-permute-start.37 = (bf16[1,224,128]{2,1,0:T(8,128)(2,1)S(1)}, bf16[1,224,128]{2,1,0:T(8,128)(2,1)S(1)}, u32[]{:S(2)}, u32[]{:S(2)}) collective-permute-start(bf16[1,224,128]{2,1,0:T(8,128)(2,1)S(1)} %get-tuple-element.139), channel_id=1, source_target_pairs={{0,3},{1,2},{2,1},{3,0},{4,7},{5,6},{6,5},{7,4},{8,11},{9,10},{10,... | collective-permute-start | bytes 172040 | tf_op jit(solution)/shard_map/ppermute | solution.py:836
  162.2 2.0 %collective-permute-done.33.refs_1_ = bf16[1152,128]{1,0:T(8,128)(2,1)S(1)} collective-permute-done((bf16[1152,128]{1,0:T(8,128)(2,1)S(1)}, bf16[1152,128]{1,0:T(8,128)(2,1)S(1)}, u32[]{:S(2)}, u32[]{:S(2)}) %collective-permute-start.33) | collective-permute-done | bytes 294944 | tf_op jit(solution)/shard_map/ppermute | solution.py:827
  171.4 2.7 %collective-permute-done.43.refs_1_ = bf16[608,128]{1,0:T(8,128)(2,1)S(1)} collective-permute-done((bf16[608,128]{1,0:T(8,128)(2,1)S(1)}, bf16[608,128]{1,0:T(8,128)(2,1)S(1)}, u32[]{:S(2)}, u32[]{:S(2)}) %collective-permute-start.43) | collective-permute-done | bytes 155680 | tf_op jit(solution)/shard_map/ppermute | solution.py:827
  177.4 3.4 %shard_map.255 = (bf16[128,512]{1,0:T(8,128)(2,1)}, bf16[512,512]{1,0:T(8,128)(2,1)}, bf16[512,512]{1,0:T(8,128)(2,1)}, f32[4,24,2,8,128]{4,3,2,1,0:T(8,128)}) custom-call(s32[18]{0:T(128)S(1)} %stack.97.meta, s32[192]{0:T(256)S(1)} %get-tuple-element.155.blocks, bf16[1152,128]{1,0:T(8,128)(2,1)S(1)} %shard_map.253.refs_0_, ...), custom_call_target="tpu_custom_call" | custom-call | flops 1048576 | bytes 4194304 | tf_op jit(solution)/shard_map/pallas_call | solution.py:55
  182.4 5.1 %shard_map.256 = (f32[24,64,128]{2,1,0:T(8,128)}, f32[24,64,128]{2,1,0:T(8,128)}, f32[24,64,128]{2,1,0:T(8,128)}, bf16[512,384]{1,0:T(8,128)(2,1)}, f32[4,512]{1...) custom-call(s32[18]{0:T(128)S(1)} %stack.97.meta, s32[192]{0:T(256)S(1)} %get-tuple-element.154.counts, ...), custom_call_target="tpu_custom_call" | custom-call | flops 1048576 | bytes 8388608 | tf_op jit(solution)/shard_map/pallas_call | solution.py:55
  (143 shorter events, 53.2 us)
Async XLA Ops:
  1.7 12.4 %collective-permute-start.2 = (bf16[128,384]{1,0:T(8,128)(2,1)S(1)}, bf16[128,384]{1,0:T(8,128)(2,1)S(1)}, u32[]{:S(2)}, u32[]{:S(2)}) collective-permute-start(bf16[128,384]{1,0:T(8,128)(2,1)S(1)} %constant_dynamic-slice_fusion), channel_id=1, source_target_pairs={{0,1},{1,0},{2,3},{3,2},{4,5},{5,4},{6,7},{7,6},{8,9},{9,8},{10,11... | collective-permute-start | bytes 294920 | tf_op jit(solution)/shard_map/ppermute | solution.py:836
  4.7 10.5 %collective-permute-start.3 = (bf16[128,384]{1,0:T(8,128)(2,1)S(1)}, bf16[128,384]{1,0:T(8,128)(2,1)S(1)}, u32[]{:S(2)}, u32[]{:S(2)}) collective-permute-start(bf16[128,384]{1,0:T(8,128)(2,1)S(1)} %constant_dynamic-slice_fusion), channel_id=1, source_target_pairs={{0,2},{1,3},{2,0},{3,1},{4,6},{5,7},{6,4},{7,5},{8,10},{9,11},{10,... | collective-permute-start | bytes 294920 | tf_op jit(solution)/shard_map/ppermute | solution.py:836
  7.3 7.9 %collective-permute-start.4 = (bf16[128,384]{1,0:T(8,128)(2,1)S(1)}, bf16[128,384]{1,0:T(8,128)(2,1)S(1)}, u32[]{:S(2)}, u32[]{:S(2)}) collective-permute-start(bf16[128,384]{1,0:T(8,128)(2,1)S(1)} %constant_dynamic-slice_fusion), channel_id=1, source_target_pairs={{0,3},{1,2},{2,1},{3,0},{4,7},{5,6},{6,5},{7,4},{8,11},{9,10},{10,... | collective-permute-start | bytes 294920 | tf_op jit(solution)/shard_map/ppermute | solution.py:836
  8.2 7.1 %collective-permute-start = (bf16[64,512]{1,0:T(8,128)(2,1)S(1)}, bf16[64,512]{1,0:T(8,128)(2,1)S(1)}, u32[]{:S(2)}, u32[]{:S(2)}) collective-permute-start(bf16[64,512]{1,0:T(8,128)(2,1)S(1)} %get-tuple-element.157), channel_id=1, source_target_pairs={{0,1},{1,2},{2,3},{4,5},{5,6},{6,7},{8,9},{9,10},{10,11},{12,13},{... | collective-permute-start | bytes 196616 | tf_op jit(solution)/shard_map/ppermute | solution.py:833
  17.2 11.0 %collective-permute-start.8 = (bf16[4,128,384]{2,1,0:T(8,128)(2,1)S(1)}, bf16[4,128,384]{2,1,0:T(8,128)(2,1)S(1)}, u32[]{:S(2)}, u32[]{:S(2)}) collective-permute-start(bf16[4,128,384]{2,1,0:T(8,128)(2,1)S(1)} %pad_maximum_fusion.1.refs_0_), channel_id=1, source_target_pairs={{0,8},{4,20},{8,0},{12,28},{16,24},{20,4},{24,16},{28,12},{1,9},{5... | collective-permute-start | bytes 1179656 | tf_op jit(solution)/shard_map/ppermute | solution.py:827
  18.7 10.0 %collective-permute-start.5 = (bf16[144,512]{1,0:T(8,128)(2,1)S(1)}, bf16[144,512]{1,0:T(8,128)(2,1)S(1)}, u32[]{:S(2)}, u32[]{:S(2)}) collective-permute-start(bf16[144,512]{1,0:T(8,128)(2,1)S(1)} %pad_maximum_fusion.2), channel_id=1, source_target_pairs={{0,1},{1,0},{2,3},{3,2},{4,5},{5,4},{6,7},{7,6},{8,9},{9,8},{10,11... | collective-permute-start | bytes 442376 | tf_op jit(solution)/shard_map/ppermute | solution.py:836
  20.7 12.1 %collective-permute-start.6 = (bf16[144,512]{1,0:T(8,128)(2,1)S(1)}, bf16[144,512]{1,0:T(8,128)(2,1)S(1)}, u32[]{:S(2)}, u32[]{:S(2)}) collective-permute-start(bf16[144,512]{1,0:T(8,128)(2,1)S(1)} %pad_maximum_fusion.2), channel_id=1, source_target_pairs={{0,2},{1,3},{2,0},{3,1},{4,6},{5,7},{6,4},{7,5},{8,10},{9,11},{10,... | collective-permute-start | bytes 442376 | tf_op jit(solution)/shard_map/ppermute | solution.py:836
  22.2 10.6 %collective-permute-start.7 = (bf16[144,512]{1,0:T(8,128)(2,1)S(1)}, bf16[144,512]{1,0:T(8,128)(2,1)S(1)}, u32[]{:S(2)}, u32[]{:S(2)}) collective-permute-start(bf16[144,512]{1,0:T(8,128)(2,1)S(1)} %pad_maximum_fusion.2), channel_id=1, source_target_pairs={{0,3},{1,2},{2,1},{3,0},{4,7},{5,6},{6,5},{7,4},{8,11},{9,10},{10,... | collective-permute-start | bytes 442376 | tf_op jit(solution)/shard_map/ppermute | solution.py:836
  28.1 7.6 %collective-permute-start.9 = (bf16[4,128,384]{2,1,0:T(8,128)(2,1)S(1)}, bf16[4,128,384]{2,1,0:T(8,128)(2,1)S(1)}, u32[]{:S(2)}, u32[]{:S(2)}) collective-permute-start(bf16[4,128,384]{2,1,0:T(8,128)(2,1)S(1)} %pad_maximum_fusion.1.refs_0_), channel_id=1, source_target_pairs={{0,4},{4,0},{8,12},{12,8},{16,20},{20,16},{24,28},{28,24},{1,5},{5... | collective-permute-start | bytes 1179656 | tf_op jit(solution)/shard_map/ppermute | solution.py:830
  28.2 7.6 %collective-permute-start.10 = (bf16[4,128,384]{2,1,0:T(8,128)(2,1)S(1)}, bf16[4,128,384]{2,1,0:T(8,128)(2,1)S(1)}, u32[]{:S(2)}, u32[]{:S(2)}) collective-permute-start(bf16[4,128,384]{2,1,0:T(8,128)(2,1)S(1)} %collective-permute-done.8.refs_1_), channel_id=1, source_target_pairs={{0,4},{4,0},{8,12},{12,8},{16,20},{20,16},{24,28},{28,24},{1,5},{5... | collective-permute-start | bytes 1179656 | tf_op jit(solution)/shard_map/ppermute | solution.py:830
  32.9 15.0 %collective-permute-start.12 = (bf16[4,144,512]{2,1,0:T(8,128)(2,1)S(1)}, bf16[4,144,512]{2,1,0:T(8,128)(2,1)S(1)}, u32[]{:S(2)}, u32[]{:S(2)}) collective-permute-start(bf16[4,144,512]{2,1,0:T(8,128)(2,1)S(1)} %pad_maximum_fusion.refs_0_), channel_id=1, source_target_pairs={{0,8},{4,20},{8,0},{12,28},{16,24},{20,4},{24,16},{28,12},{1,9},{5... | collective-permute-start | bytes 1769480 | tf_op jit(solution)/shard_map/ppermute | solution.py:827
  34.5 13.9 %collective-permute-start.14 = (bf16[4,144,512]{2,1,0:T(8,128)(2,1)S(1)}, bf16[4,144,512]{2,1,0:T(8,128)(2,1)}, u32[]{:S(2)}, u32[]{:S(2)}) collective-permute-start(bf16[4,144,512]{2,1,0:T(8,128)(2,1)S(1)} %pad_maximum_fusion.refs_0_), channel_id=1, source_target_pairs={{0,16},{4,12},{8,24},{12,4},{16,0},{20,28},{24,8},{28,20},{1,17},{... | collective-permute-start | bytes 1769480 | tf_op jit(solution)/shard_map/ppermute | solution.py:827
  43.7 12.7 %collective-permute-start.17 = (bf16[4,144,128]{2,1,0:T(8,128)(2,1)S(1)}, bf16[4,144,128]{2,1,0:T(8,128)(2,1)S(1)}, u32[]{:S(2)}, u32[]{:S(2)}) collective-permute-start(bf16[4,144,128]{2,1,0:T(8,128)(2,1)S(1)} %get-tuple-element.90.h0), channel_id=1, source_target_pairs={{0,2},{1,3},{2,0},{3,1},{4,6},{5,7},{6,4},{7,5},{8,10},{9,11},{10,... | collective-permute-start | bytes 442376 | tf_op jit(solution)/shard_map/ppermute | solution.py:836
  45.0 11.4 %collective-permute-start.18 = (bf16[4,144,128]{2,1,0:T(8,128)(2,1)S(1)}, bf16[4,144,128]{2,1,0:T(8,128)(2,1)S(1)}, u32[]{:S(2)}, u32[]{:S(2)}) collective-permute-start(bf16[4,144,128]{2,1,0:T(8,128)(2,1)S(1)} %get-tuple-element.90.h0), channel_id=1, source_target_pairs={{0,3},{1,2},{2,1},{3,0},{4,7},{5,6},{6,5},{7,4},{8,11},{9,10},{10,... | collective-permute-start | bytes 442376 | tf_op jit(solution)/shard_map/ppermute | solution.py:836
  47.9 10.9 %collective-permute-start.11 = (bf16[4,144,512]{2,1,0:T(8,128)(2,1)S(1)}, bf16[4,144,512]{2,1,0:T(8,128)(2,1)S(1)}, u32[]{:S(2)}, u32[]{:S(2)}) collective-permute-start(bf16[4,144,512]{2,1,0:T(8,128)(2,1)S(1)} %pad_maximum_fusion.refs_0_), channel_id=1, source_target_pairs={{0,4},{4,0},{8,12},{12,8},{16,20},{20,16},{24,28},{28,24},{1,5},{5... | collective-permute-start | bytes 1769480 | tf_op jit(solution)/shard_map/ppermute | solution.py:830
  47.9 10.9 %collective-permute-start.13 = (bf16[4,144,512]{2,1,0:T(8,128)(2,1)S(1)}, bf16[4,144,512]{2,1,0:T(8,128)(2,1)S(1)}, u32[]{:S(2)}, u32[]{:S(2)}) collective-permute-start(bf16[4,144,512]{2,1,0:T(8,128)(2,1)S(1)} %collective-permute-done.12.refs_1_), channel_id=1, source_target_pairs={{0,4},{4,0},{8,12},{12,8},{16,20},{20,16},{24,28},{28,24},{1,5},{5... | collective-permute-start | bytes 1769480 | tf_op jit(solution)/shard_map/ppermute | solution.py:830
  48.4 10.5 %collective-permute-start.15 = (bf16[4,144,512]{2,1,0:T(8,128)(2,1)}, bf16[4,144,512]{2,1,0:T(8,128)(2,1)}, u32[]{:S(2)}, u32[]{:S(2)}) collective-permute-start(bf16[4,144,512]{2,1,0:T(8,128)(2,1)} %collective-permute-done.14.refs_2_), channel_id=1, source_target_pairs={{0,4},{4,0},{8,12},{12,8},{16,20},{20,16},{24,28},{28,24},{1,5},{5... | collective-permute-start | bytes 1769480 | tf_op jit(solution)/shard_map/ppermute | solution.py:830
  57.0 10.0 %collective-permute-start.19 = (bf16[4,144,512]{2,1,0:T(8,128)(2,1)S(1)}, bf16[4,144,512]{2,1,0:T(8,128)(2,1)}, u32[]{:S(2)}, u32[]{:S(2)}) collective-permute-start(bf16[4,144,512]{2,1,0:T(8,128)(2,1)S(1)} %collective-permute-done.12.refs_1_), channel_id=1, source_target_pairs={{0,16},{4,12},{8,24},{12,4},{16,0},{20,28},{24,8},{28,20},{1,17},{... | collective-permute-start | bytes 1769480 | tf_op jit(solution)/shard_map/ppermute | solution.py:827
  67.1 26.5 %all-to-all-start = ((bf16[8,4,192,128]{3,2,1,0:T(8,128)(2,1)}), bf16[8,4,192,128]{3,2,1,0:T(8,128)(2,1)}, u32[]{:S(2)}, u32[]{:S(2)}) async-start(bf16[8,4,192,128]{3,2,1,0:T(8,128)(2,1)} %shard_map.238), calls=%async_computation | async-start | bytes 3145728 | tf_op jit(solution)/shard_map/all_to_all | solution.py:839
  93.6 12.9 %collective-permute-start.21 = (bf16[4,576,512]{2,1,0:T(8,128)(2,1)}, bf16[4,576,512]{2,1,0:T(8,128)(2,1)S(1)}, u32[]{:S(2)}, u32[]{:S(2)}) collective-permute-start(bf16[4,576,512]{2,1,0:T(8,128)(2,1)} %get-tuple-element.100), channel_id=1, source_target_pairs={{0,4},{4,0},{8,12},{12,8},{16,20},{20,16},{24,28},{28,24},{1,5},{5... | collective-permute-start | bytes 7077896 | tf_op jit(solution)/shard_map/ppermute | solution.py:830
  95.4 11.2 %collective-permute-start.23 = (bf16[4,176,128]{2,1,0:T(8,128)(2,1)S(1)}, bf16[4,176,128]{2,1,0:T(8,128)(2,1)S(1)}, u32[]{:S(2)}, u32[]{:S(2)}) collective-permute-start(bf16[4,176,128]{2,1,0:T(8,128)(2,1)S(1)} %get-tuple-element.102), channel_id=1, source_target_pairs={{0,3},{1,2},{2,1},{3,0},{4,7},{5,6},{6,5},{7,4},{8,11},{9,10},{10,... | collective-permute-start | bytes 540680 | tf_op jit(solution)/shard_map/ppermute | solution.py:836
  107.1 16.3 %collective-permute-start.25 = (bf16[4,576,256]{2,1,0:T(8,128)(2,1)S(1)}, bf16[4,576,256]{2,1,0:T(8,128)(2,1)S(1)}, u32[]{:S(2)}, u32[]{:S(2)}) collective-permute-start(bf16[4,576,256]{2,1,0:T(8,128)(2,1)S(1)} %get-tuple-element.104), channel_id=1, source_target_pairs={{0,8},{4,20},{8,0},{12,28},{16,24},{20,4},{24,16},{28,12},{1,9},{5... | collective-permute-start | bytes 3538952 | tf_op jit(solution)/shard_map/ppermute | solution.py:827
  108.8 9.0 %collective-permute-start.24 = (bf16[4,176,128]{2,1,0:T(8,128)(2,1)S(1)}, bf16[4,176,128]{2,1,0:T(8,128)(2,1)S(1)}, u32[]{:S(2)}, u32[]{:S(2)}) collective-permute-start(bf16[4,176,128]{2,1,0:T(8,128)(2,1)S(1)} %get-tuple-element.101.s0), channel_id=1, source_target_pairs={{0,2},{1,3},{2,0},{3,1},{4,6},{5,7},{6,4},{7,5},{8,10},{9,11},{10,... | collective-permute-start | bytes 540680 | tf_op jit(solution)/shard_map/ppermute | solution.py:836
  123.7 15.4 %collective-permute-start.27 = (bf16[4,576,128]{2,1,0:T(8,128)(2,1)S(1)}, bf16[4,576,128]{2,1,0:T(8,128)(2,1)S(1)}, u32[]{:S(2)}, u32[]{:S(2)}) collective-permute-start(bf16[4,576,128]{2,1,0:T(8,128)(2,1)S(1)} %get-tuple-element.123), channel_id=1, source_target_pairs={{0,16},{4,12},{8,24},{12,4},{16,0},{20,28},{24,8},{28,20},{1,17},{... | collective-permute-start | bytes 1769480 | tf_op jit(solution)/shard_map/ppermute | solution.py:827
  127.1 10.3 %collective-permute-start.28 = (bf16[4,192,256]{2,1,0:T(8,128)(2,1)S(1)}, bf16[4,192,256]{2,1,0:T(8,128)(2,1)S(1)}, u32[]{:S(2)}, u32[]{:S(2)}) collective-permute-start(bf16[4,192,256]{2,1,0:T(8,128)(2,1)S(1)} %get-tuple-element.115), channel_id=1, source_target_pairs={{0,8},{4,20},{8,0},{12,28},{16,24},{20,4},{24,16},{28,12},{1,9},{5... | collective-permute-start | bytes 1179656 | tf_op jit(solution)/shard_map/ppermute | solution.py:827
  139.8 8.5 %collective-permute-start.30 = (bf16[1,576,128]{2,1,0:T(8,128)(2,1)S(1)}, bf16[1,576,128]{2,1,0:T(8,128)(2,1)S(1)}, u32[]{:S(2)}, u32[]{:S(2)}) collective-permute-start(bf16[1,576,128]{2,1,0:T(8,128)(2,1)S(1)} %get-tuple-element.133), channel_id=1, source_target_pairs={{0,1},{1,0},{2,3},{3,2},{4,5},{5,4},{6,7},{7,6},{8,9},{9,8},{10,11... | collective-permute-start | bytes 442376 | tf_op jit(solution)/shard_map/ppermute | solution.py:836
  139.9 14.0 %collective-permute-start.31 = (bf16[1,576,128]{2,1,0:T(8,128)(2,1)S(1)}, bf16[1,576,128]{2,1,0:T(8,128)(2,1)S(1)}, u32[]{:S(2)}, u32[]{:S(2)}) collective-permute-start(bf16[1,576,128]{2,1,0:T(8,128)(2,1)S(1)} %get-tuple-element.134), channel_id=1, source_target_pairs={{0,2},{1,3},{2,0},{3,1},{4,6},{5,7},{6,4},{7,5},{8,10},{9,11},{10,... | collective-permute-start | bytes 442376 | tf_op jit(solution)/shard_map/ppermute | solution.py:836
  141.8 12.1 %collective-permute-start.32 = (bf16[1,576,128]{2,1,0:T(8,128)(2,1)S(1)}, bf16[1,576,128]{2,1,0:T(8,128)(2,1)S(1)}, u32[]{:S(2)}, u32[]{:S(2)}) collective-permute-start(bf16[1,576,128]{2,1,0:T(8,128)(2,1)S(1)} %get-tuple-element.135), channel_id=1, source_target_pairs={{0,3},{1,2},{2,1},{3,0},{4,7},{5,6},{6,5},{7,4},{8,11},{9,10},{10,... | collective-permute-start | bytes 442376 | tf_op jit(solution)/shard_map/ppermute | solution.py:836
  155.0 9.3 %collective-permute-start.33 = (bf16[1152,128]{1,0:T(8,128)(2,1)S(1)}, bf16[1152,128]{1,0:T(8,128)(2,1)S(1)}, u32[]{:S(2)}, u32[]{:S(2)}) collective-permute-start(bf16[1152,128]{1,0:T(8,128)(2,1)S(1)} %shard_map.253.refs_0_), channel_id=1, source_target_pairs={{0,8},{4,20},{8,0},{12,28},{16,24},{20,4},{24,16},{28,12},{1,9},{5... | collective-permute-start | bytes 884744 | tf_op jit(solution)/shard_map/ppermute | solution.py:827
  156.2 8.0 %collective-permute-start.34 = (bf16[1152,128]{1,0:T(8,128)(2,1)S(1)}, bf16[1152,128]{1,0:T(8,128)(2,1)S(1)}, u32[]{:S(2)}, u32[]{:S(2)}) collective-permute-start(bf16[1152,128]{1,0:T(8,128)(2,1)S(1)} %shard_map.253.refs_0_), channel_id=1, source_target_pairs={{0,16},{4,12},{8,24},{12,4},{16,0},{20,28},{24,8},{28,20},{1,17},{... | collective-permute-start | bytes 884744 | tf_op jit(solution)/shard_map/ppermute | solution.py:827
  157.1 7.2 %collective-permute-start.35 = (bf16[1,224,128]{2,1,0:T(8,128)(2,1)S(1)}, bf16[1,224,128]{2,1,0:T(8,128)(2,1)S(1)}, u32[]{:S(2)}, u32[]{:S(2)}) collective-permute-start(bf16[1,224,128]{2,1,0:T(8,128)(2,1)S(1)} %get-tuple-element.137), channel_id=1, source_target_pairs={{0,1},{1,0},{2,3},{3,2},{4,5},{5,4},{6,7},{7,6},{8,9},{9,8},{10,11... | collective-permute-start | bytes 172040 | tf_op jit(solution)/shard_map/ppermute | solution.py:836
  167.1 7.0 %collective-permute-start.38 = (bf16[1152,128]{1,0:T(8,128)(2,1)S(1)}, bf16[1152,128]{1,0:T(8,128)(2,1)S(1)}, u32[]{:S(2)}, u32[]{:S(2)}) collective-permute-start(bf16[1152,128]{1,0:T(8,128)(2,1)S(1)} %collective-permute-done.33.refs_1_), channel_id=1, source_target_pairs={{0,16},{4,12},{8,24},{12,4},{16,0},{20,28},{24,8},{28,20},{1,17},{... | collective-permute-start | bytes 884744 | tf_op jit(solution)/shard_map/ppermute | solution.py:827
  (40 other events, 321.2 us)

commit v8 on v7

--- a/solution.py
+++ b/solution.py
@@ -921,7 +921,7 @@
         [all_qkv, pltpu.VMEM((rows, width), f32), pltpu.SemaphoreType.DMA], mm * 1024, 12 << 20, 16, (HB,),
     )(meta, after(qkv, slot, held, counts, *ffn_oth, *states))
     ffn_bufs = ffn_bufs + ffn_oth + [swap_core(ffn_bufs[3])]
-    held_state = exchange(after(parts, ffn_bufs[3], near), "dp")
+    held_state = exchange(after(parts, near), "dp")
 
     hid_w = w_in.shape[1]
     big = pltpu.VMEM((rows, width), f32)

time: 188 us -> 186 us (0.989)
  waiting for transfers between devices: 49.8 us -> 47.9 us
  transfers between devices with their start and end apart: 51 -> 51, of which waited for: 20 -> 19; matrix products, arithmetic and copies ran while one was open for 2% -> 2% of each run, Pallas kernels for 33% -> 34%
where the time goes in v8:
time: 186 us
  Pallas kernels  70.1 us (38%)
  starting transfers between devices  60.9 us (33%)
  waiting for transfers between devices  47.9 us (26%)
  local copies, waits for them, and re-layouts  4.34 us (2%)
  between operations  2.09 us (1%)
    pallas_call x19, Pallas kernels, fixed(): run(*[pltpu.with_memory_space_constraint(x, pltpu.HBM) if spec is HB else...  70.1 us
    ppermute x18, waiting for transfers between devices, swap_mp(): return lax.ppermute(x, 'mp', [(i, i ^ mask) for i in range(groups)])  34.2 us
    ppermute x18, starting transfers between devices, swap_mp(): return lax.ppermute(x, 'mp', [(i, i ^ mask) for i in range(groups)])  29.8 us
    ppermute x14, starting transfers between devices, swap(): lax.ppermute(x, 'dp', [(i, i ^ 1 << order[i & 1][s]) for i in range(ndp)])  18.7 us
    ppermute x14, waiting for transfers between devices, swap(): lax.ppermute(x, 'dp', [(i, i ^ 1 << order[i & 1][s]) for i in range(ndp)])  7.25 us
    ppermute x16, waiting for transfers between devices, swap_core(): return lax.ppermute(x, 'dp', [(i, i ^ 1) for i in range(ndp)])  4.65 us
    all_to_all x1, starting transfers between devices, exchange(): return lax.all_to_all(x, axis, 0, 0, tiled=True)  4.49 us
    ppermute x2, starting transfers between devices, from_mp(): lax.ppermute(x, 'mp', [(i, i + step) for i in range(groups) if 0 <= i + s...  4.1 us
  transfers between devices with their start and end apart: 51, of which 19 were waited for; matrix products, arithmetic and copies ran while one was open for 2% of the time, Pallas kernels for 34%

profile of v8, /device:TPU:0, one launch (start us, length us, event | category | flops | bytes accessed | tf_op | source)
XLA Modules:
  0.0 185.8 jit_solution(16738797656203998209)
XLA Ops:
  1.7 3.1 %collective-permute-start.2 = (bf16[128,384]{1,0:T(8,128)(2,1)S(1)}, bf16[128,384]{1,0:T(8,128)(2,1)S(1)}, u32[]{:S(2)}, u32[]{:S(2)}) collective-permute-start(bf16[128,384]{1,0:T(8,128)(2,1)S(1)} %constant_dynamic-slice_fusion), channel_id=1, source_target_pairs={{0,1},{1,0},{2,3},{3,2},{4,5},{5,4},{6,7},{7,6},{8,9},{9,8},{10,11... | collective-permute-start | bytes 294920 | tf_op jit(solution)/shard_map/ppermute | solution.py:836
  4.7 2.6 %collective-permute-start.3 = (bf16[128,384]{1,0:T(8,128)(2,1)S(1)}, bf16[128,384]{1,0:T(8,128)(2,1)S(1)}, u32[]{:S(2)}, u32[]{:S(2)}) collective-permute-start(bf16[128,384]{1,0:T(8,128)(2,1)S(1)} %constant_dynamic-slice_fusion), channel_id=1, source_target_pairs={{0,2},{1,3},{2,0},{3,1},{4,6},{5,7},{6,4},{7,5},{8,10},{9,11},{10,... | collective-permute-start | bytes 294920 | tf_op jit(solution)/shard_map/ppermute | solution.py:836
  8.2 2.8 %collective-permute-start = (bf16[64,512]{1,0:T(8,128)(2,1)S(1)}, bf16[64,512]{1,0:T(8,128)(2,1)S(1)}, u32[]{:S(2)}, u32[]{:S(2)}) collective-permute-start(bf16[64,512]{1,0:T(8,128)(2,1)S(1)} %get-tuple-element.157), channel_id=1, source_target_pairs={{0,1},{1,2},{2,3},{4,5},{5,6},{6,7},{8,9},{9,10},{10,11},{12,13},{... | collective-permute-start | bytes 196616 | tf_op jit(solution)/shard_map/ppermute | solution.py:833
  15.4 1.8 collective-permute-done.1.right
  18.7 2.0 %collective-permute-start.5 = (bf16[144,512]{1,0:T(8,128)(2,1)S(1)}, bf16[144,512]{1,0:T(8,128)(2,1)S(1)}, u32[]{:S(2)}, u32[]{:S(2)}) collective-permute-start(bf16[144,512]{1,0:T(8,128)(2,1)S(1)} %pad_maximum_fusion.2), channel_id=1, source_target_pairs={{0,1},{1,0},{2,3},{3,2},{4,5},{5,4},{6,7},{7,6},{8,9},{9,8},{10,11... | collective-permute-start | bytes 442376 | tf_op jit(solution)/shard_map/ppermute | solution.py:836
  23.6 2.5 %shard_map.238 = bf16[8,4,192,128]{3,2,1,0:T(8,128)(2,1)} custom-call(f32[1536,128]{1,0:T(8,128)} %bitcast.39, f32[1536,128]{1,0:T(8,128)} %bitcast.40, f32[1536,128]{1,0:T(8,128)} %bitcast.41), custom_call_target="tpu_custom_call" | custom-call | flops 1048576 | bytes 4194304 | tf_op jit(solution)/shard_map/pallas_call | solution.py:55
  26.2 1.9 %shard_map.239.a1e_h = bf16[640,512]{1,0:T(8,128)(2,1)} custom-call(bf16[512,512]{1,0:T(8,128)(2,1)S(1)} %bitcast.37, bf16[64,512]{1,0:T(8,128)(2,1)S(1)} %collective-permute-done.left, bf16[64,512]{1,0:T(8,128)(2,1)S(1)} %collective-permute-done.1.right, f32[2,512]{1,0:T(2,128)S(1)} %copy-done.8, f32[2,512]{1,0:T(2,128)S(1)} %copy-done.9), custom_call_target="tpu_custom_call" | custom-call | flops 2097152 | bytes 1048576 | tf_op jit(solution)/shard_map/pallas_call | solution.py:55
  28.7 4.1 %collective-permute-done.6 = bf16[144,512]{1,0:T(8,128)(2,1)S(1)} collective-permute-done((bf16[144,512]{1,0:T(8,128)(2,1)S(1)}, bf16[144,512]{1,0:T(8,128)(2,1)S(1)}, u32[]{:S(2)}, u32[]{:S(2)}) %collective-permute-start.6) | collective-permute-done | bytes 147488 | tf_op jit(solution)/shard_map/ppermute | solution.py:836
  35.8 5.6 %shard_map.240 = (bf16[4,640,384]{2,1,0:T(8,128)(2,1)}, bf16[4,144,128]{2,1,0:T(8,128)(2,1)S(1)}) custom-call(s32[18]{0:T(128)S(1)} %stack.97.meta, bf16[640,512]{1,0:T(8,128)(2,1)} %shard_map.239.a1e_h, bf16[4,128,384]{2,1,0:T(8,128)(2,1)S(1)} %pad_maximum_fusion.1.refs_0_, bf16[4,128,384]{2,1,0:T(8,128)(2,1)S(1)} %collective-permute-done.8.refs_1_, ...), custom_call_target="tpu_custom_call" | custom-call | flops 1006632960 | bytes 6291456 | tf_op jit(solution)/shard_map/pallas_call | solution.py:55
  41.5 2.2 %collective-permute-start.16 = (bf16[4,144,128]{2,1,0:T(8,128)(2,1)S(1)}, bf16[4,144,128]{2,1,0:T(8,128)(2,1)S(1)}, u32[]{:S(2)}, u32[]{:S(2)}) collective-permute-start(bf16[4,144,128]{2,1,0:T(8,128)(2,1)S(1)} %get-tuple-element.90.h0), channel_id=1, source_target_pairs={{0,1},{1,0},{2,3},{3,2},{4,5},{5,4},{6,7},{7,6},{8,9},{9,8},{10,11... | collective-permute-start | bytes 442376 | tf_op jit(solution)/shard_map/ppermute | solution.py:836
  48.5 7.9 %collective-permute-done.17.h2 = bf16[4,144,128]{2,1,0:T(8,128)(2,1)S(1)} collective-permute-done((bf16[4,144,128]{2,1,0:T(8,128)(2,1)S(1)}, bf16[4,144,128]{2,1,0:T(8,128)(2,1)S(1)}, u32[]{:S(2)}, u32[]{:S(2)}) %collective-permute-start.17) | collective-permute-done | bytes 147488 | tf_op jit(solution)/shard_map/ppermute | solution.py:836
  58.9 6.3 %shard_map.241.near_h = f32[512,512]{1,0:T(8,128)} custom-call(s32[18]{0:T(128)S(1)} %stack.97.meta, bf16[4,640,384]{2,1,0:T(8,128)(2,1)} %get-tuple-element.91.qkv_h), custom_call_target="tpu_custom_call" | custom-call | flops 536870912 | bytes 12582912 | tf_op jit(solution)/shard_map/pallas_call | solution.py:55
  65.3 4.5 %all-to-all-start = ((bf16[8,4,192,128]{3,2,1,0:T(8,128)(2,1)}), bf16[8,4,192,128]{3,2,1,0:T(8,128)(2,1)}, u32[]{:S(2)}, u32[]{:S(2)}) async-start(bf16[8,4,192,128]{3,2,1,0:T(8,128)(2,1)} %shard_map.238), calls=%async_computation | async-start | bytes 3145728 | tf_op jit(solution)/shard_map/all_to_all | solution.py:839
  70.0 2.1 %collective-permute-done.20.refs_7_ = bf16[4,144,512]{2,1,0:T(8,128)(2,1)S(1)} collective-permute-done((bf16[4,144,512]{2,1,0:T(8,128)(2,1)}, bf16[4,144,512]{2,1,0:T(8,128)(2,1)S(1)}, u32[]{:S(2)}, u32[]{:S(2)}) %collective-permute-start.20) | collective-permute-done | bytes 589856 | tf_op jit(solution)/shard_map/ppermute | solution.py:830
  72.1 19.7 %shard_map.242 = (bf16[512,512]{1,0:T(8,128)(2,1)}, bf16[4,176,128]{2,1,0:T(8,128)(2,1)S(1)}, bf16[4,176,128]{2,1,0:T(8,128)(2,1)S(1)}, f32[512,512]{1,0:T(8,128...) custom-call(s32[18]{0:T(128)S(1)} %stack.97.meta, ...), custom_call_target="tpu_custom_call" | custom-call | flops 6442450944 | bytes 25165824 | tf_op jit(solution)/shard_map/pallas_call | solution.py:55
  93.6 2.6 %collective-permute-start.23 = (bf16[4,176,128]{2,1,0:T(8,128)(2,1)S(1)}, bf16[4,176,128]{2,1,0:T(8,128)(2,1)S(1)}, u32[]{:S(2)}, u32[]{:S(2)}) collective-permute-start(bf16[4,176,128]{2,1,0:T(8,128)(2,1)S(1)} %get-tuple-element.102), channel_id=1, source_target_pairs={{0,3},{1,2},{2,1},{3,0},{4,7},{5,6},{6,5},{7,4},{8,11},{9,10},{10,... | collective-permute-start | bytes 540680 | tf_op jit(solution)/shard_map/ppermute | solution.py:836
  96.2 1.9 %shard_map.243.refs_4_ = f32[8,3,192,128]{3,2,1,0:T(8,128)S(1)} custom-call(bf16[8,4,192,128]{3,2,1,0:T(8,128)(2,1)} %all-to-all-done.recv_h), custom_call_target="tpu_custom_call" | custom-call | flops 1048576 | bytes 4194304 | tf_op jit(solution)/shard_map/pallas_call | solution.py:55
  98.9 5.9 %collective-permute-done.23.three.s3 = bf16[4,176,128]{2,1,0:T(8,128)(2,1)S(1)} collective-permute-done((bf16[4,176,128]{2,1,0:T(8,128)(2,1)S(1)}, bf16[4,176,128]{2,1,0:T(8,128)(2,1)S(1)}, u32[]{:S(2)}, u32[]{:S(2)}) %collective-permute-start.23) | collective-permute-done | bytes 180256 | tf_op jit(solution)/shard_map/ppermute | solution.py:836
  105.3 1.7 collective-permute-start.25
  107.6 6.9 %shard_map.245 = (bf16[512,512]{1,0:T(8,128)(2,1)S(1)}, f32[512,512]{1,0:T(8,128)S(1)}, f32[512,512]{1,0:T(8,128)S(1)}) custom-call(s32[18]{0:T(128)S(1)} %stack.97.meta, bf16[4,640,384]{2,1,0:T(8,128)(2,1)} %get-tuple-element.91.qkv_h, bf16[512,512]{1,0:T(8,128)(2,1)} %get-tuple-element.105.dctx_h, bf16[4,176,128]{2,1,0:T(8,128)(2,1)S(1)} %collective-permute-done.22.one.s1, ...), custom_call_target="tpu_custom_call" | custom-call | flops 1073741824 | bytes 25165824 | tf_op jit(solution)/shard_map/pallas_call | solution.py:55
  116.0 5.6 %shard_map.246 = (bf16[4,512,384]{2,1,0:T(8,128)(2,1)}, f32[4,192,512]{2,1,0:T(8,128)S(1)}, f32[4,192,512]{2,1,0:T(8,128)S(1)}) custom-call(s32[18]{0:T(128)S(1)} %stack.97.meta, bf16[4,640,384]{2,1,0:T(8,128)(2,1)} %get-tuple-element.91.qkv_h, bf16[512,512]{1,0:T(8,128)(2,1)S(1)} %get-tuple-element.108.dq, f32[512,512]{1,0:T(8,128)S(1)} %get-tuple-element.109.dkn, ...), custom_call_target="tpu_custom_call" | custom-call | flops 805306368 | bytes 25165824 | tf_op jit(solution)/shard_map/pallas_call | solution.py:55
  126.9 7.1 %shard_map.248 = (f32[512,512]{1,0:T(8,128)}, f32[16,128]{1,0:T(8,128)S(1)}) custom-call(s32[18]{0:T(128)S(1)} %stack.97.meta, bf16[4,512,384]{2,1,0:T(8,128)(2,1)} %get-tuple-element.116.dproj_h, bf16[512,512]{1,0:T(8,128)(2,1)S(1)} %bitcast.38, f32[512,512]{1,0:T(8,128)} %get-tuple-element.117.dx2_h, f32[2,512]{1,0:T(2,128)S(1)} %copy-done.8, ...), custom_call_target="tpu_custom_call" | custom-call | flops 805306368 | bytes 8388608 | tf_op jit(solution)/shard_map/pallas_call | solution.py:55
  138.1 2.0 %collective-permute-start.31 = (bf16[1,576,128]{2,1,0:T(8,128)(2,1)S(1)}, bf16[1,576,128]{2,1,0:T(8,128)(2,1)S(1)}, u32[]{:S(2)}, u32[]{:S(2)}) collective-permute-start(bf16[1,576,128]{2,1,0:T(8,128)(2,1)S(1)} %get-tuple-element.134), channel_id=1, source_target_pairs={{0,2},{1,3},{2,0},{3,1},{4,6},{5,7},{6,4},{7,5},{8,10},{9,11},{10,... | collective-permute-start | bytes 442376 | tf_op jit(solution)/shard_map/ppermute | solution.py:836
  140.1 2.3 %collective-permute-start.32 = (bf16[1,576,128]{2,1,0:T(8,128)(2,1)S(1)}, bf16[1,576,128]{2,1,0:T(8,128)(2,1)S(1)}, u32[]{:S(2)}, u32[]{:S(2)}) collective-permute-start(bf16[1,576,128]{2,1,0:T(8,128)(2,1)S(1)} %get-tuple-element.135), channel_id=1, source_target_pairs={{0,3},{1,2},{2,1},{3,0},{4,7},{5,6},{6,5},{7,4},{8,11},{9,10},{10,... | collective-permute-start | bytes 442376 | tf_op jit(solution)/shard_map/ppermute | solution.py:836
  143.0 3.4 %collective-permute-done.30.refs_1_ = bf16[1,576,128]{2,1,0:T(8,128)(2,1)S(1)} collective-permute-done((bf16[1,576,128]{2,1,0:T(8,128)(2,1)S(1)}, bf16[1,576,128]{2,1,0:T(8,128)(2,1)S(1)}, u32[]{:S(2)}, u32[]{:S(2)}) %collective-permute-start.30) | collective-permute-done | bytes 147488 | tf_op jit(solution)/shard_map/ppermute | solution.py:836
  146.4 5.7 %collective-permute-done.31.refs_2_ = bf16[1,576,128]{2,1,0:T(8,128)(2,1)S(1)} collective-permute-done((bf16[1,576,128]{2,1,0:T(8,128)(2,1)S(1)}, bf16[1,576,128]{2,1,0:T(8,128)(2,1)S(1)}, u32[]{:S(2)}, u32[]{:S(2)}) %collective-permute-start.31) | collective-permute-done | bytes 147488 | tf_op jit(solution)/shard_map/ppermute | solution.py:836
  155.3 2.8 %collective-permute-start.35 = (bf16[1,224,128]{2,1,0:T(8,128)(2,1)S(1)}, bf16[1,224,128]{2,1,0:T(8,128)(2,1)S(1)}, u32[]{:S(2)}, u32[]{:S(2)}) collective-permute-start(bf16[1,224,128]{2,1,0:T(8,128)(2,1)S(1)} %get-tuple-element.137), channel_id=1, source_target_pairs={{0,1},{1,0},{2,3},{3,2},{4,5},{5,4},{6,7},{7,6},{8,9},{9,8},{10,11... | collective-permute-start | bytes 172040 | tf_op jit(solution)/shard_map/ppermute | solution.py:836
  158.5 2.0 %collective-permute-start.37 = (bf16[1,224,128]{2,1,0:T(8,128)(2,1)S(1)}, bf16[1,224,128]{2,1,0:T(8,128)(2,1)S(1)}, u32[]{:S(2)}, u32[]{:S(2)}) collective-permute-start(bf16[1,224,128]{2,1,0:T(8,128)(2,1)S(1)} %get-tuple-element.139), channel_id=1, source_target_pairs={{0,3},{1,2},{2,1},{3,0},{4,7},{5,6},{6,5},{7,4},{8,11},{9,10},{10,... | collective-permute-start | bytes 172040 | tf_op jit(solution)/shard_map/ppermute | solution.py:836
  160.4 2.0 %collective-permute-done.33.refs_1_ = bf16[1152,128]{1,0:T(8,128)(2,1)S(1)} collective-permute-done((bf16[1152,128]{1,0:T(8,128)(2,1)S(1)}, bf16[1152,128]{1,0:T(8,128)(2,1)S(1)}, u32[]{:S(2)}, u32[]{:S(2)}) %collective-permute-start.33) | collective-permute-done | bytes 294944 | tf_op jit(solution)/shard_map/ppermute | solution.py:827
  169.6 2.7 %collective-permute-done.43.refs_1_ = bf16[608,128]{1,0:T(8,128)(2,1)S(1)} collective-permute-done((bf16[608,128]{1,0:T(8,128)(2,1)S(1)}, bf16[608,128]{1,0:T(8,128)(2,1)S(1)}, u32[]{:S(2)}, u32[]{:S(2)}) %collective-permute-start.43) | collective-permute-done | bytes 155680 | tf_op jit(solution)/shard_map/ppermute | solution.py:827
  175.6 3.4 %shard_map.255 = (bf16[128,512]{1,0:T(8,128)(2,1)}, bf16[512,512]{1,0:T(8,128)(2,1)}, bf16[512,512]{1,0:T(8,128)(2,1)}, f32[4,24,2,8,128]{4,3,2,1,0:T(8,128)}) custom-call(s32[18]{0:T(128)S(1)} %stack.97.meta, s32[192]{0:T(256)S(1)} %get-tuple-element.155.blocks, bf16[1152,128]{1,0:T(8,128)(2,1)S(1)} %shard_map.253.refs_0_, ...), custom_call_target="tpu_custom_call" | custom-call | flops 1048576 | bytes 4194304 | tf_op jit(solution)/shard_map/pallas_call | solution.py:55
  180.5 5.1 %shard_map.256 = (f32[24,64,128]{2,1,0:T(8,128)}, f32[24,64,128]{2,1,0:T(8,128)}, f32[24,64,128]{2,1,0:T(8,128)}, bf16[512,384]{1,0:T(8,128)(2,1)}, f32[4,512]{1...) custom-call(s32[18]{0:T(128)S(1)} %stack.97.meta, s32[192]{0:T(256)S(1)} %get-tuple-element.154.counts, ...), custom_call_target="tpu_custom_call" | custom-call | flops 1048576 | bytes 8388608 | tf_op jit(solution)/shard_map/pallas_call | solution.py:55
  (143 shorter events, 51.5 us)
Async XLA Ops:
  1.7 12.4 %collective-permute-start.2 = (bf16[128,384]{1,0:T(8,128)(2,1)S(1)}, bf16[128,384]{1,0:T(8,128)(2,1)S(1)}, u32[]{:S(2)}, u32[]{:S(2)}) collective-permute-start(bf16[128,384]{1,0:T(8,128)(2,1)S(1)} %constant_dynamic-slice_fusion), channel_id=1, source_target_pairs={{0,1},{1,0},{2,3},{3,2},{4,5},{5,4},{6,7},{7,6},{8,9},{9,8},{10,11... | collective-permute-start | bytes 294920 | tf_op jit(solution)/shard_map/ppermute | solution.py:836
  4.7 10.5 %collective-permute-start.3 = (bf16[128,384]{1,0:T(8,128)(2,1)S(1)}, bf16[128,384]{1,0:T(8,128)(2,1)S(1)}, u32[]{:S(2)}, u32[]{:S(2)}) collective-permute-start(bf16[128,384]{1,0:T(8,128)(2,1)S(1)} %constant_dynamic-slice_fusion), channel_id=1, source_target_pairs={{0,2},{1,3},{2,0},{3,1},{4,6},{5,7},{6,4},{7,5},{8,10},{9,11},{10,... | collective-permute-start | bytes 294920 | tf_op jit(solution)/shard_map/ppermute | solution.py:836
  7.3 7.9 %collective-permute-start.4 = (bf16[128,384]{1,0:T(8,128)(2,1)S(1)}, bf16[128,384]{1,0:T(8,128)(2,1)S(1)}, u32[]{:S(2)}, u32[]{:S(2)}) collective-permute-start(bf16[128,384]{1,0:T(8,128)(2,1)S(1)} %constant_dynamic-slice_fusion), channel_id=1, source_target_pairs={{0,3},{1,2},{2,1},{3,0},{4,7},{5,6},{6,5},{7,4},{8,11},{9,10},{10,... | collective-permute-start | bytes 294920 | tf_op jit(solution)/shard_map/ppermute | solution.py:836
  8.2 7.1 %collective-permute-start = (bf16[64,512]{1,0:T(8,128)(2,1)S(1)}, bf16[64,512]{1,0:T(8,128)(2,1)S(1)}, u32[]{:S(2)}, u32[]{:S(2)}) collective-permute-start(bf16[64,512]{1,0:T(8,128)(2,1)S(1)} %get-tuple-element.157), channel_id=1, source_target_pairs={{0,1},{1,2},{2,3},{4,5},{5,6},{6,7},{8,9},{9,10},{10,11},{12,13},{... | collective-permute-start | bytes 196616 | tf_op jit(solution)/shard_map/ppermute | solution.py:833
  17.2 11.0 %collective-permute-start.8 = (bf16[4,128,384]{2,1,0:T(8,128)(2,1)S(1)}, bf16[4,128,384]{2,1,0:T(8,128)(2,1)S(1)}, u32[]{:S(2)}, u32[]{:S(2)}) collective-permute-start(bf16[4,128,384]{2,1,0:T(8,128)(2,1)S(1)} %pad_maximum_fusion.1.refs_0_), channel_id=1, source_target_pairs={{0,8},{4,20},{8,0},{12,28},{16,24},{20,4},{24,16},{28,12},{1,9},{5... | collective-permute-start | bytes 1179656 | tf_op jit(solution)/shard_map/ppermute | solution.py:827
  18.7 10.0 %collective-permute-start.5 = (bf16[144,512]{1,0:T(8,128)(2,1)S(1)}, bf16[144,512]{1,0:T(8,128)(2,1)S(1)}, u32[]{:S(2)}, u32[]{:S(2)}) collective-permute-start(bf16[144,512]{1,0:T(8,128)(2,1)S(1)} %pad_maximum_fusion.2), channel_id=1, source_target_pairs={{0,1},{1,0},{2,3},{3,2},{4,5},{5,4},{6,7},{7,6},{8,9},{9,8},{10,11... | collective-permute-start | bytes 442376 | tf_op jit(solution)/shard_map/ppermute | solution.py:836
  20.7 12.1 %collective-permute-start.6 = (bf16[144,512]{1,0:T(8,128)(2,1)S(1)}, bf16[144,512]{1,0:T(8,128)(2,1)S(1)}, u32[]{:S(2)}, u32[]{:S(2)}) collective-permute-start(bf16[144,512]{1,0:T(8,128)(2,1)S(1)} %pad_maximum_fusion.2), channel_id=1, source_target_pairs={{0,2},{1,3},{2,0},{3,1},{4,6},{5,7},{6,4},{7,5},{8,10},{9,11},{10,... | collective-permute-start | bytes 442376 | tf_op jit(solution)/shard_map/ppermute | solution.py:836
  22.2 10.6 %collective-permute-start.7 = (bf16[144,512]{1,0:T(8,128)(2,1)S(1)}, bf16[144,512]{1,0:T(8,128)(2,1)S(1)}, u32[]{:S(2)}, u32[]{:S(2)}) collective-permute-start(bf16[144,512]{1,0:T(8,128)(2,1)S(1)} %pad_maximum_fusion.2), channel_id=1, source_target_pairs={{0,3},{1,2},{2,1},{3,0},{4,7},{5,6},{6,5},{7,4},{8,11},{9,10},{10,... | collective-permute-start | bytes 442376 | tf_op jit(solution)/shard_map/ppermute | solution.py:836
  28.1 7.6 %collective-permute-start.9 = (bf16[4,128,384]{2,1,0:T(8,128)(2,1)S(1)}, bf16[4,128,384]{2,1,0:T(8,128)(2,1)S(1)}, u32[]{:S(2)}, u32[]{:S(2)}) collective-permute-start(bf16[4,128,384]{2,1,0:T(8,128)(2,1)S(1)} %pad_maximum_fusion.1.refs_0_), channel_id=1, source_target_pairs={{0,4},{4,0},{8,12},{12,8},{16,20},{20,16},{24,28},{28,24},{1,5},{5... | collective-permute-start | bytes 1179656 | tf_op jit(solution)/shard_map/ppermute | solution.py:830
  28.2 7.6 %collective-permute-start.10 = (bf16[4,128,384]{2,1,0:T(8,128)(2,1)S(1)}, bf16[4,128,384]{2,1,0:T(8,128)(2,1)S(1)}, u32[]{:S(2)}, u32[]{:S(2)}) collective-permute-start(bf16[4,128,384]{2,1,0:T(8,128)(2,1)S(1)} %collective-permute-done.8.refs_1_), channel_id=1, source_target_pairs={{0,4},{4,0},{8,12},{12,8},{16,20},{20,16},{24,28},{28,24},{1,5},{5... | collective-permute-start | bytes 1179656 | tf_op jit(solution)/shard_map/ppermute | solution.py:830
  32.9 15.0 %collective-permute-start.12 = (bf16[4,144,512]{2,1,0:T(8,128)(2,1)S(1)}, bf16[4,144,512]{2,1,0:T(8,128)(2,1)S(1)}, u32[]{:S(2)}, u32[]{:S(2)}) collective-permute-start(bf16[4,144,512]{2,1,0:T(8,128)(2,1)S(1)} %pad_maximum_fusion.refs_0_), channel_id=1, source_target_pairs={{0,8},{4,20},{8,0},{12,28},{16,24},{20,4},{24,16},{28,12},{1,9},{5... | collective-permute-start | bytes 1769480 | tf_op jit(solution)/shard_map/ppermute | solution.py:827
  34.5 13.9 %collective-permute-start.14 = (bf16[4,144,512]{2,1,0:T(8,128)(2,1)S(1)}, bf16[4,144,512]{2,1,0:T(8,128)(2,1)}, u32[]{:S(2)}, u32[]{:S(2)}) collective-permute-start(bf16[4,144,512]{2,1,0:T(8,128)(2,1)S(1)} %pad_maximum_fusion.refs_0_), channel_id=1, source_target_pairs={{0,16},{4,12},{8,24},{12,4},{16,0},{20,28},{24,8},{28,20},{1,17},{... | collective-permute-start | bytes 1769480 | tf_op jit(solution)/shard_map/ppermute | solution.py:827
  43.7 12.7 %collective-permute-start.17 = (bf16[4,144,128]{2,1,0:T(8,128)(2,1)S(1)}, bf16[4,144,128]{2,1,0:T(8,128)(2,1)S(1)}, u32[]{:S(2)}, u32[]{:S(2)}) collective-permute-start(bf16[4,144,128]{2,1,0:T(8,128)(2,1)S(1)} %get-tuple-element.90.h0), channel_id=1, source_target_pairs={{0,2},{1,3},{2,0},{3,1},{4,6},{5,7},{6,4},{7,5},{8,10},{9,11},{10,... | collective-permute-start | bytes 442376 | tf_op jit(solution)/shard_map/ppermute | solution.py:836
  45.0 11.4 %collective-permute-start.18 = (bf16[4,144,128]{2,1,0:T(8,128)(2,1)S(1)}, bf16[4,144,128]{2,1,0:T(8,128)(2,1)S(1)}, u32[]{:S(2)}, u32[]{:S(2)}) collective-permute-start(bf16[4,144,128]{2,1,0:T(8,128)(2,1)S(1)} %get-tuple-element.90.h0), channel_id=1, source_target_pairs={{0,3},{1,2},{2,1},{3,0},{4,7},{5,6},{6,5},{7,4},{8,11},{9,10},{10,... | collective-permute-start | bytes 442376 | tf_op jit(solution)/shard_map/ppermute | solution.py:836
  47.9 10.9 %collective-permute-start.11 = (bf16[4,144,512]{2,1,0:T(8,128)(2,1)S(1)}, bf16[4,144,512]{2,1,0:T(8,128)(2,1)S(1)}, u32[]{:S(2)}, u32[]{:S(2)}) collective-permute-start(bf16[4,144,512]{2,1,0:T(8,128)(2,1)S(1)} %pad_maximum_fusion.refs_0_), channel_id=1, source_target_pairs={{0,4},{4,0},{8,12},{12,8},{16,20},{20,16},{24,28},{28,24},{1,5},{5... | collective-permute-start | bytes 1769480 | tf_op jit(solution)/shard_map/ppermute | solution.py:830
  47.9 10.9 %collective-permute-start.13 = (bf16[4,144,512]{2,1,0:T(8,128)(2,1)S(1)}, bf16[4,144,512]{2,1,0:T(8,128)(2,1)S(1)}, u32[]{:S(2)}, u32[]{:S(2)}) collective-permute-start(bf16[4,144,512]{2,1,0:T(8,128)(2,1)S(1)} %collective-permute-done.12.refs_1_), channel_id=1, source_target_pairs={{0,4},{4,0},{8,12},{12,8},{16,20},{20,16},{24,28},{28,24},{1,5},{5... | collective-permute-start | bytes 1769480 | tf_op jit(solution)/shard_map/ppermute | solution.py:830
  48.4 10.5 %collective-permute-start.15 = (bf16[4,144,512]{2,1,0:T(8,128)(2,1)}, bf16[4,144,512]{2,1,0:T(8,128)(2,1)}, u32[]{:S(2)}, u32[]{:S(2)}) collective-permute-start(bf16[4,144,512]{2,1,0:T(8,128)(2,1)} %collective-permute-done.14.refs_2_), channel_id=1, source_target_pairs={{0,4},{4,0},{8,12},{12,8},{16,20},{20,16},{24,28},{28,24},{1,5},{5... | collective-permute-start | bytes 1769480 | tf_op jit(solution)/shard_map/ppermute | solution.py:830
  57.0 12.7 %collective-permute-start.19 = (bf16[4,144,512]{2,1,0:T(8,128)(2,1)S(1)}, bf16[4,144,512]{2,1,0:T(8,128)(2,1)}, u32[]{:S(2)}, u32[]{:S(2)}) collective-permute-start(bf16[4,144,512]{2,1,0:T(8,128)(2,1)S(1)} %collective-permute-done.12.refs_1_), channel_id=1, source_target_pairs={{0,16},{4,12},{8,24},{12,4},{16,0},{20,28},{24,8},{28,20},{1,17},{... | collective-permute-start | bytes 1769480 | tf_op jit(solution)/shard_map/ppermute | solution.py:827
  65.3 26.5 %all-to-all-start = ((bf16[8,4,192,128]{3,2,1,0:T(8,128)(2,1)}), bf16[8,4,192,128]{3,2,1,0:T(8,128)(2,1)}, u32[]{:S(2)}, u32[]{:S(2)}) async-start(bf16[8,4,192,128]{3,2,1,0:T(8,128)(2,1)} %shard_map.238), calls=%async_computation | async-start | bytes 3145728 | tf_op jit(solution)/shard_map/all_to_all | solution.py:839
  91.8 13.0 %collective-permute-start.21 = (bf16[4,576,512]{2,1,0:T(8,128)(2,1)}, bf16[4,576,512]{2,1,0:T(8,128)(2,1)S(1)}, u32[]{:S(2)}, u32[]{:S(2)}) collective-permute-start(bf16[4,576,512]{2,1,0:T(8,128)(2,1)} %get-tuple-element.100), channel_id=1, source_target_pairs={{0,4},{4,0},{8,12},{12,8},{16,20},{20,16},{24,28},{28,24},{1,5},{5... | collective-permute-start | bytes 7077896 | tf_op jit(solution)/shard_map/ppermute | solution.py:830
  93.6 11.2 %collective-permute-start.23 = (bf16[4,176,128]{2,1,0:T(8,128)(2,1)S(1)}, bf16[4,176,128]{2,1,0:T(8,128)(2,1)S(1)}, u32[]{:S(2)}, u32[]{:S(2)}) collective-permute-start(bf16[4,176,128]{2,1,0:T(8,128)(2,1)S(1)} %get-tuple-element.102), channel_id=1, source_target_pairs={{0,3},{1,2},{2,1},{3,0},{4,7},{5,6},{6,5},{7,4},{8,11},{9,10},{10,... | collective-permute-start | bytes 540680 | tf_op jit(solution)/shard_map/ppermute | solution.py:836
  105.3 16.3 %collective-permute-start.25 = (bf16[4,576,256]{2,1,0:T(8,128)(2,1)S(1)}, bf16[4,576,256]{2,1,0:T(8,128)(2,1)S(1)}, u32[]{:S(2)}, u32[]{:S(2)}) collective-permute-start(bf16[4,576,256]{2,1,0:T(8,128)(2,1)S(1)} %get-tuple-element.104), channel_id=1, source_target_pairs={{0,8},{4,20},{8,0},{12,28},{16,24},{20,4},{24,16},{28,12},{1,9},{5... | collective-permute-start | bytes 3538952 | tf_op jit(solution)/shard_map/ppermute | solution.py:827
  107.0 9.0 %collective-permute-start.24 = (bf16[4,176,128]{2,1,0:T(8,128)(2,1)S(1)}, bf16[4,176,128]{2,1,0:T(8,128)(2,1)S(1)}, u32[]{:S(2)}, u32[]{:S(2)}) collective-permute-start(bf16[4,176,128]{2,1,0:T(8,128)(2,1)S(1)} %get-tuple-element.101.s0), channel_id=1, source_target_pairs={{0,2},{1,3},{2,0},{3,1},{4,6},{5,7},{6,4},{7,5},{8,10},{9,11},{10,... | collective-permute-start | bytes 540680 | tf_op jit(solution)/shard_map/ppermute | solution.py:836
  121.9 15.5 %collective-permute-start.27 = (bf16[4,576,128]{2,1,0:T(8,128)(2,1)S(1)}, bf16[4,576,128]{2,1,0:T(8,128)(2,1)S(1)}, u32[]{:S(2)}, u32[]{:S(2)}) collective-permute-start(bf16[4,576,128]{2,1,0:T(8,128)(2,1)S(1)} %get-tuple-element.123), channel_id=1, source_target_pairs={{0,16},{4,12},{8,24},{12,4},{16,0},{20,28},{24,8},{28,20},{1,17},{... | collective-permute-start | bytes 1769480 | tf_op jit(solution)/shard_map/ppermute | solution.py:827
  125.3 10.3 %collective-permute-start.28 = (bf16[4,192,256]{2,1,0:T(8,128)(2,1)S(1)}, bf16[4,192,256]{2,1,0:T(8,128)(2,1)S(1)}, u32[]{:S(2)}, u32[]{:S(2)}) collective-permute-start(bf16[4,192,256]{2,1,0:T(8,128)(2,1)S(1)} %get-tuple-element.115), channel_id=1, source_target_pairs={{0,8},{4,20},{8,0},{12,28},{16,24},{20,4},{24,16},{28,12},{1,9},{5... | collective-permute-start | bytes 1179656 | tf_op jit(solution)/shard_map/ppermute | solution.py:827
  138.0 8.4 %collective-permute-start.30 = (bf16[1,576,128]{2,1,0:T(8,128)(2,1)S(1)}, bf16[1,576,128]{2,1,0:T(8,128)(2,1)S(1)}, u32[]{:S(2)}, u32[]{:S(2)}) collective-permute-start(bf16[1,576,128]{2,1,0:T(8,128)(2,1)S(1)} %get-tuple-element.133), channel_id=1, source_target_pairs={{0,1},{1,0},{2,3},{3,2},{4,5},{5,4},{6,7},{7,6},{8,9},{9,8},{10,11... | collective-permute-start | bytes 442376 | tf_op jit(solution)/shard_map/ppermute | solution.py:836
  138.1 14.0 %collective-permute-start.31 = (bf16[1,576,128]{2,1,0:T(8,128)(2,1)S(1)}, bf16[1,576,128]{2,1,0:T(8,128)(2,1)S(1)}, u32[]{:S(2)}, u32[]{:S(2)}) collective-permute-start(bf16[1,576,128]{2,1,0:T(8,128)(2,1)S(1)} %get-tuple-element.134), channel_id=1, source_target_pairs={{0,2},{1,3},{2,0},{3,1},{4,6},{5,7},{6,4},{7,5},{8,10},{9,11},{10,... | collective-permute-start | bytes 442376 | tf_op jit(solution)/shard_map/ppermute | solution.py:836
  140.1 12.0 %collective-permute-start.32 = (bf16[1,576,128]{2,1,0:T(8,128)(2,1)S(1)}, bf16[1,576,128]{2,1,0:T(8,128)(2,1)S(1)}, u32[]{:S(2)}, u32[]{:S(2)}) collective-permute-start(bf16[1,576,128]{2,1,0:T(8,128)(2,1)S(1)} %get-tuple-element.135), channel_id=1, source_target_pairs={{0,3},{1,2},{2,1},{3,0},{4,7},{5,6},{6,5},{7,4},{8,11},{9,10},{10,... | collective-permute-start | bytes 442376 | tf_op jit(solution)/shard_map/ppermute | solution.py:836
  153.2 9.2 %collective-permute-start.33 = (bf16[1152,128]{1,0:T(8,128)(2,1)S(1)}, bf16[1152,128]{1,0:T(8,128)(2,1)S(1)}, u32[]{:S(2)}, u32[]{:S(2)}) collective-permute-start(bf16[1152,128]{1,0:T(8,128)(2,1)S(1)} %shard_map.253.refs_0_), channel_id=1, source_target_pairs={{0,8},{4,20},{8,0},{12,28},{16,24},{20,4},{24,16},{28,12},{1,9},{5... | collective-permute-start | bytes 884744 | tf_op jit(solution)/shard_map/ppermute | solution.py:827
  154.5 8.0 %collective-permute-start.34 = (bf16[1152,128]{1,0:T(8,128)(2,1)S(1)}, bf16[1152,128]{1,0:T(8,128)(2,1)S(1)}, u32[]{:S(2)}, u32[]{:S(2)}) collective-permute-start(bf16[1152,128]{1,0:T(8,128)(2,1)S(1)} %shard_map.253.refs_0_), channel_id=1, source_target_pairs={{0,16},{4,12},{8,24},{12,4},{16,0},{20,28},{24,8},{28,20},{1,17},{... | collective-permute-start | bytes 884744 | tf_op jit(solution)/shard_map/ppermute | solution.py:827
  155.3 7.2 %collective-permute-start.35 = (bf16[1,224,128]{2,1,0:T(8,128)(2,1)S(1)}, bf16[1,224,128]{2,1,0:T(8,128)(2,1)S(1)}, u32[]{:S(2)}, u32[]{:S(2)}) collective-permute-start(bf16[1,224,128]{2,1,0:T(8,128)(2,1)S(1)} %get-tuple-element.137), channel_id=1, source_target_pairs={{0,1},{1,0},{2,3},{3,2},{4,5},{5,4},{6,7},{7,6},{8,9},{9,8},{10,11... | collective-permute-start | bytes 172040 | tf_op jit(solution)/shard_map/ppermute | solution.py:836
  165.3 7.0 %collective-permute-start.38 = (bf16[1152,128]{1,0:T(8,128)(2,1)S(1)}, bf16[1152,128]{1,0:T(8,128)(2,1)S(1)}, u32[]{:S(2)}, u32[]{:S(2)}) collective-permute-start(bf16[1152,128]{1,0:T(8,128)(2,1)S(1)} %collective-permute-done.33.refs_1_), channel_id=1, source_target_pairs={{0,16},{4,12},{8,24},{12,4},{16,0},{20,28},{24,8},{28,20},{1,17},{... | collective-permute-start | bytes 884744 | tf_op jit(solution)/shard_map/ppermute | solution.py:827
  (40 other events, 310.4 us)

commit v9 on v8

--- a/solution.py
+++ b/solution.py
@@ -1051,7 +1051,6 @@
     z_m[0] = after(z_m[0], part_q[0])
     fresh_m = updated(z_m, n_m, nb_q, 0)
     m_x, m_y = swap(fresh_m, 0), swap(fresh_m, 1)
-    z_q[0] = after(z_q[0], m_x, m_y)
     fresh_q = updated(z_q, n_q, 0, n_q + 2 * n_ng)
     q_x, q_y = swap(fresh_q, 0), swap(fresh_q, 1)
     m_bufs = both_cores([fresh_m, m_x, m_y, swap(after(m_x, fresh_q), 1)])

time: 186 us -> 186 us (level)
  starting transfers between devices: 60.9 us -> 59 us
where the time goes in v9:
time: 186 us
  Pallas kernels  70.1 us (38%)
  starting transfers between devices  59 us (32%)
  waiting for transfers between devices  49.5 us (27%)
  local copies, waits for them, and re-layouts  4.34 us (2%)
  between operations  2.1 us (1%)
    pallas_call x19, Pallas kernels, fixed(): run(*[pltpu.with_memory_space_constraint(x, pltpu.HBM) if spec is HB else...  70.1 us
    ppermute x18, waiting for transfers between devices, swap_mp(): return lax.ppermute(x, 'mp', [(i, i ^ mask) for i in range(groups)])  35.8 us
    ppermute x18, starting transfers between devices, swap_mp(): return lax.ppermute(x, 'mp', [(i, i ^ mask) for i in range(groups)])  29.2 us
    ppermute x14, starting transfers between devices, swap(): lax.ppermute(x, 'dp', [(i, i ^ 1 << order[i & 1][s]) for i in range(ndp)])  18.2 us
    ppermute x14, waiting for transfers between devices, swap(): lax.ppermute(x, 'dp', [(i, i ^ 1 << order[i & 1][s]) for i in range(ndp)])  6.47 us
    ppermute x16, waiting for transfers between devices, swap_core(): return lax.ppermute(x, 'dp', [(i, i ^ 1) for i in range(ndp)])  5.36 us
    all_to_all x1, starting transfers between devices, exchange(): return lax.all_to_all(x, axis, 0, 0, tiled=True)  4.49 us
    ppermute x2, starting transfers between devices, from_mp(): lax.ppermute(x, 'mp', [(i, i + step) for i in range(groups) if 0 <= i + s...  4.1 us
  transfers between devices with their start and end apart: 51, of which 19 were waited for; matrix products, arithmetic and copies ran while one was open for 2% of the time, Pallas kernels for 34%

profile of v9, /device:TPU:0, one launch (start us, length us, event | category | flops | bytes accessed | tf_op | source)
XLA Modules:
  0.0 185.5 jit_solution(8560941859415846484)
XLA Ops:
  1.7 3.1 %collective-permute-start.2 = (bf16[128,384]{1,0:T(8,128)(2,1)S(1)}, bf16[128,384]{1,0:T(8,128)(2,1)S(1)}, u32[]{:S(2)}, u32[]{:S(2)}) collective-permute-start(bf16[128,384]{1,0:T(8,128)(2,1)S(1)} %constant_dynamic-slice_fusion), channel_id=1, source_target_pairs={{0,1},{1,0},{2,3},{3,2},{4,5},{5,4},{6,7},{7,6},{8,9},{9,8},{10,11... | collective-permute-start | bytes 294920 | tf_op jit(solution)/shard_map/ppermute | solution.py:836
  4.7 2.6 %collective-permute-start.3 = (bf16[128,384]{1,0:T(8,128)(2,1)S(1)}, bf16[128,384]{1,0:T(8,128)(2,1)S(1)}, u32[]{:S(2)}, u32[]{:S(2)}) collective-permute-start(bf16[128,384]{1,0:T(8,128)(2,1)S(1)} %constant_dynamic-slice_fusion), channel_id=1, source_target_pairs={{0,2},{1,3},{2,0},{3,1},{4,6},{5,7},{6,4},{7,5},{8,10},{9,11},{10,... | collective-permute-start | bytes 294920 | tf_op jit(solution)/shard_map/ppermute | solution.py:836
  8.2 2.8 %collective-permute-start = (bf16[64,512]{1,0:T(8,128)(2,1)S(1)}, bf16[64,512]{1,0:T(8,128)(2,1)S(1)}, u32[]{:S(2)}, u32[]{:S(2)}) collective-permute-start(bf16[64,512]{1,0:T(8,128)(2,1)S(1)} %get-tuple-element.155), channel_id=1, source_target_pairs={{0,1},{1,2},{2,3},{4,5},{5,6},{6,7},{8,9},{9,10},{10,11},{12,13},{... | collective-permute-start | bytes 196616 | tf_op jit(solution)/shard_map/ppermute | solution.py:833
  15.4 1.8 collective-permute-done.1.right
  18.7 2.0 %collective-permute-start.5 = (bf16[144,512]{1,0:T(8,128)(2,1)S(1)}, bf16[144,512]{1,0:T(8,128)(2,1)S(1)}, u32[]{:S(2)}, u32[]{:S(2)}) collective-permute-start(bf16[144,512]{1,0:T(8,128)(2,1)S(1)} %pad_maximum_fusion.2), channel_id=1, source_target_pairs={{0,1},{1,0},{2,3},{3,2},{4,5},{5,4},{6,7},{7,6},{8,9},{9,8},{10,11... | collective-permute-start | bytes 442376 | tf_op jit(solution)/shard_map/ppermute | solution.py:836
  23.6 2.5 %shard_map.238 = bf16[8,4,192,128]{3,2,1,0:T(8,128)(2,1)} custom-call(f32[1536,128]{1,0:T(8,128)} %bitcast.39, f32[1536,128]{1,0:T(8,128)} %bitcast.40, f32[1536,128]{1,0:T(8,128)} %bitcast.41), custom_call_target="tpu_custom_call" | custom-call | flops 1048576 | bytes 4194304 | tf_op jit(solution)/shard_map/pallas_call | solution.py:55
  26.2 1.9 %shard_map.239.a1e_h = bf16[640,512]{1,0:T(8,128)(2,1)} custom-call(bf16[512,512]{1,0:T(8,128)(2,1)S(1)} %bitcast.37, bf16[64,512]{1,0:T(8,128)(2,1)S(1)} %collective-permute-done.left, bf16[64,512]{1,0:T(8,128)(2,1)S(1)} %collective-permute-done.1.right, f32[2,512]{1,0:T(2,128)S(1)} %copy-done.8, f32[2,512]{1,0:T(2,128)S(1)} %copy-done.9), custom_call_target="tpu_custom_call" | custom-call | flops 2097152 | bytes 1048576 | tf_op jit(solution)/shard_map/pallas_call | solution.py:55
  28.7 4.1 %collective-permute-done.6 = bf16[144,512]{1,0:T(8,128)(2,1)S(1)} collective-permute-done((bf16[144,512]{1,0:T(8,128)(2,1)S(1)}, bf16[144,512]{1,0:T(8,128)(2,1)S(1)}, u32[]{:S(2)}, u32[]{:S(2)}) %collective-permute-start.6) | collective-permute-done | bytes 147488 | tf_op jit(solution)/shard_map/ppermute | solution.py:836
  35.8 5.6 %shard_map.240 = (bf16[4,640,384]{2,1,0:T(8,128)(2,1)}, bf16[4,144,128]{2,1,0:T(8,128)(2,1)S(1)}) custom-call(s32[18]{0:T(128)S(1)} %stack.97.meta, bf16[640,512]{1,0:T(8,128)(2,1)} %shard_map.239.a1e_h, bf16[4,128,384]{2,1,0:T(8,128)(2,1)S(1)} %pad_maximum_fusion.1.refs_0_, bf16[4,128,384]{2,1,0:T(8,128)(2,1)S(1)} %collective-permute-done.8.refs_1_, ...), custom_call_target="tpu_custom_call" | custom-call | flops 1006632960 | bytes 6291456 | tf_op jit(solution)/shard_map/pallas_call | solution.py:55
  41.5 2.2 %collective-permute-start.16 = (bf16[4,144,128]{2,1,0:T(8,128)(2,1)S(1)}, bf16[4,144,128]{2,1,0:T(8,128)(2,1)S(1)}, u32[]{:S(2)}, u32[]{:S(2)}) collective-permute-start(bf16[4,144,128]{2,1,0:T(8,128)(2,1)S(1)} %get-tuple-element.89.h0), channel_id=1, source_target_pairs={{0,1},{1,0},{2,3},{3,2},{4,5},{5,4},{6,7},{7,6},{8,9},{9,8},{10,11... | collective-permute-start | bytes 442376 | tf_op jit(solution)/shard_map/ppermute | solution.py:836
  48.5 7.9 %collective-permute-done.17.h2 = bf16[4,144,128]{2,1,0:T(8,128)(2,1)S(1)} collective-permute-done((bf16[4,144,128]{2,1,0:T(8,128)(2,1)S(1)}, bf16[4,144,128]{2,1,0:T(8,128)(2,1)S(1)}, u32[]{:S(2)}, u32[]{:S(2)}) %collective-permute-start.17) | collective-permute-done | bytes 147488 | tf_op jit(solution)/shard_map/ppermute | solution.py:836
  58.9 6.3 %shard_map.241.near_h = f32[512,512]{1,0:T(8,128)} custom-call(s32[18]{0:T(128)S(1)} %stack.97.meta, bf16[4,640,384]{2,1,0:T(8,128)(2,1)} %get-tuple-element.90.qkv_h), custom_call_target="tpu_custom_call" | custom-call | flops 536870912 | bytes 12582912 | tf_op jit(solution)/shard_map/pallas_call | solution.py:55
  65.3 4.5 %all-to-all-start = ((bf16[8,4,192,128]{3,2,1,0:T(8,128)(2,1)}), bf16[8,4,192,128]{3,2,1,0:T(8,128)(2,1)}, u32[]{:S(2)}, u32[]{:S(2)}) async-start(bf16[8,4,192,128]{3,2,1,0:T(8,128)(2,1)} %shard_map.238), calls=%async_computation | async-start | bytes 3145728 | tf_op jit(solution)/shard_map/all_to_all | solution.py:839
  70.0 2.1 %collective-permute-done.20.refs_7_ = bf16[4,144,512]{2,1,0:T(8,128)(2,1)S(1)} collective-permute-done((bf16[4,144,512]{2,1,0:T(8,128)(2,1)}, bf16[4,144,512]{2,1,0:T(8,128)(2,1)S(1)}, u32[]{:S(2)}, u32[]{:S(2)}) %collective-permute-start.20) | collective-permute-done | bytes 589856 | tf_op jit(solution)/shard_map/ppermute | solution.py:830
  72.1 19.7 %shard_map.242 = (bf16[512,512]{1,0:T(8,128)(2,1)}, bf16[4,176,128]{2,1,0:T(8,128)(2,1)S(1)}, bf16[4,176,128]{2,1,0:T(8,128)(2,1)S(1)}, f32[512,512]{1,0:T(8,128...) custom-call(s32[18]{0:T(128)S(1)} %stack.97.meta, ...), custom_call_target="tpu_custom_call" | custom-call | flops 6442450944 | bytes 25165824 | tf_op jit(solution)/shard_map/pallas_call | solution.py:55
  93.6 2.6 %collective-permute-start.23 = (bf16[4,176,128]{2,1,0:T(8,128)(2,1)S(1)}, bf16[4,176,128]{2,1,0:T(8,128)(2,1)S(1)}, u32[]{:S(2)}, u32[]{:S(2)}) collective-permute-start(bf16[4,176,128]{2,1,0:T(8,128)(2,1)S(1)} %get-tuple-element.101), channel_id=1, source_target_pairs={{0,3},{1,2},{2,1},{3,0},{4,7},{5,6},{6,5},{7,4},{8,11},{9,10},{10,... | collective-permute-start | bytes 540680 | tf_op jit(solution)/shard_map/ppermute | solution.py:836
  96.2 1.9 %shard_map.243.refs_4_ = f32[8,3,192,128]{3,2,1,0:T(8,128)S(1)} custom-call(bf16[8,4,192,128]{3,2,1,0:T(8,128)(2,1)} %all-to-all-done.recv_h), custom_call_target="tpu_custom_call" | custom-call | flops 1048576 | bytes 4194304 | tf_op jit(solution)/shard_map/pallas_call | solution.py:55
  98.9 5.9 %collective-permute-done.23.three.s3 = bf16[4,176,128]{2,1,0:T(8,128)(2,1)S(1)} collective-permute-done((bf16[4,176,128]{2,1,0:T(8,128)(2,1)S(1)}, bf16[4,176,128]{2,1,0:T(8,128)(2,1)S(1)}, u32[]{:S(2)}, u32[]{:S(2)}) %collective-permute-start.23) | collective-permute-done | bytes 180256 | tf_op jit(solution)/shard_map/ppermute | solution.py:836
  105.3 1.7 collective-permute-start.25
  107.6 6.9 %shard_map.245 = (bf16[512,512]{1,0:T(8,128)(2,1)S(1)}, f32[512,512]{1,0:T(8,128)S(1)}, f32[512,512]{1,0:T(8,128)S(1)}) custom-call(s32[18]{0:T(128)S(1)} %stack.97.meta, bf16[4,640,384]{2,1,0:T(8,128)(2,1)} %get-tuple-element.90.qkv_h, bf16[512,512]{1,0:T(8,128)(2,1)} %get-tuple-element.104.dctx_h, bf16[4,176,128]{2,1,0:T(8,128)(2,1)S(1)} %collective-permute-done.22.one.s1, ...), custom_call_target="tpu_custom_call" | custom-call | flops 1073741824 | bytes 25165824 | tf_op jit(solution)/shard_map/pallas_call | solution.py:55
  116.0 5.6 %shard_map.246 = (bf16[4,512,384]{2,1,0:T(8,128)(2,1)}, f32[4,192,512]{2,1,0:T(8,128)S(1)}, f32[4,192,512]{2,1,0:T(8,128)S(1)}) custom-call(s32[18]{0:T(128)S(1)} %stack.97.meta, bf16[4,640,384]{2,1,0:T(8,128)(2,1)} %get-tuple-element.90.qkv_h, bf16[512,512]{1,0:T(8,128)(2,1)S(1)} %get-tuple-element.107.dq, f32[512,512]{1,0:T(8,128)S(1)} %get-tuple-element.108.dkn, ...), custom_call_target="tpu_custom_call" | custom-call | flops 805306368 | bytes 25165824 | tf_op jit(solution)/shard_map/pallas_call | solution.py:55
  126.9 7.1 %shard_map.248 = (f32[512,512]{1,0:T(8,128)}, f32[16,128]{1,0:T(8,128)S(1)}) custom-call(s32[18]{0:T(128)S(1)} %stack.97.meta, bf16[4,512,384]{2,1,0:T(8,128)(2,1)} %get-tuple-element.115.dproj_h, bf16[512,512]{1,0:T(8,128)(2,1)S(1)} %bitcast.38, f32[512,512]{1,0:T(8,128)} %get-tuple-element.116.dx2_h, f32[2,512]{1,0:T(2,128)S(1)} %copy-done.8, ...), custom_call_target="tpu_custom_call" | custom-call | flops 805306368 | bytes 8388608 | tf_op jit(solution)/shard_map/pallas_call | solution.py:55
  135.7 1.6 collective-permute-start.29
  138.1 2.0 %collective-permute-start.31 = (bf16[1,576,128]{2,1,0:T(8,128)(2,1)S(1)}, bf16[1,576,128]{2,1,0:T(8,128)(2,1)S(1)}, u32[]{:S(2)}, u32[]{:S(2)}) collective-permute-start(bf16[1,576,128]{2,1,0:T(8,128)(2,1)S(1)} %get-tuple-element.133), channel_id=1, source_target_pairs={{0,2},{1,3},{2,0},{3,1},{4,6},{5,7},{6,4},{7,5},{8,10},{9,11},{10,... | collective-permute-start | bytes 442376 | tf_op jit(solution)/shard_map/ppermute | solution.py:836
  140.1 2.3 %collective-permute-start.32 = (bf16[1,576,128]{2,1,0:T(8,128)(2,1)S(1)}, bf16[1,576,128]{2,1,0:T(8,128)(2,1)S(1)}, u32[]{:S(2)}, u32[]{:S(2)}) collective-permute-start(bf16[1,576,128]{2,1,0:T(8,128)(2,1)S(1)} %get-tuple-element.134), channel_id=1, source_target_pairs={{0,3},{1,2},{2,1},{3,0},{4,7},{5,6},{6,5},{7,4},{8,11},{9,10},{10,... | collective-permute-start | bytes 442376 | tf_op jit(solution)/shard_map/ppermute | solution.py:836
  143.0 3.4 %collective-permute-done.30.refs_1_ = bf16[1,576,128]{2,1,0:T(8,128)(2,1)S(1)} collective-permute-done((bf16[1,576,128]{2,1,0:T(8,128)(2,1)S(1)}, bf16[1,576,128]{2,1,0:T(8,128)(2,1)S(1)}, u32[]{:S(2)}, u32[]{:S(2)}) %collective-permute-start.30) | collective-permute-done | bytes 147488 | tf_op jit(solution)/shard_map/ppermute | solution.py:836
  146.4 5.7 %collective-permute-done.31.refs_2_ = bf16[1,576,128]{2,1,0:T(8,128)(2,1)S(1)} collective-permute-done((bf16[1,576,128]{2,1,0:T(8,128)(2,1)S(1)}, bf16[1,576,128]{2,1,0:T(8,128)(2,1)S(1)}, u32[]{:S(2)}, u32[]{:S(2)}) %collective-permute-start.31) | collective-permute-done | bytes 147488 | tf_op jit(solution)/shard_map/ppermute | solution.py:836
  154.5 2.1 %collective-permute-start.35 = (bf16[1,224,128]{2,1,0:T(8,128)(2,1)S(1)}, bf16[1,224,128]{2,1,0:T(8,128)(2,1)S(1)}, u32[]{:S(2)}, u32[]{:S(2)}) collective-permute-start(bf16[1,224,128]{2,1,0:T(8,128)(2,1)S(1)} %get-tuple-element.135), channel_id=1, source_target_pairs={{0,1},{1,0},{2,3},{3,2},{4,5},{5,4},{6,7},{7,6},{8,9},{9,8},{10,11... | collective-permute-start | bytes 172040 | tf_op jit(solution)/shard_map/ppermute | solution.py:836
  160.4 3.7 %collective-permute-done.36.refs_2_ = bf16[1,224,128]{2,1,0:T(8,128)(2,1)S(1)} collective-permute-done((bf16[1,224,128]{2,1,0:T(8,128)(2,1)S(1)}, bf16[1,224,128]{2,1,0:T(8,128)(2,1)S(1)}, u32[]{:S(2)}, u32[]{:S(2)}) %collective-permute-start.36) | collective-permute-done | bytes 57376 | tf_op jit(solution)/shard_map/ppermute | solution.py:836
  168.0 4.9 %collective-permute-done.43.refs_1_ = bf16[608,128]{1,0:T(8,128)(2,1)S(1)} collective-permute-done((bf16[608,128]{1,0:T(8,128)(2,1)S(1)}, bf16[608,128]{1,0:T(8,128)(2,1)S(1)}, u32[]{:S(2)}, u32[]{:S(2)}) %collective-permute-start.43) | collective-permute-done | bytes 155680 | tf_op jit(solution)/shard_map/ppermute | solution.py:827
  175.3 3.4 %shard_map.255 = (bf16[128,512]{1,0:T(8,128)(2,1)}, bf16[512,512]{1,0:T(8,128)(2,1)}, bf16[512,512]{1,0:T(8,128)(2,1)}, f32[4,24,2,8,128]{4,3,2,1,0:T(8,128)}) custom-call(s32[18]{0:T(128)S(1)} %stack.97.meta, s32[192]{0:T(256)S(1)} %get-tuple-element.153.blocks, bf16[1152,128]{1,0:T(8,128)(2,1)S(1)} %shard_map.253.refs_0_, ...), custom_call_target="tpu_custom_call" | custom-call | flops 1048576 | bytes 4194304 | tf_op jit(solution)/shard_map/pallas_call | solution.py:55
  180.2 5.1 %shard_map.256 = (f32[24,64,128]{2,1,0:T(8,128)}, f32[24,64,128]{2,1,0:T(8,128)}, f32[24,64,128]{2,1,0:T(8,128)}, bf16[512,384]{1,0:T(8,128)(2,1)}, f32[4,512]{1...) custom-call(s32[18]{0:T(128)S(1)} %stack.97.meta, s32[192]{0:T(256)S(1)} %get-tuple-element.152.counts, ...), custom_call_target="tpu_custom_call" | custom-call | flops 1048576 | bytes 8388608 | tf_op jit(solution)/shard_map/pallas_call | solution.py:55
  (143 shorter events, 48.2 us)
Async XLA Ops:
  1.7 12.4 %collective-permute-start.2 = (bf16[128,384]{1,0:T(8,128)(2,1)S(1)}, bf16[128,384]{1,0:T(8,128)(2,1)S(1)}, u32[]{:S(2)}, u32[]{:S(2)}) collective-permute-start(bf16[128,384]{1,0:T(8,128)(2,1)S(1)} %constant_dynamic-slice_fusion), channel_id=1, source_target_pairs={{0,1},{1,0},{2,3},{3,2},{4,5},{5,4},{6,7},{7,6},{8,9},{9,8},{10,11... | collective-permute-start | bytes 294920 | tf_op jit(solution)/shard_map/ppermute | solution.py:836
  4.7 10.5 %collective-permute-start.3 = (bf16[128,384]{1,0:T(8,128)(2,1)S(1)}, bf16[128,384]{1,0:T(8,128)(2,1)S(1)}, u32[]{:S(2)}, u32[]{:S(2)}) collective-permute-start(bf16[128,384]{1,0:T(8,128)(2,1)S(1)} %constant_dynamic-slice_fusion), channel_id=1, source_target_pairs={{0,2},{1,3},{2,0},{3,1},{4,6},{5,7},{6,4},{7,5},{8,10},{9,11},{10,... | collective-permute-start | bytes 294920 | tf_op jit(solution)/shard_map/ppermute | solution.py:836
  7.3 7.9 %collective-permute-start.4 = (bf16[128,384]{1,0:T(8,128)(2,1)S(1)}, bf16[128,384]{1,0:T(8,128)(2,1)S(1)}, u32[]{:S(2)}, u32[]{:S(2)}) collective-permute-start(bf16[128,384]{1,0:T(8,128)(2,1)S(1)} %constant_dynamic-slice_fusion), channel_id=1, source_target_pairs={{0,3},{1,2},{2,1},{3,0},{4,7},{5,6},{6,5},{7,4},{8,11},{9,10},{10,... | collective-permute-start | bytes 294920 | tf_op jit(solution)/shard_map/ppermute | solution.py:836
  8.2 7.1 %collective-permute-start = (bf16[64,512]{1,0:T(8,128)(2,1)S(1)}, bf16[64,512]{1,0:T(8,128)(2,1)S(1)}, u32[]{:S(2)}, u32[]{:S(2)}) collective-permute-start(bf16[64,512]{1,0:T(8,128)(2,1)S(1)} %get-tuple-element.155), channel_id=1, source_target_pairs={{0,1},{1,2},{2,3},{4,5},{5,6},{6,7},{8,9},{9,10},{10,11},{12,13},{... | collective-permute-start | bytes 196616 | tf_op jit(solution)/shard_map/ppermute | solution.py:833
  17.2 11.0 %collective-permute-start.8 = (bf16[4,128,384]{2,1,0:T(8,128)(2,1)S(1)}, bf16[4,128,384]{2,1,0:T(8,128)(2,1)S(1)}, u32[]{:S(2)}, u32[]{:S(2)}) collective-permute-start(bf16[4,128,384]{2,1,0:T(8,128)(2,1)S(1)} %pad_maximum_fusion.1.refs_0_), channel_id=1, source_target_pairs={{0,8},{4,20},{8,0},{12,28},{16,24},{20,4},{24,16},{28,12},{1,9},{5... | collective-permute-start | bytes 1179656 | tf_op jit(solution)/shard_map/ppermute | solution.py:827
  18.7 10.0 %collective-permute-start.5 = (bf16[144,512]{1,0:T(8,128)(2,1)S(1)}, bf16[144,512]{1,0:T(8,128)(2,1)S(1)}, u32[]{:S(2)}, u32[]{:S(2)}) collective-permute-start(bf16[144,512]{1,0:T(8,128)(2,1)S(1)} %pad_maximum_fusion.2), channel_id=1, source_target_pairs={{0,1},{1,0},{2,3},{3,2},{4,5},{5,4},{6,7},{7,6},{8,9},{9,8},{10,11... | collective-permute-start | bytes 442376 | tf_op jit(solution)/shard_map/ppermute | solution.py:836
  20.7 12.1 %collective-permute-start.6 = (bf16[144,512]{1,0:T(8,128)(2,1)S(1)}, bf16[144,512]{1,0:T(8,128)(2,1)S(1)}, u32[]{:S(2)}, u32[]{:S(2)}) collective-permute-start(bf16[144,512]{1,0:T(8,128)(2,1)S(1)} %pad_maximum_fusion.2), channel_id=1, source_target_pairs={{0,2},{1,3},{2,0},{3,1},{4,6},{5,7},{6,4},{7,5},{8,10},{9,11},{10,... | collective-permute-start | bytes 442376 | tf_op jit(solution)/shard_map/ppermute | solution.py:836
  22.2 10.6 %collective-permute-start.7 = (bf16[144,512]{1,0:T(8,128)(2,1)S(1)}, bf16[144,512]{1,0:T(8,128)(2,1)S(1)}, u32[]{:S(2)}, u32[]{:S(2)}) collective-permute-start(bf16[144,512]{1,0:T(8,128)(2,1)S(1)} %pad_maximum_fusion.2), channel_id=1, source_target_pairs={{0,3},{1,2},{2,1},{3,0},{4,7},{5,6},{6,5},{7,4},{8,11},{9,10},{10,... | collective-permute-start | bytes 442376 | tf_op jit(solution)/shard_map/ppermute | solution.py:836
  28.1 7.6 %collective-permute-start.9 = (bf16[4,128,384]{2,1,0:T(8,128)(2,1)S(1)}, bf16[4,128,384]{2,1,0:T(8,128)(2,1)S(1)}, u32[]{:S(2)}, u32[]{:S(2)}) collective-permute-start(bf16[4,128,384]{2,1,0:T(8,128)(2,1)S(1)} %pad_maximum_fusion.1.refs_0_), channel_id=1, source_target_pairs={{0,4},{4,0},{8,12},{12,8},{16,20},{20,16},{24,28},{28,24},{1,5},{5... | collective-permute-start | bytes 1179656 | tf_op jit(solution)/shard_map/ppermute | solution.py:830
  28.2 7.6 %collective-permute-start.10 = (bf16[4,128,384]{2,1,0:T(8,128)(2,1)S(1)}, bf16[4,128,384]{2,1,0:T(8,128)(2,1)S(1)}, u32[]{:S(2)}, u32[]{:S(2)}) collective-permute-start(bf16[4,128,384]{2,1,0:T(8,128)(2,1)S(1)} %collective-permute-done.8.refs_1_), channel_id=1, source_target_pairs={{0,4},{4,0},{8,12},{12,8},{16,20},{20,16},{24,28},{28,24},{1,5},{5... | collective-permute-start | bytes 1179656 | tf_op jit(solution)/shard_map/ppermute | solution.py:830
  32.9 15.0 %collective-permute-start.12 = (bf16[4,144,512]{2,1,0:T(8,128)(2,1)S(1)}, bf16[4,144,512]{2,1,0:T(8,128)(2,1)S(1)}, u32[]{:S(2)}, u32[]{:S(2)}) collective-permute-start(bf16[4,144,512]{2,1,0:T(8,128)(2,1)S(1)} %pad_maximum_fusion.refs_0_), channel_id=1, source_target_pairs={{0,8},{4,20},{8,0},{12,28},{16,24},{20,4},{24,16},{28,12},{1,9},{5... | collective-permute-start | bytes 1769480 | tf_op jit(solution)/shard_map/ppermute | solution.py:827
  34.5 13.9 %collective-permute-start.14 = (bf16[4,144,512]{2,1,0:T(8,128)(2,1)S(1)}, bf16[4,144,512]{2,1,0:T(8,128)(2,1)}, u32[]{:S(2)}, u32[]{:S(2)}) collective-permute-start(bf16[4,144,512]{2,1,0:T(8,128)(2,1)S(1)} %pad_maximum_fusion.refs_0_), channel_id=1, source_target_pairs={{0,16},{4,12},{8,24},{12,4},{16,0},{20,28},{24,8},{28,20},{1,17},{... | collective-permute-start | bytes 1769480 | tf_op jit(solution)/shard_map/ppermute | solution.py:827
  43.7 12.7 %collective-permute-start.17 = (bf16[4,144,128]{2,1,0:T(8,128)(2,1)S(1)}, bf16[4,144,128]{2,1,0:T(8,128)(2,1)S(1)}, u32[]{:S(2)}, u32[]{:S(2)}) collective-permute-start(bf16[4,144,128]{2,1,0:T(8,128)(2,1)S(1)} %get-tuple-element.89.h0), channel_id=1, source_target_pairs={{0,2},{1,3},{2,0},{3,1},{4,6},{5,7},{6,4},{7,5},{8,10},{9,11},{10,... | collective-permute-start | bytes 442376 | tf_op jit(solution)/shard_map/ppermute | solution.py:836
  45.0 11.4 %collective-permute-start.18 = (bf16[4,144,128]{2,1,0:T(8,128)(2,1)S(1)}, bf16[4,144,128]{2,1,0:T(8,128)(2,1)S(1)}, u32[]{:S(2)}, u32[]{:S(2)}) collective-permute-start(bf16[4,144,128]{2,1,0:T(8,128)(2,1)S(1)} %get-tuple-element.89.h0), channel_id=1, source_target_pairs={{0,3},{1,2},{2,1},{3,0},{4,7},{5,6},{6,5},{7,4},{8,11},{9,10},{10,... | collective-permute-start | bytes 442376 | tf_op jit(solution)/shard_map/ppermute | solution.py:836
  47.9 10.9 %collective-permute-start.11 = (bf16[4,144,512]{2,1,0:T(8,128)(2,1)S(1)}, bf16[4,144,512]{2,1,0:T(8,128)(2,1)S(1)}, u32[]{:S(2)}, u32[]{:S(2)}) collective-permute-start(bf16[4,144,512]{2,1,0:T(8,128)(2,1)S(1)} %pad_maximum_fusion.refs_0_), channel_id=1, source_target_pairs={{0,4},{4,0},{8,12},{12,8},{16,20},{20,16},{24,28},{28,24},{1,5},{5... | collective-permute-start | bytes 1769480 | tf_op jit(solution)/shard_map/ppermute | solution.py:830
  47.9 10.9 %collective-permute-start.13 = (bf16[4,144,512]{2,1,0:T(8,128)(2,1)S(1)}, bf16[4,144,512]{2,1,0:T(8,128)(2,1)S(1)}, u32[]{:S(2)}, u32[]{:S(2)}) collective-permute-start(bf16[4,144,512]{2,1,0:T(8,128)(2,1)S(1)} %collective-permute-done.12.refs_1_), channel_id=1, source_target_pairs={{0,4},{4,0},{8,12},{12,8},{16,20},{20,16},{24,28},{28,24},{1,5},{5... | collective-permute-start | bytes 1769480 | tf_op jit(solution)/shard_map/ppermute | solution.py:830
  48.4 10.5 %collective-permute-start.15 = (bf16[4,144,512]{2,1,0:T(8,128)(2,1)}, bf16[4,144,512]{2,1,0:T(8,128)(2,1)}, u32[]{:S(2)}, u32[]{:S(2)}) collective-permute-start(bf16[4,144,512]{2,1,0:T(8,128)(2,1)} %collective-permute-done.14.refs_2_), channel_id=1, source_target_pairs={{0,4},{4,0},{8,12},{12,8},{16,20},{20,16},{24,28},{28,24},{1,5},{5... | collective-permute-start | bytes 1769480 | tf_op jit(solution)/shard_map/ppermute | solution.py:830
  57.0 12.7 %collective-permute-start.19 = (bf16[4,144,512]{2,1,0:T(8,128)(2,1)S(1)}, bf16[4,144,512]{2,1,0:T(8,128)(2,1)}, u32[]{:S(2)}, u32[]{:S(2)}) collective-permute-start(bf16[4,144,512]{2,1,0:T(8,128)(2,1)S(1)} %collective-permute-done.12.refs_1_), channel_id=1, source_target_pairs={{0,16},{4,12},{8,24},{12,4},{16,0},{20,28},{24,8},{28,20},{1,17},{... | collective-permute-start | bytes 1769480 | tf_op jit(solution)/shard_map/ppermute | solution.py:827
  65.3 26.5 %all-to-all-start = ((bf16[8,4,192,128]{3,2,1,0:T(8,128)(2,1)}), bf16[8,4,192,128]{3,2,1,0:T(8,128)(2,1)}, u32[]{:S(2)}, u32[]{:S(2)}) async-start(bf16[8,4,192,128]{3,2,1,0:T(8,128)(2,1)} %shard_map.238), calls=%async_computation | async-start | bytes 3145728 | tf_op jit(solution)/shard_map/all_to_all | solution.py:839
  91.8 13.0 %collective-permute-start.21 = (bf16[4,576,512]{2,1,0:T(8,128)(2,1)}, bf16[4,576,512]{2,1,0:T(8,128)(2,1)S(1)}, u32[]{:S(2)}, u32[]{:S(2)}) collective-permute-start(bf16[4,576,512]{2,1,0:T(8,128)(2,1)} %get-tuple-element.99), channel_id=1, source_target_pairs={{0,4},{4,0},{8,12},{12,8},{16,20},{20,16},{24,28},{28,24},{1,5},{5... | collective-permute-start | bytes 7077896 | tf_op jit(solution)/shard_map/ppermute | solution.py:830
  93.6 11.2 %collective-permute-start.23 = (bf16[4,176,128]{2,1,0:T(8,128)(2,1)S(1)}, bf16[4,176,128]{2,1,0:T(8,128)(2,1)S(1)}, u32[]{:S(2)}, u32[]{:S(2)}) collective-permute-start(bf16[4,176,128]{2,1,0:T(8,128)(2,1)S(1)} %get-tuple-element.101), channel_id=1, source_target_pairs={{0,3},{1,2},{2,1},{3,0},{4,7},{5,6},{6,5},{7,4},{8,11},{9,10},{10,... | collective-permute-start | bytes 540680 | tf_op jit(solution)/shard_map/ppermute | solution.py:836
  105.3 16.3 %collective-permute-start.25 = (bf16[4,576,256]{2,1,0:T(8,128)(2,1)S(1)}, bf16[4,576,256]{2,1,0:T(8,128)(2,1)S(1)}, u32[]{:S(2)}, u32[]{:S(2)}) collective-permute-start(bf16[4,576,256]{2,1,0:T(8,128)(2,1)S(1)} %get-tuple-element.103), channel_id=1, source_target_pairs={{0,8},{4,20},{8,0},{12,28},{16,24},{20,4},{24,16},{28,12},{1,9},{5... | collective-permute-start | bytes 3538952 | tf_op jit(solution)/shard_map/ppermute | solution.py:827
  107.0 9.0 %collective-permute-start.24 = (bf16[4,176,128]{2,1,0:T(8,128)(2,1)S(1)}, bf16[4,176,128]{2,1,0:T(8,128)(2,1)S(1)}, u32[]{:S(2)}, u32[]{:S(2)}) collective-permute-start(bf16[4,176,128]{2,1,0:T(8,128)(2,1)S(1)} %get-tuple-element.100.s0), channel_id=1, source_target_pairs={{0,2},{1,3},{2,0},{3,1},{4,6},{5,7},{6,4},{7,5},{8,10},{9,11},{10,... | collective-permute-start | bytes 540680 | tf_op jit(solution)/shard_map/ppermute | solution.py:836
  121.9 15.5 %collective-permute-start.27 = (bf16[4,576,128]{2,1,0:T(8,128)(2,1)S(1)}, bf16[4,576,128]{2,1,0:T(8,128)(2,1)S(1)}, u32[]{:S(2)}, u32[]{:S(2)}) collective-permute-start(bf16[4,576,128]{2,1,0:T(8,128)(2,1)S(1)} %get-tuple-element.122), channel_id=1, source_target_pairs={{0,16},{4,12},{8,24},{12,4},{16,0},{20,28},{24,8},{28,20},{1,17},{... | collective-permute-start | bytes 1769480 | tf_op jit(solution)/shard_map/ppermute | solution.py:827
  125.3 10.3 %collective-permute-start.28 = (bf16[4,192,256]{2,1,0:T(8,128)(2,1)S(1)}, bf16[4,192,256]{2,1,0:T(8,128)(2,1)S(1)}, u32[]{:S(2)}, u32[]{:S(2)}) collective-permute-start(bf16[4,192,256]{2,1,0:T(8,128)(2,1)S(1)} %get-tuple-element.114), channel_id=1, source_target_pairs={{0,8},{4,20},{8,0},{12,28},{16,24},{20,4},{24,16},{28,12},{1,9},{5... | collective-permute-start | bytes 1179656 | tf_op jit(solution)/shard_map/ppermute | solution.py:827
  138.0 8.4 %collective-permute-start.30 = (bf16[1,576,128]{2,1,0:T(8,128)(2,1)S(1)}, bf16[1,576,128]{2,1,0:T(8,128)(2,1)S(1)}, u32[]{:S(2)}, u32[]{:S(2)}) collective-permute-start(bf16[1,576,128]{2,1,0:T(8,128)(2,1)S(1)} %get-tuple-element.132), channel_id=1, source_target_pairs={{0,1},{1,0},{2,3},{3,2},{4,5},{5,4},{6,7},{7,6},{8,9},{9,8},{10,11... | collective-permute-start | bytes 442376 | tf_op jit(solution)/shard_map/ppermute | solution.py:836
  138.1 14.0 %collective-permute-start.31 = (bf16[1,576,128]{2,1,0:T(8,128)(2,1)S(1)}, bf16[1,576,128]{2,1,0:T(8,128)(2,1)S(1)}, u32[]{:S(2)}, u32[]{:S(2)}) collective-permute-start(bf16[1,576,128]{2,1,0:T(8,128)(2,1)S(1)} %get-tuple-element.133), channel_id=1, source_target_pairs={{0,2},{1,3},{2,0},{3,1},{4,6},{5,7},{6,4},{7,5},{8,10},{9,11},{10,... | collective-permute-start | bytes 442376 | tf_op jit(solution)/shard_map/ppermute | solution.py:836
  140.1 12.0 %collective-permute-start.32 = (bf16[1,576,128]{2,1,0:T(8,128)(2,1)S(1)}, bf16[1,576,128]{2,1,0:T(8,128)(2,1)S(1)}, u32[]{:S(2)}, u32[]{:S(2)}) collective-permute-start(bf16[1,576,128]{2,1,0:T(8,128)(2,1)S(1)} %get-tuple-element.134), channel_id=1, source_target_pairs={{0,3},{1,2},{2,1},{3,0},{4,7},{5,6},{6,5},{7,4},{8,11},{9,10},{10,... | collective-permute-start | bytes 442376 | tf_op jit(solution)/shard_map/ppermute | solution.py:836
  153.2 11.7 %collective-permute-start.33 = (bf16[1152,128]{1,0:T(8,128)(2,1)S(1)}, bf16[1152,128]{1,0:T(8,128)(2,1)S(1)}, u32[]{:S(2)}, u32[]{:S(2)}) collective-permute-start(bf16[1152,128]{1,0:T(8,128)(2,1)S(1)} %shard_map.253.refs_0_), channel_id=1, source_target_pairs={{0,8},{4,20},{8,0},{12,28},{16,24},{20,4},{24,16},{28,12},{1,9},{5... | collective-permute-start | bytes 884744 | tf_op jit(solution)/shard_map/ppermute | solution.py:827
  156.6 7.5 %collective-permute-start.36 = (bf16[1,224,128]{2,1,0:T(8,128)(2,1)S(1)}, bf16[1,224,128]{2,1,0:T(8,128)(2,1)S(1)}, u32[]{:S(2)}, u32[]{:S(2)}) collective-permute-start(bf16[1,224,128]{2,1,0:T(8,128)(2,1)S(1)} %get-tuple-element.136), channel_id=1, source_target_pairs={{0,2},{1,3},{2,0},{3,1},{4,6},{5,7},{6,4},{7,5},{8,10},{9,11},{10,... | collective-permute-start | bytes 172040 | tf_op jit(solution)/shard_map/ppermute | solution.py:836
  159.1 13.9 %collective-permute-start.34 = (bf16[1152,128]{1,0:T(8,128)(2,1)S(1)}, bf16[1152,128]{1,0:T(8,128)(2,1)S(1)}, u32[]{:S(2)}, u32[]{:S(2)}) collective-permute-start(bf16[1152,128]{1,0:T(8,128)(2,1)S(1)} %shard_map.253.refs_0_), channel_id=1, source_target_pairs={{0,16},{4,12},{8,24},{12,4},{16,0},{20,28},{24,8},{28,20},{1,17},{... | collective-permute-start | bytes 884744 | tf_op jit(solution)/shard_map/ppermute | solution.py:827
  164.9 8.5 %collective-permute-start.38 = (bf16[1152,128]{1,0:T(8,128)(2,1)S(1)}, bf16[1152,128]{1,0:T(8,128)(2,1)S(1)}, u32[]{:S(2)}, u32[]{:S(2)}) collective-permute-start(bf16[1152,128]{1,0:T(8,128)(2,1)S(1)} %collective-permute-done.33.refs_1_), channel_id=1, source_target_pairs={{0,16},{4,12},{8,24},{12,4},{16,0},{20,28},{24,8},{28,20},{1,17},{... | collective-permute-start | bytes 884744 | tf_op jit(solution)/shard_map/ppermute | solution.py:827
  (40 other events, 306.9 us)
